TPU v7x, 128 devices: a whole 4x4x4 slice. The times are simulated.
128 devices in a mesh: row: 8 (over x, core), col: 16 (over z, y).
Axes of the slice: x: 4, y: 4, z: 4, core: 2. Of those that a mesh axis runs over, the one named last changes fastest.
Arguments:
- rhs: float32 [65536, 1024], P('col', 'row'), may hold values from -6 to 6
- factors: bfloat16 [65536, 2048], P('col', 'row'), may hold values from -0.15625 to 0.15625
- diag_inv: float32 [4, 512, 512], replicated, may hold values from -2 to 2, as said below
Outputs:
- solution: float32 [65536, 1024], P('col', 'row')
Inputs may be any that keep to these rules, and one draw needn't show every extreme that they name: `diag_inv`: entries off the diagonal of each block lie within 2 / sqrt(512) in magnitude; diagonal entries lie in 0.5 to 2.
All inputs are finite; a program needn't handle non-finite values.
Results may differ from a plain program's by a relative error of at most 0.0038.
Values may be sent and summed in bfloat16 or wider, within the bound.
No kernel may reach another device: no remote copies, remote signals or barrier semaphores. Data moves between devices by JAX's collectives and lax.ppermute only.
A program may use at most 128 MiB of HBM per device.

v0:
```python
import jax
import jax.numpy as jnp
from jax import lax
from jax.sharding import PartitionSpec as P


def body(rhs, factors, diag_inv):
    rows_dev = rhs.shape[0]
    steps = diag_inv.shape[0]
    block = diag_inv.shape[1]
    col_count = lax.axis_size("col")
    block_span = rows_dev * col_count // steps
    my_index = lax.axis_index("col")
    global_rows = my_index * rows_dev + jnp.arange(rows_dev)
    index = jnp.arange(block)
    strict_lower = index[:, None] > index[None, :]
    eye = jnp.eye(block, dtype=jnp.float32)
    panel_rows = lax.all_gather(factors, "row", axis=1, tiled=True)

    def solve_block(matrix, work, step):
        owner_index = step * col_count // steps
        owner = my_index == owner_index
        product = jnp.dot(
            matrix,
            work[:block],
            precision=lax.Precision.HIGHEST,
            preferred_element_type=jnp.float32,
        )
        solved = lax.psum(jnp.where(owner, product, jnp.float32(0.0)), "col")
        return (solved, owner)

    def apply_update(work, solved, owner, columns, row_mask):
        product = jnp.dot(columns, solved.astype(jnp.bfloat16), preferred_element_type=jnp.float32)
        updated = jnp.where(row_mask[:, None], work - product, work)
        leading = jnp.where(owner, solved, updated[:block])
        return jnp.concatenate([leading, updated[block:]], axis=0)

    work = rhs
    kept_columns = []
    for step in range(steps):
        lower_inv = jnp.where(strict_lower, diag_inv[step], jnp.float32(0.0)) + eye
        solved, owner = solve_block(lower_inv, work, step)
        columns = panel_rows[:, step * block : (step + 1) * block]
        kept_columns.append(columns)
        row_mask = global_rows >= step * block_span + block
        work = apply_update(work, solved, owner, columns, row_mask)
    for step in reversed(range(steps)):
        upper_inv = jnp.triu(diag_inv[step])
        solved, owner = solve_block(upper_inv, work, step)
        row_mask = global_rows < step * block_span
        work = apply_update(work, solved, owner, kept_columns[step], row_mask)
    return work


def solution(mesh):
    placed = (P("col", "row"), P("col", "row"), P())
    return jax.shard_map(
        body, mesh=mesh, in_specs=placed, out_specs=P("col", "row"), check_vma=False
    )
```

profile of v0, /device:TPU:1, one launch (start us, length us, event | category | flops | bytes accessed | tf_op | source)
XLA Modules:
  0.0 755.8 jit_solution(6097432575748463576)
XLA Ops:
  7.4 0.0 all-reduce.9.cloned.1.call-start
  7.4 3.0 convolution_select_fusion.7
  10.3 0.0 all-reduce.9.cloned.1.call-update
  10.4 0.0 all-gather.2.cloned.1.call-start
  10.4 0.5 all-gather.2.cloned.1.call-update
  10.9 0.0 all-reduce.11.cloned.1.call-start
  11.0 86.8 %all-reduce.9.cloned.1.call-done = f32[512,128]{1,0:T(8,128)} async-done(((f32[512,128]{1,0:T(8,128)}), f32[512,128]{1,0:T(8,128)}) %all-reduce.9.cloned.1.call-update) | async-done | bytes 262160 | tf_op jit(solution)/shard_map/psum | solution.py:29
  97.8 0.0 copy-start
  97.8 8.3 %all-gather.2.cloned.1.call-done = bf16[4096,2048]{1,0:T(8,128)(2,1)} async-done(((bf16[4096,256]{1,0:T(8,128)(2,1)}), bf16[4096,2048]{1,0:T(8,128)(2,1)}) %all-gather.2.cloned.1.call-update) | async-done | bytes 16777232 | tf_op jit(solution)/shard_map/all_gather | solution.py:18
  106.1 3.6 fusion.15
  109.7 0.0 copy-done
  109.8 2.9 convolution_select_fusion.6
  112.7 0.0 all-reduce.11.cloned.1.call-update
  112.7 0.0 all-reduce.13.cloned.1.call-start
  112.8 1.3 slice.106
  114.1 82.4 %all-reduce.11.cloned.1.call-done = f32[512,128]{1,0:T(8,128)} async-done(((f32[512,128]{1,0:T(8,128)}), f32[512,128]{1,0:T(8,128)}) %all-reduce.11.cloned.1.call-update) | async-done | bytes 262160 | tf_op jit(solution)/shard_map/psum | solution.py:29
  196.5 0.0 copy-start.2
  196.5 4.1 fusion.13
  200.6 0.0 copy-done.2
  200.6 2.9 convolution_select_fusion.5
  203.6 0.0 all-reduce.13.cloned.1.call-update
  203.6 0.0 all-reduce.15.cloned.1.call-start
  203.7 1.3 slice.109
  205.0 82.4 %all-reduce.13.cloned.1.call-done = f32[512,128]{1,0:T(8,128)} async-done(((f32[512,128]{1,0:T(8,128)}), f32[512,128]{1,0:T(8,128)}) %all-reduce.13.cloned.1.call-update) | async-done | bytes 262160 | tf_op jit(solution)/shard_map/psum | solution.py:29
  287.4 0.0 copy-start.1
  287.4 4.1 fusion.11
  291.5 0.0 copy-done.1
  291.5 2.9 convolution_select_fusion.4
  294.4 0.0 all-reduce.15.cloned.1.call-update
  294.5 0.0 all-reduce.17.cloned.1.call-start
  294.5 1.3 slice.112
  295.9 82.4 %all-reduce.15.cloned.1.call-done = f32[512,128]{1,0:T(8,128)} async-done(((f32[512,128]{1,0:T(8,128)}), f32[512,128]{1,0:T(8,128)}) %all-reduce.15.cloned.1.call-update) | async-done | bytes 262160 | tf_op jit(solution)/shard_map/psum | solution.py:29
  378.3 4.2 fusion.9
  382.5 0.0 copy-done.4
  382.5 3.0 convolution_select_fusion.3
  385.5 0.0 all-reduce.17.cloned.1.call-update
  385.5 0.0 all-reduce.19.cloned.1.call-start
  385.6 1.3 slice.115
  387.0 82.4 %all-reduce.17.cloned.1.call-done = f32[512,128]{1,0:T(8,128)} async-done(((f32[512,128]{1,0:T(8,128)}), f32[512,128]{1,0:T(8,128)}) %all-reduce.17.cloned.1.call-update) | async-done | bytes 262160 | tf_op jit(solution)/shard_map/psum | solution.py:29
  469.4 4.2 fusion.7
  473.6 0.0 copy-done.5
  473.6 3.0 convolution_select_fusion.2
  476.6 0.0 all-reduce.19.cloned.1.call-update
  476.6 0.2 all-reduce.21.cloned.1.call-start
  476.9 1.3 slice.117
  478.2 82.2 %all-reduce.19.cloned.1.call-done = f32[512,128]{1,0:T(8,128)} async-done(((f32[512,128]{1,0:T(8,128)}), f32[512,128]{1,0:T(8,128)}) %all-reduce.19.cloned.1.call-update) | async-done | bytes 262160 | tf_op jit(solution)/shard_map/psum | solution.py:29
  560.4 4.1 fusion.5
  564.5 0.0 copy-done.6
  564.6 3.0 convolution_select_fusion.1
  567.6 0.0 all-reduce.21.cloned.1.call-update
  567.6 0.0 all-reduce.23.cloned.1.call-start
  567.7 1.3 slice.119
  569.0 82.4 %all-reduce.21.cloned.1.call-done = f32[512,128]{1,0:T(8,128)} async-done(((f32[512,128]{1,0:T(8,128)}), f32[512,128]{1,0:T(8,128)}) %all-reduce.21.cloned.1.call-update) | async-done | bytes 262160 | tf_op jit(solution)/shard_map/psum | solution.py:29
  651.4 4.1 fusion.3
  655.5 0.0 copy-done.7
  655.6 3.0 convolution_select_fusion
  658.5 0.0 all-reduce.23.cloned.1.call-update
  658.6 1.3 slice.121
  659.9 82.4 %all-reduce.23.cloned.1.call-done = f32[512,128]{1,0:T(8,128)} async-done(((f32[512,128]{1,0:T(8,128)}), f32[512,128]{1,0:T(8,128)}) %all-reduce.23.cloned.1.call-update) | async-done | bytes 262160 | tf_op jit(solution)/shard_map/psum | solution.py:29
  742.4 3.6 fusion.1
  745.9 0.0 copy-start.3
  745.9 0.1 slice.123
  746.1 0.8 copy-done.3
  746.9 1.5 pad_maximum_fusion
  (21 shorter events, 0.4 us)
Async XLA Ops:
  7.4 90.4 %all-reduce.9.cloned.1.call-start = ((), (), s32[]{:S(2)}) async-start(), calls=%async_computation | async-start | bytes 524288 | tf_op jit(solution)/shard_map/psum | solution.py:29
  10.4 95.7 %all-gather.2.cloned.1.call-start = ((), (), s32[]{:S(2)}) async-start(), calls=%async_computation.1 | async-start | bytes 18874368 | tf_op jit(solution)/shard_map/all_gather | solution.py:18
  10.9 185.5 %all-reduce.11.cloned.1.call-start = ((), (), s32[]{:S(2)}) async-start(), calls=%async_computation.2 | async-start | bytes 524288 | tf_op jit(solution)/shard_map/psum | solution.py:29
  97.8 12.0 %copy-start = (f32[512,128]{1,0:T(8,128)S(1)}, f32[512,128]{1,0:T(8,128)}, u32[]{:S(2)}) copy-start(f32[512,128]{1,0:T(8,128)} %all-reduce.9.cloned.1.call-done) | copy-start | bytes 786436
  112.7 174.7 %all-reduce.13.cloned.1.call-start = ((), (), s32[]{:S(2)}) async-start(), calls=%async_computation.3 | async-start | bytes 524288 | tf_op jit(solution)/shard_map/psum | solution.py:29
  196.5 4.1 copy-start.2
  203.6 174.7 %all-reduce.15.cloned.1.call-start = ((), (), s32[]{:S(2)}) async-start(), calls=%async_computation.4 | async-start | bytes 524288 | tf_op jit(solution)/shard_map/psum | solution.py:29
  287.4 4.1 copy-start.1
  294.5 174.9 %all-reduce.17.cloned.1.call-start = ((), (), s32[]{:S(2)}) async-start(), calls=%async_computation.5 | async-start | bytes 524288 | tf_op jit(solution)/shard_map/psum | solution.py:29
  378.3 4.2 copy-start.4
  385.5 174.9 %all-reduce.19.cloned.1.call-start = ((), (), s32[]{:S(2)}) async-start(), calls=%async_computation.6 | async-start | bytes 524288 | tf_op jit(solution)/shard_map/psum | solution.py:29
  469.4 4.2 copy-start.5
  476.6 174.8 %all-reduce.21.cloned.1.call-start = ((), (), s32[]{:S(2)}) async-start(), calls=%async_computation.7 | async-start | bytes 524288 | tf_op jit(solution)/shard_map/psum | solution.py:29
  560.4 4.1 copy-start.6
  567.6 174.8 %all-reduce.23.cloned.1.call-start = ((), (), s32[]{:S(2)}) async-start(), calls=%async_computation.8 | async-start | bytes 524288 | tf_op jit(solution)/shard_map/psum | solution.py:29
  651.4 4.1 copy-start.7
  745.9 1.0 copy-start.3
Sparse Core Ops, SparseCore 0:
  11.4 86.3 all-reduce.8
  112.8 83.6 all-reduce.10
  203.7 83.6 all-reduce.12
  294.6 83.6 all-reduce.14
  385.7 83.6 all-reduce.16
  476.8 83.6 all-reduce.18
  567.7 83.6 all-reduce.20
  658.7 83.6 all-reduce.22
Sparse Core Ops, SparseCore 1:
  12.5 93.5 all-gather.1
where the time goes:
time: 757 us; the launch traced here: 756 us
  waiting for transfers between devices  672 us (89%)
  matrix products  55.6 us (7%)
  between operations  15.2 us (2%)
  local copies, waits for them, and re-layouts  10.4 us (1%)
    psum x8, waiting for transfers between devices, solve_block(): solved = lax.psum(jnp.where(owner, product, jnp.float32(0.0)), 'col')  663 us
    dot_general x8, matrix products, apply_update(): jnp.dot(columns, solved.astype(jnp.bfloat16), preferred_element_type=jnp....  32 us
    dot_general x8, matrix products, solve_block(): jnp.dot(matrix, work[:block], precision=lax.Precision.HIGHEST, preferred_...  23.6 us
  transfers between devices with their start and end apart: 9, of which 9 were waited for; matrix products, arithmetic and copies ran while one was open for 1% of the time, Pallas kernels for 0%

commit v1 on v0

v1 whole, which is shorter than its diff:
```python
import functools

import jax
import jax.numpy as jnp
from jax import lax
from jax.experimental import pallas as pl
from jax.experimental.pallas import tpu as pltpu
from jax.sharding import PartitionSpec as P

NX, NH, NZ, NY = 4, 2, 4, 4
NB = 512
HB = 256
F32, BF16 = jnp.float32, jnp.bfloat16


def pairs(move):
    out = []
    for r in range(NX * NH):
        for c in range(NZ * NY):
            x, h = divmod(r, NH)
            z, y = divmod(c, NY)
            to = move(x, h, z, y)
            if to is not None:
                x2, h2, z2, y2 = to
                out.append((r * NZ * NY + c, ((x2 % NX) * NH + h2 % NH) * NZ * NY + (z2 % NZ) * NY + y2 % NY))
    return out


def send(value, move):
    return lax.ppermute(value, ("row", "col"), pairs(move))


def x_plus(x, h, z, y):
    return (x + 1, h, z, y)


def x_minus(x, h, z, y):
    return (x - 1, h, z, y)


def other_core(x, h, z, y):
    return (x, 1 - h, z, y)


def z_move(src, dst):
    return lambda x, h, z, y: (x, h, dst, y) if (y == 0 and z == src) else None


def y_move(step):
    return lambda x, h, z, y: (x, h, z, step) if y == 0 else None


def dot(a, b):
    return jnp.dot(a, b, preferred_element_type=F32)


def split(a):
    hi = a.astype(BF16)
    return hi, (a - hi.astype(F32)).astype(BF16)


def tri_dot(matrix, v):
    mh, ml = split(matrix)
    vh, vl = split(v)
    return dot(mh, vh) + (dot(mh, vl) + dot(ml, vh))


def lower_mask(d):
    i = lax.broadcasted_iota(jnp.int32, d.shape, 0)
    j = lax.broadcasted_iota(jnp.int32, d.shape, 1)
    return jnp.where(i > j, d, 0.0)


def upper_mask(d):
    i = lax.broadcasted_iota(jnp.int32, d.shape, 0)
    j = lax.broadcasted_iota(jnp.int32, d.shape, 1)
    return jnp.where(i <= j, d, 0.0)


def start_kernel(ids, b_ref, d_ref, y_ref, yb_ref):
    w = b_ref[...]
    y = w + tri_dot(lower_mask(d_ref[0]), w)
    y_ref[...] = y
    yb_ref[...] = y.astype(BF16)


def block_product(ids, blocks, j, v_ref, acc_ref):
    x, h = ids[0], ids[1]
    for d in range(NX):
        @pl.when(lax.rem(x + d, NX) == j)
        def _():
            same, other = blocks[2 * d], blocks[2 * d + 1]
            acc_ref[...] -= dot(same[...], v_ref[pl.ds(pl.multiple_of(h * HB, HB), HB), :]) + dot(
                other[...], v_ref[pl.ds(pl.multiple_of((1 - h) * HB, HB), HB), :]
            )


def forward_kernel(j, ids, w_ref, v_ref, d_ref, *rest):
    blocks, (w_out, y_ref, yb_ref) = rest[:8], rest[8:]
    w_out[...] = w_ref[...]
    block_product(ids, blocks, j, v_ref, w_out)
    w = w_out[...]
    y = w + tri_dot(lower_mask(d_ref[0]), w)
    y_ref[...] = y
    yb_ref[...] = y.astype(BF16)


def turn_kernel(ids, w_ref, y1_ref, y2_ref, d_ref, p_same, p_other, *rest):
    blocks, (y_ref, yb_ref, x_ref, acc) = rest[:8], rest[8:]
    h = ids[1]
    acc[...] = w_ref[...]
    block_product(ids, blocks, 2, y2_ref, acc)
    w = acc[...]
    y3 = w + tri_dot(lower_mask(d_ref[3]), w)
    y_ref[...] = y3
    yb_ref[...] = y3.astype(BF16)

    def prefetched(slot, row):
        cols = slice(slot * HB, (slot + 1) * HB)
        return dot(p_same[:, cols], x_ref[pl.ds(pl.multiple_of(row + h * HB, HB), HB), :]) + dot(
            p_other[:, cols], x_ref[pl.ds(pl.multiple_of(row + (1 - h) * HB, HB), HB), :]
        )

    x_ref[2 * NB : 3 * NB, :] = tri_dot(upper_mask(d_ref[3]), y3).astype(BF16)
    t = y2_ref[...].astype(F32) - prefetched(0, 2 * NB)
    x_ref[NB : 2 * NB, :] = tri_dot(upper_mask(d_ref[2]), t).astype(BF16)
    t = y1_ref[...].astype(F32) - prefetched(1, NB) - prefetched(2, 2 * NB)
    x_ref[0:NB, :] = tri_dot(upper_mask(d_ref[1]), t).astype(BF16)


def window_kernel(ids, out_in, y_ref, v0_ref, v_ref, d_ref, *rest):
    blocks, (out_ref, acc) = rest[:8], rest[8:]
    x, h, z, owner = ids[0], ids[1], ids[2], ids[3] == 0
    acc[...] = jnp.where(owner, y_ref[...], out_in[...])
    for d in range(NX):
        j = lax.rem(x + d, NX)
        for s in range(2):
            part = h if s == 0 else 1 - h

            @pl.when(jnp.logical_and(j == 0, jnp.logical_not(owner)))
            def _():
                acc[...] -= dot(blocks[2 * d + s][...], v0_ref[pl.ds(pl.multiple_of(part * HB, HB), HB), :])

            @pl.when(jnp.logical_and(j > 0, jnp.logical_or(jnp.logical_not(owner), j > z)))
            def _():
                acc[...] -= dot(
                    blocks[2 * d + s][...], v_ref[pl.ds(pl.multiple_of((j - 1) * NB + part * HB, HB), HB), :]
                )

    @pl.when(owner)
    def _():
        out_ref[...] = tri_dot(upper_mask(d_ref[0]), acc[...])

    @pl.when(jnp.logical_not(owner))
    def _():
        out_ref[...] = acc[...]


def rows_kernel(ids, out_in, v_ref, *rest):
    blocks, out_ref = rest[:8], rest[8]
    x, h = ids[0], ids[1]
    acc = out_in[...]
    for d in range(NX):
        j = lax.rem(x + d, NX)
        for s in range(2):
            part = h if s == 0 else 1 - h
            acc -= dot(blocks[2 * d + s][...], v_ref[pl.ds(pl.multiple_of(j * NB + part * HB, HB), HB), :])
    out_ref[...] = acc


def whole(shape):
    return pl.BlockSpec(shape, lambda i, ids: (0,) * len(shape))


def diag_spec():
    return pl.BlockSpec((1, NB, NB), lambda i, ids: (ids[2], 0, 0))


def call(kernel, ids, args, specs, outs, out_specs, scratch=(), grid=(1,), aliases={}, flops=0):
    moved = sum(a.size * a.dtype.itemsize for a in args)
    return pl.pallas_call(
        kernel,
        grid_spec=pltpu.PrefetchScalarGridSpec(
            num_scalar_prefetch=1, grid=grid, in_specs=specs, out_specs=out_specs, scratch_shapes=scratch
        ),
        out_shape=outs,
        input_output_aliases=aliases,
        cost_estimate=pl.CostEstimate(flops=flops, bytes_accessed=moved, transcendentals=0),
        compiler_params=pltpu.CompilerParams(vmem_limit_bytes=48 * 1024 * 1024),
    )(ids, *args)


def ring(own):
    half = own.shape[0] // 2
    before = send(own, x_plus)
    after = send(own, x_minus)
    top = send(before[:half], x_plus)
    bottom = send(after[half:], x_minus)
    return before, after, top, bottom


def body(rhs, factors, diag_inv):
    rows, cols = rhs.shape
    r, c = lax.axis_index("row"), lax.axis_index("col")
    x, h, z, y = r // NH, r % NH, c // NY, c % NY
    ids = jnp.stack([x, h, z, y]).astype(jnp.int32)
    owner = y == 0
    vec = jax.ShapeDtypeStruct((NB, cols), F32)
    vecb = jax.ShapeDtypeStruct((NB, cols), BF16)
    vspec = whole((NB, cols))

    own0, own1 = factors[:NB], factors[NB:]
    before0, after0, top0, bottom0 = ring(own0)
    far0 = jnp.concatenate([top0, bottom0], axis=0)
    same0 = [own0, after0, far0, before0]
    window = [b for s in same0 for b in (s, send(s, other_core))]
    before1, after1, top1, bottom1 = ring(own1)
    o1, a1, b1, t1, u1 = (send(v, other_core) for v in (own1, after1, before1, top1, bottom1))

    wspecs = [whole((NB, HB))] * 8
    base = rhs[:NB]
    flops = 2 * NB * NB * cols * 4
    y_z0, yb = call(start_kernel, ids, (base, diag_inv), [vspec, diag_spec()], (vec, vecb), (vspec, vspec), flops=flops)
    moves = [send(yb, z_move(0, t)) for t in (1, 2, 3)]
    y0 = jnp.where(z == 0, yb, moves[0] + moves[1] + moves[2])
    early = [send(y0, y_move(t)) for t in (1, 2, 3)]
    v0 = jnp.where(owner, y0, early[0] + early[1] + early[2])

    def forward(j, w, v):
        return call(
            functools.partial(forward_kernel, j), ids, (w, v, diag_inv, *window),
            [vspec, vspec, diag_spec(), *wspecs], (vec, vec, vecb), (vspec, vspec, vspec), flops=2 * flops,
        )

    w, y_z1, yb = forward(0, base, y0)
    moves = [send(yb, z_move(1, t)) for t in (2, 3)]
    y1 = jnp.where(z == 1, yb, moves[0] + moves[1])
    w, y_z2, yb = forward(1, w, y1)
    y2_in = send(yb, z_move(2, 3))
    y2 = jnp.where(z == 2, yb, y2_in)

    def pick(j):
        d = (j - x + NX) % NX
        return jnp.where(d == 0, same0[0], jnp.where(d == 1, same0[1], jnp.where(d == 2, same0[2], same0[3])))

    p23 = send(pick(3), z_move(2, 3))
    p1 = send(jnp.concatenate([pick(2), pick(3)], axis=1), z_move(1, 3))
    p_same = jnp.concatenate([p23, p1], axis=1)
    p_other = send(p_same, other_core)

    pspec = whole((NB, 3 * HB))
    y_z3, yb3, xs = call(
        turn_kernel, ids, (w, y1, y2, diag_inv, p_same, p_other, *window),
        [vspec, vspec, vspec, whole((4, NB, NB)), pspec, pspec, *wspecs],
        (vec, vecb, jax.ShapeDtypeStruct((3 * NB, cols), BF16)), (vspec, vspec, whole((3 * NB, cols))),
        scratch=[pltpu.VMEM((NB, cols), F32)], flops=6 * flops,
    )
    to0 = send(xs, z_move(3, 0))
    to1 = send(xs[NB:], z_move(3, 1))
    to2 = send(xs[2 * NB :], z_move(3, 2))
    x1 = to0[:NB]
    x2 = to0[NB : 2 * NB] + to1[:NB]
    x3 = to0[2 * NB :] + to1[NB:] + to2
    late = jnp.concatenate(
        [jnp.where(z >= 1, y1, x1), jnp.where(z >= 2, y2, x2), jnp.where(z >= 3, yb3, x3)], axis=0
    )
    spread = [send(late, y_move(t)) for t in (1, 2, 3)]
    v = jnp.where(owner, late, spread[0] + spread[1] + spread[2])
    y_own = jnp.where(z == 0, y_z0, jnp.where(z == 1, y_z1, jnp.where(z == 2, y_z2, y_z3)))

    rest = rows - NB
    tile = 256
    half_tiles = rest // 2 // tile
    v_all = jnp.concatenate([v0, v], axis=0)
    out = rhs
    for first, far, far_other in ((0, top1, t1), (half_tiles, bottom1, u1)):
        near = pl.BlockSpec((tile, HB), lambda i, ids, first=first: (first + i, 0))
        local = pl.BlockSpec((tile, HB), lambda i, ids: (i, 0))
        ospec = pl.BlockSpec((tile, cols), lambda i, ids, first=first: (NB // tile + first + i, 0))
        out = call(
            rows_kernel, ids, (out, v_all, own1, o1, after1, a1, far, far_other, before1, b1),
            [ospec, whole((4 * NB, cols)), near, near, near, near, local, local, near, near],
            jax.ShapeDtypeStruct(out.shape, F32), ospec, grid=(half_tiles,), aliases={1: 0}, flops=rest * 4 * NB * cols,
        )
    ospec = pl.BlockSpec((NB, cols), lambda i, ids: (0, 0))
    return call(
        window_kernel, ids, (out, y_own, v0, v, diag_inv, *window),
        [ospec, vspec, vspec, whole((3 * NB, cols)), diag_spec(), *wspecs],
        jax.ShapeDtypeStruct(out.shape, F32), ospec, scratch=[pltpu.VMEM((NB, cols), F32)], aliases={1: 0},
        flops=2 * flops,
    )


def solution(mesh):
    placed = (P("col", "row"), P("col", "row"), P())
    return jax.shard_map(body, mesh=mesh, in_specs=placed, out_specs=P("col", "row"), check_vma=False)
```

time: 757 us -> 175 us (0.23)
  the two profiles are of different devices: /device:TPU:1 before, /device:TPU:87 now
where the time goes in v1:
time: 175 us; the launch traced here: 174 us
  waiting for transfers between devices  64.7 us (37%)
  Pallas kernels  36.5 us (21%)
  starting transfers between devices  36 us (21%)
  local copies, waits for them, and re-layouts  27.3 us (16%)
  other arithmetic  8.89 us (5%)
    ppermute x35, waiting for transfers between devices, send(): return lax.ppermute(value, ('row', 'col'), pairs(move))  64.7 us
    pallas_call x7, Pallas kernels, call(): pl.pallas_call(kernel, grid_spec=pltpu.PrefetchScalarGridSpec(num_scalar_...  36.5 us
    ppermute x35, starting transfers between devices, send(): return lax.ppermute(value, ('row', 'col'), pairs(move))  36 us
    unnamed x75, local copies, waits for them, and re-layouts  16.7 us
  transfers between devices with their start and end apart: 35, of which 6 were waited for; matrix products, arithmetic and copies ran while one was open for 11% of the time, Pallas kernels for 14%

profile of v1, /device:TPU:87, one launch (start us, length us, event | category | flops | bytes accessed | tf_op | source)
XLA Modules:
  0.0 174.0 jit_solution(14834635674746929762)
XLA Ops:
  0.0 3.0 %copy.13.out_in = f32[4096,128]{1,0:T(8,128)} copy(f32[4096,128]{1,0:T(8,128)} %param.3) | data formatting | bytes 4194304
  3.0 1.0 slice.43.rest_0_
  4.3 1.3 collective-permute-start.7
  5.6 5.7 %collective-permute-done.9.rest_6_ = bf16[512,256]{1,0:T(8,128)(2,1)S(1)} collective-permute-done((bf16[512,256]{1,0:T(8,128)(2,1)S(1)}, bf16[512,256]{1,0:T(8,128)(2,1)S(1)}, u32[]{:S(2)}, u32[]{:S(2)}) %collective-permute-start.9) | collective-permute-done | bytes 262176 | tf_op jit(solution)/shard_map/ppermute | solution.py:30
  11.3 1.5 collective-permute-start.10
  12.9 2.2 %collective-permute-done.10 = bf16[256,256]{1,0:T(8,128)(2,1)S(1)} collective-permute-done((bf16[256,256]{1,0:T(8,128)(2,1)S(1)}, bf16[256,256]{1,0:T(8,128)(2,1)S(1)}, u32[]{:S(2)}, u32[]{:S(2)}) %collective-permute-start.10) | collective-permute-done | bytes 131104 | tf_op jit(solution)/shard_map/ppermute | solution.py:30
  15.2 2.7 %collective-permute-done.11 = bf16[256,256]{1,0:T(8,128)(2,1)S(1)} collective-permute-done((bf16[256,256]{1,0:T(8,128)(2,1)S(1)}, bf16[256,256]{1,0:T(8,128)(2,1)S(1)}, u32[]{:S(2)}, u32[]{:S(2)}) %collective-permute-start.11) | collective-permute-done | bytes 131104 | tf_op jit(solution)/shard_map/ppermute | solution.py:30
  17.9 1.0 select_select_fusion.1
  19.6 0.7 collective-permute-start.18
  20.4 1.0 slice.42.b_ref.w_ref
  21.4 2.2 %copy-done = f32[4,512,512]{2,1,0:T(8,128)S(1)} copy-done((f32[4,512,512]{2,1,0:T(8,128)S(1)}, f32[4,512,512]{2,1,0:T(8,128)}, u32[]{:S(2)}) %copy-start) | copy-done | bytes 4194328
  23.6 1.1 shard_map.37
  24.7 0.7 copy-done.15
  25.4 1.3 collective-permute-start
  26.7 1.3 collective-permute-start.1
  28.0 1.3 collective-permute-start.2
  29.3 3.0 %collective-permute-start.6 = (bf16[512,256]{1,0:T(8,128)(2,1)S(1)}, bf16[512,256]{1,0:T(8,128)(2,1)S(1)}, u32[]{:S(2)}, u32[]{:S(2)}) collective-permute-start(bf16[512,256]{1,0:T(8,128)(2,1)S(1)} %slice.43.rest_0_), channel_id=1, source_target_pairs={{0,16},{1,17},{2,18},{3,19},{4,20},{5,21},{6,22},{7,23},{8,24},{9,... | collective-permute-start | bytes 786440 | tf_op jit(solution)/shard_map/ppermute | solution.py:30
  32.9 1.1 add_select_fusion.3.v_ref
  34.0 0.8 constant_dynamic-update-slice_fusion.3
  34.7 0.9 constant_dynamic-update-slice_fusion.2.p_same
  36.1 2.7 %shard_map.38 = (f32[512,128]{1,0:T(8,128)S(1)}, f32[512,128]{1,0:T(8,128)S(1)}, bf16[512,128]{1,0:T(8,128)(2,1)S(1)}) custom-call(s32[4]{0:T(128)S(1)} %pad_add_fusion.ids, f32[512,128]{1,0:T(8,128)S(1)} %slice.42.b_ref.w_ref, bf16[512,128]{1,0:T(8,128)(2,1)S(1)} %add_select_fusion.3.v_ref, f32[4,512,512]{2,1,0:T(8,128)} %d_ref.9, ...), custom_call_target="tpu_custom_call" | custom-call | flops 536870912 | bytes 6684672 | tf_op jit(solution)/shard_map/pallas_call | solution.py:181
  38.9 1.3 collective-permute-start.14
  40.2 1.3 collective-permute-start.15
  41.7 1.4 collective-permute-start.27
  43.2 1.0 add_select_fusion.1.v_ref.y1_ref
  44.2 0.9 copy-done.2
  45.1 0.9 copy-done.6
  46.1 0.9 copy-done.20
  47.0 3.3 %shard_map.39 = (f32[512,128]{1,0:T(8,128)S(1)}, f32[512,128]{1,0:T(8,128)S(1)}, bf16[512,128]{1,0:T(8,128)(2,1)}) custom-call(s32[4]{0:T(128)S(1)} %pad_add_fusion.ids, f32[512,128]{1,0:T(8,128)S(1)} %copy-done.20, bf16[512,128]{1,0:T(8,128)(2,1)S(1)} %add_select_fusion.1.v_ref.y1_ref, f32[4,512,512]{2,1,0:T(8,128)} %d_ref.9, ...), custom_call_target="tpu_custom_call" | custom-call | flops 536870912 | bytes 6684672 | tf_op jit(solution)/shard_map/pallas_call | solution.py:181
  50.4 0.7 copy-done.13
  51.8 1.3 collective-permute-start.16
  53.1 0.9 broadcast_select_fusion.y2_ref
  54.0 1.0 copy-done.3
  55.0 0.9 copy-done.7
  56.0 0.9 copy-done.14
  56.9 9.0 %shard_map.40 = (f32[512,128]{1,0:T(8,128)S(1)}, bf16[512,128]{1,0:T(8,128)(2,1)S(1)}, bf16[1536,128]{1,0:T(8,128)(2,1)}) custom-call(s32[4]{0:T(128)S(1)} %pad_add_fusion.ids, f32[512,128]{1,0:T(8,128)S(1)} %copy-done.14, bf16[512,128]{1,0:T(8,128)(2,1)S(1)} %add_select_fusion.1.v_ref.y1_ref, bf16[512,128]{1,0:T(8,128)(2,1)S(1)} %broadcast_select_fusion.y2_ref, ...), custom_call_target="tpu_custom_call" | custom-call | flops 1610612736 | bytes 8388608 | tf_op jit(solution)/shard_map/pallas_call | solution.py:181
  65.9 0.7 copy-done.18
  67.3 1.4 collective-permute-start.20
  68.7 1.7 slice.48
  70.4 1.3 collective-permute-start.21
  71.7 1.6 slice.52
  73.3 1.3 collective-permute-start.22
  74.6 0.8 collective-permute-start.3
  75.4 1.3 fusion.2
  76.8 0.8 collective-permute-start.23
  77.7 1.3 collective-permute-start.24
  79.0 0.7 collective-permute-start.25
  79.7 3.5 %collective-permute-done.29.rest_6_ = bf16[3584,256]{1,0:T(8,128)(2,1)} collective-permute-done((bf16[3584,256]{1,0:T(8,128)(2,1)S(1)}, bf16[3584,256]{1,0:T(8,128)(2,1)}, u32[]{:S(2)}, u32[]{:S(2)}) %collective-permute-start.29) | collective-permute-done | bytes 1835040 | tf_op jit(solution)/shard_map/ppermute | solution.py:30
  83.2 1.3 collective-permute-start.4
  85.2 2.2 %slice.63 = bf16[1792,256]{1,0:T(8,128)(2,1)} slice(bf16[3584,256]{1,0:T(8,128)(2,1)} %collective-permute-done.29.rest_6_), slice={[0:1792], [0:256]} | slice | bytes 1835008 | tf_op jit(solution)/shard_map/slice | solution.py:197
  87.4 2.2 %slice.64 = bf16[1792,256]{1,0:T(8,128)(2,1)} slice(bf16[3584,256]{1,0:T(8,128)(2,1)} %collective-permute-done.27.rest_2_), slice={[1792:3584], [0:256]} | slice | bytes 1835008 | tf_op jit(solution)/shard_map/slice | solution.py:198
  89.6 37.2 %collective-permute-done.4 = bf16[512,128]{1,0:T(8,128)(2,1)S(1)} collective-permute-done((bf16[512,128]{1,0:T(8,128)(2,1)S(1)}, bf16[512,128]{1,0:T(8,128)(2,1)S(1)}, u32[]{:S(2)}, u32[]{:S(2)}) %collective-permute-start.4) | collective-permute-done | bytes 131104 | tf_op jit(solution)/shard_map/ppermute | solution.py:30
  126.8 1.5 collective-permute-start.33
  128.3 2.6 %collective-permute-start.26 = (bf16[3584,256]{1,0:T(8,128)(2,1)S(1)}, bf16[3584,256]{1,0:T(8,128)(2,1)}, u32[]{:S(2)}, u32[]{:S(2)}) collective-permute-start(bf16[3584,256]{1,0:T(8,128)(2,1)S(1)} %slice.53.rest_0_), channel_id=1, source_target_pairs={{0,16},{1,17},{2,18},{3,19},{4,20},{5,21},{6,22},{7,23},{8,24},{9,... | collective-permute-start | bytes 5505032 | tf_op jit(solution)/shard_map/ppermute | solution.py:30
  131.6 0.8 copy-done.31
  132.5 1.2 add_select_fusion.2.v0_ref
  133.7 13.3 %collective-permute-done.30.rest_4_ = bf16[1792,256]{1,0:T(8,128)(2,1)} collective-permute-done((bf16[1792,256]{1,0:T(8,128)(2,1)}, bf16[1792,256]{1,0:T(8,128)(2,1)}, u32[]{:S(2)}, u32[]{:S(2)}) %collective-permute-start.30) | collective-permute-done | bytes 917536 | tf_op jit(solution)/shard_map/ppermute | solution.py:30
  147.0 3.0 %collective-permute-start.31 = (bf16[1792,256]{1,0:T(8,128)(2,1)}, bf16[1792,256]{1,0:T(8,128)(2,1)S(1)}, u32[]{:S(2)}, u32[]{:S(2)}) collective-permute-start(bf16[1792,256]{1,0:T(8,128)(2,1)} %collective-permute-done.30.rest_4_), channel_id=1, source_target_pairs={{0,16},{1,17},{2,18},{3,19},{4,20},{5,21},{6,22},{7,23},{8,24},{9,... | collective-permute-start | bytes 2752520 | tf_op jit(solution)/shard_map/ppermute | solution.py:30
  149.9 1.3 collective-permute-start.34
  151.2 1.0 select_select_fusion.y_ref
  152.2 1.2 add_select_fusion.v_ref
  153.6 7.9 %shard_map.41.out_in = f32[4096,128]{1,0:T(8,128)} custom-call(s32[4]{0:T(128)S(1)} %pad_add_fusion.ids, f32[4096,128]{1,0:T(8,128)} %copy.13.out_in, bf16[2048,128]{1,0:T(8,128)(2,1)S(1)} %pad_maximum_fusion.1.v_ref, bf16[3584,256]{1,0:T(8,128)(2,1)S(1)} %slice.53.rest_0_, ...), custom_call_target="tpu_custom_call", output_to_operand_aliasing={{}: (1, {})} | custom-call | flops 939524096 | bytes 15466496 | tf_op jit(solution)/shard_map/pallas_call | solution.py:181
  161.5 7.9 %shard_map.42.out_in = f32[4096,128]{1,0:T(8,128)} custom-call(s32[4]{0:T(128)S(1)} %pad_add_fusion.ids, f32[4096,128]{1,0:T(8,128)} %shard_map.41.out_in, bf16[2048,128]{1,0:T(8,128)(2,1)S(1)} %pad_maximum_fusion.1.v_ref, bf16[3584,256]{1,0:T(8,128)(2,1)S(1)} %slice.53.rest_0_, ...), custom_call_target="tpu_custom_call", output_to_operand_aliasing={{}: (1, {})} | custom-call | flops 939524096 | bytes 15466496 | tf_op jit(solution)/shard_map/pallas_call | solution.py:181
  169.5 4.5 %shard_map.43 = f32[4096,128]{1,0:T(8,128)} custom-call(s32[4]{0:T(128)S(1)} %pad_add_fusion.ids, f32[4096,128]{1,0:T(8,128)} %shard_map.42.out_in, f32[512,128]{1,0:T(8,128)S(1)} %select_select_fusion.y_ref, bf16[512,128]{1,0:T(8,128)(2,1)S(1)} %add_select_fusion.2.v0_ref, ...), custom_call_target="tpu_custom_call", output_to_operand_aliasing={{}: (1, {})} | custom-call | flops 536870912 | bytes 9175040 | tf_op jit(solution)/shard_map/pallas_call | solution.py:181
  (111 shorter events, 5.6 us)
Async XLA Ops:
  4.0 7.2 %collective-permute-start.9 = (bf16[512,256]{1,0:T(8,128)(2,1)S(1)}, bf16[512,256]{1,0:T(8,128)(2,1)S(1)}, u32[]{:S(2)}, u32[]{:S(2)}) collective-permute-start(bf16[512,256]{1,0:T(8,128)(2,1)S(1)} %slice.43.rest_0_), channel_id=1, source_target_pairs={{0,32},{1,33},{2,34},{3,35},{4,36},{5,37},{6,38},{7,39},{8,40},{9,... | collective-permute-start | bytes 786440 | tf_op jit(solution)/shard_map/ppermute | solution.py:30
  4.3 8.5 %collective-permute-start.7 = (bf16[512,256]{1,0:T(8,128)(2,1)S(1)}, bf16[512,256]{1,0:T(8,128)(2,1)S(1)}, u32[]{:S(2)}, u32[]{:S(2)}) collective-permute-start(bf16[512,256]{1,0:T(8,128)(2,1)S(1)} %slice.43.rest_0_), channel_id=1, source_target_pairs={{0,96},{1,97},{2,98},{3,99},{4,100},{5,101},{6,102},{7,103},{8,104... | collective-permute-start | bytes 786440 | tf_op jit(solution)/shard_map/ppermute | solution.py:30
  11.3 3.9 %collective-permute-start.10 = (bf16[256,256]{1,0:T(8,128)(2,1)S(1)}, bf16[256,256]{1,0:T(8,128)(2,1)S(1)}, u32[]{:S(2)}, u32[]{:S(2)}) collective-permute-start(bf16[256,256]{1,0:T(8,128)(2,1)S(1)} %slice.56), channel_id=1, source_target_pairs={{0,32},{1,33},{2,34},{3,35},{4,36},{5,37},{6,38},{7,39},{8,40},{9,... | collective-permute-start | bytes 393224 | tf_op jit(solution)/shard_map/ppermute | solution.py:30
  12.8 5.1 %collective-permute-start.11 = (bf16[256,256]{1,0:T(8,128)(2,1)S(1)}, bf16[256,256]{1,0:T(8,128)(2,1)S(1)}, u32[]{:S(2)}, u32[]{:S(2)}) collective-permute-start(bf16[256,256]{1,0:T(8,128)(2,1)S(1)} %slice.57), channel_id=1, source_target_pairs={{0,96},{1,97},{2,98},{3,99},{4,100},{5,101},{6,102},{7,103},{8,104... | collective-permute-start | bytes 393224 | tf_op jit(solution)/shard_map/ppermute | solution.py:30
  18.9 13.9 %collective-permute-start.17 = (bf16[512,256]{1,0:T(8,128)(2,1)S(1)}, bf16[512,256]{1,0:T(8,128)(2,1)S(1)}, u32[]{:S(2)}, u32[]{:S(2)}) collective-permute-start(bf16[512,256]{1,0:T(8,128)(2,1)S(1)} %get-tuple-element.28), channel_id=1, source_target_pairs={{8,12},{24,28},{40,44},{56,60},{72,76},{88,92},{104,108},{120,124}} | collective-permute-start | bytes 786440 | tf_op jit(solution)/shard_map/ppermute | solution.py:30
  19.6 15.1 %collective-permute-start.18 = (bf16[512,512]{1,0:T(8,128)(2,1)S(1)}, bf16[512,512]{1,0:T(8,128)(2,1)S(1)}, u32[]{:S(2)}, u32[]{:S(2)}) collective-permute-start(bf16[512,512]{1,0:T(8,128)(2,1)S(1)} %pad_maximum_fusion), channel_id=1, source_target_pairs={{4,12},{20,28},{36,44},{52,60},{68,76},{84,92},{100,108},{116,124}} | collective-permute-start | bytes 1572872 | tf_op jit(solution)/shard_map/ppermute | solution.py:30
  21.4 2.2 %copy-start = (f32[4,512,512]{2,1,0:T(8,128)S(1)}, f32[4,512,512]{2,1,0:T(8,128)}, u32[]{:S(2)}) copy-start(f32[4,512,512]{2,1,0:T(8,128)} %d_ref.9) | copy-start | bytes 12582916
  25.4 3.9 %collective-permute-start = (bf16[512,128]{1,0:T(8,128)(2,1)S(1)}, bf16[512,128]{1,0:T(8,128)(2,1)}, u32[]{:S(2)}, u32[]{:S(2)}) collective-permute-start(bf16[512,128]{1,0:T(8,128)(2,1)S(1)} %get-tuple-element.16), channel_id=1, source_target_pairs={{0,4},{16,20},{32,36},{48,52},{64,68},{80,84},{96,100},{112,116}} | collective-permute-start | bytes 393224 | tf_op jit(solution)/shard_map/ppermute | solution.py:30
  26.7 5.6 %collective-permute-start.1 = (bf16[512,128]{1,0:T(8,128)(2,1)S(1)}, bf16[512,128]{1,0:T(8,128)(2,1)}, u32[]{:S(2)}, u32[]{:S(2)}) collective-permute-start(bf16[512,128]{1,0:T(8,128)(2,1)S(1)} %get-tuple-element.16), channel_id=1, source_target_pairs={{0,8},{16,24},{32,40},{48,56},{64,72},{80,88},{96,104},{112,120}} | collective-permute-start | bytes 393224 | tf_op jit(solution)/shard_map/ppermute | solution.py:30
  28.0 4.4 %collective-permute-start.2 = (bf16[512,128]{1,0:T(8,128)(2,1)S(1)}, bf16[512,128]{1,0:T(8,128)(2,1)}, u32[]{:S(2)}, u32[]{:S(2)}) collective-permute-start(bf16[512,128]{1,0:T(8,128)(2,1)S(1)} %get-tuple-element.16), channel_id=1, source_target_pairs={{0,12},{16,28},{32,44},{48,60},{64,76},{80,92},{96,108},{112,124}} | collective-permute-start | bytes 393224 | tf_op jit(solution)/shard_map/ppermute | solution.py:30
  29.3 6.8 %collective-permute-start.6 = (bf16[512,256]{1,0:T(8,128)(2,1)S(1)}, bf16[512,256]{1,0:T(8,128)(2,1)S(1)}, u32[]{:S(2)}, u32[]{:S(2)}) collective-permute-start(bf16[512,256]{1,0:T(8,128)(2,1)S(1)} %slice.43.rest_0_), channel_id=1, source_target_pairs={{0,16},{1,17},{2,18},{3,19},{4,20},{5,21},{6,22},{7,23},{8,24},{9,... | collective-permute-start | bytes 786440 | tf_op jit(solution)/shard_map/ppermute | solution.py:30
  32.3 3.8 %collective-permute-start.13 = (bf16[512,256]{1,0:T(8,128)(2,1)S(1)}, bf16[512,256]{1,0:T(8,128)(2,1)S(1)}, u32[]{:S(2)}, u32[]{:S(2)}) collective-permute-start(bf16[512,256]{1,0:T(8,128)(2,1)S(1)} %collective-permute-done.9.rest_6_), channel_id=1, source_target_pairs={{0,16},{1,17},{2,18},{3,19},{4,20},{5,21},{6,22},{7,23},{8,24},{9,... | collective-permute-start | bytes 786440 | tf_op jit(solution)/shard_map/ppermute | solution.py:30
  32.4 3.7 %collective-permute-start.8 = (bf16[512,256]{1,0:T(8,128)(2,1)S(1)}, bf16[512,256]{1,0:T(8,128)(2,1)S(1)}, u32[]{:S(2)}, u32[]{:S(2)}) collective-permute-start(bf16[512,256]{1,0:T(8,128)(2,1)S(1)} %collective-permute-done.7.rest_2_), channel_id=1, source_target_pairs={{0,16},{1,17},{2,18},{3,19},{4,20},{5,21},{6,22},{7,23},{8,24},{9,... | collective-permute-start | bytes 786440 | tf_op jit(solution)/shard_map/ppermute | solution.py:30
  32.8 3.3 %collective-permute-start.12 = (bf16[512,256]{1,0:T(8,128)(2,1)S(1)}, bf16[512,256]{1,0:T(8,128)(2,1)S(1)}, u32[]{:S(2)}, u32[]{:S(2)}) collective-permute-start(bf16[512,256]{1,0:T(8,128)(2,1)S(1)} %constant_dynamic-update-slice_fusion.rest_4_), channel_id=1, source_target_pairs={{0,16},{1,17},{2,18},{3,19},{4,20},{5,21},{6,22},{7,23},{8,24},{9,... | collective-permute-start | bytes 786440 | tf_op jit(solution)/shard_map/ppermute | solution.py:30
  34.0 4.9 %copy-start.10 = (bf16[512,128]{1,0:T(8,128)(2,1)}, bf16[512,128]{1,0:T(8,128)(2,1)S(1)}, u32[]{:S(2)}) copy-start(bf16[512,128]{1,0:T(8,128)(2,1)S(1)} %add_select_fusion.3.v_ref) | copy-start | bytes 393220
  35.6 5.8 %copy-start.23 = (bf16[4096,256]{1,0:T(8,128)(2,1)S(1)}, bf16[4096,256]{1,0:T(8,128)(2,1)}, u32[]{:S(2)}) copy-start(bf16[4096,256]{1,0:T(8,128)(2,1)} %param.4) | copy-start | bytes 6291460
  35.6 18.4 %collective-permute-start.19 = (bf16[512,768]{1,0:T(8,128)(2,1)}, bf16[512,768]{1,0:T(8,128)(2,1)}, u32[]{:S(2)}, u32[]{:S(2)}) collective-permute-start(bf16[512,768]{1,0:T(8,128)(2,1)} %constant_dynamic-update-slice_fusion.2.p_same), channel_id=1, source_target_pairs={{0,16},{1,17},{2,18},{3,19},{4,20},{5,21},{6,22},{7,23},{8,24},{9,... | collective-permute-start | bytes 2359304 | tf_op jit(solution)/shard_map/ppermute | solution.py:30
  36.1 2.7 %copy-start.1 = (bf16[512,256]{1,0:T(8,128)(2,1)}, bf16[512,256]{1,0:T(8,128)(2,1)S(1)}, u32[]{:S(2)}) copy-start(bf16[512,256]{1,0:T(8,128)(2,1)S(1)} %collective-permute-done.8.rest_3_) | copy-start | bytes 786436
  36.1 2.7 %copy-start.5 = (bf16[512,256]{1,0:T(8,128)(2,1)}, bf16[512,256]{1,0:T(8,128)(2,1)S(1)}, u32[]{:S(2)}) copy-start(bf16[512,256]{1,0:T(8,128)(2,1)S(1)} %collective-permute-done.12.rest_5_) | copy-start | bytes 786436
  38.8 2.8 %copy-start.16 = (f32[512,128]{1,0:T(8,128)}, f32[512,128]{1,0:T(8,128)S(1)}, u32[]{:S(2)}) copy-start(f32[512,128]{1,0:T(8,128)S(1)} %get-tuple-element.24) | copy-start | bytes 786436
  38.8 2.9 %copy-start.19 = (f32[512,128]{1,0:T(8,128)}, f32[512,128]{1,0:T(8,128)S(1)}, u32[]{:S(2)}) copy-start(f32[512,128]{1,0:T(8,128)S(1)} %get-tuple-element.18.w_ref) | copy-start | bytes 786436
  38.9 4.3 %copy-start.22 = (bf16[512,128]{1,0:T(8,128)(2,1)}, bf16[512,128]{1,0:T(8,128)(2,1)S(1)}, u32[]{:S(2)}) copy-start(bf16[512,128]{1,0:T(8,128)(2,1)S(1)} %get-tuple-element.17) | copy-start | bytes 393220
  38.9 4.3 %collective-permute-start.14 = (bf16[512,128]{1,0:T(8,128)(2,1)S(1)}, bf16[512,128]{1,0:T(8,128)(2,1)}, u32[]{:S(2)}, u32[]{:S(2)}) collective-permute-start(bf16[512,128]{1,0:T(8,128)(2,1)S(1)} %get-tuple-element.17), channel_id=1, source_target_pairs={{4,8},{20,24},{36,40},{52,56},{68,72},{84,88},{100,104},{116,120}} | collective-permute-start | bytes 393224 | tf_op jit(solution)/shard_map/ppermute | solution.py:30
  40.2 3.0 %collective-permute-start.15 = (bf16[512,128]{1,0:T(8,128)(2,1)S(1)}, bf16[512,128]{1,0:T(8,128)(2,1)}, u32[]{:S(2)}, u32[]{:S(2)}) collective-permute-start(bf16[512,128]{1,0:T(8,128)(2,1)S(1)} %get-tuple-element.17), channel_id=1, source_target_pairs={{4,12},{20,28},{36,44},{52,60},{68,76},{84,92},{100,108},{116,124}} | collective-permute-start | bytes 393224 | tf_op jit(solution)/shard_map/ppermute | solution.py:30
  41.6 41.6 %collective-permute-start.29 = (bf16[3584,256]{1,0:T(8,128)(2,1)S(1)}, bf16[3584,256]{1,0:T(8,128)(2,1)}, u32[]{:S(2)}, u32[]{:S(2)}) collective-permute-start(bf16[3584,256]{1,0:T(8,128)(2,1)S(1)} %slice.53.rest_0_), channel_id=1, source_target_pairs={{0,32},{1,33},{2,34},{3,35},{4,36},{5,37},{6,38},{7,39},{8,40},{9,... | collective-permute-start | bytes 5505032 | tf_op jit(solution)/shard_map/ppermute | solution.py:30
  41.7 42.8 %collective-permute-start.27 = (bf16[3584,256]{1,0:T(8,128)(2,1)S(1)}, bf16[3584,256]{1,0:T(8,128)(2,1)}, u32[]{:S(2)}, u32[]{:S(2)}) collective-permute-start(bf16[3584,256]{1,0:T(8,128)(2,1)S(1)} %slice.53.rest_0_), channel_id=1, source_target_pairs={{0,96},{1,97},{2,98},{3,99},{4,100},{5,101},{6,102},{7,103},{8,104... | collective-permute-start | bytes 5505032 | tf_op jit(solution)/shard_map/ppermute | solution.py:30
  44.2 1.0 copy-start.2
  45.1 0.9 copy-start.6
  46.1 0.9 copy-start.20
  51.8 1.3 collective-permute-start.16
  54.0 11.9 %copy-start.9 = (bf16[512,128]{1,0:T(8,128)(2,1)}, bf16[512,128]{1,0:T(8,128)(2,1)S(1)}, u32[]{:S(2)}) copy-start(bf16[512,128]{1,0:T(8,128)(2,1)S(1)} %broadcast_select_fusion.y2_ref) | copy-start | bytes 393220
  54.0 1.0 copy-start.3
  55.0 0.9 copy-start.7
  56.0 0.9 copy-start.14
  67.3 8.1 %collective-permute-start.20 = (bf16[1536,128]{1,0:T(8,128)(2,1)}, bf16[1536,128]{1,0:T(8,128)(2,1)}, u32[]{:S(2)}, u32[]{:S(2)}) collective-permute-start(bf16[1536,128]{1,0:T(8,128)(2,1)} %get-tuple-element.21), channel_id=1, source_target_pairs={{12,0},{28,16},{44,32},{60,48},{76,64},{92,80},{108,96},{124,112}} | collective-permute-start | bytes 1179656 | tf_op jit(solution)/shard_map/ppermute | solution.py:30
  70.4 5.0 %collective-permute-start.21 = (bf16[1024,128]{1,0:T(8,128)(2,1)}, bf16[1024,128]{1,0:T(8,128)(2,1)}, u32[]{:S(2)}, u32[]{:S(2)}) collective-permute-start(bf16[1024,128]{1,0:T(8,128)(2,1)} %slice.48), channel_id=1, source_target_pairs={{12,4},{28,20},{44,36},{60,52},{76,68},{92,84},{108,100},{124,116}} | collective-permute-start | bytes 786440 | tf_op jit(solution)/shard_map/ppermute | solution.py:30
  73.3 1.3 collective-permute-start.22
  74.6 8.6 %copy-start.11 = (bf16[512,128]{1,0:T(8,128)(2,1)S(1)}, bf16[512,128]{1,0:T(8,128)(2,1)}, u32[]{:S(2)}) copy-start(bf16[512,128]{1,0:T(8,128)(2,1)} %copy-done.10) | copy-start | bytes 393220
  74.6 4.3 %collective-permute-start.3 = (bf16[512,128]{1,0:T(8,128)(2,1)}, bf16[512,128]{1,0:T(8,128)(2,1)S(1)}, u32[]{:S(2)}, u32[]{:S(2)}) collective-permute-start(bf16[512,128]{1,0:T(8,128)(2,1)} %copy-done.10), channel_id=1, source_target_pairs={{0,1},{4,5},{8,9},{12,13},{16,17},{20,21},{24,25},{28,29},{32,33},... | collective-permute-start | bytes 393224 | tf_op jit(solution)/shard_map/ppermute | solution.py:30
  76.8 7.7 %copy-start.24 = (bf16[512,128]{1,0:T(8,128)(2,1)}, bf16[512,128]{1,0:T(8,128)(2,1)S(1)}, u32[]{:S(2)}) copy-start(bf16[512,128]{1,0:T(8,128)(2,1)S(1)} %get-tuple-element.29) | copy-start | bytes 393220
  76.8 7.7 %copy-start.25 = (bf16[512,128]{1,0:T(8,128)(2,1)}, bf16[512,128]{1,0:T(8,128)(2,1)S(1)}, u32[]{:S(2)}) copy-start(bf16[512,128]{1,0:T(8,128)(2,1)S(1)} %get-tuple-element.30) | copy-start | bytes 393220
  76.8 7.7 %copy-start.26 = (bf16[512,128]{1,0:T(8,128)(2,1)}, bf16[512,128]{1,0:T(8,128)(2,1)S(1)}, u32[]{:S(2)}) copy-start(bf16[512,128]{1,0:T(8,128)(2,1)S(1)} %get-tuple-element.31) | copy-start | bytes 393220
  76.8 55.7 %copy-start.12 = (bf16[512,128]{1,0:T(8,128)(2,1)S(1)}, bf16[512,128]{1,0:T(8,128)(2,1)}, u32[]{:S(2)}) copy-start(bf16[512,128]{1,0:T(8,128)(2,1)} %copy-done.10) | copy-start | bytes 393220
  76.8 51.5 %collective-permute-start.23 = (bf16[1536,128]{1,0:T(8,128)(2,1)S(1)}, bf16[1536,128]{1,0:T(8,128)(2,1)S(1)}, u32[]{:S(2)}, u32[]{:S(2)}) collective-permute-start(bf16[1536,128]{1,0:T(8,128)(2,1)S(1)} %pad_maximum_fusion.2), channel_id=1, source_target_pairs={{0,1},{4,5},{8,9},{12,13},{16,17},{20,21},{24,25},{28,29},{32,33},... | collective-permute-start | bytes 1179656 | tf_op jit(solution)/shard_map/ppermute | solution.py:30
  77.7 53.2 %collective-permute-start.24 = (bf16[1536,128]{1,0:T(8,128)(2,1)S(1)}, bf16[1536,128]{1,0:T(8,128)(2,1)S(1)}, u32[]{:S(2)}, u32[]{:S(2)}) collective-permute-start(bf16[1536,128]{1,0:T(8,128)(2,1)S(1)} %pad_maximum_fusion.2), channel_id=1, source_target_pairs={{0,2},{4,6},{8,10},{12,14},{16,18},{20,22},{24,26},{28,30},{32,34}... | collective-permute-start | bytes 1179656 | tf_op jit(solution)/shard_map/ppermute | solution.py:30
  79.0 5.6 %copy-start.33 = (bf16[512,128]{1,0:T(8,128)(2,1)}, bf16[512,128]{1,0:T(8,128)(2,1)S(1)}, u32[]{:S(2)}) copy-start(bf16[512,128]{1,0:T(8,128)(2,1)S(1)} %collective-permute-done.3) | copy-start | bytes 393220
  79.0 52.0 %collective-permute-start.25 = (bf16[1536,128]{1,0:T(8,128)(2,1)S(1)}, bf16[1536,128]{1,0:T(8,128)(2,1)S(1)}, u32[]{:S(2)}, u32[]{:S(2)}) collective-permute-start(bf16[1536,128]{1,0:T(8,128)(2,1)S(1)} %pad_maximum_fusion.2), channel_id=1, source_target_pairs={{0,3},{4,7},{8,11},{12,15},{16,19},{20,23},{24,27},{28,31},{32,35}... | collective-permute-start | bytes 1179656 | tf_op jit(solution)/shard_map/ppermute | solution.py:30
  83.2 43.6 %collective-permute-start.4 = (bf16[512,128]{1,0:T(8,128)(2,1)S(1)}, bf16[512,128]{1,0:T(8,128)(2,1)S(1)}, u32[]{:S(2)}, u32[]{:S(2)}) collective-permute-start(bf16[512,128]{1,0:T(8,128)(2,1)S(1)} %copy-done.11), channel_id=1, source_target_pairs={{0,2},{4,6},{8,10},{12,14},{16,18},{20,22},{24,26},{28,30},{32,34}... | collective-permute-start | bytes 393224 | tf_op jit(solution)/shard_map/ppermute | solution.py:30
  84.5 42.3 %collective-permute-start.5 = (bf16[512,128]{1,0:T(8,128)(2,1)S(1)}, bf16[512,128]{1,0:T(8,128)(2,1)S(1)}, u32[]{:S(2)}, u32[]{:S(2)}) collective-permute-start(bf16[512,128]{1,0:T(8,128)(2,1)S(1)} %copy-done.11), channel_id=1, source_target_pairs={{0,3},{4,7},{8,11},{12,15},{16,19},{20,23},{24,27},{28,31},{32,35}... | collective-permute-start | bytes 393224 | tf_op jit(solution)/shard_map/ppermute | solution.py:30
  126.8 4.2 %copy-start.34 = (bf16[512,128]{1,0:T(8,128)(2,1)}, bf16[512,128]{1,0:T(8,128)(2,1)S(1)}, u32[]{:S(2)}) copy-start(bf16[512,128]{1,0:T(8,128)(2,1)S(1)} %collective-permute-done.4) | copy-start | bytes 393220
  126.8 20.1 %collective-permute-start.30 = (bf16[1792,256]{1,0:T(8,128)(2,1)}, bf16[1792,256]{1,0:T(8,128)(2,1)}, u32[]{:S(2)}, u32[]{:S(2)}) collective-permute-start(bf16[1792,256]{1,0:T(8,128)(2,1)} %slice.63), channel_id=1, source_target_pairs={{0,32},{1,33},{2,34},{3,35},{4,36},{5,37},{6,38},{7,39},{8,40},{9,... | collective-permute-start | bytes 2752520 | tf_op jit(solution)/shard_map/ppermute | solution.py:30
  126.8 4.2 %copy-start.35 = (bf16[512,128]{1,0:T(8,128)(2,1)}, bf16[512,128]{1,0:T(8,128)(2,1)S(1)}, u32[]{:S(2)}) copy-start(bf16[512,128]{1,0:T(8,128)(2,1)S(1)} %collective-permute-done.5) | copy-start | bytes 393220
  126.8 23.1 %collective-permute-start.33 = (bf16[1792,256]{1,0:T(8,128)(2,1)}, bf16[1792,256]{1,0:T(8,128)(2,1)}, u32[]{:S(2)}, u32[]{:S(2)}) collective-permute-start(bf16[1792,256]{1,0:T(8,128)(2,1)} %slice.64), channel_id=1, source_target_pairs={{0,96},{1,97},{2,98},{3,99},{4,100},{5,101},{6,102},{7,103},{8,104... | collective-permute-start | bytes 2752520 | tf_op jit(solution)/shard_map/ppermute | solution.py:30
  128.3 2.7 %copy-start.27 = (bf16[1536,128]{1,0:T(8,128)(2,1)}, bf16[1536,128]{1,0:T(8,128)(2,1)S(1)}, u32[]{:S(2)}) copy-start(bf16[1536,128]{1,0:T(8,128)(2,1)S(1)} %collective-permute-done.23) | copy-start | bytes 1179652
  128.3 25.2 %collective-permute-start.26 = (bf16[3584,256]{1,0:T(8,128)(2,1)S(1)}, bf16[3584,256]{1,0:T(8,128)(2,1)}, u32[]{:S(2)}, u32[]{:S(2)}) collective-permute-start(bf16[3584,256]{1,0:T(8,128)(2,1)S(1)} %slice.53.rest_0_), channel_id=1, source_target_pairs={{0,16},{1,17},{2,18},{3,19},{4,20},{5,21},{6,22},{7,23},{8,24},{9,... | collective-permute-start | bytes 5505032 | tf_op jit(solution)/shard_map/ppermute | solution.py:30
  130.9 22.7 %collective-permute-start.28 = (bf16[3584,256]{1,0:T(8,128)(2,1)}, bf16[3584,256]{1,0:T(8,128)(2,1)}, u32[]{:S(2)}, u32[]{:S(2)}) collective-permute-start(bf16[3584,256]{1,0:T(8,128)(2,1)} %collective-permute-done.27.rest_2_), channel_id=1, source_target_pairs={{0,16},{1,17},{2,18},{3,19},{4,20},{5,21},{6,22},{7,23},{8,24},{9,... | collective-permute-start | bytes 5505032 | tf_op jit(solution)/shard_map/ppermute | solution.py:30
  132.4 21.2 %collective-permute-start.32 = (bf16[3584,256]{1,0:T(8,128)(2,1)}, bf16[3584,256]{1,0:T(8,128)(2,1)}, u32[]{:S(2)}, u32[]{:S(2)}) collective-permute-start(bf16[3584,256]{1,0:T(8,128)(2,1)} %collective-permute-done.29.rest_6_), channel_id=1, source_target_pairs={{0,16},{1,17},{2,18},{3,19},{4,20},{5,21},{6,22},{7,23},{8,24},{9,... | collective-permute-start | bytes 5505032 | tf_op jit(solution)/shard_map/ppermute | solution.py:30
  132.5 19.7 %copy-start.28 = (bf16[1536,128]{1,0:T(8,128)(2,1)S(1)}, bf16[1536,128]{1,0:T(8,128)(2,1)}, u32[]{:S(2)}) copy-start(bf16[1536,128]{1,0:T(8,128)(2,1)} %copy-done.27) | copy-start | bytes 1179652
  132.5 19.7 %copy-start.30 = (bf16[1536,128]{1,0:T(8,128)(2,1)S(1)}, bf16[1536,128]{1,0:T(8,128)(2,1)}, u32[]{:S(2)}) copy-start(bf16[1536,128]{1,0:T(8,128)(2,1)} %copy-done.29) | copy-start | bytes 1179652
  132.5 19.7 %copy-start.32 = (bf16[1536,128]{1,0:T(8,128)(2,1)S(1)}, bf16[1536,128]{1,0:T(8,128)(2,1)}, u32[]{:S(2)}) copy-start(bf16[1536,128]{1,0:T(8,128)(2,1)} %copy-done.31) | copy-start | bytes 1179652
  147.0 6.6 %collective-permute-start.31 = (bf16[1792,256]{1,0:T(8,128)(2,1)}, bf16[1792,256]{1,0:T(8,128)(2,1)S(1)}, u32[]{:S(2)}, u32[]{:S(2)}) collective-permute-start(bf16[1792,256]{1,0:T(8,128)(2,1)} %collective-permute-done.30.rest_4_), channel_id=1, source_target_pairs={{0,16},{1,17},{2,18},{3,19},{4,20},{5,21},{6,22},{7,23},{8,24},{9,... | collective-permute-start | bytes 2752520 | tf_op jit(solution)/shard_map/ppermute | solution.py:30
  149.9 11.6 %collective-permute-start.34 = (bf16[1792,256]{1,0:T(8,128)(2,1)}, bf16[1792,256]{1,0:T(8,128)(2,1)S(1)}, u32[]{:S(2)}, u32[]{:S(2)}) collective-permute-start(bf16[1792,256]{1,0:T(8,128)(2,1)} %collective-permute-done.33.rest_4_), channel_id=1, source_target_pairs={{0,16},{1,17},{2,18},{3,19},{4,20},{5,21},{6,22},{7,23},{8,24},{9,... | collective-permute-start | bytes 2752520 | tf_op jit(solution)/shard_map/ppermute | solution.py:30
  161.5 8.0 %copy-start.4 = (bf16[512,256]{1,0:T(8,128)(2,1)S(1)}, bf16[512,256]{1,0:T(8,128)(2,1)}, u32[]{:S(2)}) copy-start(bf16[512,256]{1,0:T(8,128)(2,1)} %copy-done.1) | copy-start | bytes 786436
  161.5 8.0 %copy-start.8 = (bf16[512,256]{1,0:T(8,128)(2,1)S(1)}, bf16[512,256]{1,0:T(8,128)(2,1)}, u32[]{:S(2)}) copy-start(bf16[512,256]{1,0:T(8,128)(2,1)} %copy-done.5) | copy-start | bytes 786436
  (7 other events, 5.0 us)

commit v2 on v1

v2 whole, which is shorter than its diff:
```python
import functools

import jax
import jax.numpy as jnp
from jax import lax
from jax.experimental import pallas as pl
from jax.experimental.pallas import tpu as pltpu
from jax.sharding import PartitionSpec as P

NX, NH, NZ, NY = 4, 2, 4, 4
NB = 512
HB = 256
F32, BF16 = jnp.float32, jnp.bfloat16


def pairs(move):
    out = []
    for r in range(NX * NH):
        for c in range(NZ * NY):
            x, h = divmod(r, NH)
            z, y = divmod(c, NY)
            to = move(x, h, z, y)
            if to is not None:
                x2, h2, z2, y2 = to
                out.append((r * NZ * NY + c, ((x2 % NX) * NH + h2 % NH) * NZ * NY + (z2 % NZ) * NY + y2 % NY))
    return out


def send(value, move):
    return lax.ppermute(value, ("row", "col"), pairs(move))


def x_plus(x, h, z, y):
    return (x + 1, h, z, y)


def x_minus(x, h, z, y):
    return (x - 1, h, z, y)


def x_far(x, h, z, y):
    return (x + 2, h, z, y)


def other_core(x, h, z, y):
    return (x, 1 - h, z, y)


def z_move(src, dst):
    return lambda x, h, z, y: (x, h, dst, y) if (y == 0 and z == src) else None


def y_move(step):
    return lambda x, h, z, y: (x, h, z, step) if y == 0 else None


def dot(a, b):
    return jnp.dot(a, b, preferred_element_type=F32)


def split(a):
    hi = a.astype(BF16)
    return hi, (a - hi.astype(F32)).astype(BF16)


def apply(hi_ref, lo_ref, v):
    vh, vl = split(v)
    return dot(hi_ref[...], vh) + (dot(hi_ref[...], vl) + dot(lo_ref[...], vh))


def lower_mask(d):
    i = lax.broadcasted_iota(jnp.int32, d.shape, 0)
    j = lax.broadcasted_iota(jnp.int32, d.shape, 1)
    return jnp.where(i > j, d, 0.0)


def upper_mask(d):
    i = lax.broadcasted_iota(jnp.int32, d.shape, 0)
    j = lax.broadcasted_iota(jnp.int32, d.shape, 1)
    return jnp.where(i <= j, d, 0.0)


def start_kernel(ids, b_ref, d_ref, y_ref, yb_ref, lh_ref, ll_ref):
    lh_ref[...], ll_ref[...] = split(lower_mask(d_ref[0]))
    w = b_ref[...]
    y = w + apply(lh_ref, ll_ref, w)
    y_ref[...] = y
    yb_ref[...] = y.astype(BF16)


def upper_kernel(ids, d_ref, *out):
    for n, j in enumerate((ids[2], 1, 2)):
        out[2 * n][...], out[2 * n + 1][...] = split(upper_mask(d_ref[j]))


def block_product(ids, blocks, j, v_ref, acc_ref):
    x, h = ids[0], ids[1]
    for d in range(NX):
        @pl.when(lax.rem(x + d, NX) == j)
        def _():
            same, other = blocks[2 * d], blocks[2 * d + 1]
            acc_ref[...] -= dot(same[...], v_ref[pl.ds(pl.multiple_of(h * HB, HB), HB), :]) + dot(
                other[...], v_ref[pl.ds(pl.multiple_of((1 - h) * HB, HB), HB), :]
            )


def gather_own(ids, j, v_ref, own_ref, received):
    total = received[0][...]
    for piece in received[1:]:
        total = total + piece[...]
    v_ref[...] = jnp.where(ids[2] == j, own_ref[...], total)


def forward_kernel(j, count, ids, w_ref, own_ref, lh_ref, ll_ref, *rest):
    received, blocks = rest[:count], rest[count : count + 8]
    v_ref, w_out, y_ref, yb_ref = rest[count + 8 :]
    gather_own(ids, j, v_ref, own_ref, received)
    w_out[...] = w_ref[...]
    block_product(ids, blocks, j, v_ref, w_out)
    w = w_out[...]
    y = w + apply(lh_ref, ll_ref, w)
    y_ref[...] = y
    yb_ref[...] = y.astype(BF16)


def turn_kernel(ids, w_ref, y1_ref, own_ref, y2_in, lh, ll, uzh, uzl, u1h, u1l, u2h, u2l, p_same, p_other, *rest):
    blocks, (y2_ref, y_ref, yb_ref, x_ref, x23_ref, x3_ref, acc) = rest[:8], rest[-7:]
    h = ids[1]
    gather_own(ids, 2, y2_ref, own_ref, [y2_in])
    acc[...] = w_ref[...]
    block_product(ids, blocks, 2, y2_ref, acc)
    w = acc[...]
    y3 = w + apply(lh, ll, w)
    y_ref[...] = y3
    yb_ref[...] = y3.astype(BF16)

    def prefetched(slot, row):
        cols = slice(slot * HB, (slot + 1) * HB)
        return dot(p_same[:, cols], x_ref[pl.ds(pl.multiple_of(row + h * HB, HB), HB), :]) + dot(
            p_other[:, cols], x_ref[pl.ds(pl.multiple_of(row + (1 - h) * HB, HB), HB), :]
        )

    x3 = apply(uzh, uzl, y3).astype(BF16)
    x_ref[2 * NB : 3 * NB, :] = x3
    x23_ref[NB : 2 * NB, :] = x3
    x3_ref[...] = x3
    t = y2_ref[...].astype(F32) - prefetched(0, 2 * NB)
    x2 = apply(u2h, u2l, t).astype(BF16)
    x_ref[NB : 2 * NB, :] = x2
    x23_ref[0:NB, :] = x2
    t = y1_ref[...].astype(F32) - prefetched(1, NB) - prefetched(2, 2 * NB)
    x_ref[0:NB, :] = apply(u1h, u1l, t).astype(BF16)


def window_kernel(ids, out_in, b_ref, y_ref, v0_ref, v_ref, uh_ref, ul_ref, *rest):
    blocks, (out_ref, acc) = rest[:8], rest[8:]
    x, h, z, owner = ids[0], ids[1], ids[2], ids[3] == 0
    acc[...] = jnp.where(owner, y_ref[...], b_ref[...])
    for d in range(NX):
        j = lax.rem(x + d, NX)
        for s in range(2):
            part = h if s == 0 else 1 - h

            @pl.when(jnp.logical_and(j == 0, jnp.logical_not(owner)))
            def _():
                acc[...] -= dot(blocks[2 * d + s][...], v0_ref[pl.ds(pl.multiple_of(part * HB, HB), HB), :])

            @pl.when(jnp.logical_and(j > 0, jnp.logical_or(jnp.logical_not(owner), j > z)))
            def _():
                acc[...] -= dot(
                    blocks[2 * d + s][...], v_ref[pl.ds(pl.multiple_of((j - 1) * NB + part * HB, HB), HB), :]
                )

    @pl.when(owner)
    def _():
        out_ref[...] = apply(uh_ref, ul_ref, acc[...])

    @pl.when(jnp.logical_not(owner))
    def _():
        out_ref[...] = acc[...]


def rows_of(ids, d, s, v_ref):
    part = ids[1] if s == 0 else 1 - ids[1]
    return v_ref[pl.ds(pl.multiple_of(lax.rem(ids[0] + d, NX) * NB + part * HB, HB), HB), :]


def rows_kernel(distances, aliased, ids, b_ref, v_ref, *rest):
    rest = rest[1:] if aliased else rest
    out_ref = rest[-1]
    acc = b_ref[...]
    for n, d in enumerate(distances):
        for s in range(2):
            acc -= dot(rest[2 * n + s][...], rows_of(ids, d, s, v_ref))
    out_ref[...] = acc
    if len(rest) > 2 * len(distances) + 1:
        pair = rest[2 * len(distances) : -1]
        for t in range(2):
            @pl.when(pl.program_id(0) == t)
            def _():
                for s in range(2):
                    out_ref[...] -= dot(pair[2 * t + s][...], rows_of(ids, 2, s, v_ref))


def late_kernel(ids, to0, to1, to2, y1, y2, y3, *rest):
    late_ref, z = rest[-1], ids[2]
    late_ref[0:NB, :] = jnp.where(z >= 1, y1[...], to0[0:NB, :])
    late_ref[NB : 2 * NB, :] = jnp.where(z >= 2, y2[...], to0[NB : 2 * NB, :] + to1[0:NB, :])
    late_ref[2 * NB :, :] = jnp.where(z >= 3, y3[...], to0[2 * NB :, :] + to1[NB:, :] + to2[...])


def whole(shape):
    return pl.BlockSpec(shape, lambda i, ids: (0,) * len(shape))


ANY = pl.BlockSpec(memory_space=pl.ANY)


def call(kernel, ids, args, specs, outs, out_specs, scratch=(), grid=(1,), aliases={}, limit=14):
    return pl.pallas_call(
        kernel,
        grid_spec=pltpu.PrefetchScalarGridSpec(
            num_scalar_prefetch=1, grid=grid, in_specs=specs, out_specs=out_specs, scratch_shapes=scratch
        ),
        out_shape=outs,
        input_output_aliases=aliases,
        cost_estimate=pl.CostEstimate(flops=1, bytes_accessed=1, transcendentals=0),
        compiler_params=pltpu.CompilerParams(vmem_limit_bytes=limit * 1024 * 1024),
    )(ids, *args)


def ring(own):
    half = own.shape[0] // 2
    before = send(own, x_plus)
    after = send(own, x_minus)
    top = send(before[:half], x_plus)
    bottom = send(after[half:], x_minus)
    return before, after, top, bottom


def body(rhs, factors, diag_inv):
    rows, cols = rhs.shape
    r, c = lax.axis_index("row"), lax.axis_index("col")
    x, h, z, y = r // NH, r % NH, c // NY, c % NY
    ids = jnp.stack([x, h, z, y]).astype(jnp.int32)
    owner = y == 0
    vec = jax.ShapeDtypeStruct((NB, cols), F32)
    vecb = jax.ShapeDtypeStruct((NB, cols), BF16)
    vspec = whole((NB, cols))

    own0 = factors[:NB]
    near0, behind0, far0 = send(own0, x_minus), send(own0, x_plus), send(own0, x_far)
    part = (rows - NB) // 2
    own1, own2 = factors[NB : NB + part], factors[NB + part :]
    before1, after1, top1, bottom1 = ring(own1)
    before2, after2, top2, bottom2 = ring(own2)
    same0 = [own0, near0, far0, behind0]
    window = [b for s in same0 for b in (s, send(s, other_core))]
    o1, a1, b1, t1, u1 = (send(v, other_core) for v in (own1, after1, before1, top1, bottom1))
    o2, a2, b2, t2, u2 = (send(v, other_core) for v in (own2, after2, before2, top2, bottom2))

    wspecs = [whole((NB, HB))] * 8
    mat = jax.ShapeDtypeStruct((NB, NB), BF16)
    mspec = whole((NB, NB))
    first = pl.BlockSpec((NB, cols), lambda i, ids: (0, 0))
    y_z0, yb, lh, ll = call(
        start_kernel, ids, (rhs, diag_inv), [first, pl.BlockSpec((1, NB, NB), lambda i, ids: (ids[2], 0, 0))],
        (vec, vecb, mat, mat), (vspec, vspec, mspec, mspec),
    )
    moves = [send(yb, z_move(0, t)) for t in (1, 2, 3)]
    uppers = call(upper_kernel, ids, (diag_inv,), [whole((4, NB, NB))], (mat,) * 6, (mspec,) * 6)

    def forward(j, w, wspec, own, received):
        return call(
            functools.partial(forward_kernel, j, len(received)), ids, (w, own, lh, ll, *received, *window),
            [wspec, vspec, mspec, mspec, *[vspec] * len(received), *wspecs], (vecb, vec, vec, vecb), (vspec,) * 4,
        )

    y0, w, y_z1, yb = forward(0, rhs, first, yb, moves)
    early = [send(y0, y_move(t)) for t in (1, 2, 3)]
    moves = [send(yb, z_move(1, t)) for t in (2, 3)]
    y1, w, y_z2, yb = forward(1, w, vspec, yb, moves)
    y2_in = send(yb, z_move(2, 3))

    def pick(j):
        d = (j - x + NX) % NX
        return jnp.where(d == 0, same0[0], jnp.where(d == 1, same0[1], jnp.where(d == 2, same0[2], same0[3])))

    p23 = send(pick(3), z_move(2, 3))
    p1 = send(jnp.concatenate([pick(2), pick(3)], axis=1), z_move(1, 3))
    p_same = jnp.concatenate([p23, p1], axis=1)
    p_other = send(p_same, other_core)

    pspec = whole((NB, 3 * HB))
    shape = lambda n: jax.ShapeDtypeStruct((n * NB, cols), BF16)
    y2, y_z3, yb3, xs, x23s, x3s = call(
        turn_kernel, ids, (w, y1, yb, y2_in, lh, ll, *uppers, p_same, p_other, *window, before1, after1, o1, o2, *early),
        [vspec] * 4 + [mspec] * 8 + [pspec] * 2 + wspecs + [ANY] * 7,
        (vecb, vec, vecb, shape(3), shape(2), shape(1)),
        (vspec, vspec, vspec, whole((3 * NB, cols)), whole((2 * NB, cols)), vspec),
        scratch=[pltpu.VMEM((NB, cols), F32)], limit=16,
    )
    to0 = send(xs, z_move(3, 0))
    to1 = send(x23s, z_move(3, 1))
    to2 = send(x3s, z_move(3, 2))
    hold = (top1, bottom1, before2, after2, a1, b1)
    late = call(
        late_kernel, ids, (to0, to1, to2, y1, y2, yb3, *hold),
        [whole((3 * NB, cols)), whole((2 * NB, cols))] + [vspec] * 4 + [ANY] * len(hold),
        shape(3), whole((3 * NB, cols)),
    )
    spread = [send(late, y_move(t)) for t in (1, 2, 3)]
    y_own = jnp.where(z == 0, y_z0, jnp.where(z == 1, y_z1, jnp.where(z == 2, y_z2, y_z3)))
    v0 = jnp.where(owner, y0, early[0] + early[1] + early[2])
    v = jnp.where(owner, late, spread[0] + spread[1] + spread[2])
    v_all = jnp.concatenate([v0, v], axis=0)

    tile = part // 2
    block = pl.BlockSpec((tile, HB), lambda i, ids: (i, 0))
    fixed = whole((tile, HB))
    vall_spec = whole((4 * NB, cols))
    out = jax.ShapeDtypeStruct((rows, cols), F32)

    def product(n, distances, source, buffer, near, far):
        at = pl.BlockSpec(
            (pl.Element(tile), pl.Element(cols)), lambda i, ids: (pl.multiple_of(NB + n * part + i * tile, 128), 0)
        )
        buffers = () if buffer is None else (buffer,)
        alias = {3: 0} if buffers else ({1: 0} if source is not rhs else {})
        return call(
            functools.partial(rows_kernel, distances, bool(buffers)), ids, (source, v_all, *buffers, *near, *far),
            [at, vall_spec] + [ANY] * len(buffers) + [block] * len(near) + [fixed] * len(far),
            out, at, grid=(2,), aliases=alias,
        )

    done = product(0, (0, 1, 3), rhs, None, (own1, o1, after1, a1, before1, b1), (top1, t1, bottom1, u1))
    done = product(1, (0, 1, 3), rhs, done, (own2, o2, after2, a2, before2, b2), ())
    done = call(
        window_kernel, ids, (done, rhs, y_own, v0, v, uppers[0], uppers[1], *window),
        [ANY, first, vspec, vspec, whole((3 * NB, cols)), mspec, mspec, *wspecs],
        out, first, scratch=[pltpu.VMEM((NB, cols), F32)], aliases={1: 0},
    )
    return product(1, (), done, None, (), (top2, t2, bottom2, u2))


def solution(mesh):
    placed = (P("col", "row"), P("col", "row"), P())
    return jax.shard_map(body, mesh=mesh, in_specs=placed, out_specs=P("col", "row"), check_vma=False)
```

time: 175 us -> 158 us (0.903)
  the two profiles are of different devices: /device:TPU:87 before, /device:TPU:1 now
where the time goes in v2:
time: 158 us; the launch traced here: 157 us
  starting transfers between devices  52.7 us (33%)
  waiting for transfers between devices  46.7 us (30%)
  Pallas kernels  30.8 us (19%)
  local copies, waits for them, and re-layouts  24.8 us (16%)
    ppermute x43, starting transfers between devices, send(): return lax.ppermute(value, ('row', 'col'), pairs(move))  52.7 us
    ppermute x43, waiting for transfers between devices, send(): return lax.ppermute(value, ('row', 'col'), pairs(move))  46.7 us
    pallas_call x10, Pallas kernels, call(): pl.pallas_call(kernel, grid_spec=pltpu.PrefetchScalarGridSpec(num_scalar_...  30.8 us
    unnamed x129, local copies, waits for them, and re-layouts  18.6 us
  transfers between devices with their start and end apart: 43, of which 8 were waited for; matrix products, arithmetic and copies ran while one was open for 5% of the time, Pallas kernels for 17%

profile of v2, /device:TPU:1, one launch (start us, length us, event | category | flops | bytes accessed | tf_op | source)
XLA Modules:
  0.0 157.3 jit_solution(16601258803896930752)
XLA Ops:
  0.1 1.6 %copy-done = f32[4096,128]{1,0:T(8,128)S(1)} copy-done((f32[4096,128]{1,0:T(8,128)S(1)}, f32[4096,128]{1,0:T(8,128)}, u32[]{:S(2)}) %copy-start) | copy-done | bytes 2097176
  1.7 2.2 %copy-done.2 = f32[4,512,512]{2,1,0:T(8,128)S(1)} copy-done((f32[4,512,512]{2,1,0:T(8,128)S(1)}, f32[4,512,512]{2,1,0:T(8,128)}, u32[]{:S(2)}) %copy-start.2) | copy-done | bytes 4194328
  3.9 1.2 shard_map.37
  5.1 0.8 copy-done.8
  5.8 0.7 copy-done.43
  6.5 4.4 %collective-permute-start = (bf16[512,128]{1,0:T(8,128)(2,1)S(1)}, bf16[512,128]{1,0:T(8,128)(2,1)S(1)}, u32[]{:S(2)}, u32[]{:S(2)}) collective-permute-start(bf16[512,128]{1,0:T(8,128)(2,1)S(1)} %get-tuple-element.29.own_ref), channel_id=1, source_target_pairs={{0,4},{16,20},{32,36},{48,52},{64,68},{80,84},{96,100},{112,116}} | collective-permute-start | bytes 393224 | tf_op jit(solution)/shard_map/ppermute | solution.py:30
  11.0 2.5 %collective-permute-start.4 = (bf16[512,256]{1,0:T(8,128)(2,1)S(1)}, bf16[512,256]{1,0:T(8,128)(2,1)S(1)}, u32[]{:S(2)}, u32[]{:S(2)}) collective-permute-start(bf16[512,256]{1,0:T(8,128)(2,1)S(1)} %slice.21.rest_3_.rest_2_.rest_0_), channel_id=1, source_target_pairs={{0,96},{1,97},{2,98},{3,99},{4,100},{5,101},{6,102},{7,103},{8,104... | collective-permute-start | bytes 786440 | tf_op jit(solution)/shard_map/ppermute | solution.py:30
  14.6 2.6 %collective-permute-start.1 = (bf16[512,128]{1,0:T(8,128)(2,1)S(1)}, bf16[512,128]{1,0:T(8,128)(2,1)S(1)}, u32[]{:S(2)}, u32[]{:S(2)}) collective-permute-start(bf16[512,128]{1,0:T(8,128)(2,1)S(1)} %get-tuple-element.29.own_ref), channel_id=1, source_target_pairs={{0,8},{16,24},{32,40},{48,56},{64,72},{80,88},{96,104},{112,120}} | collective-permute-start | bytes 393224 | tf_op jit(solution)/shard_map/ppermute | solution.py:30
  17.9 1.9 %collective-permute-start.2 = (bf16[512,128]{1,0:T(8,128)(2,1)S(1)}, bf16[512,128]{1,0:T(8,128)(2,1)}, u32[]{:S(2)}, u32[]{:S(2)}) collective-permute-start(bf16[512,128]{1,0:T(8,128)(2,1)S(1)} %get-tuple-element.29.own_ref), channel_id=1, source_target_pairs={{0,12},{16,28},{32,44},{48,60},{64,76},{80,92},{96,108},{112,124}} | collective-permute-start | bytes 393224 | tf_op jit(solution)/shard_map/ppermute | solution.py:30
  19.9 1.3 fusion
  21.9 1.8 %collective-permute-start.3 = (bf16[512,256]{1,0:T(8,128)(2,1)S(1)}, bf16[512,256]{1,0:T(8,128)(2,1)S(1)}, u32[]{:S(2)}, u32[]{:S(2)}) collective-permute-start(bf16[512,256]{1,0:T(8,128)(2,1)S(1)} %slice.21.rest_3_.rest_2_.rest_0_), channel_id=1, source_target_pairs={{0,16},{1,17},{2,18},{3,19},{4,20},{5,21},{6,22},{7,23},{8,24},{9,... | collective-permute-start | bytes 786440 | tf_op jit(solution)/shard_map/ppermute | solution.py:30
  23.7 1.5 collective-permute-start.19
  25.7 3.2 %collective-permute-done.8.rest_9_.rest_8_.rest_6_ = bf16[512,256]{1,0:T(8,128)(2,1)S(1)} collective-permute-done((bf16[512,256]{1,0:T(8,128)(2,1)S(1)}, bf16[512,256]{1,0:T(8,128)(2,1)S(1)}, u32[]{:S(2)}, u32[]{:S(2)}) %collective-permute-start.8) | collective-permute-done | bytes 262176 | tf_op jit(solution)/shard_map/ppermute | solution.py:30
  29.4 1.0 select_select_fusion.1
  31.2 0.7 collective-permute-start.17
  32.0 1.2 copy-done.9
  33.2 0.9 copy-done.52
  34.1 0.9 copy-done.54
  35.0 2.4 %shard_map.38 = (bf16[512,128]{1,0:T(8,128)(2,1)S(1)}, f32[512,128]{1,0:T(8,128)S(1)}, f32[512,128]{1,0:T(8,128)S(1)}, bf16[512,128]{1,0:T(8,128)(2,1)S(1)}) custom-call(s32[4]{0:T(128)S(1)} %pad_add_fusion.ids, f32[4096,128]{1,0:T(8,128)S(1)} %copy-done.1, bf16[512,128]{1,0:T(8,128)(2,1)S(1)} %get-tuple-element.29.own_ref, bf16[512,512]{1,0:T(8,128)(2,1)S(1)} %copy-done.7, ...), custom_call_target="tpu_custom_call" | custom-call | flops 1 | bytes 1 | tf_op jit(solution)/shard_map/pallas_call | solution.py:220
  37.5 0.7 copy-done.45
  38.2 0.8 collective-permute-start.13
  39.0 0.9 collective-permute-start.20
  40.5 1.3 collective-permute-start.10
  41.8 2.2 %collective-permute-start.11 = (bf16[512,128]{1,0:T(8,128)(2,1)S(1)}, bf16[512,128]{1,0:T(8,128)(2,1)S(1)}, u32[]{:S(2)}, u32[]{:S(2)}) collective-permute-start(bf16[512,128]{1,0:T(8,128)(2,1)S(1)} %get-tuple-element.32), channel_id=1, source_target_pairs={{0,2},{4,6},{8,10},{12,14},{16,18},{20,22},{24,26},{28,30},{32,34}... | collective-permute-start | bytes 393224 | tf_op jit(solution)/shard_map/ppermute | solution.py:30
  44.5 1.3 collective-permute-start.12
  45.8 1.5 shard_map.39
  47.3 0.7 copy-done.47
  48.7 1.6 %collective-permute-start.21 = (bf16[1792,256]{1,0:T(8,128)(2,1)S(1)}, bf16[1792,256]{1,0:T(8,128)(2,1)S(1)}, u32[]{:S(2)}, u32[]{:S(2)}) collective-permute-start(bf16[1792,256]{1,0:T(8,128)(2,1)S(1)} %copy-done.23), channel_id=1, source_target_pairs={{0,16},{1,17},{2,18},{3,19},{4,20},{5,21},{6,22},{7,23},{8,24},{9,... | collective-permute-start | bytes 2752520 | tf_op jit(solution)/shard_map/ppermute | solution.py:30
  51.1 0.8 collective-permute-start.18
  51.8 9.3 %collective-permute-done.20.rest_9_.rest_2_ = bf16[1792,256]{1,0:T(8,128)(2,1)S(1)} collective-permute-done((bf16[1792,256]{1,0:T(8,128)(2,1)S(1)}, bf16[1792,256]{1,0:T(8,128)(2,1)S(1)}, u32[]{:S(2)}, u32[]{:S(2)}) %collective-permute-start.20) | collective-permute-done | bytes 917536 | tf_op jit(solution)/shard_map/ppermute | solution.py:30
  61.1 1.9 %collective-permute-start.29 = (bf16[1792,256]{1,0:T(8,128)(2,1)S(1)}, bf16[1792,256]{1,0:T(8,128)(2,1)}, u32[]{:S(2)}, u32[]{:S(2)}) collective-permute-start(bf16[1792,256]{1,0:T(8,128)(2,1)S(1)} %copy-done.21), channel_id=1, source_target_pairs={{0,96},{1,97},{2,98},{3,99},{4,100},{5,101},{6,102},{7,103},{8,104... | collective-permute-start | bytes 2752520 | tf_op jit(solution)/shard_map/ppermute | solution.py:30
  63.0 1.1 collective-permute-start.30
  64.1 1.0 slice.28
  65.3 8.0 %collective-permute-done.28.rest_2_.rest_5_ = bf16[1792,256]{1,0:T(8,128)(2,1)} collective-permute-done((bf16[1792,256]{1,0:T(8,128)(2,1)S(1)}, bf16[1792,256]{1,0:T(8,128)(2,1)}, u32[]{:S(2)}, u32[]{:S(2)}) %collective-permute-start.28) | collective-permute-done | bytes 917536 | tf_op jit(solution)/shard_map/ppermute | solution.py:30
  73.3 2.1 %collective-permute-start.31 = (bf16[1792,256]{1,0:T(8,128)(2,1)}, bf16[1792,256]{1,0:T(8,128)(2,1)}, u32[]{:S(2)}, u32[]{:S(2)}) collective-permute-start(bf16[1792,256]{1,0:T(8,128)(2,1)} %collective-permute-done.19.rest_8_.rest_4_), channel_id=1, source_target_pairs={{0,16},{1,17},{2,18},{3,19},{4,20},{5,21},{6,22},{7,23},{8,24},{9,... | collective-permute-start | bytes 2752520 | tf_op jit(solution)/shard_map/ppermute | solution.py:30
  75.5 1.0 shard_map.40
  76.6 6.4 %shard_map.41 = (bf16[512,128]{1,0:T(8,128)(2,1)S(1)}, f32[512,128]{1,0:T(8,128)S(1)}, bf16[512,128]{1,0:T(8,128)(2,1)S(1)}, bf16[1536,128]{1,0:T(8,128)(2,1)}, ...) custom-call(s32[4]{0:T(128)S(1)} %pad_add_fusion.ids, f32[512,128]{1,0:T(8,128)S(1)} %get-tuple-element.35.w_ref, ...), custom_call_target="tpu_custom_call" | custom-call | flops 1 | bytes 1 | tf_op jit(solution)/shard_map/pallas_call | solution.py:220
  84.4 1.8 %slice.30 = bf16[896,256]{1,0:T(8,128)(2,1)} slice(bf16[1792,256]{1,0:T(8,128)(2,1)} %collective-permute-done.28.rest_2_.rest_5_), slice={[0:896], [0:256]} | slice | bytes 917504 | tf_op jit(solution)/shard_map/slice | solution.py:236
  86.2 6.0 %collective-permute-done.27.rest_1_.rest_8_ = bf16[896,256]{1,0:T(8,128)(2,1)S(1)} collective-permute-done((bf16[896,256]{1,0:T(8,128)(2,1)S(1)}, bf16[896,256]{1,0:T(8,128)(2,1)S(1)}, u32[]{:S(2)}, u32[]{:S(2)}) %collective-permute-start.27) | collective-permute-done | bytes 458784 | tf_op jit(solution)/shard_map/ppermute | solution.py:30
  92.2 1.3 collective-permute-start.23
  93.5 1.8 %slice.31 = bf16[896,256]{1,0:T(8,128)(2,1)} slice(bf16[1792,256]{1,0:T(8,128)(2,1)} %collective-permute-done.29.rest_3_), slice={[896:1792], [0:256]} | slice | bytes 917504 | tf_op jit(solution)/shard_map/slice | solution.py:237
  96.1 3.0 %collective-permute-start.41 = (bf16[896,256]{1,0:T(8,128)(2,1)}, bf16[896,256]{1,0:T(8,128)(2,1)}, u32[]{:S(2)}, u32[]{:S(2)}) collective-permute-start(bf16[896,256]{1,0:T(8,128)(2,1)} %slice.31), channel_id=1, source_target_pairs={{0,96},{1,97},{2,98},{3,99},{4,100},{5,101},{6,102},{7,103},{8,104... | collective-permute-start | bytes 1376264 | tf_op jit(solution)/shard_map/ppermute | solution.py:30
  99.1 0.9 copy-done.25
  100.0 2.0 %collective-permute-start.35 = (bf16[896,256]{1,0:T(8,128)(2,1)}, bf16[896,256]{1,0:T(8,128)(2,1)}, u32[]{:S(2)}, u32[]{:S(2)}) collective-permute-start(bf16[896,256]{1,0:T(8,128)(2,1)} %collective-permute-done.26.rest_0_.rest_6_), channel_id=1, source_target_pairs={{0,16},{1,17},{2,18},{3,19},{4,20},{5,21},{6,22},{7,23},{8,24},{9,... | collective-permute-start | bytes 1376264 | tf_op jit(solution)/shard_map/ppermute | solution.py:30
  101.9 11.7 %collective-permute-done.23.to0 = bf16[1536,128]{1,0:T(8,128)(2,1)} collective-permute-done((bf16[1536,128]{1,0:T(8,128)(2,1)}, bf16[1536,128]{1,0:T(8,128)(2,1)}, u32[]{:S(2)}, u32[]{:S(2)}) %collective-permute-start.23) | collective-permute-done | bytes 393248 | tf_op jit(solution)/shard_map/ppermute | solution.py:30
  113.7 1.2 copy-done.26
  114.9 1.0 copy-done.33
  115.9 0.9 copy-done.42
  116.8 0.9 copy-done.56
  117.7 0.9 copy-done.58
  118.6 0.9 copy-done.60
  119.6 1.8 %shard_map.42 = bf16[1536,128]{1,0:T(8,128)(2,1)S(1)} custom-call(s32[4]{0:T(128)S(1)} %pad_add_fusion.ids, bf16[1536,128]{1,0:T(8,128)(2,1)} %collective-permute-done.23.to0, bf16[1024,128]{1,0:T(8,128)(2,1)S(1)} %copy-done.42, bf16[512,128]{1,0:T(8,128)(2,1)S(1)} %copy-done.60, bf16[512,128]{1,0:T(8,128)(2,1)S(1)} %get-tuple-element.36.y1_ref.y1, ...), custom_call_target="tpu_custom_call" | custom-call | flops 1 | bytes 1 | tf_op jit(solution)/shard_map/pallas_call | solution.py:220
  121.4 1.3 collective-permute-start.32
  122.7 1.3 collective-permute-start.33
  124.0 1.3 collective-permute-start.34
  125.5 1.4 collective-permute-start.37
  127.0 3.0 %collective-permute-done.32 = bf16[1536,128]{1,0:T(8,128)(2,1)S(1)} collective-permute-done((bf16[1536,128]{1,0:T(8,128)(2,1)S(1)}, bf16[1536,128]{1,0:T(8,128)(2,1)S(1)}, u32[]{:S(2)}, u32[]{:S(2)}) %collective-permute-start.32) | collective-permute-done | bytes 393248 | tf_op jit(solution)/shard_map/ppermute | solution.py:30
  130.1 3.5 %collective-permute-start.36 = (bf16[896,256]{1,0:T(8,128)(2,1)S(1)}, bf16[896,256]{1,0:T(8,128)(2,1)S(1)}, u32[]{:S(2)}, u32[]{:S(2)}) collective-permute-start(bf16[896,256]{1,0:T(8,128)(2,1)S(1)} %copy-done.34), channel_id=1, source_target_pairs={{0,16},{1,17},{2,18},{3,19},{4,20},{5,21},{6,22},{7,23},{8,24},{9,... | collective-permute-start | bytes 1376264 | tf_op jit(solution)/shard_map/ppermute | solution.py:30
  133.5 5.0 %collective-permute-done.33 = bf16[1536,128]{1,0:T(8,128)(2,1)S(1)} collective-permute-done((bf16[1536,128]{1,0:T(8,128)(2,1)S(1)}, bf16[1536,128]{1,0:T(8,128)(2,1)S(1)}, u32[]{:S(2)}, u32[]{:S(2)}) %collective-permute-start.33) | collective-permute-done | bytes 393248 | tf_op jit(solution)/shard_map/ppermute | solution.py:30
  138.5 1.9 %collective-permute-start.40 = (bf16[896,256]{1,0:T(8,128)(2,1)}, bf16[896,256]{1,0:T(8,128)(2,1)S(1)}, u32[]{:S(2)}, u32[]{:S(2)}) collective-permute-start(bf16[896,256]{1,0:T(8,128)(2,1)} %collective-permute-done.39.rest_0_), channel_id=1, source_target_pairs={{0,16},{1,17},{2,18},{3,19},{4,20},{5,21},{6,22},{7,23},{8,24},{9,... | collective-permute-start | bytes 1376264 | tf_op jit(solution)/shard_map/ppermute | solution.py:30
  140.6 5.4 %shard_map.43.rest_0_ = f32[4096,128]{1,0:T(8,128)} custom-call(s32[4]{0:T(128)S(1)} %pad_add_fusion.ids, f32[4096,128]{1,0:T(8,128)S(1)} %copy-done.1, bf16[2048,128]{1,0:T(8,128)(2,1)S(1)} %pad_maximum_fusion.1.v_ref, bf16[1792,256]{1,0:T(8,128)(2,1)S(1)} %copy-done.24, bf16[1792,256]{1,0:T(8,128)(2,1)S(1)} %copy-done.20, bf16[1792,256]{1,0:T(8,128)(2,1)S(1)} %copy-done.5, ...), custom_call_target="tpu_custom_call" | custom-call | flops 1 | bytes 1 | tf_op jit(solution)/shard_map/pallas_call | solution.py:220
  146.1 4.3 %shard_map.44.out_in = f32[4096,128]{1,0:T(8,128)} custom-call(s32[4]{0:T(128)S(1)} %pad_add_fusion.ids, f32[4096,128]{1,0:T(8,128)S(1)} %copy-done.1, bf16[2048,128]{1,0:T(8,128)(2,1)S(1)} %pad_maximum_fusion.1.v_ref, f32[4096,128]{1,0:T(8,128)} %shard_map.43.rest_0_, bf16[1792,256]{1,0:T(8,128)(2,1)S(1)} %copy-done.22, ...), custom_call_target="tpu_custom_call", output_to_operand_aliasing={{}: (3, {})} | custom-call | flops 1 | bytes 1 | tf_op jit(solution)/shard_map/pallas_call | solution.py:220
  150.4 3.3 %shard_map.45.b_ref = f32[4096,128]{1,0:T(8,128)} custom-call(s32[4]{0:T(128)S(1)} %pad_add_fusion.ids, f32[4096,128]{1,0:T(8,128)} %shard_map.44.out_in, f32[4096,128]{1,0:T(8,128)S(1)} %copy-done.1, f32[512,128]{1,0:T(8,128)S(1)} %select_select_fusion.y_ref, bf16[512,128]{1,0:T(8,128)(2,1)S(1)} %add_select_fusion.1.v0_ref, ...), custom_call_target="tpu_custom_call", output_to_operand_aliasing={{}: (1, {})} | custom-call | flops 1 | bytes 1 | tf_op jit(solution)/shard_map/pallas_call | solution.py:220
  153.8 3.5 %shard_map.46 = f32[4096,128]{1,0:T(8,128)} custom-call(s32[4]{0:T(128)S(1)} %pad_add_fusion.ids, f32[4096,128]{1,0:T(8,128)} %shard_map.45.b_ref, bf16[2048,128]{1,0:T(8,128)(2,1)S(1)} %pad_maximum_fusion.1.v_ref, bf16[896,256]{1,0:T(8,128)(2,1)} %collective-permute-done.39.rest_0_, ...), custom_call_target="tpu_custom_call", output_to_operand_aliasing={{}: (1, {})} | custom-call | flops 1 | bytes 1 | tf_op jit(solution)/shard_map/pallas_call | solution.py:220
  (175 shorter events, 9.6 us)
Async XLA Ops:
  6.5 13.3 %copy-start.6 = (bf16[512,512]{1,0:T(8,128)(2,1)}, bf16[512,512]{1,0:T(8,128)(2,1)S(1)}, u32[]{:S(2)}) copy-start(bf16[512,512]{1,0:T(8,128)(2,1)S(1)} %get-tuple-element.30.lh_ref.lh) | copy-start | bytes 1572868
  6.5 10.7 %collective-permute-start = (bf16[512,128]{1,0:T(8,128)(2,1)S(1)}, bf16[512,128]{1,0:T(8,128)(2,1)S(1)}, u32[]{:S(2)}, u32[]{:S(2)}) collective-permute-start(bf16[512,128]{1,0:T(8,128)(2,1)S(1)} %get-tuple-element.29.own_ref), channel_id=1, source_target_pairs={{0,4},{16,20},{32,36},{48,52},{64,68},{80,84},{96,100},{112,116}} | collective-permute-start | bytes 393224 | tf_op jit(solution)/shard_map/ppermute | solution.py:30
  11.0 14.2 %collective-permute-start.4 = (bf16[512,256]{1,0:T(8,128)(2,1)S(1)}, bf16[512,256]{1,0:T(8,128)(2,1)S(1)}, u32[]{:S(2)}, u32[]{:S(2)}) collective-permute-start(bf16[512,256]{1,0:T(8,128)(2,1)S(1)} %slice.21.rest_3_.rest_2_.rest_0_), channel_id=1, source_target_pairs={{0,96},{1,97},{2,98},{3,99},{4,100},{5,101},{6,102},{7,103},{8,104... | collective-permute-start | bytes 786440 | tf_op jit(solution)/shard_map/ppermute | solution.py:30
  13.5 12.2 %collective-permute-start.6 = (bf16[512,256]{1,0:T(8,128)(2,1)S(1)}, bf16[512,256]{1,0:T(8,128)(2,1)S(1)}, u32[]{:S(2)}, u32[]{:S(2)}) collective-permute-start(bf16[512,256]{1,0:T(8,128)(2,1)S(1)} %slice.21.rest_3_.rest_2_.rest_0_), channel_id=1, source_target_pairs={{0,64},{1,65},{2,66},{3,67},{4,68},{5,69},{6,70},{7,71},{8,72},{9,... | collective-permute-start | bytes 786440 | tf_op jit(solution)/shard_map/ppermute | solution.py:30
  14.0 14.8 %collective-permute-start.8 = (bf16[512,256]{1,0:T(8,128)(2,1)S(1)}, bf16[512,256]{1,0:T(8,128)(2,1)S(1)}, u32[]{:S(2)}, u32[]{:S(2)}) collective-permute-start(bf16[512,256]{1,0:T(8,128)(2,1)S(1)} %slice.21.rest_3_.rest_2_.rest_0_), channel_id=1, source_target_pairs={{0,32},{1,33},{2,34},{3,35},{4,36},{5,37},{6,38},{7,39},{8,40},{9,... | collective-permute-start | bytes 786440 | tf_op jit(solution)/shard_map/ppermute | solution.py:30
  14.6 6.6 %collective-permute-start.1 = (bf16[512,128]{1,0:T(8,128)(2,1)S(1)}, bf16[512,128]{1,0:T(8,128)(2,1)S(1)}, u32[]{:S(2)}, u32[]{:S(2)}) collective-permute-start(bf16[512,128]{1,0:T(8,128)(2,1)S(1)} %get-tuple-element.29.own_ref), channel_id=1, source_target_pairs={{0,8},{16,24},{32,40},{48,56},{64,72},{80,88},{96,104},{112,120}} | collective-permute-start | bytes 393224 | tf_op jit(solution)/shard_map/ppermute | solution.py:30
  17.9 5.7 %collective-permute-start.2 = (bf16[512,128]{1,0:T(8,128)(2,1)S(1)}, bf16[512,128]{1,0:T(8,128)(2,1)}, u32[]{:S(2)}, u32[]{:S(2)}) collective-permute-start(bf16[512,128]{1,0:T(8,128)(2,1)S(1)} %get-tuple-element.29.own_ref), channel_id=1, source_target_pairs={{0,12},{16,28},{32,44},{48,60},{64,76},{80,92},{96,108},{112,124}} | collective-permute-start | bytes 393224 | tf_op jit(solution)/shard_map/ppermute | solution.py:30
  21.2 10.8 %copy-start.7 = (bf16[512,512]{1,0:T(8,128)(2,1)S(1)}, bf16[512,512]{1,0:T(8,128)(2,1)}, u32[]{:S(2)}) copy-start(bf16[512,512]{1,0:T(8,128)(2,1)} %copy-done.6) | copy-start | bytes 1572868
  21.9 8.6 %collective-permute-start.3 = (bf16[512,256]{1,0:T(8,128)(2,1)S(1)}, bf16[512,256]{1,0:T(8,128)(2,1)S(1)}, u32[]{:S(2)}, u32[]{:S(2)}) collective-permute-start(bf16[512,256]{1,0:T(8,128)(2,1)S(1)} %slice.21.rest_3_.rest_2_.rest_0_), channel_id=1, source_target_pairs={{0,16},{1,17},{2,18},{3,19},{4,20},{5,21},{6,22},{7,23},{8,24},{9,... | collective-permute-start | bytes 786440 | tf_op jit(solution)/shard_map/ppermute | solution.py:30
  23.7 27.4 %collective-permute-start.19 = (bf16[1792,256]{1,0:T(8,128)(2,1)}, bf16[1792,256]{1,0:T(8,128)(2,1)}, u32[]{:S(2)}, u32[]{:S(2)}) collective-permute-start(bf16[1792,256]{1,0:T(8,128)(2,1)} %get-tuple-element.56.rest_0_), channel_id=1, source_target_pairs={{0,32},{1,33},{2,34},{3,35},{4,36},{5,37},{6,38},{7,39},{8,40},{9,... | collective-permute-start | bytes 2752520 | tf_op jit(solution)/shard_map/ppermute | solution.py:30
  25.2 6.0 %collective-permute-start.5 = (bf16[512,256]{1,0:T(8,128)(2,1)S(1)}, bf16[512,256]{1,0:T(8,128)(2,1)S(1)}, u32[]{:S(2)}, u32[]{:S(2)}) collective-permute-start(bf16[512,256]{1,0:T(8,128)(2,1)S(1)} %collective-permute-done.4.rest_5_.rest_4_.rest_2_), channel_id=1, source_target_pairs={{0,16},{1,17},{2,18},{3,19},{4,20},{5,21},{6,22},{7,23},{8,24},{9,... | collective-permute-start | bytes 786440 | tf_op jit(solution)/shard_map/ppermute | solution.py:30
  25.7 6.3 %collective-permute-start.7 = (bf16[512,256]{1,0:T(8,128)(2,1)S(1)}, bf16[512,256]{1,0:T(8,128)(2,1)S(1)}, u32[]{:S(2)}, u32[]{:S(2)}) collective-permute-start(bf16[512,256]{1,0:T(8,128)(2,1)S(1)} %collective-permute-done.6.rest_7_.rest_6_.rest_4_), channel_id=1, source_target_pairs={{0,16},{1,17},{2,18},{3,19},{4,20},{5,21},{6,22},{7,23},{8,24},{9,... | collective-permute-start | bytes 786440 | tf_op jit(solution)/shard_map/ppermute | solution.py:30
  28.9 3.1 %collective-permute-start.9 = (bf16[512,256]{1,0:T(8,128)(2,1)S(1)}, bf16[512,256]{1,0:T(8,128)(2,1)S(1)}, u32[]{:S(2)}, u32[]{:S(2)}) collective-permute-start(bf16[512,256]{1,0:T(8,128)(2,1)S(1)} %collective-permute-done.8.rest_9_.rest_8_.rest_6_), channel_id=1, source_target_pairs={{0,16},{1,17},{2,18},{3,19},{4,20},{5,21},{6,22},{7,23},{8,24},{9,... | collective-permute-start | bytes 786440 | tf_op jit(solution)/shard_map/ppermute | solution.py:30
  30.5 9.4 %collective-permute-start.16 = (bf16[512,256]{1,0:T(8,128)(2,1)S(1)}, bf16[512,256]{1,0:T(8,128)(2,1)S(1)}, u32[]{:S(2)}, u32[]{:S(2)}) collective-permute-start(bf16[512,256]{1,0:T(8,128)(2,1)S(1)} %get-tuple-element.54), channel_id=1, source_target_pairs={{8,12},{24,28},{40,44},{56,60},{72,76},{88,92},{104,108},{120,124}} | collective-permute-start | bytes 786440 | tf_op jit(solution)/shard_map/ppermute | solution.py:30
  31.2 45.3 %copy-start.11 = (bf16[512,256]{1,0:T(8,128)(2,1)}, bf16[512,256]{1,0:T(8,128)(2,1)S(1)}, u32[]{:S(2)}) copy-start(bf16[512,256]{1,0:T(8,128)(2,1)S(1)} %collective-permute-done.5.rest_6_.rest_5_.rest_3_) | copy-start | bytes 786436
  31.2 19.1 %collective-permute-start.17 = (bf16[512,512]{1,0:T(8,128)(2,1)S(1)}, bf16[512,512]{1,0:T(8,128)(2,1)S(1)}, u32[]{:S(2)}, u32[]{:S(2)}) collective-permute-start(bf16[512,512]{1,0:T(8,128)(2,1)S(1)} %pad_maximum_fusion), channel_id=1, source_target_pairs={{4,12},{20,28},{36,44},{52,60},{68,76},{84,92},{100,108},{116,124}} | collective-permute-start | bytes 1572872 | tf_op jit(solution)/shard_map/ppermute | solution.py:30
  31.9 44.6 %copy-start.13 = (bf16[512,256]{1,0:T(8,128)(2,1)}, bf16[512,256]{1,0:T(8,128)(2,1)S(1)}, u32[]{:S(2)}) copy-start(bf16[512,256]{1,0:T(8,128)(2,1)S(1)} %collective-permute-done.7.rest_8_.rest_7_.rest_5_) | copy-start | bytes 786436
  32.0 44.5 %copy-start.15 = (bf16[512,256]{1,0:T(8,128)(2,1)}, bf16[512,256]{1,0:T(8,128)(2,1)S(1)}, u32[]{:S(2)}) copy-start(bf16[512,256]{1,0:T(8,128)(2,1)S(1)} %collective-permute-done.9.rest_10_.rest_9_.rest_7_) | copy-start | bytes 786436
  38.2 12.8 %copy-start.61 = (bf16[512,128]{1,0:T(8,128)(2,1)}, bf16[512,128]{1,0:T(8,128)(2,1)S(1)}, u32[]{:S(2)}) copy-start(bf16[512,128]{1,0:T(8,128)(2,1)S(1)} %get-tuple-element.32) | copy-start | bytes 393220
  38.2 12.1 %copy-start.21 = (bf16[1792,256]{1,0:T(8,128)(2,1)S(1)}, bf16[1792,256]{1,0:T(8,128)(2,1)}, u32[]{:S(2)}) copy-start(bf16[1792,256]{1,0:T(8,128)(2,1)} %get-tuple-element.55.rest_1_) | copy-start | bytes 2752516
  38.2 2.3 %collective-permute-start.13 = (bf16[512,128]{1,0:T(8,128)(2,1)S(1)}, bf16[512,128]{1,0:T(8,128)(2,1)S(1)}, u32[]{:S(2)}, u32[]{:S(2)}) collective-permute-start(bf16[512,128]{1,0:T(8,128)(2,1)S(1)} %get-tuple-element.34.own_ref), channel_id=1, source_target_pairs={{4,8},{20,24},{36,40},{52,56},{68,72},{84,88},{100,104},{116,120}} | collective-permute-start | bytes 393224 | tf_op jit(solution)/shard_map/ppermute | solution.py:30
  39.0 22.2 %collective-permute-start.20 = (bf16[1792,256]{1,0:T(8,128)(2,1)S(1)}, bf16[1792,256]{1,0:T(8,128)(2,1)S(1)}, u32[]{:S(2)}, u32[]{:S(2)}) collective-permute-start(bf16[1792,256]{1,0:T(8,128)(2,1)S(1)} %copy-done.23), channel_id=1, source_target_pairs={{0,96},{1,97},{2,98},{3,99},{4,100},{5,101},{6,102},{7,103},{8,104... | collective-permute-start | bytes 2752520 | tf_op jit(solution)/shard_map/ppermute | solution.py:30
  39.8 2.0 %collective-permute-start.14 = (bf16[512,128]{1,0:T(8,128)(2,1)S(1)}, bf16[512,128]{1,0:T(8,128)(2,1)S(1)}, u32[]{:S(2)}, u32[]{:S(2)}) collective-permute-start(bf16[512,128]{1,0:T(8,128)(2,1)S(1)} %get-tuple-element.34.own_ref), channel_id=1, source_target_pairs={{4,12},{20,28},{36,44},{52,60},{68,76},{84,92},{100,108},{116,124}} | collective-permute-start | bytes 393224 | tf_op jit(solution)/shard_map/ppermute | solution.py:30
  40.5 3.9 %collective-permute-start.10 = (bf16[512,128]{1,0:T(8,128)(2,1)S(1)}, bf16[512,128]{1,0:T(8,128)(2,1)S(1)}, u32[]{:S(2)}, u32[]{:S(2)}) collective-permute-start(bf16[512,128]{1,0:T(8,128)(2,1)S(1)} %get-tuple-element.32), channel_id=1, source_target_pairs={{0,1},{4,5},{8,9},{12,13},{16,17},{20,21},{24,25},{28,29},{32,33},... | collective-permute-start | bytes 393224 | tf_op jit(solution)/shard_map/ppermute | solution.py:30
  41.8 6.2 %collective-permute-start.11 = (bf16[512,128]{1,0:T(8,128)(2,1)S(1)}, bf16[512,128]{1,0:T(8,128)(2,1)S(1)}, u32[]{:S(2)}, u32[]{:S(2)}) collective-permute-start(bf16[512,128]{1,0:T(8,128)(2,1)S(1)} %get-tuple-element.32), channel_id=1, source_target_pairs={{0,2},{4,6},{8,10},{12,14},{16,18},{20,22},{24,26},{28,30},{32,34}... | collective-permute-start | bytes 393224 | tf_op jit(solution)/shard_map/ppermute | solution.py:30
  44.5 32.1 %copy-start.35 = (bf16[512,128]{1,0:T(8,128)(2,1)}, bf16[512,128]{1,0:T(8,128)(2,1)S(1)}, u32[]{:S(2)}) copy-start(bf16[512,128]{1,0:T(8,128)(2,1)S(1)} %collective-permute-done.10.rest_12_) | copy-start | bytes 393220
  44.5 4.2 %collective-permute-start.12 = (bf16[512,128]{1,0:T(8,128)(2,1)S(1)}, bf16[512,128]{1,0:T(8,128)(2,1)S(1)}, u32[]{:S(2)}, u32[]{:S(2)}) collective-permute-start(bf16[512,128]{1,0:T(8,128)(2,1)S(1)} %get-tuple-element.32), channel_id=1, source_target_pairs={{0,3},{4,7},{8,11},{12,15},{16,19},{20,23},{24,27},{28,31},{32,35}... | collective-permute-start | bytes 393224 | tf_op jit(solution)/shard_map/ppermute | solution.py:30
  45.8 29.7 %copy-start.3 = (f32[4,512,512]{2,1,0:T(8,128)S(1)}, f32[4,512,512]{2,1,0:T(8,128)}, u32[]{:S(2)}) copy-start(f32[4,512,512]{2,1,0:T(8,128)} %d_ref.3) | copy-start | bytes 12582916
  48.0 28.5 %copy-start.37 = (bf16[512,128]{1,0:T(8,128)(2,1)}, bf16[512,128]{1,0:T(8,128)(2,1)S(1)}, u32[]{:S(2)}) copy-start(bf16[512,128]{1,0:T(8,128)(2,1)S(1)} %collective-permute-done.11.rest_13_) | copy-start | bytes 393220
  48.0 2.4 %collective-permute-start.15 = (bf16[512,128]{1,0:T(8,128)(2,1)S(1)}, bf16[512,128]{1,0:T(8,128)(2,1)S(1)}, u32[]{:S(2)}, u32[]{:S(2)}) collective-permute-start(bf16[512,128]{1,0:T(8,128)(2,1)S(1)} %get-tuple-element.37.own_ref), channel_id=1, source_target_pairs={{8,12},{24,28},{40,44},{56,60},{72,76},{88,92},{104,108},{120,124}} | collective-permute-start | bytes 393224 | tf_op jit(solution)/shard_map/ppermute | solution.py:30
  48.7 27.9 %copy-start.39 = (bf16[512,128]{1,0:T(8,128)(2,1)}, bf16[512,128]{1,0:T(8,128)(2,1)S(1)}, u32[]{:S(2)}) copy-start(bf16[512,128]{1,0:T(8,128)(2,1)S(1)} %collective-permute-done.12.rest_14_) | copy-start | bytes 393220
  48.7 14.3 %collective-permute-start.21 = (bf16[1792,256]{1,0:T(8,128)(2,1)S(1)}, bf16[1792,256]{1,0:T(8,128)(2,1)S(1)}, u32[]{:S(2)}, u32[]{:S(2)}) collective-permute-start(bf16[1792,256]{1,0:T(8,128)(2,1)S(1)} %copy-done.23), channel_id=1, source_target_pairs={{0,16},{1,17},{2,18},{3,19},{4,20},{5,21},{6,22},{7,23},{8,24},{9,... | collective-permute-start | bytes 2752520 | tf_op jit(solution)/shard_map/ppermute | solution.py:30
  50.3 14.8 %collective-permute-start.22 = (bf16[1792,256]{1,0:T(8,128)(2,1)S(1)}, bf16[1792,256]{1,0:T(8,128)(2,1)S(1)}, u32[]{:S(2)}, u32[]{:S(2)}) collective-permute-start(bf16[1792,256]{1,0:T(8,128)(2,1)S(1)} %copy-done.21), channel_id=1, source_target_pairs={{0,16},{1,17},{2,18},{3,19},{4,20},{5,21},{6,22},{7,23},{8,24},{9,... | collective-permute-start | bytes 2752520 | tf_op jit(solution)/shard_map/ppermute | solution.py:30
  50.4 22.8 %collective-permute-start.28 = (bf16[1792,256]{1,0:T(8,128)(2,1)S(1)}, bf16[1792,256]{1,0:T(8,128)(2,1)}, u32[]{:S(2)}, u32[]{:S(2)}) collective-permute-start(bf16[1792,256]{1,0:T(8,128)(2,1)S(1)} %copy-done.21), channel_id=1, source_target_pairs={{0,32},{1,33},{2,34},{3,35},{4,36},{5,37},{6,38},{7,39},{8,40},{9,... | collective-permute-start | bytes 2752520 | tf_op jit(solution)/shard_map/ppermute | solution.py:30
  51.1 24.3 %collective-permute-start.18 = (bf16[512,768]{1,0:T(8,128)(2,1)S(1)}, bf16[512,768]{1,0:T(8,128)(2,1)S(1)}, u32[]{:S(2)}, u32[]{:S(2)}) collective-permute-start(bf16[512,768]{1,0:T(8,128)(2,1)S(1)} %constant_dynamic-update-slice_fusion.p_same), channel_id=1, source_target_pairs={{0,16},{1,17},{2,18},{3,19},{4,20},{5,21},{6,22},{7,23},{8,24},{9,... | collective-permute-start | bytes 2359304 | tf_op jit(solution)/shard_map/ppermute | solution.py:30
  61.1 15.4 %copy-start.4 = (bf16[1792,256]{1,0:T(8,128)(2,1)}, bf16[1792,256]{1,0:T(8,128)(2,1)S(1)}, u32[]{:S(2)}) copy-start(bf16[1792,256]{1,0:T(8,128)(2,1)S(1)} %collective-permute-done.20.rest_9_.rest_2_) | copy-start | bytes 2752516
  61.1 21.9 %collective-permute-start.29 = (bf16[1792,256]{1,0:T(8,128)(2,1)S(1)}, bf16[1792,256]{1,0:T(8,128)(2,1)}, u32[]{:S(2)}, u32[]{:S(2)}) collective-permute-start(bf16[1792,256]{1,0:T(8,128)(2,1)S(1)} %copy-done.21), channel_id=1, source_target_pairs={{0,96},{1,97},{2,98},{3,99},{4,100},{5,101},{6,102},{7,103},{8,104... | collective-permute-start | bytes 2752520 | tf_op jit(solution)/shard_map/ppermute | solution.py:30
  63.0 13.5 %copy-start.19 = (bf16[1792,256]{1,0:T(8,128)(2,1)}, bf16[1792,256]{1,0:T(8,128)(2,1)S(1)}, u32[]{:S(2)}) copy-start(bf16[1792,256]{1,0:T(8,128)(2,1)S(1)} %collective-permute-done.21.rest_10_.rest_1_) | copy-start | bytes 2752516
  63.0 36.0 %collective-permute-start.30 = (bf16[1792,256]{1,0:T(8,128)(2,1)S(1)}, bf16[1792,256]{1,0:T(8,128)(2,1)S(1)}, u32[]{:S(2)}, u32[]{:S(2)}) collective-permute-start(bf16[1792,256]{1,0:T(8,128)(2,1)S(1)} %collective-permute-done.20.rest_9_.rest_2_), channel_id=1, source_target_pairs={{0,16},{1,17},{2,18},{3,19},{4,20},{5,21},{6,22},{7,23},{8,24},{9,... | collective-permute-start | bytes 2752520 | tf_op jit(solution)/shard_map/ppermute | solution.py:30
  65.2 11.4 %copy-start.17 = (bf16[1792,256]{1,0:T(8,128)(2,1)}, bf16[1792,256]{1,0:T(8,128)(2,1)S(1)}, u32[]{:S(2)}) copy-start(bf16[1792,256]{1,0:T(8,128)(2,1)S(1)} %collective-permute-done.22.rest_11_.rest_2_) | copy-start | bytes 2752516
  65.2 18.5 %collective-permute-start.26 = (bf16[896,256]{1,0:T(8,128)(2,1)S(1)}, bf16[896,256]{1,0:T(8,128)(2,1)}, u32[]{:S(2)}, u32[]{:S(2)}) collective-permute-start(bf16[896,256]{1,0:T(8,128)(2,1)S(1)} %slice.28), channel_id=1, source_target_pairs={{0,32},{1,33},{2,34},{3,35},{4,36},{5,37},{6,38},{7,39},{8,40},{9,... | collective-permute-start | bytes 1376264 | tf_op jit(solution)/shard_map/ppermute | solution.py:30
  73.3 28.7 %collective-permute-start.31 = (bf16[1792,256]{1,0:T(8,128)(2,1)}, bf16[1792,256]{1,0:T(8,128)(2,1)}, u32[]{:S(2)}, u32[]{:S(2)}) collective-permute-start(bf16[1792,256]{1,0:T(8,128)(2,1)} %collective-permute-done.19.rest_8_.rest_4_), channel_id=1, source_target_pairs={{0,16},{1,17},{2,18},{3,19},{4,20},{5,21},{6,22},{7,23},{8,24},{9,... | collective-permute-start | bytes 2752520 | tf_op jit(solution)/shard_map/ppermute | solution.py:30
  75.4 16.8 %collective-permute-start.27 = (bf16[896,256]{1,0:T(8,128)(2,1)S(1)}, bf16[896,256]{1,0:T(8,128)(2,1)S(1)}, u32[]{:S(2)}, u32[]{:S(2)}) collective-permute-start(bf16[896,256]{1,0:T(8,128)(2,1)S(1)} %slice.29), channel_id=1, source_target_pairs={{0,96},{1,97},{2,98},{3,99},{4,100},{5,101},{6,102},{7,103},{8,104... | collective-permute-start | bytes 1376264 | tf_op jit(solution)/shard_map/ppermute | solution.py:30
  83.0 16.0 %copy-start.49 = (f32[512,128]{1,0:T(8,128)}, f32[512,128]{1,0:T(8,128)S(1)}, u32[]{:S(2)}) copy-start(f32[512,128]{1,0:T(8,128)S(1)} %get-tuple-element.52) | copy-start | bytes 786436
  83.0 16.0 %copy-start.55 = (bf16[512,128]{1,0:T(8,128)(2,1)}, bf16[512,128]{1,0:T(8,128)(2,1)S(1)}, u32[]{:S(2)}) copy-start(bf16[512,128]{1,0:T(8,128)(2,1)S(1)} %get-tuple-element.47.y2) | copy-start | bytes 393220
  83.0 16.0 %copy-start.57 = (bf16[512,128]{1,0:T(8,128)(2,1)}, bf16[512,128]{1,0:T(8,128)(2,1)S(1)}, u32[]{:S(2)}) copy-start(bf16[512,128]{1,0:T(8,128)(2,1)S(1)} %get-tuple-element.48.y3) | copy-start | bytes 393220
  83.0 9.2 %collective-permute-start.25 = (bf16[512,128]{1,0:T(8,128)(2,1)S(1)}, bf16[512,128]{1,0:T(8,128)(2,1)S(1)}, u32[]{:S(2)}, u32[]{:S(2)}) collective-permute-start(bf16[512,128]{1,0:T(8,128)(2,1)S(1)} %get-tuple-element.46), channel_id=1, source_target_pairs={{12,8},{28,24},{44,40},{60,56},{76,72},{92,88},{108,104},{124,120}} | collective-permute-start | bytes 393224 | tf_op jit(solution)/shard_map/ppermute | solution.py:30
  83.7 11.7 %collective-permute-start.24 = (bf16[1024,128]{1,0:T(8,128)(2,1)S(1)}, bf16[1024,128]{1,0:T(8,128)(2,1)S(1)}, u32[]{:S(2)}, u32[]{:S(2)}) collective-permute-start(bf16[1024,128]{1,0:T(8,128)(2,1)S(1)} %get-tuple-element.45), channel_id=1, source_target_pairs={{12,4},{28,20},{44,36},{60,52},{76,68},{92,84},{108,100},{124,116}} | collective-permute-start | bytes 786440 | tf_op jit(solution)/shard_map/ppermute | solution.py:30
  92.2 31.8 %collective-permute-start.39 = (bf16[896,256]{1,0:T(8,128)(2,1)}, bf16[896,256]{1,0:T(8,128)(2,1)}, u32[]{:S(2)}, u32[]{:S(2)}) collective-permute-start(bf16[896,256]{1,0:T(8,128)(2,1)} %slice.30), channel_id=1, source_target_pairs={{0,32},{1,33},{2,34},{3,35},{4,36},{5,37},{6,38},{7,39},{8,40},{9,... | collective-permute-start | bytes 1376264 | tf_op jit(solution)/shard_map/ppermute | solution.py:30
  92.2 21.5 %collective-permute-start.23 = (bf16[1536,128]{1,0:T(8,128)(2,1)}, bf16[1536,128]{1,0:T(8,128)(2,1)}, u32[]{:S(2)}, u32[]{:S(2)}) collective-permute-start(bf16[1536,128]{1,0:T(8,128)(2,1)} %get-tuple-element.44), channel_id=1, source_target_pairs={{12,0},{28,16},{44,32},{60,48},{76,64},{92,80},{108,96},{124,112}} | collective-permute-start | bytes 1179656 | tf_op jit(solution)/shard_map/ppermute | solution.py:30
  96.1 29.4 %collective-permute-start.41 = (bf16[896,256]{1,0:T(8,128)(2,1)}, bf16[896,256]{1,0:T(8,128)(2,1)}, u32[]{:S(2)}, u32[]{:S(2)}) collective-permute-start(bf16[896,256]{1,0:T(8,128)(2,1)} %slice.31), channel_id=1, source_target_pairs={{0,96},{1,97},{2,98},{3,99},{4,100},{5,101},{6,102},{7,103},{8,104... | collective-permute-start | bytes 1376264 | tf_op jit(solution)/shard_map/ppermute | solution.py:30
  100.0 26.8 %collective-permute-start.35 = (bf16[896,256]{1,0:T(8,128)(2,1)}, bf16[896,256]{1,0:T(8,128)(2,1)}, u32[]{:S(2)}, u32[]{:S(2)}) collective-permute-start(bf16[896,256]{1,0:T(8,128)(2,1)} %collective-permute-done.26.rest_0_.rest_6_), channel_id=1, source_target_pairs={{0,16},{1,17},{2,18},{3,19},{4,20},{5,21},{6,22},{7,23},{8,24},{9,... | collective-permute-start | bytes 1376264 | tf_op jit(solution)/shard_map/ppermute | solution.py:30
  121.4 8.7 %collective-permute-start.32 = (bf16[1536,128]{1,0:T(8,128)(2,1)S(1)}, bf16[1536,128]{1,0:T(8,128)(2,1)S(1)}, u32[]{:S(2)}, u32[]{:S(2)}) collective-permute-start(bf16[1536,128]{1,0:T(8,128)(2,1)S(1)} %shard_map.42), channel_id=1, source_target_pairs={{0,1},{4,5},{8,9},{12,13},{16,17},{20,21},{24,25},{28,29},{32,33},... | collective-permute-start | bytes 1179656 | tf_op jit(solution)/shard_map/ppermute | solution.py:30
  122.7 15.8 %collective-permute-start.33 = (bf16[1536,128]{1,0:T(8,128)(2,1)S(1)}, bf16[1536,128]{1,0:T(8,128)(2,1)S(1)}, u32[]{:S(2)}, u32[]{:S(2)}) collective-permute-start(bf16[1536,128]{1,0:T(8,128)(2,1)S(1)} %shard_map.42), channel_id=1, source_target_pairs={{0,2},{4,6},{8,10},{12,14},{16,18},{20,22},{24,26},{28,30},{32,34}... | collective-permute-start | bytes 1179656 | tf_op jit(solution)/shard_map/ppermute | solution.py:30
  124.0 16.4 %collective-permute-start.34 = (bf16[1536,128]{1,0:T(8,128)(2,1)S(1)}, bf16[1536,128]{1,0:T(8,128)(2,1)S(1)}, u32[]{:S(2)}, u32[]{:S(2)}) collective-permute-start(bf16[1536,128]{1,0:T(8,128)(2,1)S(1)} %shard_map.42), channel_id=1, source_target_pairs={{0,3},{4,7},{8,11},{12,15},{16,19},{20,23},{24,27},{28,31},{32,35}... | collective-permute-start | bytes 1179656 | tf_op jit(solution)/shard_map/ppermute | solution.py:30
  125.5 20.6 %collective-permute-start.37 = (bf16[1792,256]{1,0:T(8,128)(2,1)}, bf16[1792,256]{1,0:T(8,128)(2,1)S(1)}, u32[]{:S(2)}, u32[]{:S(2)}) collective-permute-start(bf16[1792,256]{1,0:T(8,128)(2,1)} %collective-permute-done.29.rest_3_), channel_id=1, source_target_pairs={{0,16},{1,17},{2,18},{3,19},{4,20},{5,21},{6,22},{7,23},{8,24},{9,... | collective-permute-start | bytes 2752520 | tf_op jit(solution)/shard_map/ppermute | solution.py:30
  126.8 19.3 %collective-permute-start.38 = (bf16[1792,256]{1,0:T(8,128)(2,1)}, bf16[1792,256]{1,0:T(8,128)(2,1)S(1)}, u32[]{:S(2)}, u32[]{:S(2)}) collective-permute-start(bf16[1792,256]{1,0:T(8,128)(2,1)} %collective-permute-done.28.rest_2_.rest_5_), channel_id=1, source_target_pairs={{0,16},{1,17},{2,18},{3,19},{4,20},{5,21},{6,22},{7,23},{8,24},{9,... | collective-permute-start | bytes 2752520 | tf_op jit(solution)/shard_map/ppermute | solution.py:30
  126.9 13.7 %copy-start.5 = (bf16[1792,256]{1,0:T(8,128)(2,1)S(1)}, bf16[1792,256]{1,0:T(8,128)(2,1)}, u32[]{:S(2)}) copy-start(bf16[1792,256]{1,0:T(8,128)(2,1)} %copy-done.4) | copy-start | bytes 2752516
  126.9 13.7 %copy-start.20 = (bf16[1792,256]{1,0:T(8,128)(2,1)S(1)}, bf16[1792,256]{1,0:T(8,128)(2,1)}, u32[]{:S(2)}) copy-start(bf16[1792,256]{1,0:T(8,128)(2,1)} %copy-done.19) | copy-start | bytes 2752516
  127.0 13.7 %copy-start.24 = (bf16[1792,256]{1,0:T(8,128)(2,1)S(1)}, bf16[1792,256]{1,0:T(8,128)(2,1)}, u32[]{:S(2)}) copy-start(bf16[1792,256]{1,0:T(8,128)(2,1)} %get-tuple-element.56.rest_0_) | copy-start | bytes 2752516
  127.0 13.6 %copy-start.27 = (bf16[1792,256]{1,0:T(8,128)(2,1)S(1)}, bf16[1792,256]{1,0:T(8,128)(2,1)}, u32[]{:S(2)}) copy-start(bf16[1792,256]{1,0:T(8,128)(2,1)} %copy-done.25) | copy-start | bytes 2752516
  130.1 10.5 %collective-permute-start.36 = (bf16[896,256]{1,0:T(8,128)(2,1)S(1)}, bf16[896,256]{1,0:T(8,128)(2,1)S(1)}, u32[]{:S(2)}, u32[]{:S(2)}) collective-permute-start(bf16[896,256]{1,0:T(8,128)(2,1)S(1)} %copy-done.34), channel_id=1, source_target_pairs={{0,16},{1,17},{2,18},{3,19},{4,20},{5,21},{6,22},{7,23},{8,24},{9,... | collective-permute-start | bytes 1376264 | tf_op jit(solution)/shard_map/ppermute | solution.py:30
  138.5 15.3 %collective-permute-start.40 = (bf16[896,256]{1,0:T(8,128)(2,1)}, bf16[896,256]{1,0:T(8,128)(2,1)S(1)}, u32[]{:S(2)}, u32[]{:S(2)}) collective-permute-start(bf16[896,256]{1,0:T(8,128)(2,1)} %collective-permute-done.39.rest_0_), channel_id=1, source_target_pairs={{0,16},{1,17},{2,18},{3,19},{4,20},{5,21},{6,22},{7,23},{8,24},{9,... | collective-permute-start | bytes 1376264 | tf_op jit(solution)/shard_map/ppermute | solution.py:30
  140.4 13.4 %collective-permute-start.42 = (bf16[896,256]{1,0:T(8,128)(2,1)}, bf16[896,256]{1,0:T(8,128)(2,1)S(1)}, u32[]{:S(2)}, u32[]{:S(2)}) collective-permute-start(bf16[896,256]{1,0:T(8,128)(2,1)} %collective-permute-done.41.rest_2_), channel_id=1, source_target_pairs={{0,16},{1,17},{2,18},{3,19},{4,20},{5,21},{6,22},{7,23},{8,24},{9,... | collective-permute-start | bytes 1376264 | tf_op jit(solution)/shard_map/ppermute | solution.py:30
  (43 other events, 173.9 us)

commit v3 on v0

v3 whole, which is shorter than its diff:
```python
import functools

import jax
import jax.numpy as jnp
from jax import lax
from jax.experimental import pallas as pl
from jax.experimental.pallas import tpu as pltpu
from jax.sharding import PartitionSpec as P

NX, NH, NZ, NY = 4, 2, 4, 4
NB = 512
HB = 256
F32, BF16 = jnp.float32, jnp.bfloat16


def pairs(move):
    out = []
    for r in range(NX * NH):
        for c in range(NZ * NY):
            x, h = divmod(r, NH)
            z, y = divmod(c, NY)
            to = move(x, h, z, y)
            if to is not None:
                x2, h2, z2, y2 = to
                out.append((r * NZ * NY + c, ((x2 % NX) * NH + h2 % NH) * NZ * NY + (z2 % NZ) * NY + y2 % NY))
    return out


def send(value, move):
    return lax.ppermute(value, ("row", "col"), pairs(move))


def other_core(x, h, z, y):
    return (x, 1 - h, z, y)


def z_move(src, dst):
    return lambda x, h, z, y: (x, h, dst, y) if (y == 0 and z == src) else None


def y_move(step):
    return lambda x, h, z, y: (x, h, z, step) if y == 0 else None


def dot(a, b):
    return jnp.dot(a, b, preferred_element_type=F32)


def split(a):
    hi = a.astype(BF16)
    return hi, (a - hi.astype(F32)).astype(BF16)


def apply(hi_ref, lo_ref, v):
    vh, vl = split(v)
    return dot(hi_ref[...], vh) + (dot(hi_ref[...], vl) + dot(lo_ref[...], vh))


def lower_mask(d):
    i = lax.broadcasted_iota(jnp.int32, d.shape, 0)
    j = lax.broadcasted_iota(jnp.int32, d.shape, 1)
    return jnp.where(i > j, d, 0.0)


def upper_mask(d):
    i = lax.broadcasted_iota(jnp.int32, d.shape, 0)
    j = lax.broadcasted_iota(jnp.int32, d.shape, 1)
    return jnp.where(i <= j, d, 0.0)


def start_kernel(ids, b_ref, d_ref, y_ref, yb_ref, lh_ref, ll_ref):
    lh_ref[...], ll_ref[...] = split(lower_mask(d_ref[0]))
    w = b_ref[...]
    y = w + apply(lh_ref, ll_ref, w)
    y_ref[...] = y
    yb_ref[...] = y.astype(BF16)


def upper_kernel(ids, d_ref, *out):
    for n, j in enumerate((ids[2], 1, 2)):
        out[2 * n][...], out[2 * n + 1][...] = split(upper_mask(d_ref[j]))


def own_or_received(ids, j, own_ref, received):
    total = received[0][...]
    for piece in received[1:]:
        total = total + piece[...]
    return jnp.where(ids[2] == j, own_ref[...], total)


def columns(j):
    return slice(j * NB, (j + 1) * NB)


def forward_kernel(j, ids, w_ref, own_ref, prior_ref, lh_ref, ll_ref, f_ref, *rest):
    received, (v_ref, w_out, y_ref, yb_ref) = rest[:-4], rest[-4:]
    v = own_or_received(ids, j, own_ref, received)
    v_ref[...] = v
    w = w_ref[...] - dot(f_ref[...], v)
    w_out[...] = w
    y = w + apply(lh_ref, ll_ref, w)
    y_ref[...] = jnp.where(ids[2] == j + 1, y, prior_ref[...])
    yb_ref[...] = y.astype(BF16)


def pick_kernel(ids, f2_ref, f3_ref, after_ref, p23_ref, p1_ref):
    p23_ref[...] = f3_ref[...]
    p1_ref[:, 0:HB] = f2_ref[...]
    p1_ref[:, HB:] = f3_ref[...]


def turn_kernel(
    ids, w_ref, y1_ref, own_ref, y2_in, prior_ref, lh, ll, u3h, u3l, u1h, u1l, u2h, u2l, f_ref, p23, p23_other, p1, p1_other,
    e1, e2, e3, y2_ref, y_ref, yb_ref, x_ref, x23_ref, x3_ref,
):
    h = ids[1]
    y2 = own_or_received(ids, 2, own_ref, (y2_in,))
    y2_ref[...] = y2
    w = w_ref[...] - dot(f_ref[...], y2)
    y3 = w + apply(lh, ll, w)
    y_ref[...] = jnp.where(ids[2] == 3, y3, prior_ref[...])
    yb_ref[...] = y3.astype(BF16)

    def product(same, other, row):
        return dot(same, x_ref[pl.ds(pl.multiple_of(row + h * HB, HB), HB), :]) + dot(
            other, x_ref[pl.ds(pl.multiple_of(row + (1 - h) * HB, HB), HB), :]
        )

    x3 = apply(u3h, u3l, y3).astype(BF16)
    x_ref[2 * NB :, :] = x3
    x23_ref[NB:, :] = x3
    x3_ref[...] = x3
    t = y2.astype(F32) - product(p23[...], p23_other[...], 2 * NB)
    x2 = apply(u2h, u2l, t).astype(BF16)
    x_ref[NB : 2 * NB, :] = x2
    x23_ref[0:NB, :] = x2
    t = y1_ref[...].astype(F32) - product(p1[:, 0:HB], p1_other[:, 0:HB], NB) - product(p1[:, HB:], p1_other[:, HB:], 2 * NB)
    x_ref[0:NB, :] = apply(u1h, u1l, t).astype(BF16)


def late_kernel(ids, to0, to1, to2, y1, y2, y3, *rest):
    late_ref, z = rest[-1], ids[2]
    late_ref[0:NB, :] = jnp.where(z >= 1, y1[...], to0[0:NB, :])
    late_ref[NB : 2 * NB, :] = jnp.where(z >= 2, y2[...], to0[NB : 2 * NB, :] + to1[0:NB, :])
    late_ref[2 * NB :, :] = jnp.where(z >= 3, y3[...], to0[2 * NB :, :] + to1[NB:, :] + to2[...])


def rows_kernel(ids, b_ref, f_ref, v0, e1, e2, e3, late, s1, s2, s3, own_ref, uh_ref, ul_ref, out_ref, v_ref):
    z, owner = ids[2], ids[3] == 0
    window = jnp.logical_and(owner, pl.program_id(0) == 0)

    @pl.when(pl.program_id(0) == 0)
    def _():
        v_ref[0:NB, :] = jnp.where(owner, v0[...], e1[...] + e2[...] + e3[...])
        v_ref[NB:, :] = jnp.where(owner, late[...], s1[...] + s2[...] + s3[...])

    @pl.when(window)
    def _():
        out_ref[...] = own_ref[...]
        for j in range(1, NZ):
            @pl.when(j > z)
            def _():
                out_ref[...] -= dot(f_ref[:, columns(j)], v_ref[columns(j), :])
        out_ref[...] = apply(uh_ref, ul_ref, out_ref[...])

    @pl.when(jnp.logical_not(window))
    def _():
        out_ref[...] = b_ref[...] - dot(f_ref[...], v_ref[...])


def whole(shape):
    return pl.BlockSpec(memory_space=pltpu.VMEM)


def in_hbm(a):
    return pltpu.with_memory_space_constraint(a, pltpu.HBM)


ANY = pl.BlockSpec(memory_space=pl.ANY)


def call(kernel, ids, args, specs, outs, scratch=(), grid=(1,), out_spec=None, limit=12):
    out_specs = jax.tree.map(lambda o: whole(o.shape), outs) if out_spec is None else out_spec
    return pl.pallas_call(
        kernel,
        grid_spec=pltpu.PrefetchScalarGridSpec(
            num_scalar_prefetch=1, grid=grid, in_specs=specs, out_specs=out_specs, scratch_shapes=scratch
        ),
        out_shape=outs,
        cost_estimate=pl.CostEstimate(flops=1, bytes_accessed=1, transcendentals=0),
        compiler_params=pltpu.CompilerParams(vmem_limit_bytes=limit * 1024 * 1024),
    )(ids, *args)


def body(rhs, factors, diag_inv):
    rows, cols = rhs.shape
    r, c = lax.axis_index("row"), lax.axis_index("col")
    ids = jnp.stack([r // NH, r % NH, c // NY, c % NY]).astype(jnp.int32)

    def bf(n, width=cols):
        return jax.ShapeDtypeStruct((n, width), BF16)

    vec, mat = jax.ShapeDtypeStruct((NB, cols), F32), bf(NB, NB)
    vspec, mspec = whole((NB, cols)), whole((NB, NB))
    first = pl.BlockSpec((NB, cols), lambda i, ids: (0, 0))

    window = lax.all_gather(factors[:NB], "row", axis=1, tiled=True)
    gathered = lax.all_gather(factors, "row", axis=1, tiled=True)

    y_z0, yb0, lh, ll = call(
        start_kernel, ids, (in_hbm(rhs), in_hbm(diag_inv)), [first, pl.BlockSpec((1, NB, NB), lambda i, ids: (ids[2], 0, 0))],
        (vec, bf(NB), mat, mat), limit=16,
    )
    hops = [send(yb0, z_move(0, t)) for t in (1, 2, 3)]
    uppers = call(upper_kernel, ids, (in_hbm(diag_inv),), [pl.BlockSpec((4, NB, NB), lambda i, ids: (0, 0, 0))], (mat,) * 6, limit=16)
    wide = lambda j: pl.BlockSpec((NB, NB), lambda i, ids: (0, j))
    half = lambda j: pl.BlockSpec((NB, HB), lambda i, ids: (0, NH * j + ids[1]))

    def forward(j, w, wspec, own, prior, received):
        return call(
            functools.partial(forward_kernel, j), ids, (w, own, prior, lh, ll, in_hbm(window), *received),
            [wspec, vspec, vspec, mspec, mspec, wide(j)] + [vspec] * len(received), (bf(NB), vec, vec, bf(NB)),
        )

    y0, w, y_own, yb1 = forward(0, in_hbm(rhs), first, yb0, y_z0, hops)
    hops = [send(yb1, z_move(1, t)) for t in (2, 3)]
    p23, p1 = call(
        pick_kernel, ids, (in_hbm(window), in_hbm(window), yb1), [half(2), half(3), ANY], (bf(NB, HB), bf(NB, 2 * HB))
    )
    p23 = send(p23, z_move(2, 3))
    p1 = send(p1, z_move(1, 3))
    early = [send(y0, y_move(t)) for t in (1, 2, 3)]
    y1, w, y_own, yb2 = forward(1, w, vspec, yb1, y_own, hops)
    y2_in = send(yb2, z_move(2, 3))
    p23_other, p1_other = send(p23, other_core), send(p1, other_core)
    y2, y_own, yb3, xs, x23s, x3s = call(
        turn_kernel, ids,
        (w, y1, yb2, y2_in, y_own, lh, ll, *uppers, in_hbm(window), p23, p23_other, p1, p1_other, *early),
        [vspec] * 5 + [mspec] * 8 + [wide(2)] + [whole((NB, HB))] * 2 + [mspec] * 2 + [ANY] * 3,
        (bf(NB), vec, bf(NB), bf(3 * NB), bf(2 * NB), bf(NB)),
    )
    to0, to1, to2 = send(xs, z_move(3, 0)), send(x23s, z_move(3, 1)), send(x3s, z_move(3, 2))
    late = call(
        late_kernel, ids, (to0, to1, to2, y1, y2, yb3),
        [whole((3 * NB, cols)), whole((2 * NB, cols))] + [vspec] * 4, bf(3 * NB),
    )
    spread = [send(late, y_move(t)) for t in (1, 2, 3)]
    tile = pl.BlockSpec((NB, cols), lambda i, ids: (i, 0))
    return call(
        rows_kernel, ids, (in_hbm(rhs), in_hbm(gathered), y0, *early, late, *spread, y_own, uppers[0], uppers[1]),
        [tile, pl.BlockSpec((NB, 4 * NB), lambda i, ids: (i, 0))] + [vspec] * 4 + [whole((3 * NB, cols))] * 4
        + [vspec] + [mspec] * 2,
        jax.ShapeDtypeStruct((rows, cols), F32), scratch=[pltpu.VMEM((4 * NB, cols), BF16)],
        grid=(rows // NB,), out_spec=tile, limit=24,
    )


def solution(mesh):
    placed = (P("col", "row"), P("col", "row"), P())
    return jax.shard_map(body, mesh=mesh, in_specs=placed, out_specs=P("col", "row"), check_vma=False)
```

time: 757 us -> 155 us (0.20)
  waiting for transfers between devices: 672 us -> 78.8 us
  matrix products: 55.6 us -> 0 us
  Pallas kernels: 0 us -> 33.2 us
  starting transfers between devices: 0.52 us -> 25.6 us
  local copies, waits for them, and re-layouts: 10.4 us -> 2.58 us
    psum x8 -> x0, waiting for transfers between devices: 663 us -> none  [solve_block(): solved = lax.psum(jnp.where(owner, product, jnp.float32(0.0)), 'col')]
    dot_general x16 -> x0, matrix products: 55.6 us -> none  [the longest x8 32 us: apply_update(): jnp.dot(columns, solved.astype(jnp.bfloat16), preferred_element_type=jnp....]
    ppermute x0 -> x19, waiting for transfers between devices: none -> 43.9 us  [send(): return lax.ppermute(value, ('row', 'col'), pairs(move))]
    pallas_call x0 -> x8, Pallas kernels: none -> 33.2 us  [call(): pl.pallas_call(kernel, grid_spec=pltpu.PrefetchScalarGridSpec(num_scalar_...]
    all_gather x1 -> x2, waiting for transfers between devices: 8.3 us -> 34.2 us  [the longest x1 17.9 us: body(): window = lax.all_gather(factors[:NB], 'row', axis=1, tiled=True)]
    ppermute x0 -> x19, starting transfers between devices: none -> 25.5 us  [send(): return lax.ppermute(value, ('row', 'col'), pairs(move))]
    slice x8 -> x1, local copies, waits for them, and re-layouts: 9.55 us -> 1.67 us  [body(): window = lax.all_gather(factors[:NB], 'row', axis=1, tiled=True)]
  transfers between devices with their start and end apart: 9 -> 21, of which waited for: 9 -> 7; matrix products, arithmetic and copies ran while one was open for 1% -> 0% of each run, Pallas kernels for 0% -> 13%
where the time goes in v3:
time: 155 us; the launch traced here: 154 us
  waiting for transfers between devices  78.8 us (51%)
  Pallas kernels  33.2 us (21%)
  starting transfers between devices  25.6 us (17%)
  between operations  13.7 us (9%)
  local copies, waits for them, and re-layouts  2.58 us (2%)
    ppermute x19, waiting for transfers between devices, send(): return lax.ppermute(value, ('row', 'col'), pairs(move))  43.9 us
    pallas_call x8, Pallas kernels, call(): pl.pallas_call(kernel, grid_spec=pltpu.PrefetchScalarGridSpec(num_scalar_...  33.2 us
    ppermute x19, starting transfers between devices, send(): return lax.ppermute(value, ('row', 'col'), pairs(move))  25.5 us
    all_gather x1, waiting for transfers between devices, body(): window = lax.all_gather(factors[:NB], 'row', axis=1, tiled=True)  17.9 us
    all_gather x1, waiting for transfers between devices, body(): gathered = lax.all_gather(factors, 'row', axis=1, tiled=True)  16.4 us
  transfers between devices with their start and end apart: 21, of which 7 were waited for; matrix products, arithmetic and copies ran while one was open for 0% of the time, Pallas kernels for 13%

profile of v3, /device:TPU:1, one launch (start us, length us, event | category | flops | bytes accessed | tf_op | source)
XLA Modules:
  0.0 154.0 jit_solution(8102221266593390724)
XLA Ops:
  6.5 0.0 all-gather.5.cloned.1.call-start
  6.5 1.7 %slice.3 = bf16[512,256]{1,0:T(8,128)(2,1)} slice(bf16[4096,256]{1,0:T(8,128)(2,1)} %param.4), slice={[0:512], [0:256]} | slice | bytes 524288 | tf_op jit(solution)/shard_map/slice | solution.py:207
  8.2 0.0 all-gather.5.cloned.1.call-update
  8.2 0.0 all-gather.3.cloned.1.call-start
  8.3 0.7 all-gather.3.cloned.1.call-update
  9.0 0.1 pad_add_fusion.ids
  9.1 2.5 %shard_map.37 = (f32[512,128]{1,0:T(8,128)S(1)}, bf16[512,128]{1,0:T(8,128)(2,1)S(1)}, bf16[512,512]{1,0:T(8,128)(2,1)S(1)}, bf16[512,512]{1,0:T(8,128)(2,1)S(1)}) custom-call(s32[4]{0:T(128)S(1)} %pad_add_fusion.ids, f32[4096,128]{1,0:T(8,128)} %b_ref.3, f32[4,512,512]{2,1,0:T(8,128)} %d_ref.3), custom_call_target="tpu_custom_call" | custom-call | flops 1 | bytes 1 | tf_op jit(solution)/shard_map/pallas_call | solution.py:184
  11.6 4.4 %collective-permute-start = (bf16[512,128]{1,0:T(8,128)(2,1)S(1)}, bf16[512,128]{1,0:T(8,128)(2,1)S(1)}, u32[]{:S(2)}, u32[]{:S(2)}) collective-permute-start(bf16[512,128]{1,0:T(8,128)(2,1)S(1)} %get-tuple-element.31.own_ref), channel_id=1, source_target_pairs={{0,4},{16,20},{32,36},{48,52},{64,68},{80,84},{96,100},{112,116}} | collective-permute-start | bytes 393224 | tf_op jit(solution)/shard_map/ppermute | solution.py:30
  16.0 2.6 %collective-permute-start.1 = (bf16[512,128]{1,0:T(8,128)(2,1)S(1)}, bf16[512,128]{1,0:T(8,128)(2,1)S(1)}, u32[]{:S(2)}, u32[]{:S(2)}) collective-permute-start(bf16[512,128]{1,0:T(8,128)(2,1)S(1)} %get-tuple-element.31.own_ref), channel_id=1, source_target_pairs={{0,8},{16,24},{32,40},{48,56},{64,72},{80,88},{96,104},{112,120}} | collective-permute-start | bytes 393224 | tf_op jit(solution)/shard_map/ppermute | solution.py:30
  18.6 1.3 collective-permute-start.2
  19.9 0.0 collective-permute-done.rest_0_
  19.9 1.2 collective-permute-done.1.rest_1_
  21.1 1.0 collective-permute-done.2.rest_2_
  22.0 17.9 %all-gather.5.cloned.1.call-done.f_ref.f2_ref.f3_ref = bf16[512,2048]{1,0:T(8,128)(2,1)} async-done(((bf16[512,256]{1,0:T(8,128)(2,1)}), bf16[512,2048]{1,0:T(8,128)(2,1)}) %all-gather.5.cloned.1.call-update) | async-done | bytes 2097168 | tf_op jit(solution)/shard_map/all_gather | solution.py:207
  39.9 2.7 %shard_map.38 = (bf16[512,128]{1,0:T(8,128)(2,1)S(1)}, f32[512,128]{1,0:T(8,128)S(1)}, f32[512,128]{1,0:T(8,128)S(1)}, bf16[512,128]{1,0:T(8,128)(2,1)S(1)}) custom-call(s32[4]{0:T(128)S(1)} %pad_add_fusion.ids, f32[4096,128]{1,0:T(8,128)} %b_ref.3, bf16[512,128]{1,0:T(8,128)(2,1)S(1)} %get-tuple-element.31.own_ref, ...), custom_call_target="tpu_custom_call" | custom-call | flops 1 | bytes 1 | tf_op jit(solution)/shard_map/pallas_call | solution.py:184
  42.6 0.0 copy-start
  42.6 1.6 %shard_map.41 = (bf16[512,256]{1,0:T(8,128)(2,1)S(1)}, bf16[512,512]{1,0:T(8,128)(2,1)S(1)}) custom-call(s32[4]{0:T(128)S(1)} %pad_add_fusion.ids, bf16[512,2048]{1,0:T(8,128)(2,1)} %all-gather.5.cloned.1.call-done.f_ref.f2_ref.f3_ref, bf16[512,2048]{1,0:T(8,128)(2,1)} %all-gather.5.cloned.1.call-done.f_ref.f2_ref.f3_ref, ...), custom_call_target="tpu_custom_call" | custom-call | flops 1 | bytes 1 | tf_op jit(solution)/shard_map/pallas_call | solution.py:184
  44.3 0.7 collective-permute-start.11
  45.0 0.7 collective-permute-start.9
  45.6 0.0 collective-permute-done.11.p1
  45.7 0.3 collective-permute-start.12
  46.0 0.7 collective-permute-start.6
  46.7 0.7 collective-permute-start.7
  47.3 3.1 %collective-permute-start.3 = (bf16[512,128]{1,0:T(8,128)(2,1)S(1)}, bf16[512,128]{1,0:T(8,128)(2,1)S(1)}, u32[]{:S(2)}, u32[]{:S(2)}) collective-permute-start(bf16[512,128]{1,0:T(8,128)(2,1)S(1)} %get-tuple-element.35.v0), channel_id=1, source_target_pairs={{0,1},{4,5},{8,9},{12,13},{16,17},{20,21},{24,25},{28,29},{32,33},... | collective-permute-start | bytes 393224 | tf_op jit(solution)/shard_map/ppermute | solution.py:30
  50.5 0.0 collective-permute-done.9.p23
  50.5 0.6 collective-permute-start.10
  51.1 0.0 collective-permute-done.6.rest_0_
  51.1 1.9 %collective-permute-start.4 = (bf16[512,128]{1,0:T(8,128)(2,1)S(1)}, bf16[512,128]{1,0:T(8,128)(2,1)S(1)}, u32[]{:S(2)}, u32[]{:S(2)}) collective-permute-start(bf16[512,128]{1,0:T(8,128)(2,1)S(1)} %get-tuple-element.35.v0), channel_id=1, source_target_pairs={{0,2},{4,6},{8,10},{12,14},{16,18},{20,22},{24,26},{28,30},{32,34}... | collective-permute-start | bytes 393224 | tf_op jit(solution)/shard_map/ppermute | solution.py:30
  53.0 0.0 collective-permute-done.7.rest_1_
  53.0 0.0 copy-done
  53.0 1.3 collective-permute-start.5
  54.3 2.7 %shard_map.39 = (bf16[512,128]{1,0:T(8,128)(2,1)S(1)}, f32[512,128]{1,0:T(8,128)S(1)}, f32[512,128]{1,0:T(8,128)S(1)}, bf16[512,128]{1,0:T(8,128)(2,1)S(1)}) custom-call(s32[4]{0:T(128)S(1)} %pad_add_fusion.ids, f32[512,128]{1,0:T(8,128)S(1)} %get-tuple-element.36.w_ref, bf16[512,128]{1,0:T(8,128)(2,1)S(1)} %get-tuple-element.37.own_ref.after_ref, ...), custom_call_target="tpu_custom_call" | custom-call | flops 1 | bytes 1 | tf_op jit(solution)/shard_map/pallas_call | solution.py:184
  57.0 0.0 collective-permute-done.3.e1
  57.0 0.7 collective-permute-start.8
  57.7 3.2 %shard_map.40 = (bf16[512,512]{1,0:T(8,128)(2,1)S(1)}, bf16[512,512]{1,0:T(8,128)(2,1)S(1)}, bf16[512,512]{1,0:T(8,128)(2,1)S(1)}, bf16[512,512]{1,0:T(8,128)(2,...) custom-call(s32[4]{0:T(128)S(1)} %pad_add_fusion.ids, f32[4,512,512]{2,1,0:T(8,128)} %d_ref.3), custom_call_target="tpu_custom_call" | custom-call | flops 1 | bytes 1 | tf_op jit(solution)/shard_map/pallas_call | solution.py:184
  60.9 0.0 collective-permute-done.4.e2
  60.9 0.0 collective-permute-done.5.e3
  61.0 0.0 collective-permute-done.8.y2_in
  61.0 0.0 collective-permute-done.10.p23_other
  61.0 0.0 collective-permute-done.12.p1_other
  61.0 6.3 %shard_map.42 = (bf16[512,128]{1,0:T(8,128)(2,1)S(1)}, f32[512,128]{1,0:T(8,128)S(1)}, bf16[512,128]{1,0:T(8,128)(2,1)S(1)}, bf16[1536,128]{1,0:T(8,128)(2,1)S(1...) custom-call(s32[4]{0:T(128)S(1)} %pad_add_fusion.ids, f32[512,128]{1,0:T(8,128)S(1)} %get-tuple-element.39.w_ref, ...), custom_call_target="tpu_custom_call" | custom-call | flops 1 | bytes 1 | tf_op jit(solution)/shard_map/pallas_call | solution.py:184
  67.3 1.3 collective-permute-start.13
  68.6 0.7 collective-permute-start.14
  69.3 0.7 collective-permute-start.15
  70.0 0.0 collective-permute-done.15.to2
  70.0 0.0 collective-permute-done.14.to1
  70.0 29.5 %collective-permute-done.13.to0 = bf16[1536,128]{1,0:T(8,128)(2,1)S(1)} collective-permute-done((bf16[1536,128]{1,0:T(8,128)(2,1)S(1)}, bf16[1536,128]{1,0:T(8,128)(2,1)S(1)}, u32[]{:S(2)}, u32[]{:S(2)}) %collective-permute-start.13) | collective-permute-done | bytes 393248 | tf_op jit(solution)/shard_map/ppermute | solution.py:30
  99.5 0.7 shard_map.43.late
  100.2 1.3 collective-permute-start.16
  101.5 1.3 collective-permute-start.17
  102.8 1.3 collective-permute-start.18
  104.1 3.8 %collective-permute-done.16.s1 = bf16[1536,128]{1,0:T(8,128)(2,1)S(1)} collective-permute-done((bf16[1536,128]{1,0:T(8,128)(2,1)S(1)}, bf16[1536,128]{1,0:T(8,128)(2,1)S(1)}, u32[]{:S(2)}, u32[]{:S(2)}) %collective-permute-start.16) | collective-permute-done | bytes 393248 | tf_op jit(solution)/shard_map/ppermute | solution.py:30
  108.0 8.4 %collective-permute-done.17.s2 = bf16[1536,128]{1,0:T(8,128)(2,1)S(1)} collective-permute-done((bf16[1536,128]{1,0:T(8,128)(2,1)S(1)}, bf16[1536,128]{1,0:T(8,128)(2,1)S(1)}, u32[]{:S(2)}, u32[]{:S(2)}) %collective-permute-start.17) | collective-permute-done | bytes 393248 | tf_op jit(solution)/shard_map/ppermute | solution.py:30
  116.4 0.0 collective-permute-done.18.s3
  116.4 16.4 %all-gather.3.cloned.1.call-done.f_ref = bf16[4096,2048]{1,0:T(8,128)(2,1)} async-done(((bf16[4096,256]{1,0:T(8,128)(2,1)}), bf16[4096,2048]{1,0:T(8,128)(2,1)}) %all-gather.3.cloned.1.call-update) | async-done | bytes 16777232 | tf_op jit(solution)/shard_map/all_gather | solution.py:208
  132.8 0.0 copy-start.1
  132.8 0.9 copy-done.1
  133.7 13.4 %shard_map.44 = f32[4096,128]{1,0:T(8,128)} custom-call(s32[4]{0:T(128)S(1)} %pad_add_fusion.ids, f32[4096,128]{1,0:T(8,128)} %b_ref.3, bf16[4096,2048]{1,0:T(8,128)(2,1)} %all-gather.3.cloned.1.call-done.f_ref, bf16[512,128]{1,0:T(8,128)(2,1)S(1)} %copy-done.1, bf16[512,128]{1,0:T(8,128)(2,1)S(1)} %collective-permute-done.3.e1, ...), custom_call_target="tpu_custom_call" | custom-call | flops 1 | bytes 1 | tf_op jit(solution)/shard_map/pallas_call | solution.py:184
Async XLA Ops:
  6.5 33.4 %all-gather.5.cloned.1.call-start = ((), (), s32[]{:S(2)}) async-start(), calls=%async_computation.1 | async-start | bytes 2359296 | tf_op jit(solution)/shard_map/all_gather | solution.py:207
  8.2 124.5 %all-gather.3.cloned.1.call-start = ((), (), s32[]{:S(2)}) async-start(), calls=%async_computation | async-start | bytes 18874368 | tf_op jit(solution)/shard_map/all_gather | solution.py:208
  11.6 8.3 %collective-permute-start = (bf16[512,128]{1,0:T(8,128)(2,1)S(1)}, bf16[512,128]{1,0:T(8,128)(2,1)S(1)}, u32[]{:S(2)}, u32[]{:S(2)}) collective-permute-start(bf16[512,128]{1,0:T(8,128)(2,1)S(1)} %get-tuple-element.31.own_ref), channel_id=1, source_target_pairs={{0,4},{16,20},{32,36},{48,52},{64,68},{80,84},{96,100},{112,116}} | collective-permute-start | bytes 393224 | tf_op jit(solution)/shard_map/ppermute | solution.py:30
  16.0 5.1 %collective-permute-start.1 = (bf16[512,128]{1,0:T(8,128)(2,1)S(1)}, bf16[512,128]{1,0:T(8,128)(2,1)S(1)}, u32[]{:S(2)}, u32[]{:S(2)}) collective-permute-start(bf16[512,128]{1,0:T(8,128)(2,1)S(1)} %get-tuple-element.31.own_ref), channel_id=1, source_target_pairs={{0,8},{16,24},{32,40},{48,56},{64,72},{80,88},{96,104},{112,120}} | collective-permute-start | bytes 393224 | tf_op jit(solution)/shard_map/ppermute | solution.py:30
  18.6 3.4 %collective-permute-start.2 = (bf16[512,128]{1,0:T(8,128)(2,1)S(1)}, bf16[512,128]{1,0:T(8,128)(2,1)S(1)}, u32[]{:S(2)}, u32[]{:S(2)}) collective-permute-start(bf16[512,128]{1,0:T(8,128)(2,1)S(1)} %get-tuple-element.31.own_ref), channel_id=1, source_target_pairs={{0,12},{16,28},{32,44},{48,60},{64,76},{80,92},{96,108},{112,124}} | collective-permute-start | bytes 393224 | tf_op jit(solution)/shard_map/ppermute | solution.py:30
  42.6 10.4 %copy-start = (bf16[512,128]{1,0:T(8,128)(2,1)}, bf16[512,128]{1,0:T(8,128)(2,1)S(1)}, u32[]{:S(2)}) copy-start(bf16[512,128]{1,0:T(8,128)(2,1)S(1)} %get-tuple-element.35.v0) | copy-start | bytes 393220
  44.3 1.4 collective-permute-start.11
  45.0 5.5 %collective-permute-start.9 = (bf16[512,256]{1,0:T(8,128)(2,1)S(1)}, bf16[512,256]{1,0:T(8,128)(2,1)S(1)}, u32[]{:S(2)}, u32[]{:S(2)}) collective-permute-start(bf16[512,256]{1,0:T(8,128)(2,1)S(1)} %get-tuple-element.49), channel_id=1, source_target_pairs={{8,12},{24,28},{40,44},{56,60},{72,76},{88,92},{104,108},{120,124}} | collective-permute-start | bytes 786440 | tf_op jit(solution)/shard_map/ppermute | solution.py:30
  45.7 15.3 %collective-permute-start.12 = (bf16[512,512]{1,0:T(8,128)(2,1)S(1)}, bf16[512,512]{1,0:T(8,128)(2,1)S(1)}, u32[]{:S(2)}, u32[]{:S(2)}) collective-permute-start(bf16[512,512]{1,0:T(8,128)(2,1)S(1)} %collective-permute-done.11.p1), channel_id=1, source_target_pairs={{0,16},{1,17},{2,18},{3,19},{4,20},{5,21},{6,22},{7,23},{8,24},{9,... | collective-permute-start | bytes 1572872 | tf_op jit(solution)/shard_map/ppermute | solution.py:30
  46.0 5.1 %collective-permute-start.6 = (bf16[512,128]{1,0:T(8,128)(2,1)S(1)}, bf16[512,128]{1,0:T(8,128)(2,1)S(1)}, u32[]{:S(2)}, u32[]{:S(2)}) collective-permute-start(bf16[512,128]{1,0:T(8,128)(2,1)S(1)} %get-tuple-element.37.own_ref.after_ref), channel_id=1, source_target_pairs={{4,8},{20,24},{36,40},{52,56},{68,72},{84,88},{100,104},{116,120}} | collective-permute-start | bytes 393224 | tf_op jit(solution)/shard_map/ppermute | solution.py:30
  46.7 6.3 %collective-permute-start.7 = (bf16[512,128]{1,0:T(8,128)(2,1)S(1)}, bf16[512,128]{1,0:T(8,128)(2,1)S(1)}, u32[]{:S(2)}, u32[]{:S(2)}) collective-permute-start(bf16[512,128]{1,0:T(8,128)(2,1)S(1)} %get-tuple-element.37.own_ref.after_ref), channel_id=1, source_target_pairs={{4,12},{20,28},{36,44},{52,60},{68,76},{84,92},{100,108},{116,124}} | collective-permute-start | bytes 393224 | tf_op jit(solution)/shard_map/ppermute | solution.py:30
  47.3 9.7 %collective-permute-start.3 = (bf16[512,128]{1,0:T(8,128)(2,1)S(1)}, bf16[512,128]{1,0:T(8,128)(2,1)S(1)}, u32[]{:S(2)}, u32[]{:S(2)}) collective-permute-start(bf16[512,128]{1,0:T(8,128)(2,1)S(1)} %get-tuple-element.35.v0), channel_id=1, source_target_pairs={{0,1},{4,5},{8,9},{12,13},{16,17},{20,21},{24,25},{28,29},{32,33},... | collective-permute-start | bytes 393224 | tf_op jit(solution)/shard_map/ppermute | solution.py:30
  50.5 10.5 %collective-permute-start.10 = (bf16[512,256]{1,0:T(8,128)(2,1)S(1)}, bf16[512,256]{1,0:T(8,128)(2,1)S(1)}, u32[]{:S(2)}, u32[]{:S(2)}) collective-permute-start(bf16[512,256]{1,0:T(8,128)(2,1)S(1)} %collective-permute-done.9.p23), channel_id=1, source_target_pairs={{0,16},{1,17},{2,18},{3,19},{4,20},{5,21},{6,22},{7,23},{8,24},{9,... | collective-permute-start | bytes 786440 | tf_op jit(solution)/shard_map/ppermute | solution.py:30
  51.1 9.9 %collective-permute-start.4 = (bf16[512,128]{1,0:T(8,128)(2,1)S(1)}, bf16[512,128]{1,0:T(8,128)(2,1)S(1)}, u32[]{:S(2)}, u32[]{:S(2)}) collective-permute-start(bf16[512,128]{1,0:T(8,128)(2,1)S(1)} %get-tuple-element.35.v0), channel_id=1, source_target_pairs={{0,2},{4,6},{8,10},{12,14},{16,18},{20,22},{24,26},{28,30},{32,34}... | collective-permute-start | bytes 393224 | tf_op jit(solution)/shard_map/ppermute | solution.py:30
  53.0 7.9 %collective-permute-start.5 = (bf16[512,128]{1,0:T(8,128)(2,1)S(1)}, bf16[512,128]{1,0:T(8,128)(2,1)S(1)}, u32[]{:S(2)}, u32[]{:S(2)}) collective-permute-start(bf16[512,128]{1,0:T(8,128)(2,1)S(1)} %get-tuple-element.35.v0), channel_id=1, source_target_pairs={{0,3},{4,7},{8,11},{12,15},{16,19},{20,23},{24,27},{28,31},{32,35}... | collective-permute-start | bytes 393224 | tf_op jit(solution)/shard_map/ppermute | solution.py:30
  57.0 3.9 %collective-permute-start.8 = (bf16[512,128]{1,0:T(8,128)(2,1)S(1)}, bf16[512,128]{1,0:T(8,128)(2,1)S(1)}, u32[]{:S(2)}, u32[]{:S(2)}) collective-permute-start(bf16[512,128]{1,0:T(8,128)(2,1)S(1)} %get-tuple-element.41.own_ref), channel_id=1, source_target_pairs={{8,12},{24,28},{40,44},{56,60},{72,76},{88,92},{104,108},{120,124}} | collective-permute-start | bytes 393224 | tf_op jit(solution)/shard_map/ppermute | solution.py:30
  67.3 32.1 %collective-permute-start.13 = (bf16[1536,128]{1,0:T(8,128)(2,1)S(1)}, bf16[1536,128]{1,0:T(8,128)(2,1)S(1)}, u32[]{:S(2)}, u32[]{:S(2)}) collective-permute-start(bf16[1536,128]{1,0:T(8,128)(2,1)S(1)} %get-tuple-element.51), channel_id=1, source_target_pairs={{12,0},{28,16},{44,32},{60,48},{76,64},{92,80},{108,96},{124,112}} | collective-permute-start | bytes 1179656 | tf_op jit(solution)/shard_map/ppermute | solution.py:30
  68.6 1.4 collective-permute-start.14
  69.3 0.7 collective-permute-start.15
  100.2 7.8 %collective-permute-start.16 = (bf16[1536,128]{1,0:T(8,128)(2,1)S(1)}, bf16[1536,128]{1,0:T(8,128)(2,1)S(1)}, u32[]{:S(2)}, u32[]{:S(2)}) collective-permute-start(bf16[1536,128]{1,0:T(8,128)(2,1)S(1)} %shard_map.43.late), channel_id=1, source_target_pairs={{0,1},{4,5},{8,9},{12,13},{16,17},{20,21},{24,25},{28,29},{32,33},... | collective-permute-start | bytes 1179656 | tf_op jit(solution)/shard_map/ppermute | solution.py:30
  101.5 14.9 %collective-permute-start.17 = (bf16[1536,128]{1,0:T(8,128)(2,1)S(1)}, bf16[1536,128]{1,0:T(8,128)(2,1)S(1)}, u32[]{:S(2)}, u32[]{:S(2)}) collective-permute-start(bf16[1536,128]{1,0:T(8,128)(2,1)S(1)} %shard_map.43.late), channel_id=1, source_target_pairs={{0,2},{4,6},{8,10},{12,14},{16,18},{20,22},{24,26},{28,30},{32,34}... | collective-permute-start | bytes 1179656 | tf_op jit(solution)/shard_map/ppermute | solution.py:30
  102.8 13.6 %collective-permute-start.18 = (bf16[1536,128]{1,0:T(8,128)(2,1)S(1)}, bf16[1536,128]{1,0:T(8,128)(2,1)S(1)}, u32[]{:S(2)}, u32[]{:S(2)}) collective-permute-start(bf16[1536,128]{1,0:T(8,128)(2,1)S(1)} %shard_map.43.late), channel_id=1, source_target_pairs={{0,3},{4,7},{8,11},{12,15},{16,19},{20,23},{24,27},{28,31},{32,35}... | collective-permute-start | bytes 1179656 | tf_op jit(solution)/shard_map/ppermute | solution.py:30
  132.8 0.9 copy-start.1
Sparse Core Ops, SparseCore 0:
  9.0 30.8 all-gather.4
  41.6 91.1 all-gather.2

commit v4 on v3

--- a/solution.py
+++ b/solution.py
@@ -30,6 +30,18 @@
     return lax.ppermute(value, ("row", "col"), pairs(move))
 
 
+def x_plus(x, h, z, y):
+    return (x + 1, h, z, y)
+
+
+def x_minus(x, h, z, y):
+    return (x - 1, h, z, y)
+
+
+def x_far(x, h, z, y):
+    return (x + 2, h, z, y)
+
+
 def other_core(x, h, z, y):
     return (x, 1 - h, z, y)
 
@@ -88,35 +100,55 @@
     return jnp.where(ids[2] == j, own_ref[...], total)
 
 
-def columns(j):
-    return slice(j * NB, (j + 1) * NB)
-
-
-def forward_kernel(j, ids, w_ref, own_ref, prior_ref, lh_ref, ll_ref, f_ref, *rest):
-    received, (v_ref, w_out, y_ref, yb_ref) = rest[:-4], rest[-4:]
-    v = own_or_received(ids, j, own_ref, received)
-    v_ref[...] = v
-    w = w_ref[...] - dot(f_ref[...], v)
-    w_out[...] = w
+def block_product(ids, blocks, j, v_ref, acc_ref):
+    x, h = ids[0], ids[1]
+    for d in range(NX):
+        @pl.when(lax.rem(x + d, NX) == j)
+        def _():
+            same, other = blocks[2 * d], blocks[2 * d + 1]
+            acc_ref[...] -= dot(same[...], v_ref[pl.ds(pl.multiple_of(h * HB, HB), HB), :]) + dot(
+                other[...], v_ref[pl.ds(pl.multiple_of((1 - h) * HB, HB), HB), :]
+            )
+
+
+def forward_kernel(j, count, ids, w_ref, own_ref, prior_ref, lh_ref, ll_ref, *rest):
+    blocks, received, (v_ref, w_out, y_ref, yb_ref) = rest[:8], rest[8 : 8 + count], rest[-4:]
+    v_ref[...] = own_or_received(ids, j, own_ref, received)
+    w_out[...] = w_ref[...]
+    block_product(ids, blocks, j, v_ref, w_out)
+    w = w_out[...]
     y = w + apply(lh_ref, ll_ref, w)
     y_ref[...] = jnp.where(ids[2] == j + 1, y, prior_ref[...])
     yb_ref[...] = y.astype(BF16)
 
 
-def pick_kernel(ids, f2_ref, f3_ref, after_ref, p23_ref, p1_ref):
-    p23_ref[...] = f3_ref[...]
-    p1_ref[:, 0:HB] = f2_ref[...]
-    p1_ref[:, HB:] = f3_ref[...]
+def pick_kernel(ids, b0, b1, b2, b3, p23_ref, p1_ref):
+    for d, block in enumerate((b0, b1, b2, b3)):
+        @pl.when(lax.rem(ids[0] + d, NX) == 2)
+        def _():
+            p1_ref[:, 0:HB] = block[...]
+
+        @pl.when(lax.rem(ids[0] + d, NX) == 3)
+        def _():
+            p23_ref[...] = block[...]
+            p1_ref[:, HB:] = block[...]
+
+
+def relay_kernel(ids, p23_ref, p1_ref, after_ref, q23_ref, q1_ref):
+    q23_ref[...] = p23_ref[...]
+    q1_ref[...] = p1_ref[...]
 
 
 def turn_kernel(
-    ids, w_ref, y1_ref, own_ref, y2_in, prior_ref, lh, ll, u3h, u3l, u1h, u1l, u2h, u2l, f_ref, p23, p23_other, p1, p1_other,
-    e1, e2, e3, y2_ref, y_ref, yb_ref, x_ref, x23_ref, x3_ref,
+    ids, w_ref, y1_ref, own_ref, y2_in, prior_ref, lh, ll, u3h, u3l, u1h, u1l, u2h, u2l, p23, p23_other, p1, p1_other, *rest
 ):
+    blocks, (y2_ref, y_ref, yb_ref, x_ref, x23_ref, x3_ref, acc) = rest[:8], rest[-7:]
     h = ids[1]
     y2 = own_or_received(ids, 2, own_ref, (y2_in,))
     y2_ref[...] = y2
-    w = w_ref[...] - dot(f_ref[...], y2)
+    acc[...] = w_ref[...]
+    block_product(ids, blocks, 2, y2_ref, acc)
+    w = acc[...]
     y3 = w + apply(lh, ll, w)
     y_ref[...] = jnp.where(ids[2] == 3, y3, prior_ref[...])
     yb_ref[...] = y3.astype(BF16)
@@ -145,27 +177,32 @@
     late_ref[2 * NB :, :] = jnp.where(z >= 3, y3[...], to0[2 * NB :, :] + to1[NB:, :] + to2[...])
 
 
-def rows_kernel(ids, b_ref, f_ref, v0, e1, e2, e3, late, s1, s2, s3, own_ref, uh_ref, ul_ref, out_ref, v_ref):
-    z, owner = ids[2], ids[3] == 0
-    window = jnp.logical_and(owner, pl.program_id(0) == 0)
-
-    @pl.when(pl.program_id(0) == 0)
+def window_kernel(ids, b_ref, v0, e1, e2, e3, late, s1, s2, s3, own_ref, uh_ref, ul_ref, *rest):
+    blocks, (out_ref, v_ref, acc) = rest[:8], rest[8:]
+    x, h, z, owner = ids[0], ids[1], ids[2], ids[3] == 0
+    v_ref[0:NB, :] = jnp.where(owner, v0[...], e1[...] + e2[...] + e3[...])
+    v_ref[NB:, :] = jnp.where(owner, late[...], s1[...] + s2[...] + s3[...])
+    acc[...] = jnp.where(owner, own_ref[...], b_ref[...])
+    for d in range(NX):
+        j = lax.rem(x + d, NX)
+        for s in range(2):
+            part = h if s == 0 else 1 - h
+
+            @pl.when(jnp.logical_or(jnp.logical_not(owner), j > z))
+            def _():
+                acc[...] -= dot(blocks[2 * d + s][...], v_ref[pl.ds(pl.multiple_of(j * NB + part * HB, HB), HB), :])
+
+    @pl.when(owner)
     def _():
-        v_ref[0:NB, :] = jnp.where(owner, v0[...], e1[...] + e2[...] + e3[...])
-        v_ref[NB:, :] = jnp.where(owner, late[...], s1[...] + s2[...] + s3[...])
-
-    @pl.when(window)
+        out_ref[...] = apply(uh_ref, ul_ref, acc[...])
+
+    @pl.when(jnp.logical_not(owner))
     def _():
-        out_ref[...] = own_ref[...]
-        for j in range(1, NZ):
-            @pl.when(j > z)
-            def _():
-                out_ref[...] -= dot(f_ref[:, columns(j)], v_ref[columns(j), :])
-        out_ref[...] = apply(uh_ref, ul_ref, out_ref[...])
-
-    @pl.when(jnp.logical_not(window))
-    def _():
-        out_ref[...] = b_ref[...] - dot(f_ref[...], v_ref[...])
+        out_ref[...] = acc[...]
+
+
+def rows_kernel(ids, out_in, b_ref, f_ref, v_ref, out_ref):
+    out_ref[...] = b_ref[...] - dot(f_ref[...], v_ref[...])
 
 
 def whole(shape):
@@ -179,7 +216,7 @@
 ANY = pl.BlockSpec(memory_space=pl.ANY)
 
 
-def call(kernel, ids, args, specs, outs, scratch=(), grid=(1,), out_spec=None, limit=12):
+def call(kernel, ids, args, specs, outs, scratch=(), grid=(1,), out_spec=None, limit=12, aliases={}):
     out_specs = jax.tree.map(lambda o: whole(o.shape), outs) if out_spec is None else out_spec
     return pl.pallas_call(
         kernel,
@@ -187,6 +224,7 @@
             num_scalar_prefetch=1, grid=grid, in_specs=specs, out_specs=out_specs, scratch_shapes=scratch
         ),
         out_shape=outs,
+        input_output_aliases=aliases,
         cost_estimate=pl.CostEstimate(flops=1, bytes_accessed=1, transcendentals=0),
         compiler_params=pltpu.CompilerParams(vmem_limit_bytes=limit * 1024 * 1024),
     )(ids, *args)
@@ -204,8 +242,11 @@
     vspec, mspec = whole((NB, cols)), whole((NB, NB))
     first = pl.BlockSpec((NB, cols), lambda i, ids: (0, 0))
 
-    window = lax.all_gather(factors[:NB], "row", axis=1, tiled=True)
-    gathered = lax.all_gather(factors, "row", axis=1, tiled=True)
+    own = factors[:NB]
+    same = [own, send(own, x_minus), send(own, x_far), send(own, x_plus)]
+    gathered = lax.all_gather(factors[NB:], "row", axis=1, tiled=True)
+    window = [b for s in same for b in (s, send(s, other_core))]
+    wspecs = [whole((NB, HB))] * 8
 
     y_z0, yb0, lh, ll = call(
         start_kernel, ids, (in_hbm(rhs), in_hbm(diag_inv)), [first, pl.BlockSpec((1, NB, NB), lambda i, ids: (ids[2], 0, 0))],
@@ -213,31 +254,28 @@
     )
     hops = [send(yb0, z_move(0, t)) for t in (1, 2, 3)]
     uppers = call(upper_kernel, ids, (in_hbm(diag_inv),), [pl.BlockSpec((4, NB, NB), lambda i, ids: (0, 0, 0))], (mat,) * 6, limit=16)
-    wide = lambda j: pl.BlockSpec((NB, NB), lambda i, ids: (0, j))
-    half = lambda j: pl.BlockSpec((NB, HB), lambda i, ids: (0, NH * j + ids[1]))
-
-    def forward(j, w, wspec, own, prior, received):
+    p23, p1 = call(pick_kernel, ids, same, [whole((NB, HB))] * 4, (bf(NB, HB), bf(NB, 2 * HB)))
+    p23 = send(p23, z_move(2, 3))
+    p1 = send(p1, z_move(1, 3))
+
+    def forward(j, w, wspec, own, prior, received, after=()):
         return call(
-            functools.partial(forward_kernel, j), ids, (w, own, prior, lh, ll, in_hbm(window), *received),
-            [wspec, vspec, vspec, mspec, mspec, wide(j)] + [vspec] * len(received), (bf(NB), vec, vec, bf(NB)),
+            functools.partial(forward_kernel, j, len(received)), ids, (w, own, prior, lh, ll, *window, *received, *after),
+            [wspec, vspec, vspec, mspec, mspec, *wspecs] + [vspec] * len(received) + [ANY] * len(after), (bf(NB), vec, vec, bf(NB)),
         )
 
     y0, w, y_own, yb1 = forward(0, in_hbm(rhs), first, yb0, y_z0, hops)
     hops = [send(yb1, z_move(1, t)) for t in (2, 3)]
-    p23, p1 = call(
-        pick_kernel, ids, (in_hbm(window), in_hbm(window), yb1), [half(2), half(3), ANY], (bf(NB, HB), bf(NB, 2 * HB))
-    )
-    p23 = send(p23, z_move(2, 3))
-    p1 = send(p1, z_move(1, 3))
     early = [send(y0, y_move(t)) for t in (1, 2, 3)]
-    y1, w, y_own, yb2 = forward(1, w, vspec, yb1, y_own, hops)
+    y1, w, y_own, yb2 = forward(1, w, vspec, yb1, y_own, hops, early)
     y2_in = send(yb2, z_move(2, 3))
+    p23, p1 = call(relay_kernel, ids, (p23, p1, yb2), [whole((NB, HB)), mspec, ANY], (bf(NB, HB), bf(NB, 2 * HB)))
     p23_other, p1_other = send(p23, other_core), send(p1, other_core)
     y2, y_own, yb3, xs, x23s, x3s = call(
         turn_kernel, ids,
-        (w, y1, yb2, y2_in, y_own, lh, ll, *uppers, in_hbm(window), p23, p23_other, p1, p1_other, *early),
-        [vspec] * 5 + [mspec] * 8 + [wide(2)] + [whole((NB, HB))] * 2 + [mspec] * 2 + [ANY] * 3,
-        (bf(NB), vec, bf(NB), bf(3 * NB), bf(2 * NB), bf(NB)),
+        (w, y1, yb2, y2_in, y_own, lh, ll, *uppers, p23, p23_other, p1, p1_other, *window),
+        [vspec] * 5 + [mspec] * 8 + [whole((NB, HB))] * 2 + [mspec] * 2 + wspecs,
+        (bf(NB), vec, bf(NB), bf(3 * NB), bf(2 * NB), bf(NB)), scratch=[pltpu.VMEM((NB, cols), F32)],
     )
     to0, to1, to2 = send(xs, z_move(3, 0)), send(x23s, z_move(3, 1)), send(x3s, z_move(3, 2))
     late = call(
@@ -245,13 +283,21 @@
         [whole((3 * NB, cols)), whole((2 * NB, cols))] + [vspec] * 4, bf(3 * NB),
     )
     spread = [send(late, y_move(t)) for t in (1, 2, 3)]
-    tile = pl.BlockSpec((NB, cols), lambda i, ids: (i, 0))
+    out = jax.ShapeDtypeStruct((rows, cols), F32)
+    vall = bf(4 * NB)
+    done, v = call(
+        window_kernel, ids, (in_hbm(rhs), y0, *early, late, *spread, y_own, uppers[0], uppers[1], *window),
+        [first] + [vspec] * 4 + [whole((3 * NB, cols))] * 4 + [vspec] + [mspec] * 2 + wspecs,
+        (out, vall), out_spec=(first, whole(vall.shape)), scratch=[pltpu.VMEM((NB, cols), F32)],
+    )
+    tile = (rows - NB) // 4
+    at = pl.BlockSpec(
+        (pl.Element(tile), pl.Element(cols)), lambda i, ids: (pl.multiple_of(NB + i * tile, 128), 0)
+    )
     return call(
-        rows_kernel, ids, (in_hbm(rhs), in_hbm(gathered), y0, *early, late, *spread, y_own, uppers[0], uppers[1]),
-        [tile, pl.BlockSpec((NB, 4 * NB), lambda i, ids: (i, 0))] + [vspec] * 4 + [whole((3 * NB, cols))] * 4
-        + [vspec] + [mspec] * 2,
-        jax.ShapeDtypeStruct((rows, cols), F32), scratch=[pltpu.VMEM((4 * NB, cols), BF16)],
-        grid=(rows // NB,), out_spec=tile, limit=24,
+        rows_kernel, ids, (done, in_hbm(rhs), in_hbm(gathered), v),
+        [ANY, at, pl.BlockSpec((tile, 4 * NB), lambda i, ids: (i, 0)), whole(vall.shape)],
+        out, grid=(4,), out_spec=at, limit=32, aliases={1: 0},
     )
 
 

time: 155 us -> 123 us (0.79)
  waiting for transfers between devices: 78.8 us -> 39.5 us
  starting transfers between devices: 25.6 us -> 33 us
  Pallas kernels: 33.2 us -> 31.2 us
    all_gather x2 -> x1, waiting for transfers between devices: 34.2 us -> 0.01 us  [body(): gathered = lax.all_gather(factors[NB:], 'row', axis=1, tiled=True)]
    ppermute x19 -> x26, starting transfers between devices: 25.5 us -> 33 us  [send(): return lax.ppermute(value, ('row', 'col'), pairs(move))]
    ppermute x19 -> x26, waiting for transfers between devices: 43.9 us -> 39.5 us  [send(): return lax.ppermute(value, ('row', 'col'), pairs(move))]
    slice x1 -> x2, local copies, waits for them, and re-layouts: 1.67 us -> 3.81 us  [the longest x1 2.84 us: body(): gathered = lax.all_gather(factors[NB:], 'row', axis=1, tiled=True)]
    pallas_call x8 -> x10, Pallas kernels: 33.2 us -> 31.2 us  [call(): pl.pallas_call(kernel, grid_spec=pltpu.PrefetchScalarGridSpec(num_scalar_...]
  transfers between devices with their start and end apart: 21 -> 27, of which waited for: 7 -> 7; matrix products, arithmetic and copies ran while one was open for 0% -> 1% of each run, Pallas kernels for 13% -> 18%
where the time goes in v4:
time: 123 us; the launch traced here: 121 us
  waiting for transfers between devices  39.5 us (32%)
  starting transfers between devices  33 us (27%)
  Pallas kernels  31.2 us (25%)
  between operations  13.7 us (11%)
  local copies, waits for them, and re-layouts  3.81 us (3%)
    ppermute x26, waiting for transfers between devices, send(): return lax.ppermute(value, ('row', 'col'), pairs(move))  39.5 us
    ppermute x26, starting transfers between devices, send(): return lax.ppermute(value, ('row', 'col'), pairs(move))  33 us
    pallas_call x10, Pallas kernels, call(): pl.pallas_call(kernel, grid_spec=pltpu.PrefetchScalarGridSpec(num_scalar_...  31.2 us
    slice x1, local copies, waits for them, and re-layouts, body(): gathered = lax.all_gather(factors[NB:], 'row', axis=1, tiled=True)  2.84 us
  transfers between devices with their start and end apart: 27, of which 7 were waited for; matrix products, arithmetic and copies ran while one was open for 1% of the time, Pallas kernels for 18%

profile of v4, /device:TPU:1, one launch (start us, length us, event | category | flops | bytes accessed | tf_op | source)
XLA Modules:
  0.0 121.3 jit_solution(17692130204651892301)
XLA Ops:
  6.5 2.8 %slice.7 = bf16[3584,256]{1,0:T(8,128)(2,1)} slice(bf16[4096,256]{1,0:T(8,128)(2,1)} %param.4), slice={[512:4096], [0:256]} | slice | bytes 3670016 | tf_op jit(solution)/shard_map/slice | solution.py:247
  9.4 0.0 all-gather.2.cloned.1.call-update
  9.4 1.0 slice.6.rest_0_.b0
  10.4 3.4 %collective-permute-start.1 = (bf16[512,256]{1,0:T(8,128)(2,1)S(1)}, bf16[512,256]{1,0:T(8,128)(2,1)S(1)}, u32[]{:S(2)}, u32[]{:S(2)}) collective-permute-start(bf16[512,256]{1,0:T(8,128)(2,1)S(1)} %slice.6.rest_0_.b0), channel_id=1, source_target_pairs={{0,96},{1,97},{2,98},{3,99},{4,100},{5,101},{6,102},{7,103},{8,104... | collective-permute-start | bytes 786440 | tf_op jit(solution)/shard_map/ppermute | solution.py:30
  13.8 0.5 collective-permute-start.3
  14.3 0.6 collective-permute-start.5
  14.9 0.1 pad_add_fusion.ids
  15.0 2.5 %shard_map.37 = (f32[512,128]{1,0:T(8,128)S(1)}, bf16[512,128]{1,0:T(8,128)(2,1)S(1)}, bf16[512,512]{1,0:T(8,128)(2,1)S(1)}, bf16[512,512]{1,0:T(8,128)(2,1)S(1)}) custom-call(s32[4]{0:T(128)S(1)} %pad_add_fusion.ids, f32[4096,128]{1,0:T(8,128)} %b_ref.5, f32[4,512,512]{2,1,0:T(8,128)} %d_ref.3), custom_call_target="tpu_custom_call" | custom-call | flops 1 | bytes 1 | tf_op jit(solution)/shard_map/pallas_call | solution.py:221
  17.4 3.6 %collective-permute-start.7 = (bf16[512,128]{1,0:T(8,128)(2,1)S(1)}, bf16[512,128]{1,0:T(8,128)(2,1)S(1)}, u32[]{:S(2)}, u32[]{:S(2)}) collective-permute-start(bf16[512,128]{1,0:T(8,128)(2,1)S(1)} %get-tuple-element.35.own_ref), channel_id=1, source_target_pairs={{0,4},{16,20},{32,36},{48,52},{64,68},{80,84},{96,100},{112,116}} | collective-permute-start | bytes 393224 | tf_op jit(solution)/shard_map/ppermute | solution.py:30
  21.0 2.6 %collective-permute-start.8 = (bf16[512,128]{1,0:T(8,128)(2,1)S(1)}, bf16[512,128]{1,0:T(8,128)(2,1)S(1)}, u32[]{:S(2)}, u32[]{:S(2)}) collective-permute-start(bf16[512,128]{1,0:T(8,128)(2,1)S(1)} %get-tuple-element.35.own_ref), channel_id=1, source_target_pairs={{0,8},{16,24},{32,40},{48,56},{64,72},{80,88},{96,104},{112,120}} | collective-permute-start | bytes 393224 | tf_op jit(solution)/shard_map/ppermute | solution.py:30
  23.6 0.0 collective-permute-done.7.rest_8_
  23.6 1.3 %collective-permute-start.9 = (bf16[512,128]{1,0:T(8,128)(2,1)S(1)}, bf16[512,128]{1,0:T(8,128)(2,1)S(1)}, u32[]{:S(2)}, u32[]{:S(2)}) collective-permute-start(bf16[512,128]{1,0:T(8,128)(2,1)S(1)} %get-tuple-element.35.own_ref), channel_id=1, source_target_pairs={{0,12},{16,28},{32,44},{48,60},{64,76},{80,92},{96,108},{112,124}} | collective-permute-start | bytes 393224 | tf_op jit(solution)/shard_map/ppermute | solution.py:30
  24.9 1.3 %collective-permute-done.8.rest_9_ = bf16[512,128]{1,0:T(8,128)(2,1)S(1)} collective-permute-done((bf16[512,128]{1,0:T(8,128)(2,1)S(1)}, bf16[512,128]{1,0:T(8,128)(2,1)S(1)}, u32[]{:S(2)}, u32[]{:S(2)}) %collective-permute-start.8) | collective-permute-done | bytes 131104 | tf_op jit(solution)/shard_map/ppermute | solution.py:30
  26.3 1.8 %collective-permute-start = (bf16[512,256]{1,0:T(8,128)(2,1)S(1)}, bf16[512,256]{1,0:T(8,128)(2,1)S(1)}, u32[]{:S(2)}, u32[]{:S(2)}) collective-permute-start(bf16[512,256]{1,0:T(8,128)(2,1)S(1)} %slice.6.rest_0_.b0), channel_id=1, source_target_pairs={{0,16},{1,17},{2,18},{3,19},{4,20},{5,21},{6,22},{7,23},{8,24},{9,... | collective-permute-start | bytes 786440 | tf_op jit(solution)/shard_map/ppermute | solution.py:30
  28.1 0.0 collective-permute-done.1.rest_2_.b1
  28.1 0.0 collective-permute-start.2
  28.1 0.0 collective-permute-done.3.rest_4_.b2
  28.1 0.5 collective-permute-start.4
  28.6 1.6 %collective-permute-done.5.rest_6_.b3 = bf16[512,256]{1,0:T(8,128)(2,1)S(1)} collective-permute-done((bf16[512,256]{1,0:T(8,128)(2,1)S(1)}, bf16[512,256]{1,0:T(8,128)(2,1)S(1)}, u32[]{:S(2)}, u32[]{:S(2)}) %collective-permute-start.5) | collective-permute-done | bytes 262176 | tf_op jit(solution)/shard_map/ppermute | solution.py:30
  30.1 0.6 collective-permute-start.6
  30.7 0.7 shard_map.41
  31.4 0.0 collective-permute-done.9.rest_10_
  31.4 0.7 collective-permute-start.17
  32.1 0.0 collective-permute-done.rest_1_
  32.1 0.0 collective-permute-done.2.rest_3_
  32.1 0.0 collective-permute-done.4.rest_5_
  32.1 0.0 collective-permute-done.6.rest_7_
  32.2 2.5 %shard_map.38 = (bf16[512,128]{1,0:T(8,128)(2,1)S(1)}, f32[512,128]{1,0:T(8,128)S(1)}, f32[512,128]{1,0:T(8,128)S(1)}, bf16[512,128]{1,0:T(8,128)(2,1)S(1)}) custom-call(s32[4]{0:T(128)S(1)} %pad_add_fusion.ids, f32[4096,128]{1,0:T(8,128)} %b_ref.5, bf16[512,128]{1,0:T(8,128)(2,1)S(1)} %get-tuple-element.35.own_ref, ...), custom_call_target="tpu_custom_call" | custom-call | flops 1 | bytes 1 | tf_op jit(solution)/shard_map/pallas_call | solution.py:221
  34.6 3.3 %collective-permute-start.10 = (bf16[512,128]{1,0:T(8,128)(2,1)S(1)}, bf16[512,128]{1,0:T(8,128)(2,1)S(1)}, u32[]{:S(2)}, u32[]{:S(2)}) collective-permute-start(bf16[512,128]{1,0:T(8,128)(2,1)S(1)} %get-tuple-element.39.v0), channel_id=1, source_target_pairs={{0,1},{4,5},{8,9},{12,13},{16,17},{20,21},{24,25},{28,29},{32,33},... | collective-permute-start | bytes 393224 | tf_op jit(solution)/shard_map/ppermute | solution.py:30
  38.0 2.4 %collective-permute-start.11 = (bf16[512,128]{1,0:T(8,128)(2,1)S(1)}, bf16[512,128]{1,0:T(8,128)(2,1)S(1)}, u32[]{:S(2)}, u32[]{:S(2)}) collective-permute-start(bf16[512,128]{1,0:T(8,128)(2,1)S(1)} %get-tuple-element.39.v0), channel_id=1, source_target_pairs={{0,2},{4,6},{8,10},{12,14},{16,18},{20,22},{24,26},{28,30},{32,34}... | collective-permute-start | bytes 393224 | tf_op jit(solution)/shard_map/ppermute | solution.py:30
  40.4 0.7 collective-permute-start.16
  41.0 1.3 %collective-permute-start.12 = (bf16[512,128]{1,0:T(8,128)(2,1)S(1)}, bf16[512,128]{1,0:T(8,128)(2,1)S(1)}, u32[]{:S(2)}, u32[]{:S(2)}) collective-permute-start(bf16[512,128]{1,0:T(8,128)(2,1)S(1)} %get-tuple-element.39.v0), channel_id=1, source_target_pairs={{0,3},{4,7},{8,11},{12,15},{16,19},{20,23},{24,27},{28,31},{32,35}... | collective-permute-start | bytes 393224 | tf_op jit(solution)/shard_map/ppermute | solution.py:30
  42.3 0.0 collective-permute-done.10.rest_10_.e1
  42.4 0.7 collective-permute-start.13
  43.0 0.7 collective-permute-done.11.rest_11_.e2
  43.7 0.7 collective-permute-start.14
  44.4 0.8 collective-permute-done.12.rest_12_.e3
  45.2 0.0 collective-permute-done.13.rest_8_
  45.2 0.0 collective-permute-done.14.rest_9_
  45.2 1.5 %shard_map.39 = (bf16[512,128]{1,0:T(8,128)(2,1)S(1)}, f32[512,128]{1,0:T(8,128)S(1)}, f32[512,128]{1,0:T(8,128)S(1)}, bf16[512,128]{1,0:T(8,128)(2,1)S(1)}) custom-call(s32[4]{0:T(128)S(1)} %pad_add_fusion.ids, f32[512,128]{1,0:T(8,128)S(1)} %get-tuple-element.40.w_ref, bf16[512,128]{1,0:T(8,128)(2,1)S(1)} %get-tuple-element.41.own_ref, ...), custom_call_target="tpu_custom_call" | custom-call | flops 1 | bytes 1 | tf_op jit(solution)/shard_map/pallas_call | solution.py:221
  46.7 0.0 collective-permute-done.16.p23_ref
  46.7 0.0 collective-permute-done.17.p1_ref
  46.7 0.6 shard_map.42
  47.3 0.9 collective-permute-start.19
  48.2 0.1 collective-permute-start.18
  48.3 0.7 collective-permute-start.15
  49.0 3.7 %shard_map.40 = (bf16[512,512]{1,0:T(8,128)(2,1)S(1)}, bf16[512,512]{1,0:T(8,128)(2,1)S(1)}, bf16[512,512]{1,0:T(8,128)(2,1)S(1)}, bf16[512,512]{1,0:T(8,128)(2,...) custom-call(s32[4]{0:T(128)S(1)} %pad_add_fusion.ids, f32[4,512,512]{2,1,0:T(8,128)} %d_ref.3), custom_call_target="tpu_custom_call" | custom-call | flops 1 | bytes 1 | tf_op jit(solution)/shard_map/pallas_call | solution.py:221
  52.7 0.0 collective-permute-done.15.y2_in
  52.7 0.0 collective-permute-done.18.p23_other
  52.8 0.0 collective-permute-done.19.p1_other
  52.8 5.5 %shard_map.43 = (bf16[512,128]{1,0:T(8,128)(2,1)S(1)}, f32[512,128]{1,0:T(8,128)S(1)}, bf16[512,128]{1,0:T(8,128)(2,1)S(1)}, bf16[1536,128]{1,0:T(8,128)(2,1)S(1...) custom-call(s32[4]{0:T(128)S(1)} %pad_add_fusion.ids, f32[512,128]{1,0:T(8,128)S(1)} %get-tuple-element.43.w_ref, ...), custom_call_target="tpu_custom_call" | custom-call | flops 1 | bytes 1 | tf_op jit(solution)/shard_map/pallas_call | solution.py:221
  58.3 1.5 %collective-permute-start.20 = (bf16[1536,128]{1,0:T(8,128)(2,1)S(1)}, bf16[1536,128]{1,0:T(8,128)(2,1)S(1)}, u32[]{:S(2)}, u32[]{:S(2)}) collective-permute-start(bf16[1536,128]{1,0:T(8,128)(2,1)S(1)} %get-tuple-element.57), channel_id=1, source_target_pairs={{12,0},{28,16},{44,32},{60,48},{76,64},{92,80},{108,96},{124,112}} | collective-permute-start | bytes 1179656 | tf_op jit(solution)/shard_map/ppermute | solution.py:30
  59.7 0.7 collective-permute-start.21
  60.4 0.7 collective-permute-start.22
  61.1 0.0 collective-permute-done.22.to2
  61.1 22.3 %collective-permute-done.20.to0 = bf16[1536,128]{1,0:T(8,128)(2,1)S(1)} collective-permute-done((bf16[1536,128]{1,0:T(8,128)(2,1)S(1)}, bf16[1536,128]{1,0:T(8,128)(2,1)S(1)}, u32[]{:S(2)}, u32[]{:S(2)}) %collective-permute-start.20) | collective-permute-done | bytes 393248 | tf_op jit(solution)/shard_map/ppermute | solution.py:30
  83.4 0.7 shard_map.44.late
  84.1 1.3 %collective-permute-start.23 = (bf16[1536,128]{1,0:T(8,128)(2,1)S(1)}, bf16[1536,128]{1,0:T(8,128)(2,1)S(1)}, u32[]{:S(2)}, u32[]{:S(2)}) collective-permute-start(bf16[1536,128]{1,0:T(8,128)(2,1)S(1)} %shard_map.44.late), channel_id=1, source_target_pairs={{0,1},{4,5},{8,9},{12,13},{16,17},{20,21},{24,25},{28,29},{32,33},... | collective-permute-start | bytes 1179656 | tf_op jit(solution)/shard_map/ppermute | solution.py:30
  85.4 1.3 %collective-permute-start.24 = (bf16[1536,128]{1,0:T(8,128)(2,1)S(1)}, bf16[1536,128]{1,0:T(8,128)(2,1)S(1)}, u32[]{:S(2)}, u32[]{:S(2)}) collective-permute-start(bf16[1536,128]{1,0:T(8,128)(2,1)S(1)} %shard_map.44.late), channel_id=1, source_target_pairs={{0,2},{4,6},{8,10},{12,14},{16,18},{20,22},{24,26},{28,30},{32,34}... | collective-permute-start | bytes 1179656 | tf_op jit(solution)/shard_map/ppermute | solution.py:30
  86.8 1.3 %collective-permute-start.25 = (bf16[1536,128]{1,0:T(8,128)(2,1)S(1)}, bf16[1536,128]{1,0:T(8,128)(2,1)S(1)}, u32[]{:S(2)}, u32[]{:S(2)}) collective-permute-start(bf16[1536,128]{1,0:T(8,128)(2,1)S(1)} %shard_map.44.late), channel_id=1, source_target_pairs={{0,3},{4,7},{8,11},{12,15},{16,19},{20,23},{24,27},{28,31},{32,35}... | collective-permute-start | bytes 1179656 | tf_op jit(solution)/shard_map/ppermute | solution.py:30
  88.1 4.3 %collective-permute-done.23.s1 = bf16[1536,128]{1,0:T(8,128)(2,1)S(1)} collective-permute-done((bf16[1536,128]{1,0:T(8,128)(2,1)S(1)}, bf16[1536,128]{1,0:T(8,128)(2,1)S(1)}, u32[]{:S(2)}, u32[]{:S(2)}) %collective-permute-start.23) | collective-permute-done | bytes 393248 | tf_op jit(solution)/shard_map/ppermute | solution.py:30
  92.4 8.4 %collective-permute-done.24.s2 = bf16[1536,128]{1,0:T(8,128)(2,1)S(1)} collective-permute-done((bf16[1536,128]{1,0:T(8,128)(2,1)S(1)}, bf16[1536,128]{1,0:T(8,128)(2,1)S(1)}, u32[]{:S(2)}, u32[]{:S(2)}) %collective-permute-start.24) | collective-permute-done | bytes 393248 | tf_op jit(solution)/shard_map/ppermute | solution.py:30
  100.8 3.9 %shard_map.45 = (f32[4096,128]{1,0:T(8,128)}, bf16[2048,128]{1,0:T(8,128)(2,1)S(1)}) custom-call(s32[4]{0:T(128)S(1)} %pad_add_fusion.ids, f32[4096,128]{1,0:T(8,128)} %b_ref.5, bf16[512,128]{1,0:T(8,128)(2,1)S(1)} %get-tuple-element.39.v0, bf16[512,128]{1,0:T(8,128)(2,1)S(1)} %collective-permute-done.10.rest_10_.e1, ...), custom_call_target="tpu_custom_call" | custom-call | flops 1 | bytes 1 | tf_op jit(solution)/shard_map/pallas_call | solution.py:221
  104.8 9.6 %shard_map.46 = f32[4096,128]{1,0:T(8,128)} custom-call(s32[4]{0:T(128)S(1)} %pad_add_fusion.ids, f32[4096,128]{1,0:T(8,128)} %get-tuple-element.63.out_in, f32[4096,128]{1,0:T(8,128)} %b_ref.5, bf16[3584,2048]{1,0:T(8,128)(2,1)} %all-gather.2.cloned.1.call-done.f_ref, bf16[2048,128]{1,0:T(8,128)(2,1)S(1)} %get-tuple-element.64.v_ref), custom_call_target="tpu_custom_call", output_to_operand_aliasing={{}: (1, {})} | custom-call | flops 1 | bytes 1 | tf_op jit(solution)/shard_map/pallas_call | solution.py:221
  (4 shorter events, 0.0 us)
Async XLA Ops:
  6.5 98.3 %all-gather.2.cloned.1.call-start = ((), (), s32[]{:S(2)}) async-start(), calls=%async_computation | async-start | bytes 16515072 | tf_op jit(solution)/shard_map/all_gather | solution.py:247
  10.4 17.7 %collective-permute-start.1 = (bf16[512,256]{1,0:T(8,128)(2,1)S(1)}, bf16[512,256]{1,0:T(8,128)(2,1)S(1)}, u32[]{:S(2)}, u32[]{:S(2)}) collective-permute-start(bf16[512,256]{1,0:T(8,128)(2,1)S(1)} %slice.6.rest_0_.b0), channel_id=1, source_target_pairs={{0,96},{1,97},{2,98},{3,99},{4,100},{5,101},{6,102},{7,103},{8,104... | collective-permute-start | bytes 786440 | tf_op jit(solution)/shard_map/ppermute | solution.py:30
  13.8 14.3 %collective-permute-start.3 = (bf16[512,256]{1,0:T(8,128)(2,1)S(1)}, bf16[512,256]{1,0:T(8,128)(2,1)S(1)}, u32[]{:S(2)}, u32[]{:S(2)}) collective-permute-start(bf16[512,256]{1,0:T(8,128)(2,1)S(1)} %slice.6.rest_0_.b0), channel_id=1, source_target_pairs={{0,64},{1,65},{2,66},{3,67},{4,68},{5,69},{6,70},{7,71},{8,72},{9,... | collective-permute-start | bytes 786440 | tf_op jit(solution)/shard_map/ppermute | solution.py:30
  14.3 15.9 %collective-permute-start.5 = (bf16[512,256]{1,0:T(8,128)(2,1)S(1)}, bf16[512,256]{1,0:T(8,128)(2,1)S(1)}, u32[]{:S(2)}, u32[]{:S(2)}) collective-permute-start(bf16[512,256]{1,0:T(8,128)(2,1)S(1)} %slice.6.rest_0_.b0), channel_id=1, source_target_pairs={{0,32},{1,33},{2,34},{3,35},{4,36},{5,37},{6,38},{7,39},{8,40},{9,... | collective-permute-start | bytes 786440 | tf_op jit(solution)/shard_map/ppermute | solution.py:30
  17.4 6.2 %collective-permute-start.7 = (bf16[512,128]{1,0:T(8,128)(2,1)S(1)}, bf16[512,128]{1,0:T(8,128)(2,1)S(1)}, u32[]{:S(2)}, u32[]{:S(2)}) collective-permute-start(bf16[512,128]{1,0:T(8,128)(2,1)S(1)} %get-tuple-element.35.own_ref), channel_id=1, source_target_pairs={{0,4},{16,20},{32,36},{48,52},{64,68},{80,84},{96,100},{112,116}} | collective-permute-start | bytes 393224 | tf_op jit(solution)/shard_map/ppermute | solution.py:30
  21.0 5.3 %collective-permute-start.8 = (bf16[512,128]{1,0:T(8,128)(2,1)S(1)}, bf16[512,128]{1,0:T(8,128)(2,1)S(1)}, u32[]{:S(2)}, u32[]{:S(2)}) collective-permute-start(bf16[512,128]{1,0:T(8,128)(2,1)S(1)} %get-tuple-element.35.own_ref), channel_id=1, source_target_pairs={{0,8},{16,24},{32,40},{48,56},{64,72},{80,88},{96,104},{112,120}} | collective-permute-start | bytes 393224 | tf_op jit(solution)/shard_map/ppermute | solution.py:30
  23.6 7.8 %collective-permute-start.9 = (bf16[512,128]{1,0:T(8,128)(2,1)S(1)}, bf16[512,128]{1,0:T(8,128)(2,1)S(1)}, u32[]{:S(2)}, u32[]{:S(2)}) collective-permute-start(bf16[512,128]{1,0:T(8,128)(2,1)S(1)} %get-tuple-element.35.own_ref), channel_id=1, source_target_pairs={{0,12},{16,28},{32,44},{48,60},{64,76},{80,92},{96,108},{112,124}} | collective-permute-start | bytes 393224 | tf_op jit(solution)/shard_map/ppermute | solution.py:30
  26.3 5.9 %collective-permute-start = (bf16[512,256]{1,0:T(8,128)(2,1)S(1)}, bf16[512,256]{1,0:T(8,128)(2,1)S(1)}, u32[]{:S(2)}, u32[]{:S(2)}) collective-permute-start(bf16[512,256]{1,0:T(8,128)(2,1)S(1)} %slice.6.rest_0_.b0), channel_id=1, source_target_pairs={{0,16},{1,17},{2,18},{3,19},{4,20},{5,21},{6,22},{7,23},{8,24},{9,... | collective-permute-start | bytes 786440 | tf_op jit(solution)/shard_map/ppermute | solution.py:30
  28.1 4.1 %collective-permute-start.2 = (bf16[512,256]{1,0:T(8,128)(2,1)S(1)}, bf16[512,256]{1,0:T(8,128)(2,1)S(1)}, u32[]{:S(2)}, u32[]{:S(2)}) collective-permute-start(bf16[512,256]{1,0:T(8,128)(2,1)S(1)} %collective-permute-done.1.rest_2_.b1), channel_id=1, source_target_pairs={{0,16},{1,17},{2,18},{3,19},{4,20},{5,21},{6,22},{7,23},{8,24},{9,... | collective-permute-start | bytes 786440 | tf_op jit(solution)/shard_map/ppermute | solution.py:30
  28.1 4.1 %collective-permute-start.4 = (bf16[512,256]{1,0:T(8,128)(2,1)S(1)}, bf16[512,256]{1,0:T(8,128)(2,1)S(1)}, u32[]{:S(2)}, u32[]{:S(2)}) collective-permute-start(bf16[512,256]{1,0:T(8,128)(2,1)S(1)} %collective-permute-done.3.rest_4_.b2), channel_id=1, source_target_pairs={{0,16},{1,17},{2,18},{3,19},{4,20},{5,21},{6,22},{7,23},{8,24},{9,... | collective-permute-start | bytes 786440 | tf_op jit(solution)/shard_map/ppermute | solution.py:30
  30.1 2.0 %collective-permute-start.6 = (bf16[512,256]{1,0:T(8,128)(2,1)S(1)}, bf16[512,256]{1,0:T(8,128)(2,1)S(1)}, u32[]{:S(2)}, u32[]{:S(2)}) collective-permute-start(bf16[512,256]{1,0:T(8,128)(2,1)S(1)} %collective-permute-done.5.rest_6_.b3), channel_id=1, source_target_pairs={{0,16},{1,17},{2,18},{3,19},{4,20},{5,21},{6,22},{7,23},{8,24},{9,... | collective-permute-start | bytes 786440 | tf_op jit(solution)/shard_map/ppermute | solution.py:30
  31.4 15.3 %collective-permute-start.17 = (bf16[512,512]{1,0:T(8,128)(2,1)S(1)}, bf16[512,512]{1,0:T(8,128)(2,1)S(1)}, u32[]{:S(2)}, u32[]{:S(2)}) collective-permute-start(bf16[512,512]{1,0:T(8,128)(2,1)S(1)} %get-tuple-element.54), channel_id=1, source_target_pairs={{4,12},{20,28},{36,44},{52,60},{68,76},{84,92},{100,108},{116,124}} | collective-permute-start | bytes 1572872 | tf_op jit(solution)/shard_map/ppermute | solution.py:30
  34.6 7.7 %collective-permute-start.10 = (bf16[512,128]{1,0:T(8,128)(2,1)S(1)}, bf16[512,128]{1,0:T(8,128)(2,1)S(1)}, u32[]{:S(2)}, u32[]{:S(2)}) collective-permute-start(bf16[512,128]{1,0:T(8,128)(2,1)S(1)} %get-tuple-element.39.v0), channel_id=1, source_target_pairs={{0,1},{4,5},{8,9},{12,13},{16,17},{20,21},{24,25},{28,29},{32,33},... | collective-permute-start | bytes 393224 | tf_op jit(solution)/shard_map/ppermute | solution.py:30
  38.0 5.7 %collective-permute-start.11 = (bf16[512,128]{1,0:T(8,128)(2,1)S(1)}, bf16[512,128]{1,0:T(8,128)(2,1)S(1)}, u32[]{:S(2)}, u32[]{:S(2)}) collective-permute-start(bf16[512,128]{1,0:T(8,128)(2,1)S(1)} %get-tuple-element.39.v0), channel_id=1, source_target_pairs={{0,2},{4,6},{8,10},{12,14},{16,18},{20,22},{24,26},{28,30},{32,34}... | collective-permute-start | bytes 393224 | tf_op jit(solution)/shard_map/ppermute | solution.py:30
  40.4 6.3 %collective-permute-start.16 = (bf16[512,256]{1,0:T(8,128)(2,1)S(1)}, bf16[512,256]{1,0:T(8,128)(2,1)S(1)}, u32[]{:S(2)}, u32[]{:S(2)}) collective-permute-start(bf16[512,256]{1,0:T(8,128)(2,1)S(1)} %get-tuple-element.53), channel_id=1, source_target_pairs={{8,12},{24,28},{40,44},{56,60},{72,76},{88,92},{104,108},{120,124}} | collective-permute-start | bytes 786440 | tf_op jit(solution)/shard_map/ppermute | solution.py:30
  41.0 4.1 %collective-permute-start.12 = (bf16[512,128]{1,0:T(8,128)(2,1)S(1)}, bf16[512,128]{1,0:T(8,128)(2,1)S(1)}, u32[]{:S(2)}, u32[]{:S(2)}) collective-permute-start(bf16[512,128]{1,0:T(8,128)(2,1)S(1)} %get-tuple-element.39.v0), channel_id=1, source_target_pairs={{0,3},{4,7},{8,11},{12,15},{16,19},{20,23},{24,27},{28,31},{32,35}... | collective-permute-start | bytes 393224 | tf_op jit(solution)/shard_map/ppermute | solution.py:30
  42.4 2.8 %collective-permute-start.13 = (bf16[512,128]{1,0:T(8,128)(2,1)S(1)}, bf16[512,128]{1,0:T(8,128)(2,1)S(1)}, u32[]{:S(2)}, u32[]{:S(2)}) collective-permute-start(bf16[512,128]{1,0:T(8,128)(2,1)S(1)} %get-tuple-element.41.own_ref), channel_id=1, source_target_pairs={{4,8},{20,24},{36,40},{52,56},{68,72},{84,88},{100,104},{116,120}} | collective-permute-start | bytes 393224 | tf_op jit(solution)/shard_map/ppermute | solution.py:30
  43.7 1.5 %collective-permute-start.14 = (bf16[512,128]{1,0:T(8,128)(2,1)S(1)}, bf16[512,128]{1,0:T(8,128)(2,1)S(1)}, u32[]{:S(2)}, u32[]{:S(2)}) collective-permute-start(bf16[512,128]{1,0:T(8,128)(2,1)S(1)} %get-tuple-element.41.own_ref), channel_id=1, source_target_pairs={{4,12},{20,28},{36,44},{52,60},{68,76},{84,92},{100,108},{116,124}} | collective-permute-start | bytes 393224 | tf_op jit(solution)/shard_map/ppermute | solution.py:30
  47.3 5.5 %collective-permute-start.19 = (bf16[512,512]{1,0:T(8,128)(2,1)S(1)}, bf16[512,512]{1,0:T(8,128)(2,1)S(1)}, u32[]{:S(2)}, u32[]{:S(2)}) collective-permute-start(bf16[512,512]{1,0:T(8,128)(2,1)S(1)} %get-tuple-element.56.p1), channel_id=1, source_target_pairs={{0,16},{1,17},{2,18},{3,19},{4,20},{5,21},{6,22},{7,23},{8,24},{9,... | collective-permute-start | bytes 1572872 | tf_op jit(solution)/shard_map/ppermute | solution.py:30
  48.2 4.5 %collective-permute-start.18 = (bf16[512,256]{1,0:T(8,128)(2,1)S(1)}, bf16[512,256]{1,0:T(8,128)(2,1)S(1)}, u32[]{:S(2)}, u32[]{:S(2)}) collective-permute-start(bf16[512,256]{1,0:T(8,128)(2,1)S(1)} %get-tuple-element.55.p23), channel_id=1, source_target_pairs={{0,16},{1,17},{2,18},{3,19},{4,20},{5,21},{6,22},{7,23},{8,24},{9,... | collective-permute-start | bytes 786440 | tf_op jit(solution)/shard_map/ppermute | solution.py:30
  48.3 4.4 %collective-permute-start.15 = (bf16[512,128]{1,0:T(8,128)(2,1)S(1)}, bf16[512,128]{1,0:T(8,128)(2,1)S(1)}, u32[]{:S(2)}, u32[]{:S(2)}) collective-permute-start(bf16[512,128]{1,0:T(8,128)(2,1)S(1)} %get-tuple-element.45.after_ref.own_ref), channel_id=1, source_target_pairs={{8,12},{24,28},{40,44},{56,60},{72,76},{88,92},{104,108},{120,124}} | collective-permute-start | bytes 393224 | tf_op jit(solution)/shard_map/ppermute | solution.py:30
  58.3 25.2 %collective-permute-start.20 = (bf16[1536,128]{1,0:T(8,128)(2,1)S(1)}, bf16[1536,128]{1,0:T(8,128)(2,1)S(1)}, u32[]{:S(2)}, u32[]{:S(2)}) collective-permute-start(bf16[1536,128]{1,0:T(8,128)(2,1)S(1)} %get-tuple-element.57), channel_id=1, source_target_pairs={{12,0},{28,16},{44,32},{60,48},{76,64},{92,80},{108,96},{124,112}} | collective-permute-start | bytes 1179656 | tf_op jit(solution)/shard_map/ppermute | solution.py:30
  59.7 1.4 %collective-permute-start.21 = (bf16[1024,128]{1,0:T(8,128)(2,1)S(1)}, bf16[1024,128]{1,0:T(8,128)(2,1)S(1)}, u32[]{:S(2)}, u32[]{:S(2)}) collective-permute-start(bf16[1024,128]{1,0:T(8,128)(2,1)S(1)} %get-tuple-element.58), channel_id=1, source_target_pairs={{12,4},{28,20},{44,36},{60,52},{76,68},{92,84},{108,100},{124,116}} | collective-permute-start | bytes 786440 | tf_op jit(solution)/shard_map/ppermute | solution.py:30
  60.4 0.7 collective-permute-start.22
  84.1 8.3 %collective-permute-start.23 = (bf16[1536,128]{1,0:T(8,128)(2,1)S(1)}, bf16[1536,128]{1,0:T(8,128)(2,1)S(1)}, u32[]{:S(2)}, u32[]{:S(2)}) collective-permute-start(bf16[1536,128]{1,0:T(8,128)(2,1)S(1)} %shard_map.44.late), channel_id=1, source_target_pairs={{0,1},{4,5},{8,9},{12,13},{16,17},{20,21},{24,25},{28,29},{32,33},... | collective-permute-start | bytes 1179656 | tf_op jit(solution)/shard_map/ppermute | solution.py:30
  85.4 15.4 %collective-permute-start.24 = (bf16[1536,128]{1,0:T(8,128)(2,1)S(1)}, bf16[1536,128]{1,0:T(8,128)(2,1)S(1)}, u32[]{:S(2)}, u32[]{:S(2)}) collective-permute-start(bf16[1536,128]{1,0:T(8,128)(2,1)S(1)} %shard_map.44.late), channel_id=1, source_target_pairs={{0,2},{4,6},{8,10},{12,14},{16,18},{20,22},{24,26},{28,30},{32,34}... | collective-permute-start | bytes 1179656 | tf_op jit(solution)/shard_map/ppermute | solution.py:30
  86.8 14.1 %collective-permute-start.25 = (bf16[1536,128]{1,0:T(8,128)(2,1)S(1)}, bf16[1536,128]{1,0:T(8,128)(2,1)S(1)}, u32[]{:S(2)}, u32[]{:S(2)}) collective-permute-start(bf16[1536,128]{1,0:T(8,128)(2,1)S(1)} %shard_map.44.late), channel_id=1, source_target_pairs={{0,3},{4,7},{8,11},{12,15},{16,19},{20,23},{24,27},{28,31},{32,35}... | collective-permute-start | bytes 1179656 | tf_op jit(solution)/shard_map/ppermute | solution.py:30
Sparse Core Ops, SparseCore 0:
  9.5 86.3 all-gather.1

commit v5 on v4

--- a/solution.py
+++ b/solution.py
@@ -65,7 +65,8 @@
 
 def apply(hi_ref, lo_ref, v):
     vh, vl = split(v)
-    return dot(hi_ref[...], vh) + (dot(hi_ref[...], vl) + dot(lo_ref[...], vh))
+    wide = dot(hi_ref[...], jnp.concatenate([vh, vl], axis=1))
+    return wide[:, 0:128] + (wide[:, 128:] + dot(lo_ref[...], vh))
 
 
 def lower_mask(d):
@@ -93,7 +94,13 @@
         out[2 * n][...], out[2 * n + 1][...] = split(upper_mask(d_ref[j]))
 
 
+def combine_kernel(ids, own_ref, r1, r2, r3, v_ref):
+    v_ref[...] = own_or_received(ids, 0, own_ref, (r1, r2, r3))
+
+
 def own_or_received(ids, j, own_ref, received):
+    if not received:
+        return own_ref[...]
     total = received[0][...]
     for piece in received[1:]:
         total = total + piece[...]
@@ -177,11 +184,19 @@
     late_ref[2 * NB :, :] = jnp.where(z >= 3, y3[...], to0[2 * NB :, :] + to1[NB:, :] + to2[...])
 
 
-def window_kernel(ids, b_ref, v0, e1, e2, e3, late, s1, s2, s3, own_ref, uh_ref, ul_ref, *rest):
-    blocks, (out_ref, v_ref, acc) = rest[:8], rest[8:]
-    x, h, z, owner = ids[0], ids[1], ids[2], ids[3] == 0
+def unknowns_kernel(ids, v0, e1, e2, e3, late, s1, s2, s3, v_ref, mine_ref, theirs_ref):
+    h, owner = ids[1], ids[3] == 0
     v_ref[0:NB, :] = jnp.where(owner, v0[...], e1[...] + e2[...] + e3[...])
     v_ref[NB:, :] = jnp.where(owner, late[...], s1[...] + s2[...] + s3[...])
+    for j in range(4):
+        rows = slice(j * HB, (j + 1) * HB)
+        mine_ref[rows, :] = v_ref[pl.ds(pl.multiple_of(j * NB + h * HB, HB), HB), :]
+        theirs_ref[rows, :] = v_ref[pl.ds(pl.multiple_of(j * NB + (1 - h) * HB, HB), HB), :]
+
+
+def window_kernel(ids, b_ref, v_ref, own_ref, uh_ref, ul_ref, *rest):
+    blocks, (out_ref, acc) = rest[:8], rest[8:]
+    x, h, z, owner = ids[0], ids[1], ids[2], ids[3] == 0
     acc[...] = jnp.where(owner, own_ref[...], b_ref[...])
     for d in range(NX):
         j = lax.rem(x + d, NX)
@@ -201,8 +216,25 @@
         out_ref[...] = acc[...]
 
 
-def rows_kernel(ids, out_in, b_ref, f_ref, v_ref, out_ref):
-    out_ref[...] = b_ref[...] - dot(f_ref[...], v_ref[...])
+def rows_kernel(ids, out_in, b_ref, mine_ref, other_ref, *rest):
+    blocks, (out_ref, part_ref, v_ref) = rest[:4], rest[4:]
+
+    @pl.when(pl.program_id(0) == 0)
+    def _():
+        v_ref[:, 0:128] = mine_ref[...]
+        v_ref[:, 128:] = other_ref[...]
+
+    total = None
+    for d in range(NX):
+        j = lax.rem(ids[0] + d, NX)
+        term = dot(blocks[d][...], v_ref[pl.ds(pl.multiple_of(j * HB, HB), HB), :])
+        total = term if total is None else total + term
+    out_ref[...] = b_ref[...] - total[:, 0:128]
+    part_ref[...] = total[:, 128:].astype(BF16)
+
+
+def add_kernel(ids, a_ref, part_ref, out_ref):
+    out_ref[...] = a_ref[...] - part_ref[...].astype(F32)
 
 
 def whole(shape):
@@ -244,7 +276,11 @@
 
     own = factors[:NB]
     same = [own, send(own, x_minus), send(own, x_far), send(own, x_plus)]
-    gathered = lax.all_gather(factors[NB:], "row", axis=1, tiled=True)
+    half = (rows - NB) // 2
+    own_t, own_b = factors[NB : NB + half], factors[NB + half :]
+    before_t, after_b = send(own_t, x_plus), send(own_b, x_minus)
+    before_b, after_t = send(own_b, x_plus), send(own_t, x_minus)
+    far_t, far_b = send(before_t, x_plus), send(after_b, x_minus)
     window = [b for s in same for b in (s, send(s, other_core))]
     wspecs = [whole((NB, HB))] * 8
 
@@ -264,10 +300,11 @@
             [wspec, vspec, vspec, mspec, mspec, *wspecs] + [vspec] * len(received) + [ANY] * len(after), (bf(NB), vec, vec, bf(NB)),
         )
 
-    y0, w, y_own, yb1 = forward(0, in_hbm(rhs), first, yb0, y_z0, hops)
+    y0 = call(combine_kernel, ids, (yb0, *hops), [vspec] * 4, bf(NB))
+    early = [send(y0, y_move(t)) for t in (1, 2, 3)]
+    _, w, y_own, yb1 = forward(0, in_hbm(rhs), first, y0, y_z0, ())
     hops = [send(yb1, z_move(1, t)) for t in (2, 3)]
-    early = [send(y0, y_move(t)) for t in (1, 2, 3)]
-    y1, w, y_own, yb2 = forward(1, w, vspec, yb1, y_own, hops, early)
+    y1, w, y_own, yb2 = forward(1, w, vspec, yb1, y_own, hops, (*early, before_t, after_b))
     y2_in = send(yb2, z_move(2, 3))
     p23, p1 = call(relay_kernel, ids, (p23, p1, yb2), [whole((NB, HB)), mspec, ANY], (bf(NB, HB), bf(NB, 2 * HB)))
     p23_other, p1_other = send(p23, other_core), send(p1, other_core)
@@ -279,26 +316,41 @@
     )
     to0, to1, to2 = send(xs, z_move(3, 0)), send(x23s, z_move(3, 1)), send(x3s, z_move(3, 2))
     late = call(
-        late_kernel, ids, (to0, to1, to2, y1, y2, yb3),
-        [whole((3 * NB, cols)), whole((2 * NB, cols))] + [vspec] * 4, bf(3 * NB),
+        late_kernel, ids, (to0, to1, to2, y1, y2, yb3, before_b, after_t),
+        [whole((3 * NB, cols)), whole((2 * NB, cols))] + [vspec] * 4 + [ANY] * 2, bf(3 * NB),
     )
     spread = [send(late, y_move(t)) for t in (1, 2, 3)]
     out = jax.ShapeDtypeStruct((rows, cols), F32)
-    vall = bf(4 * NB)
-    done, v = call(
-        window_kernel, ids, (in_hbm(rhs), y0, *early, late, *spread, y_own, uppers[0], uppers[1], *window),
-        [first] + [vspec] * 4 + [whole((3 * NB, cols))] * 4 + [vspec] + [mspec] * 2 + wspecs,
-        (out, vall), out_spec=(first, whole(vall.shape)), scratch=[pltpu.VMEM((NB, cols), F32)],
-    )
-    tile = (rows - NB) // 4
-    at = pl.BlockSpec(
-        (pl.Element(tile), pl.Element(cols)), lambda i, ids: (pl.multiple_of(NB + i * tile, 128), 0)
-    )
-    return call(
-        rows_kernel, ids, (done, in_hbm(rhs), in_hbm(gathered), v),
-        [ANY, at, pl.BlockSpec((tile, 4 * NB), lambda i, ids: (i, 0)), whole(vall.shape)],
-        out, grid=(4,), out_spec=at, limit=32, aliases={1: 0},
-    )
+    v, mine, theirs = call(
+        unknowns_kernel, ids, (y0, *early, late, *spread), [vspec] * 4 + [whole((3 * NB, cols))] * 4,
+        (bf(4 * NB), bf(4 * HB), bf(4 * HB)),
+    )
+    other = send(theirs, other_core)
+    done = call(
+        window_kernel, ids, (in_hbm(rhs), v, y_own, uppers[0], uppers[1], *window),
+        [first, whole((4 * NB, cols)), vspec, mspec, mspec, *wspecs], out, out_spec=first, scratch=[pltpu.VMEM((NB, cols), F32)],
+    )
+    tile = half // 2
+    near = pl.BlockSpec((tile, HB), lambda i, ids: (i, 0))
+    narrow = pl.BlockSpec((tile, cols), lambda i, ids: (i, 0))
+
+    def at(n):
+        return pl.BlockSpec(
+            (pl.Element(tile), pl.Element(cols)), lambda i, ids: (pl.multiple_of(NB + n * half + i * tile, 128), 0)
+        )
+
+    parts = []
+    for n, blocks in enumerate(((own_t, after_t, far_t, before_t), (own_b, after_b, far_b, before_b))):
+        done, part = call(
+            rows_kernel, ids, (done, in_hbm(rhs), mine, other, *blocks),
+            [ANY, at(n), whole(mine.shape), whole(mine.shape)] + [near] * 4,
+            (out, bf(half)), grid=(2,), out_spec=(at(n), narrow), scratch=[pltpu.VMEM((4 * HB, 2 * cols), BF16)],
+            limit=24, aliases={1: 0},
+        )
+        parts.append(send(part, other_core))
+    for n, part in enumerate(parts):
+        done = call(add_kernel, ids, (done, part), [at(n), narrow], out, grid=(2,), out_spec=at(n), aliases={1: 0})
+    return done
 
 
 def solution(mesh):

time: 123 us -> 117 us (0.951)
  between operations: 13.7 us -> 0.35 us
  starting transfers between devices: 33 us -> 43.7 us
  local copies, waits for them, and re-layouts: 3.81 us -> 0.14 us
  Pallas kernels: 31.2 us -> 32.9 us
    ppermute x26 -> x35, starting transfers between devices: 33 us -> 43.7 us  [send(): return lax.ppermute(value, ('row', 'col'), pairs(move))]
    slice x1, local copies, waits for them, and re-layouts: 2.84 us -> 0.12 us  [body(): own_t, own_b = (factors[NB:NB + half], factors[NB + half:])]
    pallas_call x10 -> x15, Pallas kernels: 31.2 us -> 32.9 us  [call(): pl.pallas_call(kernel, grid_spec=pltpu.PrefetchScalarGridSpec(num_scalar_...]
    ppermute x26 -> x35, waiting for transfers between devices: 39.5 us -> 39.2 us  [send(): return lax.ppermute(value, ('row', 'col'), pairs(move))]
  transfers between devices with their start and end apart: 27 -> 35, of which waited for: 7 -> 9; matrix products, arithmetic and copies ran while one was open for 1% -> 0% of each run, Pallas kernels for 18% -> 24%
where the time goes in v5:
time: 117 us; the launch traced here: 116 us
  starting transfers between devices  43.7 us (37%)
  waiting for transfers between devices  39.2 us (34%)
  Pallas kernels  32.9 us (28%)
    ppermute x35, starting transfers between devices, send(): return lax.ppermute(value, ('row', 'col'), pairs(move))  43.7 us
    ppermute x35, waiting for transfers between devices, send(): return lax.ppermute(value, ('row', 'col'), pairs(move))  39.2 us
    pallas_call x15, Pallas kernels, call(): pl.pallas_call(kernel, grid_spec=pltpu.PrefetchScalarGridSpec(num_scalar_...  32.9 us
  transfers between devices with their start and end apart: 35, of which 9 were waited for; matrix products, arithmetic and copies ran while one was open for 0% of the time, Pallas kernels for 24%

profile of v5, /device:TPU:1, one launch (start us, length us, event | category | flops | bytes accessed | tf_op | source)
XLA Modules:
  0.0 116.3 jit_solution(17651325658289431829)
XLA Ops:
  0.0 0.1 pad_add_fusion.ids
  0.1 2.4 %shard_map.37 = (f32[512,128]{1,0:T(8,128)S(1)}, bf16[512,128]{1,0:T(8,128)(2,1)S(1)}, bf16[512,512]{1,0:T(8,128)(2,1)S(1)}, bf16[512,512]{1,0:T(8,128)(2,1)S(1)}) custom-call(s32[4]{0:T(128)S(1)} %pad_add_fusion.ids, f32[4096,128]{1,0:T(8,128)} %b_ref.7, f32[4,512,512]{2,1,0:T(8,128)} %d_ref.3), custom_call_target="tpu_custom_call" | custom-call | flops 1 | bytes 1 | tf_op jit(solution)/shard_map/pallas_call | solution.py:253
  2.5 4.4 %collective-permute-start = (bf16[512,128]{1,0:T(8,128)(2,1)S(1)}, bf16[512,128]{1,0:T(8,128)(2,1)S(1)}, u32[]{:S(2)}, u32[]{:S(2)}) collective-permute-start(bf16[512,128]{1,0:T(8,128)(2,1)S(1)} %get-tuple-element.39.own_ref), channel_id=1, source_target_pairs={{0,4},{16,20},{32,36},{48,52},{64,68},{80,84},{96,100},{112,116}} | collective-permute-start | bytes 393224 | tf_op jit(solution)/shard_map/ppermute | solution.py:30
  6.9 2.6 %collective-permute-start.1 = (bf16[512,128]{1,0:T(8,128)(2,1)S(1)}, bf16[512,128]{1,0:T(8,128)(2,1)S(1)}, u32[]{:S(2)}, u32[]{:S(2)}) collective-permute-start(bf16[512,128]{1,0:T(8,128)(2,1)S(1)} %get-tuple-element.39.own_ref), channel_id=1, source_target_pairs={{0,8},{16,24},{32,40},{48,56},{64,72},{80,88},{96,104},{112,120}} | collective-permute-start | bytes 393224 | tf_op jit(solution)/shard_map/ppermute | solution.py:30
  9.5 1.3 %collective-permute-start.2 = (bf16[512,128]{1,0:T(8,128)(2,1)S(1)}, bf16[512,128]{1,0:T(8,128)(2,1)S(1)}, u32[]{:S(2)}, u32[]{:S(2)}) collective-permute-start(bf16[512,128]{1,0:T(8,128)(2,1)S(1)} %get-tuple-element.39.own_ref), channel_id=1, source_target_pairs={{0,12},{16,28},{32,44},{48,60},{64,76},{80,92},{96,108},{112,124}} | collective-permute-start | bytes 393224 | tf_op jit(solution)/shard_map/ppermute | solution.py:30
  10.8 2.8 %collective-permute-start.9 = (bf16[512,256]{1,0:T(8,128)(2,1)S(1)}, bf16[512,256]{1,0:T(8,128)(2,1)S(1)}, u32[]{:S(2)}, u32[]{:S(2)}) collective-permute-start(bf16[512,256]{1,0:T(8,128)(2,1)S(1)} %slice.9.rest_0_.b0), channel_id=1, source_target_pairs={{0,64},{1,65},{2,66},{3,67},{4,68},{5,69},{6,70},{7,71},{8,72},{9,... | collective-permute-start | bytes 786440 | tf_op jit(solution)/shard_map/ppermute | solution.py:30
  13.7 0.3 collective-permute-start.11
  14.0 0.0 collective-permute-done.r1
  14.0 2.4 %collective-permute-start.7 = (bf16[512,256]{1,0:T(8,128)(2,1)S(1)}, bf16[512,256]{1,0:T(8,128)(2,1)S(1)}, u32[]{:S(2)}, u32[]{:S(2)}) collective-permute-start(bf16[512,256]{1,0:T(8,128)(2,1)S(1)} %slice.9.rest_0_.b0), channel_id=1, source_target_pairs={{0,96},{1,97},{2,98},{3,99},{4,100},{5,101},{6,102},{7,103},{8,104... | collective-permute-start | bytes 786440 | tf_op jit(solution)/shard_map/ppermute | solution.py:30
  16.3 0.0 collective-permute-done.1.r2
  16.4 1.8 %collective-permute-start.6 = (bf16[512,256]{1,0:T(8,128)(2,1)S(1)}, bf16[512,256]{1,0:T(8,128)(2,1)S(1)}, u32[]{:S(2)}, u32[]{:S(2)}) collective-permute-start(bf16[512,256]{1,0:T(8,128)(2,1)S(1)} %slice.9.rest_0_.b0), channel_id=1, source_target_pairs={{0,16},{1,17},{2,18},{3,19},{4,20},{5,21},{6,22},{7,23},{8,24},{9,... | collective-permute-start | bytes 786440 | tf_op jit(solution)/shard_map/ppermute | solution.py:30
  18.1 0.1 fusion
  18.3 0.0 collective-permute-done.2.r3
  18.3 0.1 collective-permute-start.15
  18.4 0.9 collective-permute-done.9.rest_4_.b2
  19.3 2.5 %collective-permute-start.16 = (bf16[1792,256]{1,0:T(8,128)(2,1)S(1)}, bf16[1792,256]{1,0:T(8,128)(2,1)S(1)}, u32[]{:S(2)}, u32[]{:S(2)}) collective-permute-start(bf16[1792,256]{1,0:T(8,128)(2,1)S(1)} %get-tuple-element.73.rest_0_), channel_id=1, source_target_pairs={{0,96},{1,97},{2,98},{3,99},{4,100},{5,101},{6,102},{7,103},{8,104... | collective-permute-start | bytes 2752520 | tf_op jit(solution)/shard_map/ppermute | solution.py:30
  21.8 0.6 shard_map.38.own_ref.v0
  22.4 3.9 %collective-permute-done.11.rest_6_.b3 = bf16[512,256]{1,0:T(8,128)(2,1)S(1)} collective-permute-done((bf16[512,256]{1,0:T(8,128)(2,1)S(1)}, bf16[512,256]{1,0:T(8,128)(2,1)S(1)}, u32[]{:S(2)}, u32[]{:S(2)}) %collective-permute-start.11) | collective-permute-done | bytes 262176 | tf_op jit(solution)/shard_map/ppermute | solution.py:30
  26.3 1.3 %collective-permute-start.3 = (bf16[512,128]{1,0:T(8,128)(2,1)S(1)}, bf16[512,128]{1,0:T(8,128)(2,1)S(1)}, u32[]{:S(2)}, u32[]{:S(2)}) collective-permute-start(bf16[512,128]{1,0:T(8,128)(2,1)S(1)} %shard_map.38.own_ref.v0), channel_id=1, source_target_pairs={{0,1},{4,5},{8,9},{12,13},{16,17},{20,21},{24,25},{28,29},{32,33},... | collective-permute-start | bytes 393224 | tf_op jit(solution)/shard_map/ppermute | solution.py:30
  27.6 1.1 collective-permute-start.10
  28.7 0.0 collective-permute-done.6.rest_1_
  28.7 0.1 collective-permute-start.12
  28.8 0.7 collective-permute-done.3.rest_10_.e1
  29.5 1.8 %collective-permute-start.8 = (bf16[512,256]{1,0:T(8,128)(2,1)S(1)}, bf16[512,256]{1,0:T(8,128)(2,1)S(1)}, u32[]{:S(2)}, u32[]{:S(2)}) collective-permute-start(bf16[512,256]{1,0:T(8,128)(2,1)S(1)} %collective-permute-done.7.rest_2_.b1), channel_id=1, source_target_pairs={{0,16},{1,17},{2,18},{3,19},{4,20},{5,21},{6,22},{7,23},{8,24},{9,... | collective-permute-start | bytes 786440 | tf_op jit(solution)/shard_map/ppermute | solution.py:30
  31.3 0.0 collective-permute-done.10.rest_5_
  31.3 1.3 %collective-permute-start.4 = (bf16[512,128]{1,0:T(8,128)(2,1)S(1)}, bf16[512,128]{1,0:T(8,128)(2,1)S(1)}, u32[]{:S(2)}, u32[]{:S(2)}) collective-permute-start(bf16[512,128]{1,0:T(8,128)(2,1)S(1)} %shard_map.38.own_ref.v0), channel_id=1, source_target_pairs={{0,2},{4,6},{8,10},{12,14},{16,18},{20,22},{24,26},{28,30},{32,34}... | collective-permute-start | bytes 393224 | tf_op jit(solution)/shard_map/ppermute | solution.py:30
  32.6 0.7 shard_map.42
  33.2 0.7 collective-permute-start.19
  34.0 1.3 %collective-permute-start.5 = (bf16[512,128]{1,0:T(8,128)(2,1)S(1)}, bf16[512,128]{1,0:T(8,128)(2,1)S(1)}, u32[]{:S(2)}, u32[]{:S(2)}) collective-permute-start(bf16[512,128]{1,0:T(8,128)(2,1)S(1)} %shard_map.38.own_ref.v0), channel_id=1, source_target_pairs={{0,3},{4,7},{8,11},{12,15},{16,19},{20,23},{24,27},{28,31},{32,35}... | collective-permute-start | bytes 393224 | tf_op jit(solution)/shard_map/ppermute | solution.py:30
  35.3 2.8 %shard_map.39 = (bf16[512,128]{1,0:T(8,128)(2,1)}, f32[512,128]{1,0:T(8,128)S(1)}, f32[512,128]{1,0:T(8,128)S(1)}, bf16[512,128]{1,0:T(8,128)(2,1)S(1)}) custom-call(s32[4]{0:T(128)S(1)} %pad_add_fusion.ids, f32[4096,128]{1,0:T(8,128)} %b_ref.7, bf16[512,128]{1,0:T(8,128)(2,1)S(1)} %shard_map.38.own_ref.v0, f32[512,128]{1,0:T(8,128)S(1)} %get-tuple-element.40.prior_ref, ...), custom_call_target="tpu_custom_call" | custom-call | flops 1 | bytes 1 | tf_op jit(solution)/shard_map/pallas_call | solution.py:253
  38.0 0.7 collective-permute-start.13
  38.7 0.7 collective-permute-start.14
  39.4 0.7 collective-permute-start.18
  40.1 2.1 %collective-permute-start.25 = (bf16[1792,256]{1,0:T(8,128)(2,1)S(1)}, bf16[1792,256]{1,0:T(8,128)(2,1)S(1)}, u32[]{:S(2)}, u32[]{:S(2)}) collective-permute-start(bf16[1792,256]{1,0:T(8,128)(2,1)S(1)} %get-tuple-element.73.rest_0_), channel_id=1, source_target_pairs={{0,32},{1,33},{2,34},{3,35},{4,36},{5,37},{6,38},{7,39},{8,40},{9,... | collective-permute-start | bytes 2752520 | tf_op jit(solution)/shard_map/ppermute | solution.py:30
  42.2 3.8 %collective-permute-done.15.rest_13_.rest_3_ = bf16[1792,256]{1,0:T(8,128)(2,1)S(1)} collective-permute-done((bf16[1792,256]{1,0:T(8,128)(2,1)S(1)}, bf16[1792,256]{1,0:T(8,128)(2,1)S(1)}, u32[]{:S(2)}, u32[]{:S(2)}) %collective-permute-start.15) | collective-permute-done | bytes 917536 | tf_op jit(solution)/shard_map/ppermute | solution.py:30
  45.9 1.4 %shard_map.40 = (bf16[512,128]{1,0:T(8,128)(2,1)S(1)}, f32[512,128]{1,0:T(8,128)S(1)}, f32[512,128]{1,0:T(8,128)S(1)}, bf16[512,128]{1,0:T(8,128)(2,1)S(1)}) custom-call(s32[4]{0:T(128)S(1)} %pad_add_fusion.ids, f32[512,128]{1,0:T(8,128)S(1)} %get-tuple-element.43.w_ref, bf16[512,128]{1,0:T(8,128)(2,1)S(1)} %get-tuple-element.44.own_ref, ...), custom_call_target="tpu_custom_call" | custom-call | flops 1 | bytes 1 | tf_op jit(solution)/shard_map/pallas_call | solution.py:253
  47.3 0.6 shard_map.43
  47.9 2.6 %collective-permute-start.21 = (bf16[512,512]{1,0:T(8,128)(2,1)S(1)}, bf16[512,512]{1,0:T(8,128)(2,1)S(1)}, u32[]{:S(2)}, u32[]{:S(2)}) collective-permute-start(bf16[512,512]{1,0:T(8,128)(2,1)S(1)} %get-tuple-element.59.p1), channel_id=1, source_target_pairs={{0,16},{1,17},{2,18},{3,19},{4,20},{5,21},{6,22},{7,23},{8,24},{9,... | collective-permute-start | bytes 1572872 | tf_op jit(solution)/shard_map/ppermute | solution.py:30
  50.6 0.1 collective-permute-start.20
  50.7 0.7 collective-permute-start.17
  51.3 3.2 %shard_map.41 = (bf16[512,512]{1,0:T(8,128)(2,1)S(1)}, bf16[512,512]{1,0:T(8,128)(2,1)S(1)}, bf16[512,512]{1,0:T(8,128)(2,1)S(1)}, bf16[512,512]{1,0:T(8,128)(2,...) custom-call(s32[4]{0:T(128)S(1)} %pad_add_fusion.ids, f32[4,512,512]{2,1,0:T(8,128)} %d_ref.3), custom_call_target="tpu_custom_call" | custom-call | flops 1 | bytes 1 | tf_op jit(solution)/shard_map/pallas_call | solution.py:253
  54.5 3.4 %shard_map.44 = (bf16[512,128]{1,0:T(8,128)(2,1)S(1)}, f32[512,128]{1,0:T(8,128)S(1)}, bf16[512,128]{1,0:T(8,128)(2,1)S(1)}, bf16[1536,128]{1,0:T(8,128)(2,1)S(1...) custom-call(s32[4]{0:T(128)S(1)} %pad_add_fusion.ids, f32[512,128]{1,0:T(8,128)S(1)} %get-tuple-element.46.w_ref, ...), custom_call_target="tpu_custom_call" | custom-call | flops 1 | bytes 1 | tf_op jit(solution)/shard_map/pallas_call | solution.py:253
  58.0 1.3 %collective-permute-start.22 = (bf16[1536,128]{1,0:T(8,128)(2,1)S(1)}, bf16[1536,128]{1,0:T(8,128)(2,1)S(1)}, u32[]{:S(2)}, u32[]{:S(2)}) collective-permute-start(bf16[1536,128]{1,0:T(8,128)(2,1)S(1)} %get-tuple-element.60), channel_id=1, source_target_pairs={{12,0},{28,16},{44,32},{60,48},{76,64},{92,80},{108,96},{124,112}} | collective-permute-start | bytes 1179656 | tf_op jit(solution)/shard_map/ppermute | solution.py:30
  59.3 0.7 collective-permute-start.23
  59.9 0.9 collective-permute-start.31
  60.9 4.8 %collective-permute-done.25.rest_0_.rest_3_ = bf16[1792,256]{1,0:T(8,128)(2,1)S(1)} collective-permute-done((bf16[1792,256]{1,0:T(8,128)(2,1)S(1)}, bf16[1792,256]{1,0:T(8,128)(2,1)S(1)}, u32[]{:S(2)}, u32[]{:S(2)}) %collective-permute-start.25) | collective-permute-done | bytes 917536 | tf_op jit(solution)/shard_map/ppermute | solution.py:30
  65.6 0.7 collective-permute-done.26.rest_1_
  66.3 0.7 collective-permute-start.24
  67.0 11.8 %collective-permute-done.22.to0 = bf16[1536,128]{1,0:T(8,128)(2,1)S(1)} collective-permute-done((bf16[1536,128]{1,0:T(8,128)(2,1)S(1)}, bf16[1536,128]{1,0:T(8,128)(2,1)S(1)}, u32[]{:S(2)}, u32[]{:S(2)}) %collective-permute-start.22) | collective-permute-done | bytes 393248 | tf_op jit(solution)/shard_map/ppermute | solution.py:30
  78.8 0.7 shard_map.45.late
  79.5 1.3 %collective-permute-start.27 = (bf16[1536,128]{1,0:T(8,128)(2,1)S(1)}, bf16[1536,128]{1,0:T(8,128)(2,1)S(1)}, u32[]{:S(2)}, u32[]{:S(2)}) collective-permute-start(bf16[1536,128]{1,0:T(8,128)(2,1)S(1)} %shard_map.45.late), channel_id=1, source_target_pairs={{0,1},{4,5},{8,9},{12,13},{16,17},{20,21},{24,25},{28,29},{32,33},... | collective-permute-start | bytes 1179656 | tf_op jit(solution)/shard_map/ppermute | solution.py:30
  80.8 1.3 %collective-permute-start.28 = (bf16[1536,128]{1,0:T(8,128)(2,1)S(1)}, bf16[1536,128]{1,0:T(8,128)(2,1)S(1)}, u32[]{:S(2)}, u32[]{:S(2)}) collective-permute-start(bf16[1536,128]{1,0:T(8,128)(2,1)S(1)} %shard_map.45.late), channel_id=1, source_target_pairs={{0,2},{4,6},{8,10},{12,14},{16,18},{20,22},{24,26},{28,30},{32,34}... | collective-permute-start | bytes 1179656 | tf_op jit(solution)/shard_map/ppermute | solution.py:30
  82.1 1.3 %collective-permute-start.29 = (bf16[1536,128]{1,0:T(8,128)(2,1)S(1)}, bf16[1536,128]{1,0:T(8,128)(2,1)S(1)}, u32[]{:S(2)}, u32[]{:S(2)}) collective-permute-start(bf16[1536,128]{1,0:T(8,128)(2,1)S(1)} %shard_map.45.late), channel_id=1, source_target_pairs={{0,3},{4,7},{8,11},{12,15},{16,19},{20,23},{24,27},{28,31},{32,35}... | collective-permute-start | bytes 1179656 | tf_op jit(solution)/shard_map/ppermute | solution.py:30
  83.5 4.1 %collective-permute-done.27.s1 = bf16[1536,128]{1,0:T(8,128)(2,1)S(1)} collective-permute-done((bf16[1536,128]{1,0:T(8,128)(2,1)S(1)}, bf16[1536,128]{1,0:T(8,128)(2,1)S(1)}, u32[]{:S(2)}, u32[]{:S(2)}) %collective-permute-start.27) | collective-permute-done | bytes 393248 | tf_op jit(solution)/shard_map/ppermute | solution.py:30
  87.6 8.4 %collective-permute-done.28.s2 = bf16[1536,128]{1,0:T(8,128)(2,1)S(1)} collective-permute-done((bf16[1536,128]{1,0:T(8,128)(2,1)S(1)}, bf16[1536,128]{1,0:T(8,128)(2,1)S(1)}, u32[]{:S(2)}, u32[]{:S(2)}) %collective-permute-start.28) | collective-permute-done | bytes 393248 | tf_op jit(solution)/shard_map/ppermute | solution.py:30
  96.0 1.0 shard_map.46
  97.0 2.6 %collective-permute-start.30 = (bf16[1024,128]{1,0:T(8,128)(2,1)S(1)}, bf16[1024,128]{1,0:T(8,128)(2,1)S(1)}, u32[]{:S(2)}, u32[]{:S(2)}) collective-permute-start(bf16[1024,128]{1,0:T(8,128)(2,1)S(1)} %get-tuple-element.68), channel_id=1, source_target_pairs={{0,16},{1,17},{2,18},{3,19},{4,20},{5,21},{6,22},{7,23},{8,24},{9,... | collective-permute-start | bytes 786440 | tf_op jit(solution)/shard_map/ppermute | solution.py:30
  99.6 3.6 %shard_map.47.out_in = f32[4096,128]{1,0:T(8,128)} custom-call(s32[4]{0:T(128)S(1)} %pad_add_fusion.ids, f32[4096,128]{1,0:T(8,128)} %b_ref.7, bf16[2048,128]{1,0:T(8,128)(2,1)S(1)} %get-tuple-element.65.v_ref, f32[512,128]{1,0:T(8,128)S(1)} %get-tuple-element.66.own_ref, bf16[512,512]{1,0:T(8,128)(2,1)S(1)} %get-tuple-element.50.u3h.uh_ref, ...), custom_call_target="tpu_custom_call" | custom-call | flops 1 | bytes 1 | tf_op jit(solution)/shard_map/pallas_call | solution.py:253
  103.2 3.8 %shard_map.48 = (f32[4096,128]{1,0:T(8,128)}, bf16[1792,128]{1,0:T(8,128)(2,1)S(1)}) custom-call(s32[4]{0:T(128)S(1)} %pad_add_fusion.ids, f32[4096,128]{1,0:T(8,128)} %shard_map.47.out_in, f32[4096,128]{1,0:T(8,128)} %b_ref.7, bf16[1024,128]{1,0:T(8,128)(2,1)S(1)} %get-tuple-element.67.mine_ref, ...), custom_call_target="tpu_custom_call", output_to_operand_aliasing={{0}: (1, {})} | custom-call | flops 1 | bytes 1 | tf_op jit(solution)/shard_map/pallas_call | solution.py:253
  107.0 0.0 collective-permute-start.33
  107.0 3.8 %shard_map.49 = (f32[4096,128]{1,0:T(8,128)}, bf16[1792,128]{1,0:T(8,128)(2,1)S(1)}) custom-call(s32[4]{0:T(128)S(1)} %pad_add_fusion.ids, f32[4096,128]{1,0:T(8,128)} %get-tuple-element.69.out_in, f32[4096,128]{1,0:T(8,128)} %b_ref.7, bf16[1024,128]{1,0:T(8,128)(2,1)S(1)} %get-tuple-element.67.mine_ref, ...), custom_call_target="tpu_custom_call", output_to_operand_aliasing={{0}: (1, {})} | custom-call | flops 1 | bytes 1 | tf_op jit(solution)/shard_map/pallas_call | solution.py:253
  110.8 0.5 collective-permute-start.34
  111.3 2.5 %shard_map.50.a_ref = f32[4096,128]{1,0:T(8,128)} custom-call(s32[4]{0:T(128)S(1)} %pad_add_fusion.ids, f32[4096,128]{1,0:T(8,128)} %get-tuple-element.70.a_ref, bf16[1792,128]{1,0:T(8,128)(2,1)S(1)} %collective-permute-done.33.part_ref), custom_call_target="tpu_custom_call", output_to_operand_aliasing={{}: (1, {})} | custom-call | flops 1 | bytes 1 | tf_op jit(solution)/shard_map/pallas_call | solution.py:253
  113.8 2.5 %shard_map.51 = f32[4096,128]{1,0:T(8,128)} custom-call(s32[4]{0:T(128)S(1)} %pad_add_fusion.ids, f32[4096,128]{1,0:T(8,128)} %shard_map.50.a_ref, bf16[1792,128]{1,0:T(8,128)(2,1)S(1)} %collective-permute-done.34.part_ref), custom_call_target="tpu_custom_call", output_to_operand_aliasing={{}: (1, {})} | custom-call | flops 1 | bytes 1 | tf_op jit(solution)/shard_map/pallas_call | solution.py:253
  (26 shorter events, 0.1 us)
Async XLA Ops:
  0.1 10.7 %copy-start = (bf16[4096,256]{1,0:T(8,128)(2,1)S(1)}, bf16[4096,256]{1,0:T(8,128)(2,1)}, u32[]{:S(2)}) copy-start(bf16[4096,256]{1,0:T(8,128)(2,1)} %param.4) | copy-start | bytes 6291460
  2.5 11.5 %collective-permute-start = (bf16[512,128]{1,0:T(8,128)(2,1)S(1)}, bf16[512,128]{1,0:T(8,128)(2,1)S(1)}, u32[]{:S(2)}, u32[]{:S(2)}) collective-permute-start(bf16[512,128]{1,0:T(8,128)(2,1)S(1)} %get-tuple-element.39.own_ref), channel_id=1, source_target_pairs={{0,4},{16,20},{32,36},{48,52},{64,68},{80,84},{96,100},{112,116}} | collective-permute-start | bytes 393224 | tf_op jit(solution)/shard_map/ppermute | solution.py:30
  6.9 9.5 %collective-permute-start.1 = (bf16[512,128]{1,0:T(8,128)(2,1)S(1)}, bf16[512,128]{1,0:T(8,128)(2,1)S(1)}, u32[]{:S(2)}, u32[]{:S(2)}) collective-permute-start(bf16[512,128]{1,0:T(8,128)(2,1)S(1)} %get-tuple-element.39.own_ref), channel_id=1, source_target_pairs={{0,8},{16,24},{32,40},{48,56},{64,72},{80,88},{96,104},{112,120}} | collective-permute-start | bytes 393224 | tf_op jit(solution)/shard_map/ppermute | solution.py:30
  9.5 8.8 %collective-permute-start.2 = (bf16[512,128]{1,0:T(8,128)(2,1)S(1)}, bf16[512,128]{1,0:T(8,128)(2,1)S(1)}, u32[]{:S(2)}, u32[]{:S(2)}) collective-permute-start(bf16[512,128]{1,0:T(8,128)(2,1)S(1)} %get-tuple-element.39.own_ref), channel_id=1, source_target_pairs={{0,12},{16,28},{32,44},{48,60},{64,76},{80,92},{96,108},{112,124}} | collective-permute-start | bytes 393224 | tf_op jit(solution)/shard_map/ppermute | solution.py:30
  10.8 8.5 %collective-permute-start.9 = (bf16[512,256]{1,0:T(8,128)(2,1)S(1)}, bf16[512,256]{1,0:T(8,128)(2,1)S(1)}, u32[]{:S(2)}, u32[]{:S(2)}) collective-permute-start(bf16[512,256]{1,0:T(8,128)(2,1)S(1)} %slice.9.rest_0_.b0), channel_id=1, source_target_pairs={{0,64},{1,65},{2,66},{3,67},{4,68},{5,69},{6,70},{7,71},{8,72},{9,... | collective-permute-start | bytes 786440 | tf_op jit(solution)/shard_map/ppermute | solution.py:30
  13.7 12.6 %collective-permute-start.11 = (bf16[512,256]{1,0:T(8,128)(2,1)S(1)}, bf16[512,256]{1,0:T(8,128)(2,1)S(1)}, u32[]{:S(2)}, u32[]{:S(2)}) collective-permute-start(bf16[512,256]{1,0:T(8,128)(2,1)S(1)} %slice.9.rest_0_.b0), channel_id=1, source_target_pairs={{0,32},{1,33},{2,34},{3,35},{4,36},{5,37},{6,38},{7,39},{8,40},{9,... | collective-permute-start | bytes 786440 | tf_op jit(solution)/shard_map/ppermute | solution.py:30
  14.0 13.6 %collective-permute-start.7 = (bf16[512,256]{1,0:T(8,128)(2,1)S(1)}, bf16[512,256]{1,0:T(8,128)(2,1)S(1)}, u32[]{:S(2)}, u32[]{:S(2)}) collective-permute-start(bf16[512,256]{1,0:T(8,128)(2,1)S(1)} %slice.9.rest_0_.b0), channel_id=1, source_target_pairs={{0,96},{1,97},{2,98},{3,99},{4,100},{5,101},{6,102},{7,103},{8,104... | collective-permute-start | bytes 786440 | tf_op jit(solution)/shard_map/ppermute | solution.py:30
  16.4 12.3 %collective-permute-start.6 = (bf16[512,256]{1,0:T(8,128)(2,1)S(1)}, bf16[512,256]{1,0:T(8,128)(2,1)S(1)}, u32[]{:S(2)}, u32[]{:S(2)}) collective-permute-start(bf16[512,256]{1,0:T(8,128)(2,1)S(1)} %slice.9.rest_0_.b0), channel_id=1, source_target_pairs={{0,16},{1,17},{2,18},{3,19},{4,20},{5,21},{6,22},{7,23},{8,24},{9,... | collective-permute-start | bytes 786440 | tf_op jit(solution)/shard_map/ppermute | solution.py:30
  18.3 27.7 %collective-permute-start.15 = (bf16[1792,256]{1,0:T(8,128)(2,1)S(1)}, bf16[1792,256]{1,0:T(8,128)(2,1)S(1)}, u32[]{:S(2)}, u32[]{:S(2)}) collective-permute-start(bf16[1792,256]{1,0:T(8,128)(2,1)S(1)} %get-tuple-element.74.rest_0_), channel_id=1, source_target_pairs={{0,32},{1,33},{2,34},{3,35},{4,36},{5,37},{6,38},{7,39},{8,40},{9,... | collective-permute-start | bytes 2752520 | tf_op jit(solution)/shard_map/ppermute | solution.py:30
  19.3 26.6 %collective-permute-start.16 = (bf16[1792,256]{1,0:T(8,128)(2,1)S(1)}, bf16[1792,256]{1,0:T(8,128)(2,1)S(1)}, u32[]{:S(2)}, u32[]{:S(2)}) collective-permute-start(bf16[1792,256]{1,0:T(8,128)(2,1)S(1)} %get-tuple-element.73.rest_0_), channel_id=1, source_target_pairs={{0,96},{1,97},{2,98},{3,99},{4,100},{5,101},{6,102},{7,103},{8,104... | collective-permute-start | bytes 2752520 | tf_op jit(solution)/shard_map/ppermute | solution.py:30
  26.3 3.2 %collective-permute-start.3 = (bf16[512,128]{1,0:T(8,128)(2,1)S(1)}, bf16[512,128]{1,0:T(8,128)(2,1)S(1)}, u32[]{:S(2)}, u32[]{:S(2)}) collective-permute-start(bf16[512,128]{1,0:T(8,128)(2,1)S(1)} %shard_map.38.own_ref.v0), channel_id=1, source_target_pairs={{0,1},{4,5},{8,9},{12,13},{16,17},{20,21},{24,25},{28,29},{32,33},... | collective-permute-start | bytes 393224 | tf_op jit(solution)/shard_map/ppermute | solution.py:30
  27.6 3.7 %collective-permute-start.10 = (bf16[512,256]{1,0:T(8,128)(2,1)S(1)}, bf16[512,256]{1,0:T(8,128)(2,1)S(1)}, u32[]{:S(2)}, u32[]{:S(2)}) collective-permute-start(bf16[512,256]{1,0:T(8,128)(2,1)S(1)} %collective-permute-done.9.rest_4_.b2), channel_id=1, source_target_pairs={{0,16},{1,17},{2,18},{3,19},{4,20},{5,21},{6,22},{7,23},{8,24},{9,... | collective-permute-start | bytes 786440 | tf_op jit(solution)/shard_map/ppermute | solution.py:30
  28.7 4.6 %collective-permute-start.12 = (bf16[512,256]{1,0:T(8,128)(2,1)S(1)}, bf16[512,256]{1,0:T(8,128)(2,1)S(1)}, u32[]{:S(2)}, u32[]{:S(2)}) collective-permute-start(bf16[512,256]{1,0:T(8,128)(2,1)S(1)} %collective-permute-done.11.rest_6_.b3), channel_id=1, source_target_pairs={{0,16},{1,17},{2,18},{3,19},{4,20},{5,21},{6,22},{7,23},{8,24},{9,... | collective-permute-start | bytes 786440 | tf_op jit(solution)/shard_map/ppermute | solution.py:30
  29.5 4.5 %collective-permute-start.8 = (bf16[512,256]{1,0:T(8,128)(2,1)S(1)}, bf16[512,256]{1,0:T(8,128)(2,1)S(1)}, u32[]{:S(2)}, u32[]{:S(2)}) collective-permute-start(bf16[512,256]{1,0:T(8,128)(2,1)S(1)} %collective-permute-done.7.rest_2_.b1), channel_id=1, source_target_pairs={{0,16},{1,17},{2,18},{3,19},{4,20},{5,21},{6,22},{7,23},{8,24},{9,... | collective-permute-start | bytes 786440 | tf_op jit(solution)/shard_map/ppermute | solution.py:30
  31.3 6.8 %collective-permute-start.4 = (bf16[512,128]{1,0:T(8,128)(2,1)S(1)}, bf16[512,128]{1,0:T(8,128)(2,1)S(1)}, u32[]{:S(2)}, u32[]{:S(2)}) collective-permute-start(bf16[512,128]{1,0:T(8,128)(2,1)S(1)} %shard_map.38.own_ref.v0), channel_id=1, source_target_pairs={{0,2},{4,6},{8,10},{12,14},{16,18},{20,22},{24,26},{28,30},{32,34}... | collective-permute-start | bytes 393224 | tf_op jit(solution)/shard_map/ppermute | solution.py:30
  33.2 14.1 %collective-permute-start.19 = (bf16[512,512]{1,0:T(8,128)(2,1)S(1)}, bf16[512,512]{1,0:T(8,128)(2,1)S(1)}, u32[]{:S(2)}, u32[]{:S(2)}) collective-permute-start(bf16[512,512]{1,0:T(8,128)(2,1)S(1)} %get-tuple-element.57), channel_id=1, source_target_pairs={{4,12},{20,28},{36,44},{52,60},{68,76},{84,92},{100,108},{116,124}} | collective-permute-start | bytes 1572872 | tf_op jit(solution)/shard_map/ppermute | solution.py:30
  34.0 4.7 %collective-permute-start.5 = (bf16[512,128]{1,0:T(8,128)(2,1)S(1)}, bf16[512,128]{1,0:T(8,128)(2,1)S(1)}, u32[]{:S(2)}, u32[]{:S(2)}) collective-permute-start(bf16[512,128]{1,0:T(8,128)(2,1)S(1)} %shard_map.38.own_ref.v0), channel_id=1, source_target_pairs={{0,3},{4,7},{8,11},{12,15},{16,19},{20,23},{24,27},{28,31},{32,35}... | collective-permute-start | bytes 393224 | tf_op jit(solution)/shard_map/ppermute | solution.py:30
  38.0 1.4 %collective-permute-start.13 = (bf16[512,128]{1,0:T(8,128)(2,1)S(1)}, bf16[512,128]{1,0:T(8,128)(2,1)S(1)}, u32[]{:S(2)}, u32[]{:S(2)}) collective-permute-start(bf16[512,128]{1,0:T(8,128)(2,1)S(1)} %get-tuple-element.44.own_ref), channel_id=1, source_target_pairs={{4,8},{20,24},{36,40},{52,56},{68,72},{84,88},{100,104},{116,120}} | collective-permute-start | bytes 393224 | tf_op jit(solution)/shard_map/ppermute | solution.py:30
  38.7 1.4 %collective-permute-start.14 = (bf16[512,128]{1,0:T(8,128)(2,1)S(1)}, bf16[512,128]{1,0:T(8,128)(2,1)S(1)}, u32[]{:S(2)}, u32[]{:S(2)}) collective-permute-start(bf16[512,128]{1,0:T(8,128)(2,1)S(1)} %get-tuple-element.44.own_ref), channel_id=1, source_target_pairs={{4,12},{20,28},{36,44},{52,60},{68,76},{84,92},{100,108},{116,124}} | collective-permute-start | bytes 393224 | tf_op jit(solution)/shard_map/ppermute | solution.py:30
  39.4 7.9 %collective-permute-start.18 = (bf16[512,256]{1,0:T(8,128)(2,1)S(1)}, bf16[512,256]{1,0:T(8,128)(2,1)S(1)}, u32[]{:S(2)}, u32[]{:S(2)}) collective-permute-start(bf16[512,256]{1,0:T(8,128)(2,1)S(1)} %get-tuple-element.56), channel_id=1, source_target_pairs={{8,12},{24,28},{40,44},{56,60},{72,76},{88,92},{104,108},{120,124}} | collective-permute-start | bytes 786440 | tf_op jit(solution)/shard_map/ppermute | solution.py:30
  40.1 25.5 %collective-permute-start.25 = (bf16[1792,256]{1,0:T(8,128)(2,1)S(1)}, bf16[1792,256]{1,0:T(8,128)(2,1)S(1)}, u32[]{:S(2)}, u32[]{:S(2)}) collective-permute-start(bf16[1792,256]{1,0:T(8,128)(2,1)S(1)} %get-tuple-element.73.rest_0_), channel_id=1, source_target_pairs={{0,32},{1,33},{2,34},{3,35},{4,36},{5,37},{6,38},{7,39},{8,40},{9,... | collective-permute-start | bytes 2752520 | tf_op jit(solution)/shard_map/ppermute | solution.py:30
  45.9 20.4 %collective-permute-start.26 = (bf16[1792,256]{1,0:T(8,128)(2,1)S(1)}, bf16[1792,256]{1,0:T(8,128)(2,1)S(1)}, u32[]{:S(2)}, u32[]{:S(2)}) collective-permute-start(bf16[1792,256]{1,0:T(8,128)(2,1)S(1)} %get-tuple-element.74.rest_0_), channel_id=1, source_target_pairs={{0,96},{1,97},{2,98},{3,99},{4,100},{5,101},{6,102},{7,103},{8,104... | collective-permute-start | bytes 2752520 | tf_op jit(solution)/shard_map/ppermute | solution.py:30
  47.9 6.6 %collective-permute-start.21 = (bf16[512,512]{1,0:T(8,128)(2,1)S(1)}, bf16[512,512]{1,0:T(8,128)(2,1)S(1)}, u32[]{:S(2)}, u32[]{:S(2)}) collective-permute-start(bf16[512,512]{1,0:T(8,128)(2,1)S(1)} %get-tuple-element.59.p1), channel_id=1, source_target_pairs={{0,16},{1,17},{2,18},{3,19},{4,20},{5,21},{6,22},{7,23},{8,24},{9,... | collective-permute-start | bytes 1572872 | tf_op jit(solution)/shard_map/ppermute | solution.py:30
  50.6 3.9 %collective-permute-start.20 = (bf16[512,256]{1,0:T(8,128)(2,1)S(1)}, bf16[512,256]{1,0:T(8,128)(2,1)S(1)}, u32[]{:S(2)}, u32[]{:S(2)}) collective-permute-start(bf16[512,256]{1,0:T(8,128)(2,1)S(1)} %get-tuple-element.58.p23), channel_id=1, source_target_pairs={{0,16},{1,17},{2,18},{3,19},{4,20},{5,21},{6,22},{7,23},{8,24},{9,... | collective-permute-start | bytes 786440 | tf_op jit(solution)/shard_map/ppermute | solution.py:30
  50.7 3.8 %collective-permute-start.17 = (bf16[512,128]{1,0:T(8,128)(2,1)S(1)}, bf16[512,128]{1,0:T(8,128)(2,1)S(1)}, u32[]{:S(2)}, u32[]{:S(2)}) collective-permute-start(bf16[512,128]{1,0:T(8,128)(2,1)S(1)} %get-tuple-element.48.after_ref.own_ref), channel_id=1, source_target_pairs={{8,12},{24,28},{40,44},{56,60},{72,76},{88,92},{104,108},{120,124}} | collective-permute-start | bytes 393224 | tf_op jit(solution)/shard_map/ppermute | solution.py:30
  58.0 20.8 %collective-permute-start.22 = (bf16[1536,128]{1,0:T(8,128)(2,1)S(1)}, bf16[1536,128]{1,0:T(8,128)(2,1)S(1)}, u32[]{:S(2)}, u32[]{:S(2)}) collective-permute-start(bf16[1536,128]{1,0:T(8,128)(2,1)S(1)} %get-tuple-element.60), channel_id=1, source_target_pairs={{12,0},{28,16},{44,32},{60,48},{76,64},{92,80},{108,96},{124,112}} | collective-permute-start | bytes 1179656 | tf_op jit(solution)/shard_map/ppermute | solution.py:30
  59.3 7.7 %collective-permute-start.23 = (bf16[1024,128]{1,0:T(8,128)(2,1)S(1)}, bf16[1024,128]{1,0:T(8,128)(2,1)S(1)}, u32[]{:S(2)}, u32[]{:S(2)}) collective-permute-start(bf16[1024,128]{1,0:T(8,128)(2,1)S(1)} %get-tuple-element.61), channel_id=1, source_target_pairs={{12,4},{28,20},{44,36},{60,52},{76,68},{92,84},{108,100},{124,116}} | collective-permute-start | bytes 786440 | tf_op jit(solution)/shard_map/ppermute | solution.py:30
  59.9 43.3 %collective-permute-start.31 = (bf16[1792,256]{1,0:T(8,128)(2,1)S(1)}, bf16[1792,256]{1,0:T(8,128)(2,1)S(1)}, u32[]{:S(2)}, u32[]{:S(2)}) collective-permute-start(bf16[1792,256]{1,0:T(8,128)(2,1)S(1)} %collective-permute-done.15.rest_13_.rest_3_), channel_id=1, source_target_pairs={{0,32},{1,33},{2,34},{3,35},{4,36},{5,37},{6,38},{7,39},{8,40},{9,... | collective-permute-start | bytes 2752520 | tf_op jit(solution)/shard_map/ppermute | solution.py:30
  65.6 41.4 %collective-permute-start.32 = (bf16[1792,256]{1,0:T(8,128)(2,1)S(1)}, bf16[1792,256]{1,0:T(8,128)(2,1)S(1)}, u32[]{:S(2)}, u32[]{:S(2)}) collective-permute-start(bf16[1792,256]{1,0:T(8,128)(2,1)S(1)} %collective-permute-done.16.rest_14_.rest_1_), channel_id=1, source_target_pairs={{0,96},{1,97},{2,98},{3,99},{4,100},{5,101},{6,102},{7,103},{8,104... | collective-permute-start | bytes 2752520 | tf_op jit(solution)/shard_map/ppermute | solution.py:30
  66.3 0.7 collective-permute-start.24
  79.5 8.1 %collective-permute-start.27 = (bf16[1536,128]{1,0:T(8,128)(2,1)S(1)}, bf16[1536,128]{1,0:T(8,128)(2,1)S(1)}, u32[]{:S(2)}, u32[]{:S(2)}) collective-permute-start(bf16[1536,128]{1,0:T(8,128)(2,1)S(1)} %shard_map.45.late), channel_id=1, source_target_pairs={{0,1},{4,5},{8,9},{12,13},{16,17},{20,21},{24,25},{28,29},{32,33},... | collective-permute-start | bytes 1179656 | tf_op jit(solution)/shard_map/ppermute | solution.py:30
  80.8 15.2 %collective-permute-start.28 = (bf16[1536,128]{1,0:T(8,128)(2,1)S(1)}, bf16[1536,128]{1,0:T(8,128)(2,1)S(1)}, u32[]{:S(2)}, u32[]{:S(2)}) collective-permute-start(bf16[1536,128]{1,0:T(8,128)(2,1)S(1)} %shard_map.45.late), channel_id=1, source_target_pairs={{0,2},{4,6},{8,10},{12,14},{16,18},{20,22},{24,26},{28,30},{32,34}... | collective-permute-start | bytes 1179656 | tf_op jit(solution)/shard_map/ppermute | solution.py:30
  82.1 13.9 %collective-permute-start.29 = (bf16[1536,128]{1,0:T(8,128)(2,1)S(1)}, bf16[1536,128]{1,0:T(8,128)(2,1)S(1)}, u32[]{:S(2)}, u32[]{:S(2)}) collective-permute-start(bf16[1536,128]{1,0:T(8,128)(2,1)S(1)} %shard_map.45.late), channel_id=1, source_target_pairs={{0,3},{4,7},{8,11},{12,15},{16,19},{20,23},{24,27},{28,31},{32,35}... | collective-permute-start | bytes 1179656 | tf_op jit(solution)/shard_map/ppermute | solution.py:30
  97.0 6.2 %collective-permute-start.30 = (bf16[1024,128]{1,0:T(8,128)(2,1)S(1)}, bf16[1024,128]{1,0:T(8,128)(2,1)S(1)}, u32[]{:S(2)}, u32[]{:S(2)}) collective-permute-start(bf16[1024,128]{1,0:T(8,128)(2,1)S(1)} %get-tuple-element.68), channel_id=1, source_target_pairs={{0,16},{1,17},{2,18},{3,19},{4,20},{5,21},{6,22},{7,23},{8,24},{9,... | collective-permute-start | bytes 786440 | tf_op jit(solution)/shard_map/ppermute | solution.py:30
  107.0 4.3 %collective-permute-start.33 = (bf16[1792,128]{1,0:T(8,128)(2,1)S(1)}, bf16[1792,128]{1,0:T(8,128)(2,1)S(1)}, u32[]{:S(2)}, u32[]{:S(2)}) collective-permute-start(bf16[1792,128]{1,0:T(8,128)(2,1)S(1)} %get-tuple-element.71), channel_id=1, source_target_pairs={{0,16},{1,17},{2,18},{3,19},{4,20},{5,21},{6,22},{7,23},{8,24},{9,... | collective-permute-start | bytes 1376264 | tf_op jit(solution)/shard_map/ppermute | solution.py:30
  110.8 3.0 %collective-permute-start.34 = (bf16[1792,128]{1,0:T(8,128)(2,1)S(1)}, bf16[1792,128]{1,0:T(8,128)(2,1)S(1)}, u32[]{:S(2)}, u32[]{:S(2)}) collective-permute-start(bf16[1792,128]{1,0:T(8,128)(2,1)S(1)} %get-tuple-element.72), channel_id=1, source_target_pairs={{0,16},{1,17},{2,18},{3,19},{4,20},{5,21},{6,22},{7,23},{8,24},{9,... | collective-permute-start | bytes 1376264 | tf_op jit(solution)/shard_map/ppermute | solution.py:30

commit v6 on v5

--- a/solution.py
+++ b/solution.py
@@ -81,7 +81,7 @@
     return jnp.where(i <= j, d, 0.0)
 
 
-def start_kernel(ids, b_ref, d_ref, y_ref, yb_ref, lh_ref, ll_ref):
+def start_kernel(ids, b_ref, d_ref, after_ref, y_ref, yb_ref, lh_ref, ll_ref):
     lh_ref[...], ll_ref[...] = split(lower_mask(d_ref[0]))
     w = b_ref[...]
     y = w + apply(lh_ref, ll_ref, w)
@@ -177,17 +177,17 @@
     x_ref[0:NB, :] = apply(u1h, u1l, t).astype(BF16)
 
 
-def late_kernel(ids, to0, to1, to2, y1, y2, y3, *rest):
+def late_kernel(ids, to0, to1, to2, y0, y1, y2, y3, *rest):
     late_ref, z = rest[-1], ids[2]
-    late_ref[0:NB, :] = jnp.where(z >= 1, y1[...], to0[0:NB, :])
-    late_ref[NB : 2 * NB, :] = jnp.where(z >= 2, y2[...], to0[NB : 2 * NB, :] + to1[0:NB, :])
-    late_ref[2 * NB :, :] = jnp.where(z >= 3, y3[...], to0[2 * NB :, :] + to1[NB:, :] + to2[...])
-
-
-def unknowns_kernel(ids, v0, e1, e2, e3, late, s1, s2, s3, v_ref, mine_ref, theirs_ref):
+    late_ref[0:NB, :] = y0[...]
+    late_ref[NB : 2 * NB, :] = jnp.where(z >= 1, y1[...], to0[0:NB, :])
+    late_ref[2 * NB : 3 * NB, :] = jnp.where(z >= 2, y2[...], to0[NB : 2 * NB, :] + to1[0:NB, :])
+    late_ref[3 * NB :, :] = jnp.where(z >= 3, y3[...], to0[2 * NB :, :] + to1[NB:, :] + to2[...])
+
+
+def unknowns_kernel(ids, late, s1, s2, s3, v_ref, mine_ref, theirs_ref):
     h, owner = ids[1], ids[3] == 0
-    v_ref[0:NB, :] = jnp.where(owner, v0[...], e1[...] + e2[...] + e3[...])
-    v_ref[NB:, :] = jnp.where(owner, late[...], s1[...] + s2[...] + s3[...])
+    v_ref[...] = jnp.where(owner, late[...], s1[...] + s2[...] + s3[...])
     for j in range(4):
         rows = slice(j * HB, (j + 1) * HB)
         mine_ref[rows, :] = v_ref[pl.ds(pl.multiple_of(j * NB + h * HB, HB), HB), :]
@@ -216,25 +216,30 @@
         out_ref[...] = acc[...]
 
 
-def rows_kernel(ids, out_in, b_ref, mine_ref, other_ref, *rest):
-    blocks, (out_ref, part_ref, v_ref) = rest[:4], rest[4:]
-
-    @pl.when(pl.program_id(0) == 0)
-    def _():
-        v_ref[:, 0:128] = mine_ref[...]
-        v_ref[:, 128:] = other_ref[...]
-
-    total = None
-    for d in range(NX):
-        j = lax.rem(ids[0] + d, NX)
-        term = dot(blocks[d][...], v_ref[pl.ds(pl.multiple_of(j * HB, HB), HB), :])
-        total = term if total is None else total + term
-    out_ref[...] = b_ref[...] - total[:, 0:128]
-    part_ref[...] = total[:, 128:].astype(BF16)
-
-
-def add_kernel(ids, a_ref, part_ref, out_ref):
-    out_ref[...] = a_ref[...] - part_ref[...].astype(F32)
+def rows_kernel(tiles, ids, mine_ref, other_ref, *rest):
+    blocks, (own_ref, part_ref, v_ref) = rest[:4], rest[4:]
+    v_ref[:, 0:128] = mine_ref[...]
+    v_ref[:, 128:] = other_ref[...]
+    tile = own_ref.shape[0] // tiles
+    for t in range(tiles):
+        rows = slice(t * tile, (t + 1) * tile)
+        total = None
+        for d in range(NX):
+            j = lax.rem(ids[0] + d, NX)
+            term = dot(blocks[d][rows, :], v_ref[pl.ds(pl.multiple_of(j * HB, HB), HB), :])
+            total = term if total is None else total + term
+        own_ref[rows, :] = total[:, 0:128]
+        part_ref[rows, :] = total[:, 128:].astype(BF16)
+
+
+def add_kernel(ids, out_in, b_ref, own_t, part_t, own_b, part_b, out_ref):
+    i, n = pl.program_id(0), b_ref.shape[0]
+    half = own_t.shape[0] // n
+    for top, own, part in ((True, own_t, part_t), (False, own_b, part_b)):
+        @pl.when((i < half) == top)
+        def _():
+            rows = pl.ds(pl.multiple_of((i if top else i - half) * n, n), n)
+            out_ref[...] = b_ref[...] - own[rows, :] - part[rows, :].astype(F32)
 
 
 def whole(shape):
@@ -285,7 +290,7 @@
     wspecs = [whole((NB, HB))] * 8
 
     y_z0, yb0, lh, ll = call(
-        start_kernel, ids, (in_hbm(rhs), in_hbm(diag_inv)), [first, pl.BlockSpec((1, NB, NB), lambda i, ids: (ids[2], 0, 0))],
+        start_kernel, ids, (in_hbm(rhs), in_hbm(diag_inv), own), [first, pl.BlockSpec((1, NB, NB), lambda i, ids: (ids[2], 0, 0)), ANY],
         (vec, bf(NB), mat, mat), limit=16,
     )
     hops = [send(yb0, z_move(0, t)) for t in (1, 2, 3)]
@@ -301,28 +306,27 @@
         )
 
     y0 = call(combine_kernel, ids, (yb0, *hops), [vspec] * 4, bf(NB))
-    early = [send(y0, y_move(t)) for t in (1, 2, 3)]
-    _, w, y_own, yb1 = forward(0, in_hbm(rhs), first, y0, y_z0, ())
+    y0, w, y_own, yb1 = forward(0, in_hbm(rhs), first, y0, y_z0, ())
     hops = [send(yb1, z_move(1, t)) for t in (2, 3)]
-    y1, w, y_own, yb2 = forward(1, w, vspec, yb1, y_own, hops, (*early, before_t, after_b))
+    y1, w, y_own, yb2 = forward(1, w, vspec, yb1, y_own, hops)
     y2_in = send(yb2, z_move(2, 3))
     p23, p1 = call(relay_kernel, ids, (p23, p1, yb2), [whole((NB, HB)), mspec, ANY], (bf(NB, HB), bf(NB, 2 * HB)))
     p23_other, p1_other = send(p23, other_core), send(p1, other_core)
     y2, y_own, yb3, xs, x23s, x3s = call(
         turn_kernel, ids,
-        (w, y1, yb2, y2_in, y_own, lh, ll, *uppers, p23, p23_other, p1, p1_other, *window),
-        [vspec] * 5 + [mspec] * 8 + [whole((NB, HB))] * 2 + [mspec] * 2 + wspecs,
+        (w, y1, yb2, y2_in, y_own, lh, ll, *uppers, p23, p23_other, p1, p1_other, *window, before_t, after_b),
+        [vspec] * 5 + [mspec] * 8 + [whole((NB, HB))] * 2 + [mspec] * 2 + wspecs + [ANY] * 2,
         (bf(NB), vec, bf(NB), bf(3 * NB), bf(2 * NB), bf(NB)), scratch=[pltpu.VMEM((NB, cols), F32)],
     )
     to0, to1, to2 = send(xs, z_move(3, 0)), send(x23s, z_move(3, 1)), send(x3s, z_move(3, 2))
     late = call(
-        late_kernel, ids, (to0, to1, to2, y1, y2, yb3, before_b, after_t),
-        [whole((3 * NB, cols)), whole((2 * NB, cols))] + [vspec] * 4 + [ANY] * 2, bf(3 * NB),
+        late_kernel, ids, (to0, to1, to2, y0, y1, y2, yb3, before_b, after_t),
+        [whole((3 * NB, cols)), whole((2 * NB, cols))] + [vspec] * 5 + [ANY] * 2, bf(4 * NB),
     )
     spread = [send(late, y_move(t)) for t in (1, 2, 3)]
     out = jax.ShapeDtypeStruct((rows, cols), F32)
     v, mine, theirs = call(
-        unknowns_kernel, ids, (y0, *early, late, *spread), [vspec] * 4 + [whole((3 * NB, cols))] * 4,
+        unknowns_kernel, ids, (late, *spread), [whole((4 * NB, cols))] * 4,
         (bf(4 * NB), bf(4 * HB), bf(4 * HB)),
     )
     other = send(theirs, other_core)
@@ -330,27 +334,21 @@
         window_kernel, ids, (in_hbm(rhs), v, y_own, uppers[0], uppers[1], *window),
         [first, whole((4 * NB, cols)), vspec, mspec, mspec, *wspecs], out, out_spec=first, scratch=[pltpu.VMEM((NB, cols), F32)],
     )
+    sums, parts = [], []
+    for blocks in ((own_t, after_t, far_t, before_t), (own_b, after_b, far_b, before_b)):
+        total, part = call(
+            functools.partial(rows_kernel, 2), ids, (mine, other, *blocks),
+            [vspec] * 2 + [mspec] * 4, (jax.ShapeDtypeStruct((half, cols), F32), bf(half)),
+            scratch=[pltpu.VMEM((4 * HB, 2 * cols), BF16)], limit=24,
+        )
+        sums.append(total)
+        parts.append(send(part, other_core))
     tile = half // 2
-    near = pl.BlockSpec((tile, HB), lambda i, ids: (i, 0))
-    narrow = pl.BlockSpec((tile, cols), lambda i, ids: (i, 0))
-
-    def at(n):
-        return pl.BlockSpec(
-            (pl.Element(tile), pl.Element(cols)), lambda i, ids: (pl.multiple_of(NB + n * half + i * tile, 128), 0)
-        )
-
-    parts = []
-    for n, blocks in enumerate(((own_t, after_t, far_t, before_t), (own_b, after_b, far_b, before_b))):
-        done, part = call(
-            rows_kernel, ids, (done, in_hbm(rhs), mine, other, *blocks),
-            [ANY, at(n), whole(mine.shape), whole(mine.shape)] + [near] * 4,
-            (out, bf(half)), grid=(2,), out_spec=(at(n), narrow), scratch=[pltpu.VMEM((4 * HB, 2 * cols), BF16)],
-            limit=24, aliases={1: 0},
-        )
-        parts.append(send(part, other_core))
-    for n, part in enumerate(parts):
-        done = call(add_kernel, ids, (done, part), [at(n), narrow], out, grid=(2,), out_spec=at(n), aliases={1: 0})
-    return done
+    at = pl.BlockSpec((pl.Element(tile), pl.Element(cols)), lambda i, ids: (pl.multiple_of(NB + i * tile, 128), 0))
+    return call(
+        add_kernel, ids, (done, in_hbm(rhs), sums[0], parts[0], sums[1], parts[1]),
+        [ANY, at] + [vspec] * 4, out, grid=(4,), out_spec=at, aliases={1: 0},
+    )
 
 
 def solution(mesh):

time: 117 us -> 114 us (0.974)
  the two profiles are of different devices: /device:TPU:1 before, /device:TPU:53 now
where the time goes in v6:
time: 114 us; the launch traced here: 113 us
  waiting for transfers between devices  52.3 us (46%)
  starting transfers between devices  31.6 us (28%)
  Pallas kernels  27.7 us (24%)
    ppermute x32, waiting for transfers between devices, send(): return lax.ppermute(value, ('row', 'col'), pairs(move))  52.3 us
    ppermute x32, starting transfers between devices, send(): return lax.ppermute(value, ('row', 'col'), pairs(move))  31.6 us
    pallas_call x14, Pallas kernels, call(): pl.pallas_call(kernel, grid_spec=pltpu.PrefetchScalarGridSpec(num_scalar_...  27.7 us
  transfers between devices with their start and end apart: 32, of which 7 were waited for; matrix products, arithmetic and copies ran while one was open for 0% of the time, Pallas kernels for 21%

profile of v6, /device:TPU:53, one launch (start us, length us, event | category | flops | bytes accessed | tf_op | source)
XLA Modules:
  0.0 113.1 jit_solution(10677776990399200722)
XLA Ops:
  0.0 1.0 slice.9.after_ref.rest_0_.b0
  1.0 0.3 collective-permute-start.4
  1.3 2.5 %collective-permute-start.6 = (bf16[512,256]{1,0:T(8,128)(2,1)S(1)}, bf16[512,256]{1,0:T(8,128)(2,1)S(1)}, u32[]{:S(2)}, u32[]{:S(2)}) collective-permute-start(bf16[512,256]{1,0:T(8,128)(2,1)S(1)} %slice.9.after_ref.rest_0_.b0), channel_id=1, source_target_pairs={{0,64},{1,65},{2,66},{3,67},{4,68},{5,69},{6,70},{7,71},{8,72},{9,... | collective-permute-start | bytes 786440 | tf_op jit(solution)/shard_map/ppermute | solution.py:30
  3.7 0.0 collective-permute-start.8
  3.7 0.1 pad_add_fusion.ids
  3.8 2.4 %shard_map.37 = (f32[512,128]{1,0:T(8,128)S(1)}, bf16[512,128]{1,0:T(8,128)(2,1)S(1)}, bf16[512,512]{1,0:T(8,128)(2,1)S(1)}, bf16[512,512]{1,0:T(8,128)(2,1)S(1)}) custom-call(s32[4]{0:T(128)S(1)} %pad_add_fusion.ids, f32[4096,128]{1,0:T(8,128)} %b_ref.5, f32[4,512,512]{2,1,0:T(8,128)} %d_ref.3, bf16[512,256]{1,0:T(8,128)(2,1)S(1)} %slice.9.after_ref.rest_0_.b0), custom_call_target="tpu_custom_call" | custom-call | flops 1 | bytes 1 | tf_op jit(solution)/shard_map/pallas_call | solution.py:258
  6.2 0.7 collective-permute-start
  6.9 0.7 collective-permute-start.1
  7.6 0.0 collective-permute-done.r1
  7.6 0.7 collective-permute-start.2
  8.3 0.0 collective-permute-done.1.r2
  8.3 1.3 %collective-permute-start.3 = (bf16[512,256]{1,0:T(8,128)(2,1)S(1)}, bf16[512,256]{1,0:T(8,128)(2,1)S(1)}, u32[]{:S(2)}, u32[]{:S(2)}) collective-permute-start(bf16[512,256]{1,0:T(8,128)(2,1)S(1)} %slice.9.after_ref.rest_0_.b0), channel_id=1, source_target_pairs={{0,16},{1,17},{2,18},{3,19},{4,20},{5,21},{6,22},{7,23},{8,24},{9,... | collective-permute-start | bytes 786440 | tf_op jit(solution)/shard_map/ppermute | solution.py:30
  9.6 1.3 %collective-permute-start.5 = (bf16[512,256]{1,0:T(8,128)(2,1)S(1)}, bf16[512,256]{1,0:T(8,128)(2,1)S(1)}, u32[]{:S(2)}, u32[]{:S(2)}) collective-permute-start(bf16[512,256]{1,0:T(8,128)(2,1)S(1)} %collective-permute-done.4.rest_2_.b1), channel_id=1, source_target_pairs={{0,16},{1,17},{2,18},{3,19},{4,20},{5,21},{6,22},{7,23},{8,24},{9,... | collective-permute-start | bytes 786440 | tf_op jit(solution)/shard_map/ppermute | solution.py:30
  10.9 2.1 %collective-permute-start.7 = (bf16[512,256]{1,0:T(8,128)(2,1)S(1)}, bf16[512,256]{1,0:T(8,128)(2,1)S(1)}, u32[]{:S(2)}, u32[]{:S(2)}) collective-permute-start(bf16[512,256]{1,0:T(8,128)(2,1)S(1)} %collective-permute-done.6.rest_4_.b2), channel_id=1, source_target_pairs={{0,16},{1,17},{2,18},{3,19},{4,20},{5,21},{6,22},{7,23},{8,24},{9,... | collective-permute-start | bytes 786440 | tf_op jit(solution)/shard_map/ppermute | solution.py:30
  13.0 3.6 %collective-permute-done.8.rest_6_.b3 = bf16[512,256]{1,0:T(8,128)(2,1)S(1)} collective-permute-done((bf16[512,256]{1,0:T(8,128)(2,1)S(1)}, bf16[512,256]{1,0:T(8,128)(2,1)S(1)}, u32[]{:S(2)}, u32[]{:S(2)}) %collective-permute-start.8) | collective-permute-done | bytes 262176 | tf_op jit(solution)/shard_map/ppermute | solution.py:30
  16.6 0.5 collective-permute-start.9
  17.1 0.1 fusion
  17.3 0.0 collective-permute-done.2.r3
  17.3 1.1 collective-permute-start.17
  18.3 0.7 shard_map.42
  19.0 0.7 collective-permute-start.14
  19.7 0.6 shard_map.38.own_ref
  20.3 0.0 collective-permute-done.5.rest_3_
  20.4 0.0 collective-permute-done.9.rest_7_
  20.4 2.3 %shard_map.39 = (bf16[512,128]{1,0:T(8,128)(2,1)S(1)}, f32[512,128]{1,0:T(8,128)S(1)}, f32[512,128]{1,0:T(8,128)S(1)}, bf16[512,128]{1,0:T(8,128)(2,1)S(1)}) custom-call(s32[4]{0:T(128)S(1)} %pad_add_fusion.ids, f32[4096,128]{1,0:T(8,128)} %b_ref.5, bf16[512,128]{1,0:T(8,128)(2,1)S(1)} %shard_map.38.own_ref, f32[512,128]{1,0:T(8,128)S(1)} %get-tuple-element.41.prior_ref, ...), custom_call_target="tpu_custom_call" | custom-call | flops 1 | bytes 1 | tf_op jit(solution)/shard_map/pallas_call | solution.py:258
  22.7 0.7 collective-permute-start.10
  23.3 0.6 collective-permute-start.18
  23.9 0.7 collective-permute-start.13
  24.6 0.7 collective-permute-start.11
  25.2 0.0 collective-permute-done.11.rest_9_
  25.3 1.4 %shard_map.40 = (bf16[512,128]{1,0:T(8,128)(2,1)S(1)}, f32[512,128]{1,0:T(8,128)S(1)}, f32[512,128]{1,0:T(8,128)S(1)}, bf16[512,128]{1,0:T(8,128)(2,1)S(1)}) custom-call(s32[4]{0:T(128)S(1)} %pad_add_fusion.ids, f32[512,128]{1,0:T(8,128)S(1)} %get-tuple-element.44.w_ref, bf16[512,128]{1,0:T(8,128)(2,1)S(1)} %get-tuple-element.45.own_ref, ...), custom_call_target="tpu_custom_call" | custom-call | flops 1 | bytes 1 | tf_op jit(solution)/shard_map/pallas_call | solution.py:258
  26.6 0.7 collective-permute-start.12
  27.3 0.0 collective-permute-done.13.p23_ref
  27.3 1.9 %collective-permute-start.22 = (bf16[1792,256]{1,0:T(8,128)(2,1)S(1)}, bf16[1792,256]{1,0:T(8,128)(2,1)S(1)}, u32[]{:S(2)}, u32[]{:S(2)}) collective-permute-start(bf16[1792,256]{1,0:T(8,128)(2,1)S(1)} %get-tuple-element.75.rest_0_), channel_id=1, source_target_pairs={{0,32},{1,33},{2,34},{3,35},{4,36},{5,37},{6,38},{7,39},{8,40},{9,... | collective-permute-start | bytes 2752520 | tf_op jit(solution)/shard_map/ppermute | solution.py:30
  29.3 0.0 collective-permute-done.14.p1_ref
  29.3 0.0 collective-permute-start.23
  29.3 0.6 shard_map.43
  29.9 0.8 collective-permute-start.16
  30.7 8.6 %collective-permute-done.17.rest_8_.rest_3_ = bf16[1792,256]{1,0:T(8,128)(2,1)S(1)} collective-permute-done((bf16[1792,256]{1,0:T(8,128)(2,1)S(1)}, bf16[1792,256]{1,0:T(8,128)(2,1)S(1)}, u32[]{:S(2)}, u32[]{:S(2)}) %collective-permute-start.17) | collective-permute-done | bytes 917536 | tf_op jit(solution)/shard_map/ppermute | solution.py:30
  39.3 1.2 %collective-permute-start.15 = (bf16[512,256]{1,0:T(8,128)(2,1)S(1)}, bf16[512,256]{1,0:T(8,128)(2,1)S(1)}, u32[]{:S(2)}, u32[]{:S(2)}) collective-permute-start(bf16[512,256]{1,0:T(8,128)(2,1)S(1)} %get-tuple-element.59.p23), channel_id=1, source_target_pairs={{0,16},{1,17},{2,18},{3,19},{4,20},{5,21},{6,22},{7,23},{8,24},{9,... | collective-permute-start | bytes 786440 | tf_op jit(solution)/shard_map/ppermute | solution.py:30
  40.5 3.2 %shard_map.41 = (bf16[512,512]{1,0:T(8,128)(2,1)S(1)}, bf16[512,512]{1,0:T(8,128)(2,1)S(1)}, bf16[512,512]{1,0:T(8,128)(2,1)S(1)}, bf16[512,512]{1,0:T(8,128)(2,...) custom-call(s32[4]{0:T(128)S(1)} %pad_add_fusion.ids, f32[4,512,512]{2,1,0:T(8,128)} %d_ref.3), custom_call_target="tpu_custom_call" | custom-call | flops 1 | bytes 1 | tf_op jit(solution)/shard_map/pallas_call | solution.py:258
  43.7 2.6 %collective-permute-done.18.rest_9_.rest_1_ = bf16[1792,256]{1,0:T(8,128)(2,1)S(1)} collective-permute-done((bf16[1792,256]{1,0:T(8,128)(2,1)S(1)}, bf16[1792,256]{1,0:T(8,128)(2,1)S(1)}, u32[]{:S(2)}, u32[]{:S(2)}) %collective-permute-start.18) | collective-permute-done | bytes 917536 | tf_op jit(solution)/shard_map/ppermute | solution.py:30
  46.3 3.4 %shard_map.44 = (bf16[512,128]{1,0:T(8,128)(2,1)S(1)}, f32[512,128]{1,0:T(8,128)S(1)}, bf16[512,128]{1,0:T(8,128)(2,1)S(1)}, bf16[1536,128]{1,0:T(8,128)(2,1)S(1...) custom-call(s32[4]{0:T(128)S(1)} %pad_add_fusion.ids, f32[512,128]{1,0:T(8,128)S(1)} %get-tuple-element.47.w_ref, ...), custom_call_target="tpu_custom_call" | custom-call | flops 1 | bytes 1 | tf_op jit(solution)/shard_map/pallas_call | solution.py:258
  49.7 0.7 collective-permute-start.19
  50.4 0.7 collective-permute-start.20
  51.1 0.7 collective-permute-start.21
  51.7 7.2 %collective-permute-done.22.rest_0_.rest_3_ = bf16[1792,256]{1,0:T(8,128)(2,1)S(1)} collective-permute-done((bf16[1792,256]{1,0:T(8,128)(2,1)S(1)}, bf16[1792,256]{1,0:T(8,128)(2,1)S(1)}, u32[]{:S(2)}, u32[]{:S(2)}) %collective-permute-start.22) | collective-permute-done | bytes 917536 | tf_op jit(solution)/shard_map/ppermute | solution.py:30
  59.0 1.5 %collective-permute-start.30 = (bf16[1792,256]{1,0:T(8,128)(2,1)S(1)}, bf16[1792,256]{1,0:T(8,128)(2,1)S(1)}, u32[]{:S(2)}, u32[]{:S(2)}) collective-permute-start(bf16[1792,256]{1,0:T(8,128)(2,1)S(1)} %collective-permute-done.18.rest_9_.rest_1_), channel_id=1, source_target_pairs={{0,96},{1,97},{2,98},{3,99},{4,100},{5,101},{6,102},{7,103},{8,104... | collective-permute-start | bytes 2752520 | tf_op jit(solution)/shard_map/ppermute | solution.py:30
  60.5 5.5 %collective-permute-done.23.rest_1_ = bf16[1792,256]{1,0:T(8,128)(2,1)S(1)} collective-permute-done((bf16[1792,256]{1,0:T(8,128)(2,1)S(1)}, bf16[1792,256]{1,0:T(8,128)(2,1)S(1)}, u32[]{:S(2)}, u32[]{:S(2)}) %collective-permute-start.23) | collective-permute-done | bytes 917536 | tf_op jit(solution)/shard_map/ppermute | solution.py:30
  65.9 2.4 %collective-permute-start.28 = (bf16[1792,256]{1,0:T(8,128)(2,1)S(1)}, bf16[1792,256]{1,0:T(8,128)(2,1)S(1)}, u32[]{:S(2)}, u32[]{:S(2)}) collective-permute-start(bf16[1792,256]{1,0:T(8,128)(2,1)S(1)} %collective-permute-done.17.rest_8_.rest_3_), channel_id=1, source_target_pairs={{0,32},{1,33},{2,34},{3,35},{4,36},{5,37},{6,38},{7,39},{8,40},{9,... | collective-permute-start | bytes 2752520 | tf_op jit(solution)/shard_map/ppermute | solution.py:30
  68.3 0.7 shard_map.45.late
  69.0 0.7 collective-permute-start.24
  69.7 1.3 %collective-permute-start.25 = (bf16[2048,128]{1,0:T(8,128)(2,1)S(1)}, bf16[2048,128]{1,0:T(8,128)(2,1)S(1)}, u32[]{:S(2)}, u32[]{:S(2)}) collective-permute-start(bf16[2048,128]{1,0:T(8,128)(2,1)S(1)} %shard_map.45.late), channel_id=1, source_target_pairs={{0,2},{4,6},{8,10},{12,14},{16,18},{20,22},{24,26},{28,30},{32,34}... | collective-permute-start | bytes 1572872 | tf_op jit(solution)/shard_map/ppermute | solution.py:30
  71.0 0.7 collective-permute-start.26
  71.7 23.6 %collective-permute-done.25.s2 = bf16[2048,128]{1,0:T(8,128)(2,1)S(1)} collective-permute-done((bf16[2048,128]{1,0:T(8,128)(2,1)S(1)}, bf16[2048,128]{1,0:T(8,128)(2,1)S(1)}, u32[]{:S(2)}, u32[]{:S(2)}) %collective-permute-start.25) | collective-permute-done | bytes 524320 | tf_op jit(solution)/shard_map/ppermute | solution.py:30
  95.3 1.0 shard_map.46
  96.3 3.5 %collective-permute-start.27 = (bf16[1024,128]{1,0:T(8,128)(2,1)S(1)}, bf16[1024,128]{1,0:T(8,128)(2,1)S(1)}, u32[]{:S(2)}, u32[]{:S(2)}) collective-permute-start(bf16[1024,128]{1,0:T(8,128)(2,1)S(1)} %get-tuple-element.70), channel_id=1, source_target_pairs={{0,16},{1,17},{2,18},{3,19},{4,20},{5,21},{6,22},{7,23},{8,24},{9,... | collective-permute-start | bytes 786440 | tf_op jit(solution)/shard_map/ppermute | solution.py:30
  99.8 1.2 %collective-permute-done.27.other_ref = bf16[1024,128]{1,0:T(8,128)(2,1)S(1)} collective-permute-done((bf16[1024,128]{1,0:T(8,128)(2,1)S(1)}, bf16[1024,128]{1,0:T(8,128)(2,1)S(1)}, u32[]{:S(2)}, u32[]{:S(2)}) %collective-permute-start.27) | collective-permute-done | bytes 262176 | tf_op jit(solution)/shard_map/ppermute | solution.py:30
  101.0 1.8 %shard_map.49 = (f32[1792,128]{1,0:T(8,128)S(1)}, bf16[1792,128]{1,0:T(8,128)(2,1)S(1)}) custom-call(s32[4]{0:T(128)S(1)} %pad_add_fusion.ids, bf16[1024,128]{1,0:T(8,128)(2,1)S(1)} %get-tuple-element.69.mine_ref, bf16[1024,128]{1,0:T(8,128)(2,1)S(1)} %collective-permute-done.27.other_ref, bf16[1792,256]{1,0:T(8,128)(2,1)S(1)} %get-tuple-element.75.rest_0_, ...), custom_call_target="tpu_custom_call" | custom-call | flops 1 | bytes 1 | tf_op jit(solution)/shard_map/pallas_call | solution.py:258
  102.7 0.5 collective-permute-start.31
  103.2 1.7 %shard_map.48 = (f32[1792,128]{1,0:T(8,128)S(1)}, bf16[1792,128]{1,0:T(8,128)(2,1)S(1)}) custom-call(s32[4]{0:T(128)S(1)} %pad_add_fusion.ids, bf16[1024,128]{1,0:T(8,128)(2,1)S(1)} %get-tuple-element.69.mine_ref, bf16[1024,128]{1,0:T(8,128)(2,1)S(1)} %collective-permute-done.27.other_ref, bf16[1792,256]{1,0:T(8,128)(2,1)S(1)} %get-tuple-element.76.rest_0_, ...), custom_call_target="tpu_custom_call" | custom-call | flops 1 | bytes 1 | tf_op jit(solution)/shard_map/pallas_call | solution.py:258
  104.9 0.2 collective-permute-start.29
  105.1 3.6 %shard_map.47.out_in = f32[4096,128]{1,0:T(8,128)} custom-call(s32[4]{0:T(128)S(1)} %pad_add_fusion.ids, f32[4096,128]{1,0:T(8,128)} %b_ref.5, bf16[2048,128]{1,0:T(8,128)(2,1)S(1)} %get-tuple-element.67.v_ref, f32[512,128]{1,0:T(8,128)S(1)} %get-tuple-element.68.own_ref, bf16[512,512]{1,0:T(8,128)(2,1)S(1)} %get-tuple-element.51.u3h.uh_ref, ...), custom_call_target="tpu_custom_call" | custom-call | flops 1 | bytes 1 | tf_op jit(solution)/shard_map/pallas_call | solution.py:258
  108.8 4.3 %shard_map.50 = f32[4096,128]{1,0:T(8,128)} custom-call(s32[4]{0:T(128)S(1)} %pad_add_fusion.ids, f32[4096,128]{1,0:T(8,128)} %shard_map.47.out_in, f32[4096,128]{1,0:T(8,128)} %b_ref.5, f32[1792,128]{1,0:T(8,128)S(1)} %get-tuple-element.71.own_t, bf16[1792,128]{1,0:T(8,128)(2,1)S(1)} %collective-permute-done.29.part_t, ...), custom_call_target="tpu_custom_call", output_to_operand_aliasing={{}: (1, {})} | custom-call | flops 1 | bytes 1 | tf_op jit(solution)/shard_map/pallas_call | solution.py:258
  (19 shorter events, 0.0 us)
Async XLA Ops:
  1.0 8.6 %collective-permute-start.4 = (bf16[512,256]{1,0:T(8,128)(2,1)S(1)}, bf16[512,256]{1,0:T(8,128)(2,1)S(1)}, u32[]{:S(2)}, u32[]{:S(2)}) collective-permute-start(bf16[512,256]{1,0:T(8,128)(2,1)S(1)} %slice.9.after_ref.rest_0_.b0), channel_id=1, source_target_pairs={{0,96},{1,97},{2,98},{3,99},{4,100},{5,101},{6,102},{7,103},{8,104... | collective-permute-start | bytes 786440 | tf_op jit(solution)/shard_map/ppermute | solution.py:30
  1.3 9.6 %collective-permute-start.6 = (bf16[512,256]{1,0:T(8,128)(2,1)S(1)}, bf16[512,256]{1,0:T(8,128)(2,1)S(1)}, u32[]{:S(2)}, u32[]{:S(2)}) collective-permute-start(bf16[512,256]{1,0:T(8,128)(2,1)S(1)} %slice.9.after_ref.rest_0_.b0), channel_id=1, source_target_pairs={{0,64},{1,65},{2,66},{3,67},{4,68},{5,69},{6,70},{7,71},{8,72},{9,... | collective-permute-start | bytes 786440 | tf_op jit(solution)/shard_map/ppermute | solution.py:30
  3.7 12.9 %collective-permute-start.8 = (bf16[512,256]{1,0:T(8,128)(2,1)S(1)}, bf16[512,256]{1,0:T(8,128)(2,1)S(1)}, u32[]{:S(2)}, u32[]{:S(2)}) collective-permute-start(bf16[512,256]{1,0:T(8,128)(2,1)S(1)} %slice.9.after_ref.rest_0_.b0), channel_id=1, source_target_pairs={{0,32},{1,33},{2,34},{3,35},{4,36},{5,37},{6,38},{7,39},{8,40},{9,... | collective-permute-start | bytes 786440 | tf_op jit(solution)/shard_map/ppermute | solution.py:30
  3.8 13.3 %copy-start = (bf16[4096,256]{1,0:T(8,128)(2,1)S(1)}, bf16[4096,256]{1,0:T(8,128)(2,1)}, u32[]{:S(2)}) copy-start(bf16[4096,256]{1,0:T(8,128)(2,1)} %param.4) | copy-start | bytes 6291460
  6.2 1.4 %collective-permute-start = (bf16[512,128]{1,0:T(8,128)(2,1)S(1)}, bf16[512,128]{1,0:T(8,128)(2,1)S(1)}, u32[]{:S(2)}, u32[]{:S(2)}) collective-permute-start(bf16[512,128]{1,0:T(8,128)(2,1)S(1)} %get-tuple-element.40.own_ref), channel_id=1, source_target_pairs={{0,4},{16,20},{32,36},{48,52},{64,68},{80,84},{96,100},{112,116}} | collective-permute-start | bytes 393224 | tf_op jit(solution)/shard_map/ppermute | solution.py:30
  6.9 1.4 %collective-permute-start.1 = (bf16[512,128]{1,0:T(8,128)(2,1)S(1)}, bf16[512,128]{1,0:T(8,128)(2,1)S(1)}, u32[]{:S(2)}, u32[]{:S(2)}) collective-permute-start(bf16[512,128]{1,0:T(8,128)(2,1)S(1)} %get-tuple-element.40.own_ref), channel_id=1, source_target_pairs={{0,8},{16,24},{32,40},{48,56},{64,72},{80,88},{96,104},{112,120}} | collective-permute-start | bytes 393224 | tf_op jit(solution)/shard_map/ppermute | solution.py:30
  7.6 9.7 %collective-permute-start.2 = (bf16[512,128]{1,0:T(8,128)(2,1)S(1)}, bf16[512,128]{1,0:T(8,128)(2,1)S(1)}, u32[]{:S(2)}, u32[]{:S(2)}) collective-permute-start(bf16[512,128]{1,0:T(8,128)(2,1)S(1)} %get-tuple-element.40.own_ref), channel_id=1, source_target_pairs={{0,12},{16,28},{32,44},{48,60},{64,76},{80,92},{96,108},{112,124}} | collective-permute-start | bytes 393224 | tf_op jit(solution)/shard_map/ppermute | solution.py:30
  8.3 10.7 %collective-permute-start.3 = (bf16[512,256]{1,0:T(8,128)(2,1)S(1)}, bf16[512,256]{1,0:T(8,128)(2,1)S(1)}, u32[]{:S(2)}, u32[]{:S(2)}) collective-permute-start(bf16[512,256]{1,0:T(8,128)(2,1)S(1)} %slice.9.after_ref.rest_0_.b0), channel_id=1, source_target_pairs={{0,16},{1,17},{2,18},{3,19},{4,20},{5,21},{6,22},{7,23},{8,24},{9,... | collective-permute-start | bytes 786440 | tf_op jit(solution)/shard_map/ppermute | solution.py:30
  9.6 10.7 %collective-permute-start.5 = (bf16[512,256]{1,0:T(8,128)(2,1)S(1)}, bf16[512,256]{1,0:T(8,128)(2,1)S(1)}, u32[]{:S(2)}, u32[]{:S(2)}) collective-permute-start(bf16[512,256]{1,0:T(8,128)(2,1)S(1)} %collective-permute-done.4.rest_2_.b1), channel_id=1, source_target_pairs={{0,16},{1,17},{2,18},{3,19},{4,20},{5,21},{6,22},{7,23},{8,24},{9,... | collective-permute-start | bytes 786440 | tf_op jit(solution)/shard_map/ppermute | solution.py:30
  10.9 9.4 %collective-permute-start.7 = (bf16[512,256]{1,0:T(8,128)(2,1)S(1)}, bf16[512,256]{1,0:T(8,128)(2,1)S(1)}, u32[]{:S(2)}, u32[]{:S(2)}) collective-permute-start(bf16[512,256]{1,0:T(8,128)(2,1)S(1)} %collective-permute-done.6.rest_4_.b2), channel_id=1, source_target_pairs={{0,16},{1,17},{2,18},{3,19},{4,20},{5,21},{6,22},{7,23},{8,24},{9,... | collective-permute-start | bytes 786440 | tf_op jit(solution)/shard_map/ppermute | solution.py:30
  16.6 3.7 %collective-permute-start.9 = (bf16[512,256]{1,0:T(8,128)(2,1)S(1)}, bf16[512,256]{1,0:T(8,128)(2,1)S(1)}, u32[]{:S(2)}, u32[]{:S(2)}) collective-permute-start(bf16[512,256]{1,0:T(8,128)(2,1)S(1)} %collective-permute-done.8.rest_6_.b3), channel_id=1, source_target_pairs={{0,16},{1,17},{2,18},{3,19},{4,20},{5,21},{6,22},{7,23},{8,24},{9,... | collective-permute-start | bytes 786440 | tf_op jit(solution)/shard_map/ppermute | solution.py:30
  17.3 22.0 %collective-permute-start.17 = (bf16[1792,256]{1,0:T(8,128)(2,1)S(1)}, bf16[1792,256]{1,0:T(8,128)(2,1)S(1)}, u32[]{:S(2)}, u32[]{:S(2)}) collective-permute-start(bf16[1792,256]{1,0:T(8,128)(2,1)S(1)} %get-tuple-element.76.rest_0_), channel_id=1, source_target_pairs={{0,32},{1,33},{2,34},{3,35},{4,36},{5,37},{6,38},{7,39},{8,40},{9,... | collective-permute-start | bytes 2752520 | tf_op jit(solution)/shard_map/ppermute | solution.py:30
  19.0 10.3 %collective-permute-start.14 = (bf16[512,512]{1,0:T(8,128)(2,1)S(1)}, bf16[512,512]{1,0:T(8,128)(2,1)S(1)}, u32[]{:S(2)}, u32[]{:S(2)}) collective-permute-start(bf16[512,512]{1,0:T(8,128)(2,1)S(1)} %get-tuple-element.58), channel_id=1, source_target_pairs={{4,12},{20,28},{36,44},{52,60},{68,76},{84,92},{100,108},{116,124}} | collective-permute-start | bytes 1572872 | tf_op jit(solution)/shard_map/ppermute | solution.py:30
  22.7 1.9 %collective-permute-start.10 = (bf16[512,128]{1,0:T(8,128)(2,1)S(1)}, bf16[512,128]{1,0:T(8,128)(2,1)S(1)}, u32[]{:S(2)}, u32[]{:S(2)}) collective-permute-start(bf16[512,128]{1,0:T(8,128)(2,1)S(1)} %get-tuple-element.45.own_ref), channel_id=1, source_target_pairs={{4,8},{20,24},{36,40},{52,56},{68,72},{84,88},{100,104},{116,120}} | collective-permute-start | bytes 393224 | tf_op jit(solution)/shard_map/ppermute | solution.py:30
  23.3 22.9 %collective-permute-start.18 = (bf16[1792,256]{1,0:T(8,128)(2,1)S(1)}, bf16[1792,256]{1,0:T(8,128)(2,1)S(1)}, u32[]{:S(2)}, u32[]{:S(2)}) collective-permute-start(bf16[1792,256]{1,0:T(8,128)(2,1)S(1)} %get-tuple-element.75.rest_0_), channel_id=1, source_target_pairs={{0,96},{1,97},{2,98},{3,99},{4,100},{5,101},{6,102},{7,103},{8,104... | collective-permute-start | bytes 2752520 | tf_op jit(solution)/shard_map/ppermute | solution.py:30
  23.9 3.4 %collective-permute-start.13 = (bf16[512,256]{1,0:T(8,128)(2,1)S(1)}, bf16[512,256]{1,0:T(8,128)(2,1)S(1)}, u32[]{:S(2)}, u32[]{:S(2)}) collective-permute-start(bf16[512,256]{1,0:T(8,128)(2,1)S(1)} %get-tuple-element.57), channel_id=1, source_target_pairs={{8,12},{24,28},{40,44},{56,60},{72,76},{88,92},{104,108},{120,124}} | collective-permute-start | bytes 786440 | tf_op jit(solution)/shard_map/ppermute | solution.py:30
  24.6 0.7 collective-permute-start.11
  26.6 3.2 %collective-permute-start.12 = (bf16[512,128]{1,0:T(8,128)(2,1)S(1)}, bf16[512,128]{1,0:T(8,128)(2,1)S(1)}, u32[]{:S(2)}, u32[]{:S(2)}) collective-permute-start(bf16[512,128]{1,0:T(8,128)(2,1)S(1)} %get-tuple-element.49.after_ref.own_ref), channel_id=1, source_target_pairs={{8,12},{24,28},{40,44},{56,60},{72,76},{88,92},{104,108},{120,124}} | collective-permute-start | bytes 393224 | tf_op jit(solution)/shard_map/ppermute | solution.py:30
  27.3 31.6 %collective-permute-start.22 = (bf16[1792,256]{1,0:T(8,128)(2,1)S(1)}, bf16[1792,256]{1,0:T(8,128)(2,1)S(1)}, u32[]{:S(2)}, u32[]{:S(2)}) collective-permute-start(bf16[1792,256]{1,0:T(8,128)(2,1)S(1)} %get-tuple-element.75.rest_0_), channel_id=1, source_target_pairs={{0,32},{1,33},{2,34},{3,35},{4,36},{5,37},{6,38},{7,39},{8,40},{9,... | collective-permute-start | bytes 2752520 | tf_op jit(solution)/shard_map/ppermute | solution.py:30
  29.3 36.6 %collective-permute-start.23 = (bf16[1792,256]{1,0:T(8,128)(2,1)S(1)}, bf16[1792,256]{1,0:T(8,128)(2,1)S(1)}, u32[]{:S(2)}, u32[]{:S(2)}) collective-permute-start(bf16[1792,256]{1,0:T(8,128)(2,1)S(1)} %get-tuple-element.76.rest_0_), channel_id=1, source_target_pairs={{0,96},{1,97},{2,98},{3,99},{4,100},{5,101},{6,102},{7,103},{8,104... | collective-permute-start | bytes 2752520 | tf_op jit(solution)/shard_map/ppermute | solution.py:30
  29.9 16.4 %collective-permute-start.16 = (bf16[512,512]{1,0:T(8,128)(2,1)S(1)}, bf16[512,512]{1,0:T(8,128)(2,1)S(1)}, u32[]{:S(2)}, u32[]{:S(2)}) collective-permute-start(bf16[512,512]{1,0:T(8,128)(2,1)S(1)} %get-tuple-element.60.p1), channel_id=1, source_target_pairs={{0,16},{1,17},{2,18},{3,19},{4,20},{5,21},{6,22},{7,23},{8,24},{9,... | collective-permute-start | bytes 1572872 | tf_op jit(solution)/shard_map/ppermute | solution.py:30
  39.3 7.0 %collective-permute-start.15 = (bf16[512,256]{1,0:T(8,128)(2,1)S(1)}, bf16[512,256]{1,0:T(8,128)(2,1)S(1)}, u32[]{:S(2)}, u32[]{:S(2)}) collective-permute-start(bf16[512,256]{1,0:T(8,128)(2,1)S(1)} %get-tuple-element.59.p23), channel_id=1, source_target_pairs={{0,16},{1,17},{2,18},{3,19},{4,20},{5,21},{6,22},{7,23},{8,24},{9,... | collective-permute-start | bytes 786440 | tf_op jit(solution)/shard_map/ppermute | solution.py:30
  49.7 18.6 %collective-permute-start.19 = (bf16[1536,128]{1,0:T(8,128)(2,1)S(1)}, bf16[1536,128]{1,0:T(8,128)(2,1)S(1)}, u32[]{:S(2)}, u32[]{:S(2)}) collective-permute-start(bf16[1536,128]{1,0:T(8,128)(2,1)S(1)} %get-tuple-element.61), channel_id=1, source_target_pairs={{12,0},{28,16},{44,32},{60,48},{76,64},{92,80},{108,96},{124,112}} | collective-permute-start | bytes 1179656 | tf_op jit(solution)/shard_map/ppermute | solution.py:30
  50.4 17.9 %collective-permute-start.20 = (bf16[1024,128]{1,0:T(8,128)(2,1)S(1)}, bf16[1024,128]{1,0:T(8,128)(2,1)S(1)}, u32[]{:S(2)}, u32[]{:S(2)}) collective-permute-start(bf16[1024,128]{1,0:T(8,128)(2,1)S(1)} %get-tuple-element.62), channel_id=1, source_target_pairs={{12,4},{28,20},{44,36},{60,52},{76,68},{92,84},{108,100},{124,116}} | collective-permute-start | bytes 786440 | tf_op jit(solution)/shard_map/ppermute | solution.py:30
  51.1 17.2 %collective-permute-start.21 = (bf16[512,128]{1,0:T(8,128)(2,1)S(1)}, bf16[512,128]{1,0:T(8,128)(2,1)S(1)}, u32[]{:S(2)}, u32[]{:S(2)}) collective-permute-start(bf16[512,128]{1,0:T(8,128)(2,1)S(1)} %get-tuple-element.63), channel_id=1, source_target_pairs={{12,8},{28,24},{44,40},{60,56},{76,72},{92,88},{108,104},{124,120}} | collective-permute-start | bytes 393224 | tf_op jit(solution)/shard_map/ppermute | solution.py:30
  59.0 40.8 %collective-permute-start.30 = (bf16[1792,256]{1,0:T(8,128)(2,1)S(1)}, bf16[1792,256]{1,0:T(8,128)(2,1)S(1)}, u32[]{:S(2)}, u32[]{:S(2)}) collective-permute-start(bf16[1792,256]{1,0:T(8,128)(2,1)S(1)} %collective-permute-done.18.rest_9_.rest_1_), channel_id=1, source_target_pairs={{0,96},{1,97},{2,98},{3,99},{4,100},{5,101},{6,102},{7,103},{8,104... | collective-permute-start | bytes 2752520 | tf_op jit(solution)/shard_map/ppermute | solution.py:30
  65.9 37.2 %collective-permute-start.28 = (bf16[1792,256]{1,0:T(8,128)(2,1)S(1)}, bf16[1792,256]{1,0:T(8,128)(2,1)S(1)}, u32[]{:S(2)}, u32[]{:S(2)}) collective-permute-start(bf16[1792,256]{1,0:T(8,128)(2,1)S(1)} %collective-permute-done.17.rest_8_.rest_3_), channel_id=1, source_target_pairs={{0,32},{1,33},{2,34},{3,35},{4,36},{5,37},{6,38},{7,39},{8,40},{9,... | collective-permute-start | bytes 2752520 | tf_op jit(solution)/shard_map/ppermute | solution.py:30
  69.0 2.7 %collective-permute-start.24 = (bf16[2048,128]{1,0:T(8,128)(2,1)S(1)}, bf16[2048,128]{1,0:T(8,128)(2,1)S(1)}, u32[]{:S(2)}, u32[]{:S(2)}) collective-permute-start(bf16[2048,128]{1,0:T(8,128)(2,1)S(1)} %shard_map.45.late), channel_id=1, source_target_pairs={{0,1},{4,5},{8,9},{12,13},{16,17},{20,21},{24,25},{28,29},{32,33},... | collective-permute-start | bytes 1572872 | tf_op jit(solution)/shard_map/ppermute | solution.py:30
  69.7 25.6 %collective-permute-start.25 = (bf16[2048,128]{1,0:T(8,128)(2,1)S(1)}, bf16[2048,128]{1,0:T(8,128)(2,1)S(1)}, u32[]{:S(2)}, u32[]{:S(2)}) collective-permute-start(bf16[2048,128]{1,0:T(8,128)(2,1)S(1)} %shard_map.45.late), channel_id=1, source_target_pairs={{0,2},{4,6},{8,10},{12,14},{16,18},{20,22},{24,26},{28,30},{32,34}... | collective-permute-start | bytes 1572872 | tf_op jit(solution)/shard_map/ppermute | solution.py:30
  71.0 24.3 %collective-permute-start.26 = (bf16[2048,128]{1,0:T(8,128)(2,1)S(1)}, bf16[2048,128]{1,0:T(8,128)(2,1)S(1)}, u32[]{:S(2)}, u32[]{:S(2)}) collective-permute-start(bf16[2048,128]{1,0:T(8,128)(2,1)S(1)} %shard_map.45.late), channel_id=1, source_target_pairs={{0,3},{4,7},{8,11},{12,15},{16,19},{20,23},{24,27},{28,31},{32,35}... | collective-permute-start | bytes 1572872 | tf_op jit(solution)/shard_map/ppermute | solution.py:30
  96.3 4.6 %collective-permute-start.27 = (bf16[1024,128]{1,0:T(8,128)(2,1)S(1)}, bf16[1024,128]{1,0:T(8,128)(2,1)S(1)}, u32[]{:S(2)}, u32[]{:S(2)}) collective-permute-start(bf16[1024,128]{1,0:T(8,128)(2,1)S(1)} %get-tuple-element.70), channel_id=1, source_target_pairs={{0,16},{1,17},{2,18},{3,19},{4,20},{5,21},{6,22},{7,23},{8,24},{9,... | collective-permute-start | bytes 786440 | tf_op jit(solution)/shard_map/ppermute | solution.py:30
  102.7 6.1 %collective-permute-start.31 = (bf16[1792,128]{1,0:T(8,128)(2,1)S(1)}, bf16[1792,128]{1,0:T(8,128)(2,1)S(1)}, u32[]{:S(2)}, u32[]{:S(2)}) collective-permute-start(bf16[1792,128]{1,0:T(8,128)(2,1)S(1)} %get-tuple-element.74), channel_id=1, source_target_pairs={{0,16},{1,17},{2,18},{3,19},{4,20},{5,21},{6,22},{7,23},{8,24},{9,... | collective-permute-start | bytes 1376264 | tf_op jit(solution)/shard_map/ppermute | solution.py:30
  104.9 3.8 %collective-permute-start.29 = (bf16[1792,128]{1,0:T(8,128)(2,1)S(1)}, bf16[1792,128]{1,0:T(8,128)(2,1)S(1)}, u32[]{:S(2)}, u32[]{:S(2)}) collective-permute-start(bf16[1792,128]{1,0:T(8,128)(2,1)S(1)} %get-tuple-element.72), channel_id=1, source_target_pairs={{0,16},{1,17},{2,18},{3,19},{4,20},{5,21},{6,22},{7,23},{8,24},{9,... | collective-permute-start | bytes 1376264 | tf_op jit(solution)/shard_map/ppermute | solution.py:30

commit v7 on v6

--- a/solution.py
+++ b/solution.py
@@ -126,7 +126,11 @@
     w = w_out[...]
     y = w + apply(lh_ref, ll_ref, w)
     y_ref[...] = jnp.where(ids[2] == j + 1, y, prior_ref[...])
-    yb_ref[...] = y.astype(BF16)
+    if j == 0:
+        yb_ref[...] = y.astype(BF16)
+    else:
+        yb_ref[0:NB, :] = v_ref[...]
+        yb_ref[NB:, :] = y.astype(BF16)
 
 
 def pick_kernel(ids, b0, b1, b2, b3, p23_ref, p1_ref):
@@ -147,13 +151,16 @@
 
 
 def turn_kernel(
-    ids, w_ref, y1_ref, own_ref, y2_in, prior_ref, lh, ll, u3h, u3l, u1h, u1l, u2h, u2l, p23, p23_other, p1, p1_other, *rest
+    ids, w_ref, y12_ref, y12_in, prior_ref, lh, ll, u3h, u3l, u1h, u1l, u2h, u2l, p23, p23_other, p1, p1_other, *rest
 ):
-    blocks, (y2_ref, y_ref, yb_ref, x_ref, x23_ref, x3_ref, acc) = rest[:8], rest[-7:]
+    blocks, (y1_ref, y2_ref, y_ref, yb_ref, x_ref, x23_ref, x3_ref, acc) = rest[:8], rest[-8:]
     h = ids[1]
-    y2 = own_or_received(ids, 2, own_ref, (y2_in,))
+    last = ids[2] == 3
+    y1_ref[...] = jnp.where(last, y12_in[0:NB, :], y12_ref[0:NB, :])
+    y2 = jnp.where(last, y12_in[NB:, :], y12_ref[NB:, :])
     y2_ref[...] = y2
     acc[...] = w_ref[...]
+    block_product(ids, blocks, 1, y1_ref, acc)
     block_product(ids, blocks, 2, y2_ref, acc)
     w = acc[...]
     y3 = w + apply(lh, ll, w)
@@ -302,21 +309,21 @@
     def forward(j, w, wspec, own, prior, received, after=()):
         return call(
             functools.partial(forward_kernel, j, len(received)), ids, (w, own, prior, lh, ll, *window, *received, *after),
-            [wspec, vspec, vspec, mspec, mspec, *wspecs] + [vspec] * len(received) + [ANY] * len(after), (bf(NB), vec, vec, bf(NB)),
+            [wspec, vspec, vspec, mspec, mspec, *wspecs] + [vspec] * len(received) + [ANY] * len(after), (bf(NB), vec, vec, bf(NB if j == 0 else 2 * NB)),
         )
 
     y0 = call(combine_kernel, ids, (yb0, *hops), [vspec] * 4, bf(NB))
-    y0, w, y_own, yb1 = forward(0, in_hbm(rhs), first, y0, y_z0, ())
-    hops = [send(yb1, z_move(1, t)) for t in (2, 3)]
-    y1, w, y_own, yb2 = forward(1, w, vspec, yb1, y_own, hops)
-    y2_in = send(yb2, z_move(2, 3))
-    p23, p1 = call(relay_kernel, ids, (p23, p1, yb2), [whole((NB, HB)), mspec, ANY], (bf(NB, HB), bf(NB, 2 * HB)))
+    _, w0, y_own, yb1 = forward(0, in_hbm(rhs), first, y0, y_z0, (), uppers)
+    hops = [send(yb1, z_move(1, 2))]
+    _, _, y_own, y12 = forward(1, w0, vspec, yb1, y_own, hops)
+    y12_in = send(y12, z_move(2, 3))
+    p23, p1 = call(relay_kernel, ids, (p23, p1, y12), [whole((NB, HB)), mspec, ANY], (bf(NB, HB), bf(NB, 2 * HB)))
     p23_other, p1_other = send(p23, other_core), send(p1, other_core)
-    y2, y_own, yb3, xs, x23s, x3s = call(
+    y1, y2, y_own, yb3, xs, x23s, x3s = call(
         turn_kernel, ids,
-        (w, y1, yb2, y2_in, y_own, lh, ll, *uppers, p23, p23_other, p1, p1_other, *window, before_t, after_b),
-        [vspec] * 5 + [mspec] * 8 + [whole((NB, HB))] * 2 + [mspec] * 2 + wspecs + [ANY] * 2,
-        (bf(NB), vec, bf(NB), bf(3 * NB), bf(2 * NB), bf(NB)), scratch=[pltpu.VMEM((NB, cols), F32)],
+        (w0, y12, y12_in, y_own, lh, ll, *uppers, p23, p23_other, p1, p1_other, *window, before_t, after_b),
+        [vspec] * 4 + [mspec] * 8 + [whole((NB, HB))] * 2 + [mspec] * 2 + wspecs + [ANY] * 2,
+        (bf(NB), bf(NB), vec, bf(NB), bf(3 * NB), bf(2 * NB), bf(NB)), scratch=[pltpu.VMEM((NB, cols), F32)],
     )
     to0, to1, to2 = send(xs, z_move(3, 0)), send(x23s, z_move(3, 1)), send(x3s, z_move(3, 2))
     late = call(

time: 114 us -> 117 us (1.026)
  waiting for transfers between devices: 52.3 us -> 55.2 us
  Pallas kernels: 27.7 us -> 29.2 us
    ppermute x32 -> x31, waiting for transfers between devices: 52.3 us -> 55.2 us  [send(): return lax.ppermute(value, ('row', 'col'), pairs(move))]
    pallas_call x14, Pallas kernels: 27.7 us -> 29.2 us  [call(): pl.pallas_call(kernel, grid_spec=pltpu.PrefetchScalarGridSpec(num_scalar_...]
    ppermute x32 -> x31, starting transfers between devices: 31.6 us -> 30.9 us  [send(): return lax.ppermute(value, ('row', 'col'), pairs(move))]
  transfers between devices with their start and end apart: 32 -> 31, of which waited for: 7 -> 7; matrix products, arithmetic and copies ran while one was open for 0% -> 0% of each run, Pallas kernels for 21% -> 21%
where the time goes in v7:
time: 117 us
  waiting for transfers between devices  55.2 us (47%)
  starting transfers between devices  30.9 us (26%)
  Pallas kernels  29.2 us (25%)
    ppermute x31, waiting for transfers between devices, send(): return lax.ppermute(value, ('row', 'col'), pairs(move))  55.2 us
    ppermute x31, starting transfers between devices, send(): return lax.ppermute(value, ('row', 'col'), pairs(move))  30.9 us
    pallas_call x14, Pallas kernels, call(): pl.pallas_call(kernel, grid_spec=pltpu.PrefetchScalarGridSpec(num_scalar_...  29.2 us
  transfers between devices with their start and end apart: 31, of which 7 were waited for; matrix products, arithmetic and copies ran while one was open for 0% of the time, Pallas kernels for 21%

profile of v7, /device:TPU:53, one launch (start us, length us, event | category | flops | bytes accessed | tf_op | source)
XLA Modules:
  0.0 116.7 jit_solution(3146841501261386478)
XLA Ops:
  0.0 1.0 slice.9.after_ref.rest_0_.b0
  1.0 0.3 collective-permute-start.4
  1.3 2.5 %collective-permute-start.6 = (bf16[512,256]{1,0:T(8,128)(2,1)S(1)}, bf16[512,256]{1,0:T(8,128)(2,1)S(1)}, u32[]{:S(2)}, u32[]{:S(2)}) collective-permute-start(bf16[512,256]{1,0:T(8,128)(2,1)S(1)} %slice.9.after_ref.rest_0_.b0), channel_id=1, source_target_pairs={{0,64},{1,65},{2,66},{3,67},{4,68},{5,69},{6,70},{7,71},{8,72},{9,... | collective-permute-start | bytes 786440 | tf_op jit(solution)/shard_map/ppermute | solution.py:30
  3.7 0.0 collective-permute-start.8
  3.7 0.1 pad_add_fusion.ids
  3.8 2.4 %shard_map.37 = (f32[512,128]{1,0:T(8,128)S(1)}, bf16[512,128]{1,0:T(8,128)(2,1)S(1)}, bf16[512,512]{1,0:T(8,128)(2,1)S(1)}, bf16[512,512]{1,0:T(8,128)(2,1)S(1)}) custom-call(s32[4]{0:T(128)S(1)} %pad_add_fusion.ids, f32[4096,128]{1,0:T(8,128)} %b_ref.5, f32[4,512,512]{2,1,0:T(8,128)} %d_ref.3, bf16[512,256]{1,0:T(8,128)(2,1)S(1)} %slice.9.after_ref.rest_0_.b0), custom_call_target="tpu_custom_call" | custom-call | flops 1 | bytes 1 | tf_op jit(solution)/shard_map/pallas_call | solution.py:265
  6.2 0.7 collective-permute-start
  6.9 0.7 collective-permute-start.1
  7.6 0.0 collective-permute-done.r1
  7.6 0.7 collective-permute-start.2
  8.3 0.0 collective-permute-done.1.r2
  8.3 1.3 %collective-permute-start.3 = (bf16[512,256]{1,0:T(8,128)(2,1)S(1)}, bf16[512,256]{1,0:T(8,128)(2,1)S(1)}, u32[]{:S(2)}, u32[]{:S(2)}) collective-permute-start(bf16[512,256]{1,0:T(8,128)(2,1)S(1)} %slice.9.after_ref.rest_0_.b0), channel_id=1, source_target_pairs={{0,16},{1,17},{2,18},{3,19},{4,20},{5,21},{6,22},{7,23},{8,24},{9,... | collective-permute-start | bytes 786440 | tf_op jit(solution)/shard_map/ppermute | solution.py:30
  9.6 1.3 %collective-permute-start.5 = (bf16[512,256]{1,0:T(8,128)(2,1)S(1)}, bf16[512,256]{1,0:T(8,128)(2,1)S(1)}, u32[]{:S(2)}, u32[]{:S(2)}) collective-permute-start(bf16[512,256]{1,0:T(8,128)(2,1)S(1)} %collective-permute-done.4.rest_2_.b1), channel_id=1, source_target_pairs={{0,16},{1,17},{2,18},{3,19},{4,20},{5,21},{6,22},{7,23},{8,24},{9,... | collective-permute-start | bytes 786440 | tf_op jit(solution)/shard_map/ppermute | solution.py:30
  10.9 2.1 %collective-permute-start.7 = (bf16[512,256]{1,0:T(8,128)(2,1)S(1)}, bf16[512,256]{1,0:T(8,128)(2,1)S(1)}, u32[]{:S(2)}, u32[]{:S(2)}) collective-permute-start(bf16[512,256]{1,0:T(8,128)(2,1)S(1)} %collective-permute-done.6.rest_4_.b2), channel_id=1, source_target_pairs={{0,16},{1,17},{2,18},{3,19},{4,20},{5,21},{6,22},{7,23},{8,24},{9,... | collective-permute-start | bytes 786440 | tf_op jit(solution)/shard_map/ppermute | solution.py:30
  13.0 3.6 %collective-permute-done.8.rest_6_.b3 = bf16[512,256]{1,0:T(8,128)(2,1)S(1)} collective-permute-done((bf16[512,256]{1,0:T(8,128)(2,1)S(1)}, bf16[512,256]{1,0:T(8,128)(2,1)S(1)}, u32[]{:S(2)}, u32[]{:S(2)}) %collective-permute-start.8) | collective-permute-done | bytes 262176 | tf_op jit(solution)/shard_map/ppermute | solution.py:30
  16.6 0.5 collective-permute-start.9
  17.1 0.1 fusion
  17.3 0.0 collective-permute-done.2.r3
  17.3 1.1 collective-permute-start.16
  18.3 0.7 shard_map.42
  19.0 0.7 collective-permute-start.13
  19.7 3.2 %shard_map.39 = (bf16[512,512]{1,0:T(8,128)(2,1)S(1)}, bf16[512,512]{1,0:T(8,128)(2,1)S(1)}, bf16[512,512]{1,0:T(8,128)(2,1)S(1)}, bf16[512,512]{1,0:T(8,128)(2,...) custom-call(s32[4]{0:T(128)S(1)} %pad_add_fusion.ids, f32[4,512,512]{2,1,0:T(8,128)} %d_ref.3), custom_call_target="tpu_custom_call" | custom-call | flops 1 | bytes 1 | tf_op jit(solution)/shard_map/pallas_call | solution.py:265
  22.9 0.6 shard_map.38.own_ref.y0
  23.5 0.0 collective-permute-done.5.rest_3_
  23.5 0.0 collective-permute-done.7.rest_5_
  23.5 2.8 %shard_map.40 = (bf16[512,128]{1,0:T(8,128)(2,1)}, f32[512,128]{1,0:T(8,128)S(1)}, f32[512,128]{1,0:T(8,128)S(1)}, bf16[512,128]{1,0:T(8,128)(2,1)S(1)}) custom-call(s32[4]{0:T(128)S(1)} %pad_add_fusion.ids, f32[4096,128]{1,0:T(8,128)} %b_ref.5, bf16[512,128]{1,0:T(8,128)(2,1)S(1)} %shard_map.38.own_ref.y0, f32[512,128]{1,0:T(8,128)S(1)} %get-tuple-element.39.prior_ref, ...), custom_call_target="tpu_custom_call" | custom-call | flops 1 | bytes 1 | tf_op jit(solution)/shard_map/pallas_call | solution.py:265
  26.3 0.7 collective-permute-start.10
  26.9 0.6 collective-permute-start.17
  27.5 0.7 collective-permute-start.12
  28.2 0.0 collective-permute-done.10.rest_8_
  28.2 1.9 %shard_map.41 = (bf16[512,128]{1,0:T(8,128)(2,1)}, f32[512,128]{1,0:T(8,128)}, f32[512,128]{1,0:T(8,128)S(1)}, bf16[1024,128]{1,0:T(8,128)(2,1)S(1)}) custom-call(s32[4]{0:T(128)S(1)} %pad_add_fusion.ids, f32[512,128]{1,0:T(8,128)S(1)} %get-tuple-element.48.w_ref, bf16[512,128]{1,0:T(8,128)(2,1)S(1)} %get-tuple-element.49.own_ref, ...), custom_call_target="tpu_custom_call" | custom-call | flops 1 | bytes 1 | tf_op jit(solution)/shard_map/pallas_call | solution.py:265
  30.1 0.7 collective-permute-start.11
  30.7 0.0 collective-permute-done.12.p23_ref
  30.8 2.0 %collective-permute-start.21 = (bf16[1792,256]{1,0:T(8,128)(2,1)S(1)}, bf16[1792,256]{1,0:T(8,128)(2,1)S(1)}, u32[]{:S(2)}, u32[]{:S(2)}) collective-permute-start(bf16[1792,256]{1,0:T(8,128)(2,1)S(1)} %get-tuple-element.71.rest_0_), channel_id=1, source_target_pairs={{0,32},{1,33},{2,34},{3,35},{4,36},{5,37},{6,38},{7,39},{8,40},{9,... | collective-permute-start | bytes 2752520 | tf_op jit(solution)/shard_map/ppermute | solution.py:30
  32.7 0.0 collective-permute-done.13.p1_ref
  32.7 0.6 shard_map.43
  33.3 0.0 collective-permute-done.11.y12_in
  33.3 0.8 collective-permute-start.15
  34.1 5.2 %collective-permute-done.16.rest_8_.rest_3_ = bf16[1792,256]{1,0:T(8,128)(2,1)S(1)} collective-permute-done((bf16[1792,256]{1,0:T(8,128)(2,1)S(1)}, bf16[1792,256]{1,0:T(8,128)(2,1)S(1)}, u32[]{:S(2)}, u32[]{:S(2)}) %collective-permute-start.16) | collective-permute-done | bytes 917536 | tf_op jit(solution)/shard_map/ppermute | solution.py:30
  39.3 1.2 %collective-permute-start.14 = (bf16[512,256]{1,0:T(8,128)(2,1)S(1)}, bf16[512,256]{1,0:T(8,128)(2,1)S(1)}, u32[]{:S(2)}, u32[]{:S(2)}) collective-permute-start(bf16[512,256]{1,0:T(8,128)(2,1)S(1)} %get-tuple-element.55.p23), channel_id=1, source_target_pairs={{0,16},{1,17},{2,18},{3,19},{4,20},{5,21},{6,22},{7,23},{8,24},{9,... | collective-permute-start | bytes 786440 | tf_op jit(solution)/shard_map/ppermute | solution.py:30
  40.5 9.4 %collective-permute-done.17.rest_9_.rest_1_ = bf16[1792,256]{1,0:T(8,128)(2,1)S(1)} collective-permute-done((bf16[1792,256]{1,0:T(8,128)(2,1)S(1)}, bf16[1792,256]{1,0:T(8,128)(2,1)S(1)}, u32[]{:S(2)}, u32[]{:S(2)}) %collective-permute-start.17) | collective-permute-done | bytes 917536 | tf_op jit(solution)/shard_map/ppermute | solution.py:30
  49.9 4.0 %shard_map.44 = (bf16[512,128]{1,0:T(8,128)(2,1)S(1)}, bf16[512,128]{1,0:T(8,128)(2,1)S(1)}, f32[512,128]{1,0:T(8,128)S(1)}, bf16[512,128]{1,0:T(8,128)(2,1)S(1)...) custom-call(s32[4]{0:T(128)S(1)} %pad_add_fusion.ids, ...), custom_call_target="tpu_custom_call" | custom-call | flops 1 | bytes 1 | tf_op jit(solution)/shard_map/pallas_call | solution.py:265
  53.8 0.7 collective-permute-start.18
  54.5 0.7 collective-permute-start.19
  55.2 0.7 collective-permute-start.20
  55.9 3.1 %collective-permute-done.21.rest_0_.rest_3_ = bf16[1792,256]{1,0:T(8,128)(2,1)S(1)} collective-permute-done((bf16[1792,256]{1,0:T(8,128)(2,1)S(1)}, bf16[1792,256]{1,0:T(8,128)(2,1)S(1)}, u32[]{:S(2)}, u32[]{:S(2)}) %collective-permute-start.21) | collective-permute-done | bytes 917536 | tf_op jit(solution)/shard_map/ppermute | solution.py:30
  59.0 1.5 %collective-permute-start.29 = (bf16[1792,256]{1,0:T(8,128)(2,1)S(1)}, bf16[1792,256]{1,0:T(8,128)(2,1)S(1)}, u32[]{:S(2)}, u32[]{:S(2)}) collective-permute-start(bf16[1792,256]{1,0:T(8,128)(2,1)S(1)} %collective-permute-done.17.rest_9_.rest_1_), channel_id=1, source_target_pairs={{0,96},{1,97},{2,98},{3,99},{4,100},{5,101},{6,102},{7,103},{8,104... | collective-permute-start | bytes 2752520 | tf_op jit(solution)/shard_map/ppermute | solution.py:30
  60.5 9.1 %collective-permute-done.22.rest_1_ = bf16[1792,256]{1,0:T(8,128)(2,1)S(1)} collective-permute-done((bf16[1792,256]{1,0:T(8,128)(2,1)S(1)}, bf16[1792,256]{1,0:T(8,128)(2,1)S(1)}, u32[]{:S(2)}, u32[]{:S(2)}) %collective-permute-start.22) | collective-permute-done | bytes 917536 | tf_op jit(solution)/shard_map/ppermute | solution.py:30
  69.5 2.4 %collective-permute-start.27 = (bf16[1792,256]{1,0:T(8,128)(2,1)S(1)}, bf16[1792,256]{1,0:T(8,128)(2,1)S(1)}, u32[]{:S(2)}, u32[]{:S(2)}) collective-permute-start(bf16[1792,256]{1,0:T(8,128)(2,1)S(1)} %collective-permute-done.16.rest_8_.rest_3_), channel_id=1, source_target_pairs={{0,32},{1,33},{2,34},{3,35},{4,36},{5,37},{6,38},{7,39},{8,40},{9,... | collective-permute-start | bytes 2752520 | tf_op jit(solution)/shard_map/ppermute | solution.py:30
  71.9 0.0 collective-permute-done.19.to1
  71.9 0.7 shard_map.45.late
  72.6 0.7 collective-permute-start.23
  73.3 1.3 %collective-permute-start.24 = (bf16[2048,128]{1,0:T(8,128)(2,1)S(1)}, bf16[2048,128]{1,0:T(8,128)(2,1)S(1)}, u32[]{:S(2)}, u32[]{:S(2)}) collective-permute-start(bf16[2048,128]{1,0:T(8,128)(2,1)S(1)} %shard_map.45.late), channel_id=1, source_target_pairs={{0,2},{4,6},{8,10},{12,14},{16,18},{20,22},{24,26},{28,30},{32,34}... | collective-permute-start | bytes 1572872 | tf_op jit(solution)/shard_map/ppermute | solution.py:30
  74.6 0.7 collective-permute-start.25
  75.3 23.6 %collective-permute-done.24.s2 = bf16[2048,128]{1,0:T(8,128)(2,1)S(1)} collective-permute-done((bf16[2048,128]{1,0:T(8,128)(2,1)S(1)}, bf16[2048,128]{1,0:T(8,128)(2,1)S(1)}, u32[]{:S(2)}, u32[]{:S(2)}) %collective-permute-start.24) | collective-permute-done | bytes 524320 | tf_op jit(solution)/shard_map/ppermute | solution.py:30
  98.9 1.0 shard_map.46
  100.0 3.5 %collective-permute-start.26 = (bf16[1024,128]{1,0:T(8,128)(2,1)S(1)}, bf16[1024,128]{1,0:T(8,128)(2,1)S(1)}, u32[]{:S(2)}, u32[]{:S(2)}) collective-permute-start(bf16[1024,128]{1,0:T(8,128)(2,1)S(1)} %get-tuple-element.66), channel_id=1, source_target_pairs={{0,16},{1,17},{2,18},{3,19},{4,20},{5,21},{6,22},{7,23},{8,24},{9,... | collective-permute-start | bytes 786440 | tf_op jit(solution)/shard_map/ppermute | solution.py:30
  103.4 1.2 collective-permute-done.26.other_ref
  104.6 1.7 %shard_map.49 = (f32[1792,128]{1,0:T(8,128)S(1)}, bf16[1792,128]{1,0:T(8,128)(2,1)S(1)}) custom-call(s32[4]{0:T(128)S(1)} %pad_add_fusion.ids, bf16[1024,128]{1,0:T(8,128)(2,1)S(1)} %get-tuple-element.65.mine_ref, bf16[1024,128]{1,0:T(8,128)(2,1)S(1)} %collective-permute-done.26.other_ref, bf16[1792,256]{1,0:T(8,128)(2,1)S(1)} %get-tuple-element.71.rest_0_, ...), custom_call_target="tpu_custom_call" | custom-call | flops 1 | bytes 1 | tf_op jit(solution)/shard_map/pallas_call | solution.py:265
  106.3 0.5 collective-permute-start.30
  106.8 1.7 %shard_map.48 = (f32[1792,128]{1,0:T(8,128)S(1)}, bf16[1792,128]{1,0:T(8,128)(2,1)S(1)}) custom-call(s32[4]{0:T(128)S(1)} %pad_add_fusion.ids, bf16[1024,128]{1,0:T(8,128)(2,1)S(1)} %get-tuple-element.65.mine_ref, bf16[1024,128]{1,0:T(8,128)(2,1)S(1)} %collective-permute-done.26.other_ref, bf16[1792,256]{1,0:T(8,128)(2,1)S(1)} %get-tuple-element.72.rest_0_, ...), custom_call_target="tpu_custom_call" | custom-call | flops 1 | bytes 1 | tf_op jit(solution)/shard_map/pallas_call | solution.py:265
  108.6 0.2 collective-permute-start.28
  108.8 3.6 %shard_map.47.out_in = f32[4096,128]{1,0:T(8,128)} custom-call(s32[4]{0:T(128)S(1)} %pad_add_fusion.ids, f32[4096,128]{1,0:T(8,128)} %b_ref.5, bf16[2048,128]{1,0:T(8,128)(2,1)S(1)} %get-tuple-element.63.v_ref, f32[512,128]{1,0:T(8,128)S(1)} %get-tuple-element.64.own_ref, bf16[512,512]{1,0:T(8,128)(2,1)S(1)} %get-tuple-element.42.rest_8_.u3h.uh_ref, ...), custom_call_target="tpu_custom_call" | custom-call | flops 1 | bytes 1 | tf_op jit(solution)/shard_map/pallas_call | solution.py:265
  112.4 4.3 %shard_map.50 = f32[4096,128]{1,0:T(8,128)} custom-call(s32[4]{0:T(128)S(1)} %pad_add_fusion.ids, f32[4096,128]{1,0:T(8,128)} %shard_map.47.out_in, f32[4096,128]{1,0:T(8,128)} %b_ref.5, f32[1792,128]{1,0:T(8,128)S(1)} %get-tuple-element.67.own_t, bf16[1792,128]{1,0:T(8,128)(2,1)S(1)} %collective-permute-done.28.part_t, ...), custom_call_target="tpu_custom_call", output_to_operand_aliasing={{}: (1, {})} | custom-call | flops 1 | bytes 1 | tf_op jit(solution)/shard_map/pallas_call | solution.py:265
  (17 shorter events, 0.0 us)
Async XLA Ops:
  1.0 8.6 %collective-permute-start.4 = (bf16[512,256]{1,0:T(8,128)(2,1)S(1)}, bf16[512,256]{1,0:T(8,128)(2,1)S(1)}, u32[]{:S(2)}, u32[]{:S(2)}) collective-permute-start(bf16[512,256]{1,0:T(8,128)(2,1)S(1)} %slice.9.after_ref.rest_0_.b0), channel_id=1, source_target_pairs={{0,96},{1,97},{2,98},{3,99},{4,100},{5,101},{6,102},{7,103},{8,104... | collective-permute-start | bytes 786440 | tf_op jit(solution)/shard_map/ppermute | solution.py:30
  1.3 9.6 %collective-permute-start.6 = (bf16[512,256]{1,0:T(8,128)(2,1)S(1)}, bf16[512,256]{1,0:T(8,128)(2,1)S(1)}, u32[]{:S(2)}, u32[]{:S(2)}) collective-permute-start(bf16[512,256]{1,0:T(8,128)(2,1)S(1)} %slice.9.after_ref.rest_0_.b0), channel_id=1, source_target_pairs={{0,64},{1,65},{2,66},{3,67},{4,68},{5,69},{6,70},{7,71},{8,72},{9,... | collective-permute-start | bytes 786440 | tf_op jit(solution)/shard_map/ppermute | solution.py:30
  3.7 12.9 %collective-permute-start.8 = (bf16[512,256]{1,0:T(8,128)(2,1)S(1)}, bf16[512,256]{1,0:T(8,128)(2,1)S(1)}, u32[]{:S(2)}, u32[]{:S(2)}) collective-permute-start(bf16[512,256]{1,0:T(8,128)(2,1)S(1)} %slice.9.after_ref.rest_0_.b0), channel_id=1, source_target_pairs={{0,32},{1,33},{2,34},{3,35},{4,36},{5,37},{6,38},{7,39},{8,40},{9,... | collective-permute-start | bytes 786440 | tf_op jit(solution)/shard_map/ppermute | solution.py:30
  3.8 13.3 %copy-start = (bf16[4096,256]{1,0:T(8,128)(2,1)S(1)}, bf16[4096,256]{1,0:T(8,128)(2,1)}, u32[]{:S(2)}) copy-start(bf16[4096,256]{1,0:T(8,128)(2,1)} %param.4) | copy-start | bytes 6291460
  6.2 1.4 %collective-permute-start = (bf16[512,128]{1,0:T(8,128)(2,1)S(1)}, bf16[512,128]{1,0:T(8,128)(2,1)S(1)}, u32[]{:S(2)}, u32[]{:S(2)}) collective-permute-start(bf16[512,128]{1,0:T(8,128)(2,1)S(1)} %get-tuple-element.38.own_ref), channel_id=1, source_target_pairs={{0,4},{16,20},{32,36},{48,52},{64,68},{80,84},{96,100},{112,116}} | collective-permute-start | bytes 393224 | tf_op jit(solution)/shard_map/ppermute | solution.py:30
  6.9 1.4 %collective-permute-start.1 = (bf16[512,128]{1,0:T(8,128)(2,1)S(1)}, bf16[512,128]{1,0:T(8,128)(2,1)S(1)}, u32[]{:S(2)}, u32[]{:S(2)}) collective-permute-start(bf16[512,128]{1,0:T(8,128)(2,1)S(1)} %get-tuple-element.38.own_ref), channel_id=1, source_target_pairs={{0,8},{16,24},{32,40},{48,56},{64,72},{80,88},{96,104},{112,120}} | collective-permute-start | bytes 393224 | tf_op jit(solution)/shard_map/ppermute | solution.py:30
  7.6 9.7 %collective-permute-start.2 = (bf16[512,128]{1,0:T(8,128)(2,1)S(1)}, bf16[512,128]{1,0:T(8,128)(2,1)S(1)}, u32[]{:S(2)}, u32[]{:S(2)}) collective-permute-start(bf16[512,128]{1,0:T(8,128)(2,1)S(1)} %get-tuple-element.38.own_ref), channel_id=1, source_target_pairs={{0,12},{16,28},{32,44},{48,60},{64,76},{80,92},{96,108},{112,124}} | collective-permute-start | bytes 393224 | tf_op jit(solution)/shard_map/ppermute | solution.py:30
  8.3 10.7 %collective-permute-start.3 = (bf16[512,256]{1,0:T(8,128)(2,1)S(1)}, bf16[512,256]{1,0:T(8,128)(2,1)S(1)}, u32[]{:S(2)}, u32[]{:S(2)}) collective-permute-start(bf16[512,256]{1,0:T(8,128)(2,1)S(1)} %slice.9.after_ref.rest_0_.b0), channel_id=1, source_target_pairs={{0,16},{1,17},{2,18},{3,19},{4,20},{5,21},{6,22},{7,23},{8,24},{9,... | collective-permute-start | bytes 786440 | tf_op jit(solution)/shard_map/ppermute | solution.py:30
  9.6 13.9 %collective-permute-start.5 = (bf16[512,256]{1,0:T(8,128)(2,1)S(1)}, bf16[512,256]{1,0:T(8,128)(2,1)S(1)}, u32[]{:S(2)}, u32[]{:S(2)}) collective-permute-start(bf16[512,256]{1,0:T(8,128)(2,1)S(1)} %collective-permute-done.4.rest_2_.b1), channel_id=1, source_target_pairs={{0,16},{1,17},{2,18},{3,19},{4,20},{5,21},{6,22},{7,23},{8,24},{9,... | collective-permute-start | bytes 786440 | tf_op jit(solution)/shard_map/ppermute | solution.py:30
  10.9 12.6 %collective-permute-start.7 = (bf16[512,256]{1,0:T(8,128)(2,1)S(1)}, bf16[512,256]{1,0:T(8,128)(2,1)S(1)}, u32[]{:S(2)}, u32[]{:S(2)}) collective-permute-start(bf16[512,256]{1,0:T(8,128)(2,1)S(1)} %collective-permute-done.6.rest_4_.b2), channel_id=1, source_target_pairs={{0,16},{1,17},{2,18},{3,19},{4,20},{5,21},{6,22},{7,23},{8,24},{9,... | collective-permute-start | bytes 786440 | tf_op jit(solution)/shard_map/ppermute | solution.py:30
  16.6 6.9 %collective-permute-start.9 = (bf16[512,256]{1,0:T(8,128)(2,1)S(1)}, bf16[512,256]{1,0:T(8,128)(2,1)S(1)}, u32[]{:S(2)}, u32[]{:S(2)}) collective-permute-start(bf16[512,256]{1,0:T(8,128)(2,1)S(1)} %collective-permute-done.8.rest_6_.b3), channel_id=1, source_target_pairs={{0,16},{1,17},{2,18},{3,19},{4,20},{5,21},{6,22},{7,23},{8,24},{9,... | collective-permute-start | bytes 786440 | tf_op jit(solution)/shard_map/ppermute | solution.py:30
  17.3 22.0 %collective-permute-start.16 = (bf16[1792,256]{1,0:T(8,128)(2,1)S(1)}, bf16[1792,256]{1,0:T(8,128)(2,1)S(1)}, u32[]{:S(2)}, u32[]{:S(2)}) collective-permute-start(bf16[1792,256]{1,0:T(8,128)(2,1)S(1)} %get-tuple-element.72.rest_0_), channel_id=1, source_target_pairs={{0,32},{1,33},{2,34},{3,35},{4,36},{5,37},{6,38},{7,39},{8,40},{9,... | collective-permute-start | bytes 2752520 | tf_op jit(solution)/shard_map/ppermute | solution.py:30
  19.0 13.7 %collective-permute-start.13 = (bf16[512,512]{1,0:T(8,128)(2,1)S(1)}, bf16[512,512]{1,0:T(8,128)(2,1)S(1)}, u32[]{:S(2)}, u32[]{:S(2)}) collective-permute-start(bf16[512,512]{1,0:T(8,128)(2,1)S(1)} %get-tuple-element.54), channel_id=1, source_target_pairs={{4,12},{20,28},{36,44},{52,60},{68,76},{84,92},{100,108},{116,124}} | collective-permute-start | bytes 1572872 | tf_op jit(solution)/shard_map/ppermute | solution.py:30
  26.3 1.9 %collective-permute-start.10 = (bf16[512,128]{1,0:T(8,128)(2,1)S(1)}, bf16[512,128]{1,0:T(8,128)(2,1)S(1)}, u32[]{:S(2)}, u32[]{:S(2)}) collective-permute-start(bf16[512,128]{1,0:T(8,128)(2,1)S(1)} %get-tuple-element.49.own_ref), channel_id=1, source_target_pairs={{4,8},{20,24},{36,40},{52,56},{68,72},{84,88},{100,104},{116,120}} | collective-permute-start | bytes 393224 | tf_op jit(solution)/shard_map/ppermute | solution.py:30
  26.9 22.9 %collective-permute-start.17 = (bf16[1792,256]{1,0:T(8,128)(2,1)S(1)}, bf16[1792,256]{1,0:T(8,128)(2,1)S(1)}, u32[]{:S(2)}, u32[]{:S(2)}) collective-permute-start(bf16[1792,256]{1,0:T(8,128)(2,1)S(1)} %get-tuple-element.71.rest_0_), channel_id=1, source_target_pairs={{0,96},{1,97},{2,98},{3,99},{4,100},{5,101},{6,102},{7,103},{8,104... | collective-permute-start | bytes 2752520 | tf_op jit(solution)/shard_map/ppermute | solution.py:30
  27.5 3.2 %collective-permute-start.12 = (bf16[512,256]{1,0:T(8,128)(2,1)S(1)}, bf16[512,256]{1,0:T(8,128)(2,1)S(1)}, u32[]{:S(2)}, u32[]{:S(2)}) collective-permute-start(bf16[512,256]{1,0:T(8,128)(2,1)S(1)} %get-tuple-element.53), channel_id=1, source_target_pairs={{8,12},{24,28},{40,44},{56,60},{72,76},{88,92},{104,108},{120,124}} | collective-permute-start | bytes 786440 | tf_op jit(solution)/shard_map/ppermute | solution.py:30
  30.1 3.2 %collective-permute-start.11 = (bf16[1024,128]{1,0:T(8,128)(2,1)S(1)}, bf16[1024,128]{1,0:T(8,128)(2,1)S(1)}, u32[]{:S(2)}, u32[]{:S(2)}) collective-permute-start(bf16[1024,128]{1,0:T(8,128)(2,1)S(1)} %get-tuple-element.51.after_ref.y12_ref), channel_id=1, source_target_pairs={{8,12},{24,28},{40,44},{56,60},{72,76},{88,92},{104,108},{120,124}} | collective-permute-start | bytes 786440 | tf_op jit(solution)/shard_map/ppermute | solution.py:30
  30.8 28.2 %collective-permute-start.21 = (bf16[1792,256]{1,0:T(8,128)(2,1)S(1)}, bf16[1792,256]{1,0:T(8,128)(2,1)S(1)}, u32[]{:S(2)}, u32[]{:S(2)}) collective-permute-start(bf16[1792,256]{1,0:T(8,128)(2,1)S(1)} %get-tuple-element.71.rest_0_), channel_id=1, source_target_pairs={{0,32},{1,33},{2,34},{3,35},{4,36},{5,37},{6,38},{7,39},{8,40},{9,... | collective-permute-start | bytes 2752520 | tf_op jit(solution)/shard_map/ppermute | solution.py:30
  32.7 36.8 %collective-permute-start.22 = (bf16[1792,256]{1,0:T(8,128)(2,1)S(1)}, bf16[1792,256]{1,0:T(8,128)(2,1)S(1)}, u32[]{:S(2)}, u32[]{:S(2)}) collective-permute-start(bf16[1792,256]{1,0:T(8,128)(2,1)S(1)} %get-tuple-element.72.rest_0_), channel_id=1, source_target_pairs={{0,96},{1,97},{2,98},{3,99},{4,100},{5,101},{6,102},{7,103},{8,104... | collective-permute-start | bytes 2752520 | tf_op jit(solution)/shard_map/ppermute | solution.py:30
  33.3 16.6 %collective-permute-start.15 = (bf16[512,512]{1,0:T(8,128)(2,1)S(1)}, bf16[512,512]{1,0:T(8,128)(2,1)S(1)}, u32[]{:S(2)}, u32[]{:S(2)}) collective-permute-start(bf16[512,512]{1,0:T(8,128)(2,1)S(1)} %get-tuple-element.56.p1), channel_id=1, source_target_pairs={{0,16},{1,17},{2,18},{3,19},{4,20},{5,21},{6,22},{7,23},{8,24},{9,... | collective-permute-start | bytes 1572872 | tf_op jit(solution)/shard_map/ppermute | solution.py:30
  39.3 10.6 %collective-permute-start.14 = (bf16[512,256]{1,0:T(8,128)(2,1)S(1)}, bf16[512,256]{1,0:T(8,128)(2,1)S(1)}, u32[]{:S(2)}, u32[]{:S(2)}) collective-permute-start(bf16[512,256]{1,0:T(8,128)(2,1)S(1)} %get-tuple-element.55.p23), channel_id=1, source_target_pairs={{0,16},{1,17},{2,18},{3,19},{4,20},{5,21},{6,22},{7,23},{8,24},{9,... | collective-permute-start | bytes 786440 | tf_op jit(solution)/shard_map/ppermute | solution.py:30
  53.8 18.1 %collective-permute-start.18 = (bf16[1536,128]{1,0:T(8,128)(2,1)S(1)}, bf16[1536,128]{1,0:T(8,128)(2,1)S(1)}, u32[]{:S(2)}, u32[]{:S(2)}) collective-permute-start(bf16[1536,128]{1,0:T(8,128)(2,1)S(1)} %get-tuple-element.57), channel_id=1, source_target_pairs={{12,0},{28,16},{44,32},{60,48},{76,64},{92,80},{108,96},{124,112}} | collective-permute-start | bytes 1179656 | tf_op jit(solution)/shard_map/ppermute | solution.py:30
  54.5 17.4 %collective-permute-start.19 = (bf16[1024,128]{1,0:T(8,128)(2,1)S(1)}, bf16[1024,128]{1,0:T(8,128)(2,1)S(1)}, u32[]{:S(2)}, u32[]{:S(2)}) collective-permute-start(bf16[1024,128]{1,0:T(8,128)(2,1)S(1)} %get-tuple-element.58), channel_id=1, source_target_pairs={{12,4},{28,20},{44,36},{60,52},{76,68},{92,84},{108,100},{124,116}} | collective-permute-start | bytes 786440 | tf_op jit(solution)/shard_map/ppermute | solution.py:30
  55.2 16.7 %collective-permute-start.20 = (bf16[512,128]{1,0:T(8,128)(2,1)S(1)}, bf16[512,128]{1,0:T(8,128)(2,1)S(1)}, u32[]{:S(2)}, u32[]{:S(2)}) collective-permute-start(bf16[512,128]{1,0:T(8,128)(2,1)S(1)} %get-tuple-element.59), channel_id=1, source_target_pairs={{12,8},{28,24},{44,40},{60,56},{76,72},{92,88},{108,104},{124,120}} | collective-permute-start | bytes 393224 | tf_op jit(solution)/shard_map/ppermute | solution.py:30
  59.0 44.4 %collective-permute-start.29 = (bf16[1792,256]{1,0:T(8,128)(2,1)S(1)}, bf16[1792,256]{1,0:T(8,128)(2,1)S(1)}, u32[]{:S(2)}, u32[]{:S(2)}) collective-permute-start(bf16[1792,256]{1,0:T(8,128)(2,1)S(1)} %collective-permute-done.17.rest_9_.rest_1_), channel_id=1, source_target_pairs={{0,96},{1,97},{2,98},{3,99},{4,100},{5,101},{6,102},{7,103},{8,104... | collective-permute-start | bytes 2752520 | tf_op jit(solution)/shard_map/ppermute | solution.py:30
  69.5 37.3 %collective-permute-start.27 = (bf16[1792,256]{1,0:T(8,128)(2,1)S(1)}, bf16[1792,256]{1,0:T(8,128)(2,1)S(1)}, u32[]{:S(2)}, u32[]{:S(2)}) collective-permute-start(bf16[1792,256]{1,0:T(8,128)(2,1)S(1)} %collective-permute-done.16.rest_8_.rest_3_), channel_id=1, source_target_pairs={{0,32},{1,33},{2,34},{3,35},{4,36},{5,37},{6,38},{7,39},{8,40},{9,... | collective-permute-start | bytes 2752520 | tf_op jit(solution)/shard_map/ppermute | solution.py:30
  72.6 2.7 %collective-permute-start.23 = (bf16[2048,128]{1,0:T(8,128)(2,1)S(1)}, bf16[2048,128]{1,0:T(8,128)(2,1)S(1)}, u32[]{:S(2)}, u32[]{:S(2)}) collective-permute-start(bf16[2048,128]{1,0:T(8,128)(2,1)S(1)} %shard_map.45.late), channel_id=1, source_target_pairs={{0,1},{4,5},{8,9},{12,13},{16,17},{20,21},{24,25},{28,29},{32,33},... | collective-permute-start | bytes 1572872 | tf_op jit(solution)/shard_map/ppermute | solution.py:30
  73.3 25.6 %collective-permute-start.24 = (bf16[2048,128]{1,0:T(8,128)(2,1)S(1)}, bf16[2048,128]{1,0:T(8,128)(2,1)S(1)}, u32[]{:S(2)}, u32[]{:S(2)}) collective-permute-start(bf16[2048,128]{1,0:T(8,128)(2,1)S(1)} %shard_map.45.late), channel_id=1, source_target_pairs={{0,2},{4,6},{8,10},{12,14},{16,18},{20,22},{24,26},{28,30},{32,34}... | collective-permute-start | bytes 1572872 | tf_op jit(solution)/shard_map/ppermute | solution.py:30
  74.6 24.3 %collective-permute-start.25 = (bf16[2048,128]{1,0:T(8,128)(2,1)S(1)}, bf16[2048,128]{1,0:T(8,128)(2,1)S(1)}, u32[]{:S(2)}, u32[]{:S(2)}) collective-permute-start(bf16[2048,128]{1,0:T(8,128)(2,1)S(1)} %shard_map.45.late), channel_id=1, source_target_pairs={{0,3},{4,7},{8,11},{12,15},{16,19},{20,23},{24,27},{28,31},{32,35}... | collective-permute-start | bytes 1572872 | tf_op jit(solution)/shard_map/ppermute | solution.py:30
  100.0 4.6 %collective-permute-start.26 = (bf16[1024,128]{1,0:T(8,128)(2,1)S(1)}, bf16[1024,128]{1,0:T(8,128)(2,1)S(1)}, u32[]{:S(2)}, u32[]{:S(2)}) collective-permute-start(bf16[1024,128]{1,0:T(8,128)(2,1)S(1)} %get-tuple-element.66), channel_id=1, source_target_pairs={{0,16},{1,17},{2,18},{3,19},{4,20},{5,21},{6,22},{7,23},{8,24},{9,... | collective-permute-start | bytes 786440 | tf_op jit(solution)/shard_map/ppermute | solution.py:30
  106.3 6.1 %collective-permute-start.30 = (bf16[1792,128]{1,0:T(8,128)(2,1)S(1)}, bf16[1792,128]{1,0:T(8,128)(2,1)S(1)}, u32[]{:S(2)}, u32[]{:S(2)}) collective-permute-start(bf16[1792,128]{1,0:T(8,128)(2,1)S(1)} %get-tuple-element.70), channel_id=1, source_target_pairs={{0,16},{1,17},{2,18},{3,19},{4,20},{5,21},{6,22},{7,23},{8,24},{9,... | collective-permute-start | bytes 1376264 | tf_op jit(solution)/shard_map/ppermute | solution.py:30
  108.6 3.8 %collective-permute-start.28 = (bf16[1792,128]{1,0:T(8,128)(2,1)S(1)}, bf16[1792,128]{1,0:T(8,128)(2,1)S(1)}, u32[]{:S(2)}, u32[]{:S(2)}) collective-permute-start(bf16[1792,128]{1,0:T(8,128)(2,1)S(1)} %get-tuple-element.68), channel_id=1, source_target_pairs={{0,16},{1,17},{2,18},{3,19},{4,20},{5,21},{6,22},{7,23},{8,24},{9,... | collective-permute-start | bytes 1376264 | tf_op jit(solution)/shard_map/ppermute | solution.py:30

commit v8 on v7

--- a/solution.py
+++ b/solution.py
@@ -81,17 +81,14 @@
     return jnp.where(i <= j, d, 0.0)
 
 
-def start_kernel(ids, b_ref, d_ref, after_ref, y_ref, yb_ref, lh_ref, ll_ref):
-    lh_ref[...], ll_ref[...] = split(lower_mask(d_ref[0]))
+def start_kernel(ids, b_ref, d_ref, after_ref, y_ref, yb_ref, lh_ref, ll_ref, *uppers):
+    lh_ref[...], ll_ref[...] = split(lower_mask(d_ref[ids[2]]))
     w = b_ref[...]
     y = w + apply(lh_ref, ll_ref, w)
     y_ref[...] = y
     yb_ref[...] = y.astype(BF16)
-
-
-def upper_kernel(ids, d_ref, *out):
     for n, j in enumerate((ids[2], 1, 2)):
-        out[2 * n][...], out[2 * n + 1][...] = split(upper_mask(d_ref[j]))
+        uppers[2 * n][...], uppers[2 * n + 1][...] = split(upper_mask(d_ref[j]))
 
 
 def combine_kernel(ids, own_ref, r1, r2, r3, v_ref):
@@ -107,19 +104,23 @@
     return jnp.where(ids[2] == j, own_ref[...], total)
 
 
+def window_blocks(blocks, d):
+    return blocks[d], (blocks[4] if d == 0 else blocks[5].at[(d - 1) * NB : d * NB, :])
+
+
 def block_product(ids, blocks, j, v_ref, acc_ref):
     x, h = ids[0], ids[1]
     for d in range(NX):
         @pl.when(lax.rem(x + d, NX) == j)
         def _():
-            same, other = blocks[2 * d], blocks[2 * d + 1]
+            same, other = window_blocks(blocks, d)
             acc_ref[...] -= dot(same[...], v_ref[pl.ds(pl.multiple_of(h * HB, HB), HB), :]) + dot(
                 other[...], v_ref[pl.ds(pl.multiple_of((1 - h) * HB, HB), HB), :]
             )
 
 
 def forward_kernel(j, count, ids, w_ref, own_ref, prior_ref, lh_ref, ll_ref, *rest):
-    blocks, received, (v_ref, w_out, y_ref, yb_ref) = rest[:8], rest[8 : 8 + count], rest[-4:]
+    blocks, received, (v_ref, w_out, y_ref, yb_ref) = rest[:6], rest[6 : 6 + count], rest[-4:]
     v_ref[...] = own_or_received(ids, j, own_ref, received)
     w_out[...] = w_ref[...]
     block_product(ids, blocks, j, v_ref, w_out)
@@ -133,7 +134,9 @@
         yb_ref[NB:, :] = y.astype(BF16)
 
 
-def pick_kernel(ids, b0, b1, b2, b3, p23_ref, p1_ref):
+def pick_kernel(ids, b0, b1, b2, b3, p23_ref, p1_ref, all_ref):
+    for d, block in enumerate((b1, b2, b3)):
+        all_ref[d * NB : (d + 1) * NB, :] = block[...]
     for d, block in enumerate((b0, b1, b2, b3)):
         @pl.when(lax.rem(ids[0] + d, NX) == 2)
         def _():
@@ -153,7 +156,7 @@
 def turn_kernel(
     ids, w_ref, y12_ref, y12_in, prior_ref, lh, ll, u3h, u3l, u1h, u1l, u2h, u2l, p23, p23_other, p1, p1_other, *rest
 ):
-    blocks, (y1_ref, y2_ref, y_ref, yb_ref, x_ref, x23_ref, x3_ref, acc) = rest[:8], rest[-8:]
+    blocks, (y1_ref, y2_ref, y_ref, yb_ref, x_ref, x23_ref, x3_ref, acc) = rest[:6], rest[-8:]
     h = ids[1]
     last = ids[2] == 3
     y1_ref[...] = jnp.where(last, y12_in[0:NB, :], y12_ref[0:NB, :])
@@ -184,6 +187,11 @@
     x_ref[0:NB, :] = apply(u1h, u1l, t).astype(BF16)
 
 
+def hold_kernel(ids, top, bottom, after_ref, top_out, bottom_out):
+    top_out[...] = top[...]
+    bottom_out[...] = bottom[...]
+
+
 def late_kernel(ids, to0, to1, to2, y0, y1, y2, y3, *rest):
     late_ref, z = rest[-1], ids[2]
     late_ref[0:NB, :] = y0[...]
@@ -202,7 +210,7 @@
 
 
 def window_kernel(ids, b_ref, v_ref, own_ref, uh_ref, ul_ref, *rest):
-    blocks, (out_ref, acc) = rest[:8], rest[8:]
+    blocks, (out_ref, acc) = rest[:6], rest[6:]
     x, h, z, owner = ids[0], ids[1], ids[2], ids[3] == 0
     acc[...] = jnp.where(owner, own_ref[...], b_ref[...])
     for d in range(NX):
@@ -212,7 +220,8 @@
 
             @pl.when(jnp.logical_or(jnp.logical_not(owner), j > z))
             def _():
-                acc[...] -= dot(blocks[2 * d + s][...], v_ref[pl.ds(pl.multiple_of(j * NB + part * HB, HB), HB), :])
+                block = window_blocks(blocks, d)[s]
+                acc[...] -= dot(block[...], v_ref[pl.ds(pl.multiple_of(j * NB + part * HB, HB), HB), :])
 
     @pl.when(owner)
     def _():
@@ -240,13 +249,14 @@
 
 
 def add_kernel(ids, out_in, b_ref, own_t, part_t, own_b, part_b, out_ref):
-    i, n = pl.program_id(0), b_ref.shape[0]
+    i, n = pl.program_id(0), out_ref.shape[0]
     half = own_t.shape[0] // n
     for top, own, part in ((True, own_t, part_t), (False, own_b, part_b)):
         @pl.when((i < half) == top)
         def _():
             rows = pl.ds(pl.multiple_of((i if top else i - half) * n, n), n)
-            out_ref[...] = b_ref[...] - own[rows, :] - part[rows, :].astype(F32)
+            base = b_ref[pl.ds(pl.multiple_of(NB + i * n, 128), n), :]
+            out_ref[...] = base - own[rows, :] - part[rows, :].astype(F32)
 
 
 def whole(shape):
@@ -291,18 +301,19 @@
     half = (rows - NB) // 2
     own_t, own_b = factors[NB : NB + half], factors[NB + half :]
     before_t, after_b = send(own_t, x_plus), send(own_b, x_minus)
-    before_b, after_t = send(own_b, x_plus), send(own_t, x_minus)
     far_t, far_b = send(before_t, x_plus), send(after_b, x_minus)
-    window = [b for s in same for b in (s, send(s, other_core))]
-    wspecs = [whole((NB, HB))] * 8
-
-    y_z0, yb0, lh, ll = call(
-        start_kernel, ids, (in_hbm(rhs), in_hbm(diag_inv), own), [first, pl.BlockSpec((1, NB, NB), lambda i, ids: (ids[2], 0, 0)), ANY],
-        (vec, bf(NB), mat, mat), limit=16,
+    own_other = send(own, other_core)
+    wspecs = [whole((NB, HB))] * 6
+
+    y_z0, yb0, lh, ll, *uppers = call(
+        start_kernel, ids, (in_hbm(rhs), in_hbm(diag_inv), own), [first, pl.BlockSpec((4, NB, NB), lambda i, ids: (0, 0, 0)), ANY],
+        (vec, bf(NB), mat, mat) + (mat,) * 6, limit=16,
     )
     hops = [send(yb0, z_move(0, t)) for t in (1, 2, 3)]
-    uppers = call(upper_kernel, ids, (in_hbm(diag_inv),), [pl.BlockSpec((4, NB, NB), lambda i, ids: (0, 0, 0))], (mat,) * 6, limit=16)
-    p23, p1 = call(pick_kernel, ids, same, [whole((NB, HB))] * 4, (bf(NB, HB), bf(NB, 2 * HB)))
+    p23, p1, received = call(
+        pick_kernel, ids, same, [whole((NB, HB))] * 4, (bf(NB, HB), bf(NB, 2 * HB), bf(3 * NB, HB))
+    )
+    window = [*same, own_other, send(received, other_core)]
     p23 = send(p23, z_move(2, 3))
     p1 = send(p1, z_move(1, 3))
 
@@ -313,10 +324,12 @@
         )
 
     y0 = call(combine_kernel, ids, (yb0, *hops), [vspec] * 4, bf(NB))
-    _, w0, y_own, yb1 = forward(0, in_hbm(rhs), first, y0, y_z0, (), uppers)
+    _, w0, y_own, yb1 = forward(0, in_hbm(rhs), first, y0, y_z0, ())
     hops = [send(yb1, z_move(1, 2))]
     _, _, y_own, y12 = forward(1, w0, vspec, yb1, y_own, hops)
     y12_in = send(y12, z_move(2, 3))
+    top, bottom = call(hold_kernel, ids, (own_t, own_b, y12_in), [whole((half, HB))] * 2 + [ANY], (bf(half, HB),) * 2)
+    before_b, after_t = send(bottom, x_plus), send(top, x_minus)
     p23, p1 = call(relay_kernel, ids, (p23, p1, y12), [whole((NB, HB)), mspec, ANY], (bf(NB, HB), bf(NB, 2 * HB)))
     p23_other, p1_other = send(p23, other_core), send(p1, other_core)
     y1, y2, y_own, yb3, xs, x23s, x3s = call(
@@ -353,8 +366,8 @@
     tile = half // 2
     at = pl.BlockSpec((pl.Element(tile), pl.Element(cols)), lambda i, ids: (pl.multiple_of(NB + i * tile, 128), 0))
     return call(
-        add_kernel, ids, (done, in_hbm(rhs), sums[0], parts[0], sums[1], parts[1]),
-        [ANY, at] + [vspec] * 4, out, grid=(4,), out_spec=at, aliases={1: 0},
+        add_kernel, ids, (done, rhs, sums[0], parts[0], sums[1], parts[1]),
+        [ANY] + [vspec] * 5, out, grid=(4,), out_spec=at, aliases={1: 0},
     )
 
 

time: 117 us -> 125 us (1.068)
  the two profiles are of different devices: /device:TPU:53 before, /device:TPU:1 now
where the time goes in v8:
time: 125 us; the launch traced here: 124 us
  waiting for transfers between devices  55.7 us (45%)
  starting transfers between devices  41.2 us (33%)
  Pallas kernels  25.9 us (21%)
    ppermute x29, waiting for transfers between devices, send(): return lax.ppermute(value, ('row', 'col'), pairs(move))  55.7 us
    ppermute x29, starting transfers between devices, send(): return lax.ppermute(value, ('row', 'col'), pairs(move))  41.2 us
    pallas_call x14, Pallas kernels, call(): pl.pallas_call(kernel, grid_spec=pltpu.PrefetchScalarGridSpec(num_scalar_...  25.9 us
  transfers between devices with their start and end apart: 29, of which 7 were waited for; matrix products, arithmetic and copies ran while one was open for 0% of the time, Pallas kernels for 19%

profile of v8, /device:TPU:1, one launch (start us, length us, event | category | flops | bytes accessed | tf_op | source)
XLA Modules:
  0.0 124.3 jit_solution(11662395451419648629)
XLA Ops:
  0.0 1.0 slice.9.after_ref.b0.rest_0_
  1.0 3.4 %collective-permute-start.3 = (bf16[512,256]{1,0:T(8,128)(2,1)S(1)}, bf16[512,256]{1,0:T(8,128)(2,1)S(1)}, u32[]{:S(2)}, u32[]{:S(2)}) collective-permute-start(bf16[512,256]{1,0:T(8,128)(2,1)S(1)} %slice.9.after_ref.b0.rest_0_), channel_id=1, source_target_pairs={{0,96},{1,97},{2,98},{3,99},{4,100},{5,101},{6,102},{7,103},{8,104... | collective-permute-start | bytes 786440 | tf_op jit(solution)/shard_map/ppermute | solution.py:30
  4.3 0.5 collective-permute-start.4
  4.9 0.6 collective-permute-start.5
  5.5 0.1 pad_add_fusion.ids
  5.6 3.7 %shard_map.37 = (f32[512,128]{1,0:T(8,128)S(1)}, bf16[512,128]{1,0:T(8,128)(2,1)S(1)}, bf16[512,512]{1,0:T(8,128)(2,1)S(1)}, bf16[512,512]{1,0:T(8,128)(2,1)S(1)...) custom-call(s32[4]{0:T(128)S(1)} %pad_add_fusion.ids, ...), custom_call_target="tpu_custom_call" | custom-call | flops 1 | bytes 1 | tf_op jit(solution)/shard_map/pallas_call | solution.py:275
  9.2 3.5 %collective-permute-start = (bf16[512,128]{1,0:T(8,128)(2,1)S(1)}, bf16[512,128]{1,0:T(8,128)(2,1)S(1)}, u32[]{:S(2)}, u32[]{:S(2)}) collective-permute-start(bf16[512,128]{1,0:T(8,128)(2,1)S(1)} %get-tuple-element.41.own_ref), channel_id=1, source_target_pairs={{0,4},{16,20},{32,36},{48,52},{64,68},{80,84},{96,100},{112,116}} | collective-permute-start | bytes 393224 | tf_op jit(solution)/shard_map/ppermute | solution.py:30
  12.8 2.6 %collective-permute-start.1 = (bf16[512,128]{1,0:T(8,128)(2,1)S(1)}, bf16[512,128]{1,0:T(8,128)(2,1)S(1)}, u32[]{:S(2)}, u32[]{:S(2)}) collective-permute-start(bf16[512,128]{1,0:T(8,128)(2,1)S(1)} %get-tuple-element.41.own_ref), channel_id=1, source_target_pairs={{0,8},{16,24},{32,40},{48,56},{64,72},{80,88},{96,104},{112,120}} | collective-permute-start | bytes 393224 | tf_op jit(solution)/shard_map/ppermute | solution.py:30
  15.4 1.9 %collective-permute-start.6 = (bf16[512,256]{1,0:T(8,128)(2,1)S(1)}, bf16[512,256]{1,0:T(8,128)(2,1)S(1)}, u32[]{:S(2)}, u32[]{:S(2)}) collective-permute-start(bf16[512,256]{1,0:T(8,128)(2,1)S(1)} %slice.9.after_ref.b0.rest_0_), channel_id=1, source_target_pairs={{0,16},{1,17},{2,18},{3,19},{4,20},{5,21},{6,22},{7,23},{8,24},{9,... | collective-permute-start | bytes 786440 | tf_op jit(solution)/shard_map/ppermute | solution.py:30
  17.3 0.0 collective-permute-done.4.b2.rest_2_
  17.3 2.4 %collective-permute-done.5.b3.rest_3_ = bf16[512,256]{1,0:T(8,128)(2,1)S(1)} collective-permute-done((bf16[512,256]{1,0:T(8,128)(2,1)S(1)}, bf16[512,256]{1,0:T(8,128)(2,1)S(1)}, u32[]{:S(2)}, u32[]{:S(2)}) %collective-permute-start.5) | collective-permute-done | bytes 262176 | tf_op jit(solution)/shard_map/ppermute | solution.py:30
  19.7 0.7 shard_map.39
  20.4 0.6 collective-permute-start.7
  21.0 0.1 fusion
  21.1 0.1 collective-permute-start.14
  21.2 5.7 %collective-permute-start.2 = (bf16[512,128]{1,0:T(8,128)(2,1)S(1)}, bf16[512,128]{1,0:T(8,128)(2,1)S(1)}, u32[]{:S(2)}, u32[]{:S(2)}) collective-permute-start(bf16[512,128]{1,0:T(8,128)(2,1)S(1)} %get-tuple-element.41.own_ref), channel_id=1, source_target_pairs={{0,12},{16,28},{32,44},{48,60},{64,76},{80,92},{96,108},{112,124}} | collective-permute-start | bytes 393224 | tf_op jit(solution)/shard_map/ppermute | solution.py:30
  26.9 0.0 collective-permute-done.1.r2
  26.9 0.7 collective-permute-start.11
  27.6 13.3 %collective-permute-done.2.r3 = bf16[512,128]{1,0:T(8,128)(2,1)S(1)} collective-permute-done((bf16[512,128]{1,0:T(8,128)(2,1)S(1)}, bf16[512,128]{1,0:T(8,128)(2,1)S(1)}, u32[]{:S(2)}, u32[]{:S(2)}) %collective-permute-start.2) | collective-permute-done | bytes 131104 | tf_op jit(solution)/shard_map/ppermute | solution.py:30
  40.9 2.3 %collective-permute-start.15 = (bf16[1792,256]{1,0:T(8,128)(2,1)S(1)}, bf16[1792,256]{1,0:T(8,128)(2,1)S(1)}, u32[]{:S(2)}, u32[]{:S(2)}) collective-permute-start(bf16[1792,256]{1,0:T(8,128)(2,1)S(1)} %get-tuple-element.77.bottom.rest_0_), channel_id=1, source_target_pairs={{0,96},{1,97},{2,98},{3,99},{4,100},{5,101},{6,102},{7,103},{8,104... | collective-permute-start | bytes 2752520 | tf_op jit(solution)/shard_map/ppermute | solution.py:30
  43.2 0.6 shard_map.38.own_ref.y0
  43.8 0.0 collective-permute-done.7.rest_5_
  43.8 2.7 %shard_map.40 = (bf16[512,128]{1,0:T(8,128)(2,1)}, f32[512,128]{1,0:T(8,128)S(1)}, f32[512,128]{1,0:T(8,128)S(1)}, bf16[512,128]{1,0:T(8,128)(2,1)S(1)}) custom-call(s32[4]{0:T(128)S(1)} %pad_add_fusion.ids, f32[4096,128]{1,0:T(8,128)} %b_ref.5, bf16[512,128]{1,0:T(8,128)(2,1)S(1)} %shard_map.38.own_ref.y0, f32[512,128]{1,0:T(8,128)S(1)} %get-tuple-element.42.prior_ref, ...), custom_call_target="tpu_custom_call" | custom-call | flops 1 | bytes 1 | tf_op jit(solution)/shard_map/pallas_call | solution.py:275
  46.6 0.7 collective-permute-start.8
  47.2 0.7 collective-permute-start.10
  47.9 1.9 %shard_map.41 = (bf16[512,128]{1,0:T(8,128)(2,1)}, f32[512,128]{1,0:T(8,128)}, f32[512,128]{1,0:T(8,128)S(1)}, bf16[1024,128]{1,0:T(8,128)(2,1)S(1)}) custom-call(s32[4]{0:T(128)S(1)} %pad_add_fusion.ids, f32[512,128]{1,0:T(8,128)S(1)} %get-tuple-element.46.w_ref, bf16[512,128]{1,0:T(8,128)(2,1)S(1)} %get-tuple-element.47.own_ref, ...), custom_call_target="tpu_custom_call" | custom-call | flops 1 | bytes 1 | tf_op jit(solution)/shard_map/pallas_call | solution.py:275
  49.8 0.7 collective-permute-start.9
  50.5 0.0 collective-permute-done.10.p23_ref
  50.5 0.0 collective-permute-done.11.p1_ref
  50.5 0.6 shard_map.42
  51.1 1.7 %collective-permute-start.13 = (bf16[512,512]{1,0:T(8,128)(2,1)S(1)}, bf16[512,512]{1,0:T(8,128)(2,1)S(1)}, u32[]{:S(2)}, u32[]{:S(2)}) collective-permute-start(bf16[512,512]{1,0:T(8,128)(2,1)S(1)} %get-tuple-element.60.p1), channel_id=1, source_target_pairs={{0,16},{1,17},{2,18},{3,19},{4,20},{5,21},{6,22},{7,23},{8,24},{9,... | collective-permute-start | bytes 1572872 | tf_op jit(solution)/shard_map/ppermute | solution.py:30
  52.8 0.0 collective-permute-done.9.y12_in.after_ref
  52.8 0.7 shard_map.44
  53.4 0.1 collective-permute-start.19
  53.5 2.7 %collective-permute-start.20 = (bf16[1792,256]{1,0:T(8,128)(2,1)S(1)}, bf16[1792,256]{1,0:T(8,128)(2,1)S(1)}, u32[]{:S(2)}, u32[]{:S(2)}) collective-permute-start(bf16[1792,256]{1,0:T(8,128)(2,1)S(1)} %get-tuple-element.68), channel_id=1, source_target_pairs={{0,96},{1,97},{2,98},{3,99},{4,100},{5,101},{6,102},{7,103},{8,104... | collective-permute-start | bytes 2752520 | tf_op jit(solution)/shard_map/ppermute | solution.py:30
  56.2 0.0 collective-permute-done.14.rest_6_.rest_3_
  56.2 0.6 collective-permute-start.12
  56.8 5.0 %collective-permute-done.15.rest_7_.rest_1_ = bf16[1792,256]{1,0:T(8,128)(2,1)S(1)} collective-permute-done((bf16[1792,256]{1,0:T(8,128)(2,1)S(1)}, bf16[1792,256]{1,0:T(8,128)(2,1)S(1)}, u32[]{:S(2)}, u32[]{:S(2)}) %collective-permute-start.15) | collective-permute-done | bytes 917536 | tf_op jit(solution)/shard_map/ppermute | solution.py:30
  61.7 0.0 collective-permute-done.12.p23_other
  61.7 0.0 collective-permute-done.13.p1_other
  61.7 3.8 %shard_map.43 = (bf16[512,128]{1,0:T(8,128)(2,1)S(1)}, bf16[512,128]{1,0:T(8,128)(2,1)S(1)}, f32[512,128]{1,0:T(8,128)S(1)}, bf16[512,128]{1,0:T(8,128)(2,1)S(1)...) custom-call(s32[4]{0:T(128)S(1)} %pad_add_fusion.ids, ...), custom_call_target="tpu_custom_call" | custom-call | flops 1 | bytes 1 | tf_op jit(solution)/shard_map/pallas_call | solution.py:275
  65.5 1.3 %collective-permute-start.16 = (bf16[1536,128]{1,0:T(8,128)(2,1)S(1)}, bf16[1536,128]{1,0:T(8,128)(2,1)S(1)}, u32[]{:S(2)}, u32[]{:S(2)}) collective-permute-start(bf16[1536,128]{1,0:T(8,128)(2,1)S(1)} %get-tuple-element.61), channel_id=1, source_target_pairs={{12,0},{28,16},{44,32},{60,48},{76,64},{92,80},{108,96},{124,112}} | collective-permute-start | bytes 1179656 | tf_op jit(solution)/shard_map/ppermute | solution.py:30
  66.8 0.9 collective-permute-start.17
  67.7 0.7 collective-permute-start.18
  68.4 0.0 collective-permute-done.18.to2
  68.4 3.3 %collective-permute-start.27 = (bf16[1792,256]{1,0:T(8,128)(2,1)S(1)}, bf16[1792,256]{1,0:T(8,128)(2,1)S(1)}, u32[]{:S(2)}, u32[]{:S(2)}) collective-permute-start(bf16[1792,256]{1,0:T(8,128)(2,1)S(1)} %collective-permute-done.15.rest_7_.rest_1_), channel_id=1, source_target_pairs={{0,96},{1,97},{2,98},{3,99},{4,100},{5,101},{6,102},{7,103},{8,104... | collective-permute-start | bytes 2752520 | tf_op jit(solution)/shard_map/ppermute | solution.py:30
  71.6 0.0 collective-permute-done.17.to1
  71.6 0.0 collective-permute-start.25
  71.7 14.7 %collective-permute-done.16.to0 = bf16[1536,128]{1,0:T(8,128)(2,1)S(1)} collective-permute-done((bf16[1536,128]{1,0:T(8,128)(2,1)S(1)}, bf16[1536,128]{1,0:T(8,128)(2,1)S(1)}, u32[]{:S(2)}, u32[]{:S(2)}) %collective-permute-start.16) | collective-permute-done | bytes 393248 | tf_op jit(solution)/shard_map/ppermute | solution.py:30
  86.4 0.7 shard_map.45.late
  87.1 1.3 %collective-permute-start.21 = (bf16[2048,128]{1,0:T(8,128)(2,1)S(1)}, bf16[2048,128]{1,0:T(8,128)(2,1)S(1)}, u32[]{:S(2)}, u32[]{:S(2)}) collective-permute-start(bf16[2048,128]{1,0:T(8,128)(2,1)S(1)} %shard_map.45.late), channel_id=1, source_target_pairs={{0,1},{4,5},{8,9},{12,13},{16,17},{20,21},{24,25},{28,29},{32,33},... | collective-permute-start | bytes 1572872 | tf_op jit(solution)/shard_map/ppermute | solution.py:30
  88.4 1.3 %collective-permute-start.22 = (bf16[2048,128]{1,0:T(8,128)(2,1)S(1)}, bf16[2048,128]{1,0:T(8,128)(2,1)S(1)}, u32[]{:S(2)}, u32[]{:S(2)}) collective-permute-start(bf16[2048,128]{1,0:T(8,128)(2,1)S(1)} %shard_map.45.late), channel_id=1, source_target_pairs={{0,2},{4,6},{8,10},{12,14},{16,18},{20,22},{24,26},{28,30},{32,34}... | collective-permute-start | bytes 1572872 | tf_op jit(solution)/shard_map/ppermute | solution.py:30
  89.7 1.3 %collective-permute-start.23 = (bf16[2048,128]{1,0:T(8,128)(2,1)S(1)}, bf16[2048,128]{1,0:T(8,128)(2,1)S(1)}, u32[]{:S(2)}, u32[]{:S(2)}) collective-permute-start(bf16[2048,128]{1,0:T(8,128)(2,1)S(1)} %shard_map.45.late), channel_id=1, source_target_pairs={{0,3},{4,7},{8,11},{12,15},{16,19},{20,23},{24,27},{28,31},{32,35}... | collective-permute-start | bytes 1572872 | tf_op jit(solution)/shard_map/ppermute | solution.py:30
  91.1 8.0 %collective-permute-done.21.s1 = bf16[2048,128]{1,0:T(8,128)(2,1)S(1)} collective-permute-done((bf16[2048,128]{1,0:T(8,128)(2,1)S(1)}, bf16[2048,128]{1,0:T(8,128)(2,1)S(1)}, u32[]{:S(2)}, u32[]{:S(2)}) %collective-permute-start.21) | collective-permute-done | bytes 524320 | tf_op jit(solution)/shard_map/ppermute | solution.py:30
  99.0 11.2 %collective-permute-done.22.s2 = bf16[2048,128]{1,0:T(8,128)(2,1)S(1)} collective-permute-done((bf16[2048,128]{1,0:T(8,128)(2,1)S(1)}, bf16[2048,128]{1,0:T(8,128)(2,1)S(1)}, u32[]{:S(2)}, u32[]{:S(2)}) %collective-permute-start.22) | collective-permute-done | bytes 524320 | tf_op jit(solution)/shard_map/ppermute | solution.py:30
  110.3 1.0 shard_map.46
  111.3 1.5 %collective-permute-start.24 = (bf16[1024,128]{1,0:T(8,128)(2,1)S(1)}, bf16[1024,128]{1,0:T(8,128)(2,1)S(1)}, u32[]{:S(2)}, u32[]{:S(2)}) collective-permute-start(bf16[1024,128]{1,0:T(8,128)(2,1)S(1)} %get-tuple-element.72), channel_id=1, source_target_pairs={{0,16},{1,17},{2,18},{3,19},{4,20},{5,21},{6,22},{7,23},{8,24},{9,... | collective-permute-start | bytes 786440 | tf_op jit(solution)/shard_map/ppermute | solution.py:30
  112.9 1.2 collective-permute-done.24.other_ref
  114.0 1.7 %shard_map.49 = (f32[1792,128]{1,0:T(8,128)S(1)}, bf16[1792,128]{1,0:T(8,128)(2,1)S(1)}) custom-call(s32[4]{0:T(128)S(1)} %pad_add_fusion.ids, bf16[1024,128]{1,0:T(8,128)(2,1)S(1)} %get-tuple-element.71.mine_ref, bf16[1024,128]{1,0:T(8,128)(2,1)S(1)} %collective-permute-done.24.other_ref, bf16[1792,256]{1,0:T(8,128)(2,1)S(1)} %get-tuple-element.77.bottom.rest_0_, ...), custom_call_target="tpu_custom_call" | custom-call | flops 1 | bytes 1 | tf_op jit(solution)/shard_map/pallas_call | solution.py:275
  115.8 0.5 collective-permute-start.28
  116.2 1.7 %shard_map.48 = (f32[1792,128]{1,0:T(8,128)S(1)}, bf16[1792,128]{1,0:T(8,128)(2,1)S(1)}) custom-call(s32[4]{0:T(128)S(1)} %pad_add_fusion.ids, bf16[1024,128]{1,0:T(8,128)(2,1)S(1)} %get-tuple-element.71.mine_ref, bf16[1024,128]{1,0:T(8,128)(2,1)S(1)} %collective-permute-done.24.other_ref, bf16[1792,256]{1,0:T(8,128)(2,1)S(1)} %get-tuple-element.78.top.rest_0_, ...), custom_call_target="tpu_custom_call" | custom-call | flops 1 | bytes 1 | tf_op jit(solution)/shard_map/pallas_call | solution.py:275
  118.0 0.2 collective-permute-start.26
  118.2 3.7 %shard_map.47.out_in = f32[4096,128]{1,0:T(8,128)} custom-call(s32[4]{0:T(128)S(1)} %pad_add_fusion.ids, f32[4096,128]{1,0:T(8,128)} %b_ref.5, bf16[2048,128]{1,0:T(8,128)(2,1)S(1)} %get-tuple-element.69.v_ref, f32[512,128]{1,0:T(8,128)S(1)} %get-tuple-element.70.own_ref, bf16[512,512]{1,0:T(8,128)(2,1)S(1)} %get-tuple-element.51.u3h.uh_ref, ...), custom_call_target="tpu_custom_call" | custom-call | flops 1 | bytes 1 | tf_op jit(solution)/shard_map/pallas_call | solution.py:275
  121.9 2.4 %shard_map.50 = f32[4096,128]{1,0:T(8,128)} custom-call(s32[4]{0:T(128)S(1)} %pad_add_fusion.ids, f32[4096,128]{1,0:T(8,128)} %shard_map.47.out_in, f32[4096,128]{1,0:T(8,128)S(1)} %copy-done, f32[1792,128]{1,0:T(8,128)S(1)} %get-tuple-element.73.own_t, bf16[1792,128]{1,0:T(8,128)(2,1)S(1)} %collective-permute-done.26.part_t, ...), custom_call_target="tpu_custom_call", output_to_operand_aliasing={{}: (1, {})} | custom-call | flops 1 | bytes 1 | tf_op jit(solution)/shard_map/pallas_call | solution.py:275
  (15 shorter events, 0.0 us)
Async XLA Ops:
  1.0 14.5 %collective-permute-start.3 = (bf16[512,256]{1,0:T(8,128)(2,1)S(1)}, bf16[512,256]{1,0:T(8,128)(2,1)S(1)}, u32[]{:S(2)}, u32[]{:S(2)}) collective-permute-start(bf16[512,256]{1,0:T(8,128)(2,1)S(1)} %slice.9.after_ref.b0.rest_0_), channel_id=1, source_target_pairs={{0,96},{1,97},{2,98},{3,99},{4,100},{5,101},{6,102},{7,103},{8,104... | collective-permute-start | bytes 786440 | tf_op jit(solution)/shard_map/ppermute | solution.py:30
  4.3 13.0 %collective-permute-start.4 = (bf16[512,256]{1,0:T(8,128)(2,1)S(1)}, bf16[512,256]{1,0:T(8,128)(2,1)S(1)}, u32[]{:S(2)}, u32[]{:S(2)}) collective-permute-start(bf16[512,256]{1,0:T(8,128)(2,1)S(1)} %slice.9.after_ref.b0.rest_0_), channel_id=1, source_target_pairs={{0,64},{1,65},{2,66},{3,67},{4,68},{5,69},{6,70},{7,71},{8,72},{9,... | collective-permute-start | bytes 786440 | tf_op jit(solution)/shard_map/ppermute | solution.py:30
  4.9 14.8 %collective-permute-start.5 = (bf16[512,256]{1,0:T(8,128)(2,1)S(1)}, bf16[512,256]{1,0:T(8,128)(2,1)S(1)}, u32[]{:S(2)}, u32[]{:S(2)}) collective-permute-start(bf16[512,256]{1,0:T(8,128)(2,1)S(1)} %slice.9.after_ref.b0.rest_0_), channel_id=1, source_target_pairs={{0,32},{1,33},{2,34},{3,35},{4,36},{5,37},{6,38},{7,39},{8,40},{9,... | collective-permute-start | bytes 786440 | tf_op jit(solution)/shard_map/ppermute | solution.py:30
  5.6 15.4 %copy-start.1 = (bf16[4096,256]{1,0:T(8,128)(2,1)S(1)}, bf16[4096,256]{1,0:T(8,128)(2,1)}, u32[]{:S(2)}) copy-start(bf16[4096,256]{1,0:T(8,128)(2,1)} %param.4) | copy-start | bytes 6291460
  9.2 12.0 %collective-permute-start = (bf16[512,128]{1,0:T(8,128)(2,1)S(1)}, bf16[512,128]{1,0:T(8,128)(2,1)S(1)}, u32[]{:S(2)}, u32[]{:S(2)}) collective-permute-start(bf16[512,128]{1,0:T(8,128)(2,1)S(1)} %get-tuple-element.41.own_ref), channel_id=1, source_target_pairs={{0,4},{16,20},{32,36},{48,52},{64,68},{80,84},{96,100},{112,116}} | collective-permute-start | bytes 393224 | tf_op jit(solution)/shard_map/ppermute | solution.py:30
  12.8 14.1 %collective-permute-start.1 = (bf16[512,128]{1,0:T(8,128)(2,1)S(1)}, bf16[512,128]{1,0:T(8,128)(2,1)S(1)}, u32[]{:S(2)}, u32[]{:S(2)}) collective-permute-start(bf16[512,128]{1,0:T(8,128)(2,1)S(1)} %get-tuple-element.41.own_ref), channel_id=1, source_target_pairs={{0,8},{16,24},{32,40},{48,56},{64,72},{80,88},{96,104},{112,120}} | collective-permute-start | bytes 393224 | tf_op jit(solution)/shard_map/ppermute | solution.py:30
  15.4 28.3 %collective-permute-start.6 = (bf16[512,256]{1,0:T(8,128)(2,1)S(1)}, bf16[512,256]{1,0:T(8,128)(2,1)S(1)}, u32[]{:S(2)}, u32[]{:S(2)}) collective-permute-start(bf16[512,256]{1,0:T(8,128)(2,1)S(1)} %slice.9.after_ref.b0.rest_0_), channel_id=1, source_target_pairs={{0,16},{1,17},{2,18},{3,19},{4,20},{5,21},{6,22},{7,23},{8,24},{9,... | collective-permute-start | bytes 786440 | tf_op jit(solution)/shard_map/ppermute | solution.py:30
  20.4 23.4 %collective-permute-start.7 = (bf16[1536,256]{1,0:T(8,128)(2,1)S(1)}, bf16[1536,256]{1,0:T(8,128)(2,1)S(1)}, u32[]{:S(2)}, u32[]{:S(2)}) collective-permute-start(bf16[1536,256]{1,0:T(8,128)(2,1)S(1)} %get-tuple-element.45), channel_id=1, source_target_pairs={{0,16},{1,17},{2,18},{3,19},{4,20},{5,21},{6,22},{7,23},{8,24},{9,... | collective-permute-start | bytes 2359304 | tf_op jit(solution)/shard_map/ppermute | solution.py:30
  21.1 35.1 %collective-permute-start.14 = (bf16[1792,256]{1,0:T(8,128)(2,1)S(1)}, bf16[1792,256]{1,0:T(8,128)(2,1)S(1)}, u32[]{:S(2)}, u32[]{:S(2)}) collective-permute-start(bf16[1792,256]{1,0:T(8,128)(2,1)S(1)} %get-tuple-element.78.top.rest_0_), channel_id=1, source_target_pairs={{0,32},{1,33},{2,34},{3,35},{4,36},{5,37},{6,38},{7,39},{8,40},{9,... | collective-permute-start | bytes 2752520 | tf_op jit(solution)/shard_map/ppermute | solution.py:30
  21.2 19.6 %collective-permute-start.2 = (bf16[512,128]{1,0:T(8,128)(2,1)S(1)}, bf16[512,128]{1,0:T(8,128)(2,1)S(1)}, u32[]{:S(2)}, u32[]{:S(2)}) collective-permute-start(bf16[512,128]{1,0:T(8,128)(2,1)S(1)} %get-tuple-element.41.own_ref), channel_id=1, source_target_pairs={{0,12},{16,28},{32,44},{48,60},{64,76},{80,92},{96,108},{112,124}} | collective-permute-start | bytes 393224 | tf_op jit(solution)/shard_map/ppermute | solution.py:30
  26.9 23.6 %collective-permute-start.11 = (bf16[512,512]{1,0:T(8,128)(2,1)S(1)}, bf16[512,512]{1,0:T(8,128)(2,1)S(1)}, u32[]{:S(2)}, u32[]{:S(2)}) collective-permute-start(bf16[512,512]{1,0:T(8,128)(2,1)S(1)} %get-tuple-element.58), channel_id=1, source_target_pairs={{4,12},{20,28},{36,44},{52,60},{68,76},{84,92},{100,108},{116,124}} | collective-permute-start | bytes 1572872 | tf_op jit(solution)/shard_map/ppermute | solution.py:30
  40.9 20.9 %collective-permute-start.15 = (bf16[1792,256]{1,0:T(8,128)(2,1)S(1)}, bf16[1792,256]{1,0:T(8,128)(2,1)S(1)}, u32[]{:S(2)}, u32[]{:S(2)}) collective-permute-start(bf16[1792,256]{1,0:T(8,128)(2,1)S(1)} %get-tuple-element.77.bottom.rest_0_), channel_id=1, source_target_pairs={{0,96},{1,97},{2,98},{3,99},{4,100},{5,101},{6,102},{7,103},{8,104... | collective-permute-start | bytes 2752520 | tf_op jit(solution)/shard_map/ppermute | solution.py:30
  46.6 1.4 %collective-permute-start.8 = (bf16[512,128]{1,0:T(8,128)(2,1)S(1)}, bf16[512,128]{1,0:T(8,128)(2,1)S(1)}, u32[]{:S(2)}, u32[]{:S(2)}) collective-permute-start(bf16[512,128]{1,0:T(8,128)(2,1)S(1)} %get-tuple-element.47.own_ref), channel_id=1, source_target_pairs={{4,8},{20,24},{36,40},{52,56},{68,72},{84,88},{100,104},{116,120}} | collective-permute-start | bytes 393224 | tf_op jit(solution)/shard_map/ppermute | solution.py:30
  47.2 3.2 %collective-permute-start.10 = (bf16[512,256]{1,0:T(8,128)(2,1)S(1)}, bf16[512,256]{1,0:T(8,128)(2,1)S(1)}, u32[]{:S(2)}, u32[]{:S(2)}) collective-permute-start(bf16[512,256]{1,0:T(8,128)(2,1)S(1)} %get-tuple-element.57), channel_id=1, source_target_pairs={{8,12},{24,28},{40,44},{56,60},{72,76},{88,92},{104,108},{120,124}} | collective-permute-start | bytes 786440 | tf_op jit(solution)/shard_map/ppermute | solution.py:30
  49.8 3.0 %collective-permute-start.9 = (bf16[1024,128]{1,0:T(8,128)(2,1)S(1)}, bf16[1024,128]{1,0:T(8,128)(2,1)S(1)}, u32[]{:S(2)}, u32[]{:S(2)}) collective-permute-start(bf16[1024,128]{1,0:T(8,128)(2,1)S(1)} %get-tuple-element.49.after_ref.y12_ref), channel_id=1, source_target_pairs={{8,12},{24,28},{40,44},{56,60},{72,76},{88,92},{104,108},{120,124}} | collective-permute-start | bytes 786440 | tf_op jit(solution)/shard_map/ppermute | solution.py:30
  51.1 10.6 %collective-permute-start.13 = (bf16[512,512]{1,0:T(8,128)(2,1)S(1)}, bf16[512,512]{1,0:T(8,128)(2,1)S(1)}, u32[]{:S(2)}, u32[]{:S(2)}) collective-permute-start(bf16[512,512]{1,0:T(8,128)(2,1)S(1)} %get-tuple-element.60.p1), channel_id=1, source_target_pairs={{0,16},{1,17},{2,18},{3,19},{4,20},{5,21},{6,22},{7,23},{8,24},{9,... | collective-permute-start | bytes 1572872 | tf_op jit(solution)/shard_map/ppermute | solution.py:30
  53.4 33.0 %collective-permute-start.19 = (bf16[1792,256]{1,0:T(8,128)(2,1)S(1)}, bf16[1792,256]{1,0:T(8,128)(2,1)S(1)}, u32[]{:S(2)}, u32[]{:S(2)}) collective-permute-start(bf16[1792,256]{1,0:T(8,128)(2,1)S(1)} %get-tuple-element.67), channel_id=1, source_target_pairs={{0,32},{1,33},{2,34},{3,35},{4,36},{5,37},{6,38},{7,39},{8,40},{9,... | collective-permute-start | bytes 2752520 | tf_op jit(solution)/shard_map/ppermute | solution.py:30
  53.5 32.9 %collective-permute-start.20 = (bf16[1792,256]{1,0:T(8,128)(2,1)S(1)}, bf16[1792,256]{1,0:T(8,128)(2,1)S(1)}, u32[]{:S(2)}, u32[]{:S(2)}) collective-permute-start(bf16[1792,256]{1,0:T(8,128)(2,1)S(1)} %get-tuple-element.68), channel_id=1, source_target_pairs={{0,96},{1,97},{2,98},{3,99},{4,100},{5,101},{6,102},{7,103},{8,104... | collective-permute-start | bytes 2752520 | tf_op jit(solution)/shard_map/ppermute | solution.py:30
  56.2 5.6 %collective-permute-start.12 = (bf16[512,256]{1,0:T(8,128)(2,1)S(1)}, bf16[512,256]{1,0:T(8,128)(2,1)S(1)}, u32[]{:S(2)}, u32[]{:S(2)}) collective-permute-start(bf16[512,256]{1,0:T(8,128)(2,1)S(1)} %get-tuple-element.59.p23), channel_id=1, source_target_pairs={{0,16},{1,17},{2,18},{3,19},{4,20},{5,21},{6,22},{7,23},{8,24},{9,... | collective-permute-start | bytes 786440 | tf_op jit(solution)/shard_map/ppermute | solution.py:30
  65.5 20.9 %collective-permute-start.16 = (bf16[1536,128]{1,0:T(8,128)(2,1)S(1)}, bf16[1536,128]{1,0:T(8,128)(2,1)S(1)}, u32[]{:S(2)}, u32[]{:S(2)}) collective-permute-start(bf16[1536,128]{1,0:T(8,128)(2,1)S(1)} %get-tuple-element.61), channel_id=1, source_target_pairs={{12,0},{28,16},{44,32},{60,48},{76,64},{92,80},{108,96},{124,112}} | collective-permute-start | bytes 1179656 | tf_op jit(solution)/shard_map/ppermute | solution.py:30
  66.8 4.8 %collective-permute-start.17 = (bf16[1024,128]{1,0:T(8,128)(2,1)S(1)}, bf16[1024,128]{1,0:T(8,128)(2,1)S(1)}, u32[]{:S(2)}, u32[]{:S(2)}) collective-permute-start(bf16[1024,128]{1,0:T(8,128)(2,1)S(1)} %get-tuple-element.62), channel_id=1, source_target_pairs={{12,4},{28,20},{44,36},{60,52},{76,68},{92,84},{108,100},{124,116}} | collective-permute-start | bytes 786440 | tf_op jit(solution)/shard_map/ppermute | solution.py:30
  67.7 0.7 collective-permute-start.18
  68.4 44.5 %collective-permute-start.27 = (bf16[1792,256]{1,0:T(8,128)(2,1)S(1)}, bf16[1792,256]{1,0:T(8,128)(2,1)S(1)}, u32[]{:S(2)}, u32[]{:S(2)}) collective-permute-start(bf16[1792,256]{1,0:T(8,128)(2,1)S(1)} %collective-permute-done.15.rest_7_.rest_1_), channel_id=1, source_target_pairs={{0,96},{1,97},{2,98},{3,99},{4,100},{5,101},{6,102},{7,103},{8,104... | collective-permute-start | bytes 2752520 | tf_op jit(solution)/shard_map/ppermute | solution.py:30
  71.6 44.6 %collective-permute-start.25 = (bf16[1792,256]{1,0:T(8,128)(2,1)S(1)}, bf16[1792,256]{1,0:T(8,128)(2,1)S(1)}, u32[]{:S(2)}, u32[]{:S(2)}) collective-permute-start(bf16[1792,256]{1,0:T(8,128)(2,1)S(1)} %collective-permute-done.14.rest_6_.rest_3_), channel_id=1, source_target_pairs={{0,32},{1,33},{2,34},{3,35},{4,36},{5,37},{6,38},{7,39},{8,40},{9,... | collective-permute-start | bytes 2752520 | tf_op jit(solution)/shard_map/ppermute | solution.py:30
  87.1 11.9 %collective-permute-start.21 = (bf16[2048,128]{1,0:T(8,128)(2,1)S(1)}, bf16[2048,128]{1,0:T(8,128)(2,1)S(1)}, u32[]{:S(2)}, u32[]{:S(2)}) collective-permute-start(bf16[2048,128]{1,0:T(8,128)(2,1)S(1)} %shard_map.45.late), channel_id=1, source_target_pairs={{0,1},{4,5},{8,9},{12,13},{16,17},{20,21},{24,25},{28,29},{32,33},... | collective-permute-start | bytes 1572872 | tf_op jit(solution)/shard_map/ppermute | solution.py:30
  88.4 21.9 %collective-permute-start.22 = (bf16[2048,128]{1,0:T(8,128)(2,1)S(1)}, bf16[2048,128]{1,0:T(8,128)(2,1)S(1)}, u32[]{:S(2)}, u32[]{:S(2)}) collective-permute-start(bf16[2048,128]{1,0:T(8,128)(2,1)S(1)} %shard_map.45.late), channel_id=1, source_target_pairs={{0,2},{4,6},{8,10},{12,14},{16,18},{20,22},{24,26},{28,30},{32,34}... | collective-permute-start | bytes 1572872 | tf_op jit(solution)/shard_map/ppermute | solution.py:30
  89.7 20.5 %collective-permute-start.23 = (bf16[2048,128]{1,0:T(8,128)(2,1)S(1)}, bf16[2048,128]{1,0:T(8,128)(2,1)S(1)}, u32[]{:S(2)}, u32[]{:S(2)}) collective-permute-start(bf16[2048,128]{1,0:T(8,128)(2,1)S(1)} %shard_map.45.late), channel_id=1, source_target_pairs={{0,3},{4,7},{8,11},{12,15},{16,19},{20,23},{24,27},{28,31},{32,35}... | collective-permute-start | bytes 1572872 | tf_op jit(solution)/shard_map/ppermute | solution.py:30
  111.3 2.7 %collective-permute-start.24 = (bf16[1024,128]{1,0:T(8,128)(2,1)S(1)}, bf16[1024,128]{1,0:T(8,128)(2,1)S(1)}, u32[]{:S(2)}, u32[]{:S(2)}) collective-permute-start(bf16[1024,128]{1,0:T(8,128)(2,1)S(1)} %get-tuple-element.72), channel_id=1, source_target_pairs={{0,16},{1,17},{2,18},{3,19},{4,20},{5,21},{6,22},{7,23},{8,24},{9,... | collective-permute-start | bytes 786440 | tf_op jit(solution)/shard_map/ppermute | solution.py:30
  115.8 6.1 %collective-permute-start.28 = (bf16[1792,128]{1,0:T(8,128)(2,1)S(1)}, bf16[1792,128]{1,0:T(8,128)(2,1)S(1)}, u32[]{:S(2)}, u32[]{:S(2)}) collective-permute-start(bf16[1792,128]{1,0:T(8,128)(2,1)S(1)} %get-tuple-element.76), channel_id=1, source_target_pairs={{0,16},{1,17},{2,18},{3,19},{4,20},{5,21},{6,22},{7,23},{8,24},{9,... | collective-permute-start | bytes 1376264 | tf_op jit(solution)/shard_map/ppermute | solution.py:30
  118.0 3.9 %collective-permute-start.26 = (bf16[1792,128]{1,0:T(8,128)(2,1)S(1)}, bf16[1792,128]{1,0:T(8,128)(2,1)S(1)}, u32[]{:S(2)}, u32[]{:S(2)}) collective-permute-start(bf16[1792,128]{1,0:T(8,128)(2,1)S(1)} %get-tuple-element.74), channel_id=1, source_target_pairs={{0,16},{1,17},{2,18},{3,19},{4,20},{5,21},{6,22},{7,23},{8,24},{9,... | collective-permute-start | bytes 1376264 | tf_op jit(solution)/shard_map/ppermute | solution.py:30
  118.2 3.7 %copy-start = (f32[4096,128]{1,0:T(8,128)S(1)}, f32[4096,128]{1,0:T(8,128)}, u32[]{:S(2)}) copy-start(f32[4096,128]{1,0:T(8,128)} %b_ref.5) | copy-start | bytes 6291460

commit v9 on v8

--- a/solution.py
+++ b/solution.py
@@ -187,22 +187,23 @@
     x_ref[0:NB, :] = apply(u1h, u1l, t).astype(BF16)
 
 
-def hold_kernel(ids, top, bottom, after_ref, top_out, bottom_out):
+def hold_kernel(ids, top, bottom, *rest):
+    top_out, bottom_out = rest[-2:]
     top_out[...] = top[...]
     bottom_out[...] = bottom[...]
 
 
-def late_kernel(ids, to0, to1, to2, y0, y1, y2, y3, *rest):
+def late_kernel(ids, to0, to1, to2, y1, y2, y3, *rest):
     late_ref, z = rest[-1], ids[2]
-    late_ref[0:NB, :] = y0[...]
-    late_ref[NB : 2 * NB, :] = jnp.where(z >= 1, y1[...], to0[0:NB, :])
-    late_ref[2 * NB : 3 * NB, :] = jnp.where(z >= 2, y2[...], to0[NB : 2 * NB, :] + to1[0:NB, :])
-    late_ref[3 * NB :, :] = jnp.where(z >= 3, y3[...], to0[2 * NB :, :] + to1[NB:, :] + to2[...])
-
-
-def unknowns_kernel(ids, late, s1, s2, s3, v_ref, mine_ref, theirs_ref):
+    late_ref[0:NB, :] = jnp.where(z >= 1, y1[...], to0[0:NB, :])
+    late_ref[NB : 2 * NB, :] = jnp.where(z >= 2, y2[...], to0[NB : 2 * NB, :] + to1[0:NB, :])
+    late_ref[2 * NB :, :] = jnp.where(z >= 3, y3[...], to0[2 * NB :, :] + to1[NB:, :] + to2[...])
+
+
+def unknowns_kernel(ids, v0, e1, e2, e3, late, s1, s2, s3, v_ref, mine_ref, theirs_ref):
     h, owner = ids[1], ids[3] == 0
-    v_ref[...] = jnp.where(owner, late[...], s1[...] + s2[...] + s3[...])
+    v_ref[0:NB, :] = jnp.where(owner, v0[...], e1[...] + e2[...] + e3[...])
+    v_ref[NB:, :] = jnp.where(owner, late[...], s1[...] + s2[...] + s3[...])
     for j in range(4):
         rows = slice(j * HB, (j + 1) * HB)
         mine_ref[rows, :] = v_ref[pl.ds(pl.multiple_of(j * NB + h * HB, HB), HB), :]
@@ -300,8 +301,6 @@
     same = [own, send(own, x_minus), send(own, x_far), send(own, x_plus)]
     half = (rows - NB) // 2
     own_t, own_b = factors[NB : NB + half], factors[NB + half :]
-    before_t, after_b = send(own_t, x_plus), send(own_b, x_minus)
-    far_t, far_b = send(before_t, x_plus), send(after_b, x_minus)
     own_other = send(own, other_core)
     wspecs = [whole((NB, HB))] * 6
 
@@ -324,6 +323,12 @@
         )
 
     y0 = call(combine_kernel, ids, (yb0, *hops), [vspec] * 4, bf(NB))
+    early = [send(y0, y_move(t)) for t in (1, 2, 3)]
+    top, bottom = call(
+        hold_kernel, ids, (own_t, own_b, *early, window[5]), [whole((half, HB))] * 2 + [ANY] * 4, (bf(half, HB),) * 2
+    )
+    before_t, after_b = send(top, x_plus), send(bottom, x_minus)
+    far_t, far_b = send(before_t, x_plus), send(after_b, x_minus)
     _, w0, y_own, yb1 = forward(0, in_hbm(rhs), first, y0, y_z0, ())
     hops = [send(yb1, z_move(1, 2))]
     _, _, y_own, y12 = forward(1, w0, vspec, yb1, y_own, hops)
@@ -340,13 +345,13 @@
     )
     to0, to1, to2 = send(xs, z_move(3, 0)), send(x23s, z_move(3, 1)), send(x3s, z_move(3, 2))
     late = call(
-        late_kernel, ids, (to0, to1, to2, y0, y1, y2, yb3, before_b, after_t),
-        [whole((3 * NB, cols)), whole((2 * NB, cols))] + [vspec] * 5 + [ANY] * 2, bf(4 * NB),
+        late_kernel, ids, (to0, to1, to2, y1, y2, yb3, before_b, after_t),
+        [whole((3 * NB, cols)), whole((2 * NB, cols))] + [vspec] * 4 + [ANY] * 2, bf(3 * NB),
     )
     spread = [send(late, y_move(t)) for t in (1, 2, 3)]
     out = jax.ShapeDtypeStruct((rows, cols), F32)
     v, mine, theirs = call(
-        unknowns_kernel, ids, (late, *spread), [whole((4 * NB, cols))] * 4,
+        unknowns_kernel, ids, (y0, *early, late, *spread), [vspec] * 4 + [whole((3 * NB, cols))] * 4,
         (bf(4 * NB), bf(4 * HB), bf(4 * HB)),
     )
     other = send(theirs, other_core)

time: 125 us -> 111 us (0.89)
  waiting for transfers between devices: 55.7 us -> 35.6 us
  starting transfers between devices: 41.2 us -> 45.7 us
    ppermute x29 -> x32, waiting for transfers between devices: 55.7 us -> 35.6 us  [send(): return lax.ppermute(value, ('row', 'col'), pairs(move))]
    ppermute x29 -> x32, starting transfers between devices: 41.2 us -> 45.7 us  [send(): return lax.ppermute(value, ('row', 'col'), pairs(move))]
    pallas_call x14 -> x15, Pallas kernels: 25.9 us -> 26.7 us  [call(): pl.pallas_call(kernel, grid_spec=pltpu.PrefetchScalarGridSpec(num_scalar_...]
  transfers between devices with their start and end apart: 29 -> 32, of which waited for: 7 -> 10; matrix products, arithmetic and copies ran while one was open for 0% -> 0% of each run, Pallas kernels for 19% -> 22%
where the time goes in v9:
time: 111 us; the launch traced here: 110 us
  starting transfers between devices  45.7 us (41%)
  waiting for transfers between devices  35.6 us (32%)
  Pallas kernels  26.7 us (24%)
    ppermute x32, starting transfers between devices, send(): return lax.ppermute(value, ('row', 'col'), pairs(move))  45.7 us
    ppermute x32, waiting for transfers between devices, send(): return lax.ppermute(value, ('row', 'col'), pairs(move))  35.6 us
    pallas_call x15, Pallas kernels, call(): pl.pallas_call(kernel, grid_spec=pltpu.PrefetchScalarGridSpec(num_scalar_...  26.7 us
  transfers between devices with their start and end apart: 32, of which 10 were waited for; matrix products, arithmetic and copies ran while one was open for 0% of the time, Pallas kernels for 22%

profile of v9, /device:TPU:1, one launch (start us, length us, event | category | flops | bytes accessed | tf_op | source)
XLA Modules:
  0.0 109.5 jit_solution(8479865973972207815)
XLA Ops:
  0.0 1.0 slice.9.after_ref.b0.rest_0_
  1.0 3.4 %collective-permute-start.6 = (bf16[512,256]{1,0:T(8,128)(2,1)S(1)}, bf16[512,256]{1,0:T(8,128)(2,1)S(1)}, u32[]{:S(2)}, u32[]{:S(2)}) collective-permute-start(bf16[512,256]{1,0:T(8,128)(2,1)S(1)} %slice.9.after_ref.b0.rest_0_), channel_id=1, source_target_pairs={{0,96},{1,97},{2,98},{3,99},{4,100},{5,101},{6,102},{7,103},{8,104... | collective-permute-start | bytes 786440 | tf_op jit(solution)/shard_map/ppermute | solution.py:30
  4.3 0.5 collective-permute-start.7
  4.9 0.6 collective-permute-start.8
  5.5 0.1 pad_add_fusion.ids
  5.6 3.7 %shard_map.37 = (f32[512,128]{1,0:T(8,128)S(1)}, bf16[512,128]{1,0:T(8,128)(2,1)S(1)}, bf16[512,512]{1,0:T(8,128)(2,1)S(1)}, bf16[512,512]{1,0:T(8,128)(2,1)S(1)...) custom-call(s32[4]{0:T(128)S(1)} %pad_add_fusion.ids, ...), custom_call_target="tpu_custom_call" | custom-call | flops 1 | bytes 1 | tf_op jit(solution)/shard_map/pallas_call | solution.py:276
  9.2 3.5 %collective-permute-start = (bf16[512,128]{1,0:T(8,128)(2,1)S(1)}, bf16[512,128]{1,0:T(8,128)(2,1)S(1)}, u32[]{:S(2)}, u32[]{:S(2)}) collective-permute-start(bf16[512,128]{1,0:T(8,128)(2,1)S(1)} %get-tuple-element.43.own_ref), channel_id=1, source_target_pairs={{0,4},{16,20},{32,36},{48,52},{64,68},{80,84},{96,100},{112,116}} | collective-permute-start | bytes 393224 | tf_op jit(solution)/shard_map/ppermute | solution.py:30
  12.8 2.6 %collective-permute-start.1 = (bf16[512,128]{1,0:T(8,128)(2,1)S(1)}, bf16[512,128]{1,0:T(8,128)(2,1)S(1)}, u32[]{:S(2)}, u32[]{:S(2)}) collective-permute-start(bf16[512,128]{1,0:T(8,128)(2,1)S(1)} %get-tuple-element.43.own_ref), channel_id=1, source_target_pairs={{0,8},{16,24},{32,40},{48,56},{64,72},{80,88},{96,104},{112,120}} | collective-permute-start | bytes 393224 | tf_op jit(solution)/shard_map/ppermute | solution.py:30
  15.4 1.3 %collective-permute-start.2 = (bf16[512,128]{1,0:T(8,128)(2,1)S(1)}, bf16[512,128]{1,0:T(8,128)(2,1)S(1)}, u32[]{:S(2)}, u32[]{:S(2)}) collective-permute-start(bf16[512,128]{1,0:T(8,128)(2,1)S(1)} %get-tuple-element.43.own_ref), channel_id=1, source_target_pairs={{0,12},{16,28},{32,44},{48,60},{64,76},{80,92},{96,108},{112,124}} | collective-permute-start | bytes 393224 | tf_op jit(solution)/shard_map/ppermute | solution.py:30
  16.8 0.0 collective-permute-done.7.b2.rest_2_
  16.8 2.9 %collective-permute-done.8.b3.rest_3_ = bf16[512,256]{1,0:T(8,128)(2,1)S(1)} collective-permute-done((bf16[512,256]{1,0:T(8,128)(2,1)S(1)}, bf16[512,256]{1,0:T(8,128)(2,1)S(1)}, u32[]{:S(2)}, u32[]{:S(2)}) %collective-permute-start.8) | collective-permute-done | bytes 262176 | tf_op jit(solution)/shard_map/ppermute | solution.py:30
  19.7 0.7 shard_map.39
  20.4 2.9 %collective-permute-start.10 = (bf16[1536,256]{1,0:T(8,128)(2,1)S(1)}, bf16[1536,256]{1,0:T(8,128)(2,1)S(1)}, u32[]{:S(2)}, u32[]{:S(2)}) collective-permute-start(bf16[1536,256]{1,0:T(8,128)(2,1)S(1)} %get-tuple-element.47), channel_id=1, source_target_pairs={{0,16},{1,17},{2,18},{3,19},{4,20},{5,21},{6,22},{7,23},{8,24},{9,... | collective-permute-start | bytes 2359304 | tf_op jit(solution)/shard_map/ppermute | solution.py:30
  23.3 0.0 collective-permute-done.1.r2
  23.3 0.0 collective-permute-done.2.r3
  23.3 0.6 shard_map.38.own_ref.v0
  23.9 1.3 %collective-permute-start.3 = (bf16[512,128]{1,0:T(8,128)(2,1)S(1)}, bf16[512,128]{1,0:T(8,128)(2,1)S(1)}, u32[]{:S(2)}, u32[]{:S(2)}) collective-permute-start(bf16[512,128]{1,0:T(8,128)(2,1)S(1)} %shard_map.38.own_ref.v0), channel_id=1, source_target_pairs={{0,1},{4,5},{8,9},{12,13},{16,17},{20,21},{24,25},{28,29},{32,33},... | collective-permute-start | bytes 393224 | tf_op jit(solution)/shard_map/ppermute | solution.py:30
  25.2 1.9 %collective-permute-start.4 = (bf16[512,128]{1,0:T(8,128)(2,1)S(1)}, bf16[512,128]{1,0:T(8,128)(2,1)S(1)}, u32[]{:S(2)}, u32[]{:S(2)}) collective-permute-start(bf16[512,128]{1,0:T(8,128)(2,1)S(1)} %shard_map.38.own_ref.v0), channel_id=1, source_target_pairs={{0,2},{4,6},{8,10},{12,14},{16,18},{20,22},{24,26},{28,30},{32,34}... | collective-permute-start | bytes 393224 | tf_op jit(solution)/shard_map/ppermute | solution.py:30
  27.1 1.1 %collective-permute-start.9 = (bf16[512,256]{1,0:T(8,128)(2,1)S(1)}, bf16[512,256]{1,0:T(8,128)(2,1)S(1)}, u32[]{:S(2)}, u32[]{:S(2)}) collective-permute-start(bf16[512,256]{1,0:T(8,128)(2,1)S(1)} %slice.9.after_ref.b0.rest_0_), channel_id=1, source_target_pairs={{0,16},{1,17},{2,18},{3,19},{4,20},{5,21},{6,22},{7,23},{8,24},{9,... | collective-permute-start | bytes 786440 | tf_op jit(solution)/shard_map/ppermute | solution.py:30
  28.3 1.3 %collective-permute-start.5 = (bf16[512,128]{1,0:T(8,128)(2,1)S(1)}, bf16[512,128]{1,0:T(8,128)(2,1)S(1)}, u32[]{:S(2)}, u32[]{:S(2)}) collective-permute-start(bf16[512,128]{1,0:T(8,128)(2,1)S(1)} %shard_map.38.own_ref.v0), channel_id=1, source_target_pairs={{0,3},{4,7},{8,11},{12,15},{16,19},{20,23},{24,27},{28,31},{32,35}... | collective-permute-start | bytes 393224 | tf_op jit(solution)/shard_map/ppermute | solution.py:30
  29.5 0.0 collective-permute-done.3.rest_0_.e1
  29.6 0.7 collective-permute-start.14
  30.3 0.1 collective-permute-done.4.rest_1_.e2
  30.4 0.7 collective-permute-start.13
  31.1 0.1 fusion
  31.2 1.4 %collective-permute-done.5.rest_2_.e3 = bf16[512,128]{1,0:T(8,128)(2,1)S(1)} collective-permute-done((bf16[512,128]{1,0:T(8,128)(2,1)S(1)}, bf16[512,128]{1,0:T(8,128)(2,1)S(1)}, u32[]{:S(2)}, u32[]{:S(2)}) %collective-permute-start.5) | collective-permute-done | bytes 131104 | tf_op jit(solution)/shard_map/ppermute | solution.py:30
  32.6 0.7 shard_map.43
  33.3 0.1 collective-permute-start.17
  33.4 3.4 %collective-permute-start.18 = (bf16[1792,256]{1,0:T(8,128)(2,1)S(1)}, bf16[1792,256]{1,0:T(8,128)(2,1)S(1)}, u32[]{:S(2)}, u32[]{:S(2)}) collective-permute-start(bf16[1792,256]{1,0:T(8,128)(2,1)S(1)} %get-tuple-element.64), channel_id=1, source_target_pairs={{0,96},{1,97},{2,98},{3,99},{4,100},{5,101},{6,102},{7,103},{8,104... | collective-permute-start | bytes 2752520 | tf_op jit(solution)/shard_map/ppermute | solution.py:30
  36.8 0.0 collective-permute-done.9.rest_4_
  36.8 2.7 %shard_map.40 = (bf16[512,128]{1,0:T(8,128)(2,1)}, f32[512,128]{1,0:T(8,128)S(1)}, f32[512,128]{1,0:T(8,128)S(1)}, bf16[512,128]{1,0:T(8,128)(2,1)S(1)}) custom-call(s32[4]{0:T(128)S(1)} %pad_add_fusion.ids, f32[4096,128]{1,0:T(8,128)} %b_ref.5, bf16[512,128]{1,0:T(8,128)(2,1)S(1)} %shard_map.38.own_ref.v0, f32[512,128]{1,0:T(8,128)S(1)} %get-tuple-element.44.prior_ref, ...), custom_call_target="tpu_custom_call" | custom-call | flops 1 | bytes 1 | tf_op jit(solution)/shard_map/pallas_call | solution.py:276
  39.6 0.7 collective-permute-start.11
  40.3 1.9 %shard_map.41 = (bf16[512,128]{1,0:T(8,128)(2,1)}, f32[512,128]{1,0:T(8,128)}, f32[512,128]{1,0:T(8,128)S(1)}, bf16[1024,128]{1,0:T(8,128)(2,1)S(1)}) custom-call(s32[4]{0:T(128)S(1)} %pad_add_fusion.ids, f32[512,128]{1,0:T(8,128)S(1)} %get-tuple-element.48.w_ref, bf16[512,128]{1,0:T(8,128)(2,1)S(1)} %get-tuple-element.49.own_ref, ...), custom_call_target="tpu_custom_call" | custom-call | flops 1 | bytes 1 | tf_op jit(solution)/shard_map/pallas_call | solution.py:276
  42.1 0.7 collective-permute-start.12
  42.8 0.6 shard_map.42
  43.4 1.0 collective-permute-start.15
  44.4 0.1 collective-permute-start.16
  44.5 0.7 shard_map.45
  45.2 0.1 collective-permute-start.22
  45.2 0.3 collective-permute-done.15.p23_other
  45.6 2.3 %collective-permute-start.23 = (bf16[1792,256]{1,0:T(8,128)(2,1)S(1)}, bf16[1792,256]{1,0:T(8,128)(2,1)S(1)}, u32[]{:S(2)}, u32[]{:S(2)}) collective-permute-start(bf16[1792,256]{1,0:T(8,128)(2,1)S(1)} %get-tuple-element.72), channel_id=1, source_target_pairs={{0,96},{1,97},{2,98},{3,99},{4,100},{5,101},{6,102},{7,103},{8,104... | collective-permute-start | bytes 2752520 | tf_op jit(solution)/shard_map/ppermute | solution.py:30
  47.9 9.0 %collective-permute-done.17.rest_6_.rest_3_ = bf16[1792,256]{1,0:T(8,128)(2,1)S(1)} collective-permute-done((bf16[1792,256]{1,0:T(8,128)(2,1)S(1)}, bf16[1792,256]{1,0:T(8,128)(2,1)S(1)}, u32[]{:S(2)}, u32[]{:S(2)}) %collective-permute-start.17) | collective-permute-done | bytes 917536 | tf_op jit(solution)/shard_map/ppermute | solution.py:30
  56.9 4.0 %shard_map.44 = (bf16[512,128]{1,0:T(8,128)(2,1)S(1)}, bf16[512,128]{1,0:T(8,128)(2,1)S(1)}, f32[512,128]{1,0:T(8,128)S(1)}, bf16[512,128]{1,0:T(8,128)(2,1)S(1)...) custom-call(s32[4]{0:T(128)S(1)} %pad_add_fusion.ids, ...), custom_call_target="tpu_custom_call" | custom-call | flops 1 | bytes 1 | tf_op jit(solution)/shard_map/pallas_call | solution.py:276
  60.9 0.7 collective-permute-start.20
  61.6 1.3 %collective-permute-start.19 = (bf16[1536,128]{1,0:T(8,128)(2,1)S(1)}, bf16[1536,128]{1,0:T(8,128)(2,1)S(1)}, u32[]{:S(2)}, u32[]{:S(2)}) collective-permute-start(bf16[1536,128]{1,0:T(8,128)(2,1)S(1)} %get-tuple-element.65), channel_id=1, source_target_pairs={{12,0},{28,16},{44,32},{60,48},{76,64},{92,80},{108,96},{124,112}} | collective-permute-start | bytes 1179656 | tf_op jit(solution)/shard_map/ppermute | solution.py:30
  62.9 0.7 collective-permute-start.21
  63.5 2.5 %collective-permute-start.30 = (bf16[1792,256]{1,0:T(8,128)(2,1)S(1)}, bf16[1792,256]{1,0:T(8,128)(2,1)S(1)}, u32[]{:S(2)}, u32[]{:S(2)}) collective-permute-start(bf16[1792,256]{1,0:T(8,128)(2,1)S(1)} %collective-permute-done.18.rest_7_.rest_1_), channel_id=1, source_target_pairs={{0,96},{1,97},{2,98},{3,99},{4,100},{5,101},{6,102},{7,103},{8,104... | collective-permute-start | bytes 2752520 | tf_op jit(solution)/shard_map/ppermute | solution.py:30
  66.0 10.5 %collective-permute-done.22.rest_0_.rest_3_ = bf16[1792,256]{1,0:T(8,128)(2,1)S(1)} collective-permute-done((bf16[1792,256]{1,0:T(8,128)(2,1)S(1)}, bf16[1792,256]{1,0:T(8,128)(2,1)S(1)}, u32[]{:S(2)}, u32[]{:S(2)}) %collective-permute-start.22) | collective-permute-done | bytes 917536 | tf_op jit(solution)/shard_map/ppermute | solution.py:30
  76.6 0.7 collective-permute-done.19.to0
  77.3 0.7 shard_map.46.late
  78.0 1.3 %collective-permute-start.24 = (bf16[1536,128]{1,0:T(8,128)(2,1)S(1)}, bf16[1536,128]{1,0:T(8,128)(2,1)S(1)}, u32[]{:S(2)}, u32[]{:S(2)}) collective-permute-start(bf16[1536,128]{1,0:T(8,128)(2,1)S(1)} %shard_map.46.late), channel_id=1, source_target_pairs={{0,1},{4,5},{8,9},{12,13},{16,17},{20,21},{24,25},{28,29},{32,33},... | collective-permute-start | bytes 1179656 | tf_op jit(solution)/shard_map/ppermute | solution.py:30
  79.3 1.3 %collective-permute-start.25 = (bf16[1536,128]{1,0:T(8,128)(2,1)S(1)}, bf16[1536,128]{1,0:T(8,128)(2,1)S(1)}, u32[]{:S(2)}, u32[]{:S(2)}) collective-permute-start(bf16[1536,128]{1,0:T(8,128)(2,1)S(1)} %shard_map.46.late), channel_id=1, source_target_pairs={{0,2},{4,6},{8,10},{12,14},{16,18},{20,22},{24,26},{28,30},{32,34}... | collective-permute-start | bytes 1179656 | tf_op jit(solution)/shard_map/ppermute | solution.py:30
  80.6 3.4 %collective-permute-start.26 = (bf16[1536,128]{1,0:T(8,128)(2,1)S(1)}, bf16[1536,128]{1,0:T(8,128)(2,1)S(1)}, u32[]{:S(2)}, u32[]{:S(2)}) collective-permute-start(bf16[1536,128]{1,0:T(8,128)(2,1)S(1)} %shard_map.46.late), channel_id=1, source_target_pairs={{0,3},{4,7},{8,11},{12,15},{16,19},{20,23},{24,27},{28,31},{32,35}... | collective-permute-start | bytes 1179656 | tf_op jit(solution)/shard_map/ppermute | solution.py:30
  84.0 0.9 collective-permute-done.24.s1
  84.9 8.4 %collective-permute-done.25.s2 = bf16[1536,128]{1,0:T(8,128)(2,1)S(1)} collective-permute-done((bf16[1536,128]{1,0:T(8,128)(2,1)S(1)}, bf16[1536,128]{1,0:T(8,128)(2,1)S(1)}, u32[]{:S(2)}, u32[]{:S(2)}) %collective-permute-start.25) | collective-permute-done | bytes 393248 | tf_op jit(solution)/shard_map/ppermute | solution.py:30
  93.4 1.0 shard_map.47
  94.4 3.7 %collective-permute-start.27 = (bf16[1024,128]{1,0:T(8,128)(2,1)S(1)}, bf16[1024,128]{1,0:T(8,128)(2,1)S(1)}, u32[]{:S(2)}, u32[]{:S(2)}) collective-permute-start(bf16[1024,128]{1,0:T(8,128)(2,1)S(1)} %get-tuple-element.76), channel_id=1, source_target_pairs={{0,16},{1,17},{2,18},{3,19},{4,20},{5,21},{6,22},{7,23},{8,24},{9,... | collective-permute-start | bytes 786440 | tf_op jit(solution)/shard_map/ppermute | solution.py:30
  98.1 1.2 %collective-permute-done.27.other_ref = bf16[1024,128]{1,0:T(8,128)(2,1)S(1)} collective-permute-done((bf16[1024,128]{1,0:T(8,128)(2,1)S(1)}, bf16[1024,128]{1,0:T(8,128)(2,1)S(1)}, u32[]{:S(2)}, u32[]{:S(2)}) %collective-permute-start.27) | collective-permute-done | bytes 262176 | tf_op jit(solution)/shard_map/ppermute | solution.py:30
  99.3 1.7 %shard_map.50 = (f32[1792,128]{1,0:T(8,128)S(1)}, bf16[1792,128]{1,0:T(8,128)(2,1)S(1)}) custom-call(s32[4]{0:T(128)S(1)} %pad_add_fusion.ids, bf16[1024,128]{1,0:T(8,128)(2,1)S(1)} %get-tuple-element.75.mine_ref, bf16[1024,128]{1,0:T(8,128)(2,1)S(1)} %collective-permute-done.27.other_ref, bf16[1792,256]{1,0:T(8,128)(2,1)S(1)} %get-tuple-element.81.bottom.rest_0_, ...), custom_call_target="tpu_custom_call" | custom-call | flops 1 | bytes 1 | tf_op jit(solution)/shard_map/pallas_call | solution.py:276
  101.0 0.5 collective-permute-start.31
  101.5 1.7 %shard_map.49 = (f32[1792,128]{1,0:T(8,128)S(1)}, bf16[1792,128]{1,0:T(8,128)(2,1)S(1)}) custom-call(s32[4]{0:T(128)S(1)} %pad_add_fusion.ids, bf16[1024,128]{1,0:T(8,128)(2,1)S(1)} %get-tuple-element.75.mine_ref, bf16[1024,128]{1,0:T(8,128)(2,1)S(1)} %collective-permute-done.27.other_ref, bf16[1792,256]{1,0:T(8,128)(2,1)S(1)} %get-tuple-element.82.top.rest_0_, ...), custom_call_target="tpu_custom_call" | custom-call | flops 1 | bytes 1 | tf_op jit(solution)/shard_map/pallas_call | solution.py:276
  103.2 0.2 collective-permute-start.29
  103.4 3.7 %shard_map.48.out_in = f32[4096,128]{1,0:T(8,128)} custom-call(s32[4]{0:T(128)S(1)} %pad_add_fusion.ids, f32[4096,128]{1,0:T(8,128)} %b_ref.5, bf16[2048,128]{1,0:T(8,128)(2,1)S(1)} %get-tuple-element.73.v_ref, f32[512,128]{1,0:T(8,128)S(1)} %get-tuple-element.74.own_ref, bf16[512,512]{1,0:T(8,128)(2,1)S(1)} %get-tuple-element.53.u3h.uh_ref, ...), custom_call_target="tpu_custom_call" | custom-call | flops 1 | bytes 1 | tf_op jit(solution)/shard_map/pallas_call | solution.py:276
  107.1 2.4 %shard_map.51 = f32[4096,128]{1,0:T(8,128)} custom-call(s32[4]{0:T(128)S(1)} %pad_add_fusion.ids, f32[4096,128]{1,0:T(8,128)} %shard_map.48.out_in, f32[4096,128]{1,0:T(8,128)S(1)} %copy-done, f32[1792,128]{1,0:T(8,128)S(1)} %get-tuple-element.77.own_t, bf16[1792,128]{1,0:T(8,128)(2,1)S(1)} %collective-permute-done.29.part_t, ...), custom_call_target="tpu_custom_call", output_to_operand_aliasing={{}: (1, {})} | custom-call | flops 1 | bytes 1 | tf_op jit(solution)/shard_map/pallas_call | solution.py:276
  (22 shorter events, 0.1 us)
Async XLA Ops:
  1.0 14.5 %collective-permute-start.6 = (bf16[512,256]{1,0:T(8,128)(2,1)S(1)}, bf16[512,256]{1,0:T(8,128)(2,1)S(1)}, u32[]{:S(2)}, u32[]{:S(2)}) collective-permute-start(bf16[512,256]{1,0:T(8,128)(2,1)S(1)} %slice.9.after_ref.b0.rest_0_), channel_id=1, source_target_pairs={{0,96},{1,97},{2,98},{3,99},{4,100},{5,101},{6,102},{7,103},{8,104... | collective-permute-start | bytes 786440 | tf_op jit(solution)/shard_map/ppermute | solution.py:30
  4.3 12.4 %collective-permute-start.7 = (bf16[512,256]{1,0:T(8,128)(2,1)S(1)}, bf16[512,256]{1,0:T(8,128)(2,1)S(1)}, u32[]{:S(2)}, u32[]{:S(2)}) collective-permute-start(bf16[512,256]{1,0:T(8,128)(2,1)S(1)} %slice.9.after_ref.b0.rest_0_), channel_id=1, source_target_pairs={{0,64},{1,65},{2,66},{3,67},{4,68},{5,69},{6,70},{7,71},{8,72},{9,... | collective-permute-start | bytes 786440 | tf_op jit(solution)/shard_map/ppermute | solution.py:30
  4.9 14.8 %collective-permute-start.8 = (bf16[512,256]{1,0:T(8,128)(2,1)S(1)}, bf16[512,256]{1,0:T(8,128)(2,1)S(1)}, u32[]{:S(2)}, u32[]{:S(2)}) collective-permute-start(bf16[512,256]{1,0:T(8,128)(2,1)S(1)} %slice.9.after_ref.b0.rest_0_), channel_id=1, source_target_pairs={{0,32},{1,33},{2,34},{3,35},{4,36},{5,37},{6,38},{7,39},{8,40},{9,... | collective-permute-start | bytes 786440 | tf_op jit(solution)/shard_map/ppermute | solution.py:30
  5.6 25.5 %copy-start.1 = (bf16[4096,256]{1,0:T(8,128)(2,1)S(1)}, bf16[4096,256]{1,0:T(8,128)(2,1)}, u32[]{:S(2)}) copy-start(bf16[4096,256]{1,0:T(8,128)(2,1)} %param.4) | copy-start | bytes 6291460
  9.2 14.0 %collective-permute-start = (bf16[512,128]{1,0:T(8,128)(2,1)S(1)}, bf16[512,128]{1,0:T(8,128)(2,1)S(1)}, u32[]{:S(2)}, u32[]{:S(2)}) collective-permute-start(bf16[512,128]{1,0:T(8,128)(2,1)S(1)} %get-tuple-element.43.own_ref), channel_id=1, source_target_pairs={{0,4},{16,20},{32,36},{48,52},{64,68},{80,84},{96,100},{112,116}} | collective-permute-start | bytes 393224 | tf_op jit(solution)/shard_map/ppermute | solution.py:30
  12.8 10.5 %collective-permute-start.1 = (bf16[512,128]{1,0:T(8,128)(2,1)S(1)}, bf16[512,128]{1,0:T(8,128)(2,1)S(1)}, u32[]{:S(2)}, u32[]{:S(2)}) collective-permute-start(bf16[512,128]{1,0:T(8,128)(2,1)S(1)} %get-tuple-element.43.own_ref), channel_id=1, source_target_pairs={{0,8},{16,24},{32,40},{48,56},{64,72},{80,88},{96,104},{112,120}} | collective-permute-start | bytes 393224 | tf_op jit(solution)/shard_map/ppermute | solution.py:30
  15.4 7.8 %collective-permute-start.2 = (bf16[512,128]{1,0:T(8,128)(2,1)S(1)}, bf16[512,128]{1,0:T(8,128)(2,1)S(1)}, u32[]{:S(2)}, u32[]{:S(2)}) collective-permute-start(bf16[512,128]{1,0:T(8,128)(2,1)S(1)} %get-tuple-element.43.own_ref), channel_id=1, source_target_pairs={{0,12},{16,28},{32,44},{48,60},{64,76},{80,92},{96,108},{112,124}} | collective-permute-start | bytes 393224 | tf_op jit(solution)/shard_map/ppermute | solution.py:30
  20.4 12.2 %collective-permute-start.10 = (bf16[1536,256]{1,0:T(8,128)(2,1)S(1)}, bf16[1536,256]{1,0:T(8,128)(2,1)S(1)}, u32[]{:S(2)}, u32[]{:S(2)}) collective-permute-start(bf16[1536,256]{1,0:T(8,128)(2,1)S(1)} %get-tuple-element.47), channel_id=1, source_target_pairs={{0,16},{1,17},{2,18},{3,19},{4,20},{5,21},{6,22},{7,23},{8,24},{9,... | collective-permute-start | bytes 2359304 | tf_op jit(solution)/shard_map/ppermute | solution.py:30
  23.9 5.6 %collective-permute-start.3 = (bf16[512,128]{1,0:T(8,128)(2,1)S(1)}, bf16[512,128]{1,0:T(8,128)(2,1)S(1)}, u32[]{:S(2)}, u32[]{:S(2)}) collective-permute-start(bf16[512,128]{1,0:T(8,128)(2,1)S(1)} %shard_map.38.own_ref.v0), channel_id=1, source_target_pairs={{0,1},{4,5},{8,9},{12,13},{16,17},{20,21},{24,25},{28,29},{32,33},... | collective-permute-start | bytes 393224 | tf_op jit(solution)/shard_map/ppermute | solution.py:30
  25.2 5.2 %collective-permute-start.4 = (bf16[512,128]{1,0:T(8,128)(2,1)S(1)}, bf16[512,128]{1,0:T(8,128)(2,1)S(1)}, u32[]{:S(2)}, u32[]{:S(2)}) collective-permute-start(bf16[512,128]{1,0:T(8,128)(2,1)S(1)} %shard_map.38.own_ref.v0), channel_id=1, source_target_pairs={{0,2},{4,6},{8,10},{12,14},{16,18},{20,22},{24,26},{28,30},{32,34}... | collective-permute-start | bytes 393224 | tf_op jit(solution)/shard_map/ppermute | solution.py:30
  27.1 9.7 %collective-permute-start.9 = (bf16[512,256]{1,0:T(8,128)(2,1)S(1)}, bf16[512,256]{1,0:T(8,128)(2,1)S(1)}, u32[]{:S(2)}, u32[]{:S(2)}) collective-permute-start(bf16[512,256]{1,0:T(8,128)(2,1)S(1)} %slice.9.after_ref.b0.rest_0_), channel_id=1, source_target_pairs={{0,16},{1,17},{2,18},{3,19},{4,20},{5,21},{6,22},{7,23},{8,24},{9,... | collective-permute-start | bytes 786440 | tf_op jit(solution)/shard_map/ppermute | solution.py:30
  28.3 4.4 %collective-permute-start.5 = (bf16[512,128]{1,0:T(8,128)(2,1)S(1)}, bf16[512,128]{1,0:T(8,128)(2,1)S(1)}, u32[]{:S(2)}, u32[]{:S(2)}) collective-permute-start(bf16[512,128]{1,0:T(8,128)(2,1)S(1)} %shard_map.38.own_ref.v0), channel_id=1, source_target_pairs={{0,3},{4,7},{8,11},{12,15},{16,19},{20,23},{24,27},{28,31},{32,35}... | collective-permute-start | bytes 393224 | tf_op jit(solution)/shard_map/ppermute | solution.py:30
  29.6 13.3 %collective-permute-start.14 = (bf16[512,512]{1,0:T(8,128)(2,1)S(1)}, bf16[512,512]{1,0:T(8,128)(2,1)S(1)}, u32[]{:S(2)}, u32[]{:S(2)}) collective-permute-start(bf16[512,512]{1,0:T(8,128)(2,1)S(1)} %get-tuple-element.60), channel_id=1, source_target_pairs={{4,12},{20,28},{36,44},{52,60},{68,76},{84,92},{100,108},{116,124}} | collective-permute-start | bytes 1572872 | tf_op jit(solution)/shard_map/ppermute | solution.py:30
  30.4 12.4 %collective-permute-start.13 = (bf16[512,256]{1,0:T(8,128)(2,1)S(1)}, bf16[512,256]{1,0:T(8,128)(2,1)S(1)}, u32[]{:S(2)}, u32[]{:S(2)}) collective-permute-start(bf16[512,256]{1,0:T(8,128)(2,1)S(1)} %get-tuple-element.59), channel_id=1, source_target_pairs={{8,12},{24,28},{40,44},{56,60},{72,76},{88,92},{104,108},{120,124}} | collective-permute-start | bytes 786440 | tf_op jit(solution)/shard_map/ppermute | solution.py:30
  33.3 23.6 %collective-permute-start.17 = (bf16[1792,256]{1,0:T(8,128)(2,1)S(1)}, bf16[1792,256]{1,0:T(8,128)(2,1)S(1)}, u32[]{:S(2)}, u32[]{:S(2)}) collective-permute-start(bf16[1792,256]{1,0:T(8,128)(2,1)S(1)} %get-tuple-element.63), channel_id=1, source_target_pairs={{0,32},{1,33},{2,34},{3,35},{4,36},{5,37},{6,38},{7,39},{8,40},{9,... | collective-permute-start | bytes 2752520 | tf_op jit(solution)/shard_map/ppermute | solution.py:30
  33.4 23.5 %collective-permute-start.18 = (bf16[1792,256]{1,0:T(8,128)(2,1)S(1)}, bf16[1792,256]{1,0:T(8,128)(2,1)S(1)}, u32[]{:S(2)}, u32[]{:S(2)}) collective-permute-start(bf16[1792,256]{1,0:T(8,128)(2,1)S(1)} %get-tuple-element.64), channel_id=1, source_target_pairs={{0,96},{1,97},{2,98},{3,99},{4,100},{5,101},{6,102},{7,103},{8,104... | collective-permute-start | bytes 2752520 | tf_op jit(solution)/shard_map/ppermute | solution.py:30
  39.6 0.7 collective-permute-start.11
  42.1 2.4 %collective-permute-start.12 = (bf16[1024,128]{1,0:T(8,128)(2,1)S(1)}, bf16[1024,128]{1,0:T(8,128)(2,1)S(1)}, u32[]{:S(2)}, u32[]{:S(2)}) collective-permute-start(bf16[1024,128]{1,0:T(8,128)(2,1)S(1)} %get-tuple-element.51.after_ref.y12_ref), channel_id=1, source_target_pairs={{8,12},{24,28},{40,44},{56,60},{72,76},{88,92},{104,108},{120,124}} | collective-permute-start | bytes 786440 | tf_op jit(solution)/shard_map/ppermute | solution.py:30
  43.4 2.1 %collective-permute-start.15 = (bf16[512,256]{1,0:T(8,128)(2,1)S(1)}, bf16[512,256]{1,0:T(8,128)(2,1)S(1)}, u32[]{:S(2)}, u32[]{:S(2)}) collective-permute-start(bf16[512,256]{1,0:T(8,128)(2,1)S(1)} %get-tuple-element.61.p23), channel_id=1, source_target_pairs={{0,16},{1,17},{2,18},{3,19},{4,20},{5,21},{6,22},{7,23},{8,24},{9,... | collective-permute-start | bytes 786440 | tf_op jit(solution)/shard_map/ppermute | solution.py:30
  44.4 3.5 %collective-permute-start.16 = (bf16[512,512]{1,0:T(8,128)(2,1)S(1)}, bf16[512,512]{1,0:T(8,128)(2,1)S(1)}, u32[]{:S(2)}, u32[]{:S(2)}) collective-permute-start(bf16[512,512]{1,0:T(8,128)(2,1)S(1)} %get-tuple-element.62.p1), channel_id=1, source_target_pairs={{0,16},{1,17},{2,18},{3,19},{4,20},{5,21},{6,22},{7,23},{8,24},{9,... | collective-permute-start | bytes 1572872 | tf_op jit(solution)/shard_map/ppermute | solution.py:30
  45.2 31.4 %collective-permute-start.22 = (bf16[1792,256]{1,0:T(8,128)(2,1)S(1)}, bf16[1792,256]{1,0:T(8,128)(2,1)S(1)}, u32[]{:S(2)}, u32[]{:S(2)}) collective-permute-start(bf16[1792,256]{1,0:T(8,128)(2,1)S(1)} %get-tuple-element.71), channel_id=1, source_target_pairs={{0,32},{1,33},{2,34},{3,35},{4,36},{5,37},{6,38},{7,39},{8,40},{9,... | collective-permute-start | bytes 2752520 | tf_op jit(solution)/shard_map/ppermute | solution.py:30
  45.6 31.0 %collective-permute-start.23 = (bf16[1792,256]{1,0:T(8,128)(2,1)S(1)}, bf16[1792,256]{1,0:T(8,128)(2,1)S(1)}, u32[]{:S(2)}, u32[]{:S(2)}) collective-permute-start(bf16[1792,256]{1,0:T(8,128)(2,1)S(1)} %get-tuple-element.72), channel_id=1, source_target_pairs={{0,96},{1,97},{2,98},{3,99},{4,100},{5,101},{6,102},{7,103},{8,104... | collective-permute-start | bytes 2752520 | tf_op jit(solution)/shard_map/ppermute | solution.py:30
  60.9 5.2 %collective-permute-start.20 = (bf16[1024,128]{1,0:T(8,128)(2,1)S(1)}, bf16[1024,128]{1,0:T(8,128)(2,1)S(1)}, u32[]{:S(2)}, u32[]{:S(2)}) collective-permute-start(bf16[1024,128]{1,0:T(8,128)(2,1)S(1)} %get-tuple-element.66), channel_id=1, source_target_pairs={{12,4},{28,20},{44,36},{60,52},{76,68},{92,84},{108,100},{124,116}} | collective-permute-start | bytes 786440 | tf_op jit(solution)/shard_map/ppermute | solution.py:30
  61.6 15.7 %collective-permute-start.19 = (bf16[1536,128]{1,0:T(8,128)(2,1)S(1)}, bf16[1536,128]{1,0:T(8,128)(2,1)S(1)}, u32[]{:S(2)}, u32[]{:S(2)}) collective-permute-start(bf16[1536,128]{1,0:T(8,128)(2,1)S(1)} %get-tuple-element.65), channel_id=1, source_target_pairs={{12,0},{28,16},{44,32},{60,48},{76,64},{92,80},{108,96},{124,112}} | collective-permute-start | bytes 1179656 | tf_op jit(solution)/shard_map/ppermute | solution.py:30
  62.9 0.7 collective-permute-start.21
  63.5 34.6 %collective-permute-start.30 = (bf16[1792,256]{1,0:T(8,128)(2,1)S(1)}, bf16[1792,256]{1,0:T(8,128)(2,1)S(1)}, u32[]{:S(2)}, u32[]{:S(2)}) collective-permute-start(bf16[1792,256]{1,0:T(8,128)(2,1)S(1)} %collective-permute-done.18.rest_7_.rest_1_), channel_id=1, source_target_pairs={{0,96},{1,97},{2,98},{3,99},{4,100},{5,101},{6,102},{7,103},{8,104... | collective-permute-start | bytes 2752520 | tf_op jit(solution)/shard_map/ppermute | solution.py:30
  66.0 35.4 %collective-permute-start.28 = (bf16[1792,256]{1,0:T(8,128)(2,1)S(1)}, bf16[1792,256]{1,0:T(8,128)(2,1)S(1)}, u32[]{:S(2)}, u32[]{:S(2)}) collective-permute-start(bf16[1792,256]{1,0:T(8,128)(2,1)S(1)} %collective-permute-done.17.rest_6_.rest_3_), channel_id=1, source_target_pairs={{0,32},{1,33},{2,34},{3,35},{4,36},{5,37},{6,38},{7,39},{8,40},{9,... | collective-permute-start | bytes 2752520 | tf_op jit(solution)/shard_map/ppermute | solution.py:30
  78.0 7.0 %collective-permute-start.24 = (bf16[1536,128]{1,0:T(8,128)(2,1)S(1)}, bf16[1536,128]{1,0:T(8,128)(2,1)S(1)}, u32[]{:S(2)}, u32[]{:S(2)}) collective-permute-start(bf16[1536,128]{1,0:T(8,128)(2,1)S(1)} %shard_map.46.late), channel_id=1, source_target_pairs={{0,1},{4,5},{8,9},{12,13},{16,17},{20,21},{24,25},{28,29},{32,33},... | collective-permute-start | bytes 1179656 | tf_op jit(solution)/shard_map/ppermute | solution.py:30
  79.3 14.1 %collective-permute-start.25 = (bf16[1536,128]{1,0:T(8,128)(2,1)S(1)}, bf16[1536,128]{1,0:T(8,128)(2,1)S(1)}, u32[]{:S(2)}, u32[]{:S(2)}) collective-permute-start(bf16[1536,128]{1,0:T(8,128)(2,1)S(1)} %shard_map.46.late), channel_id=1, source_target_pairs={{0,2},{4,6},{8,10},{12,14},{16,18},{20,22},{24,26},{28,30},{32,34}... | collective-permute-start | bytes 1179656 | tf_op jit(solution)/shard_map/ppermute | solution.py:30
  80.6 12.7 %collective-permute-start.26 = (bf16[1536,128]{1,0:T(8,128)(2,1)S(1)}, bf16[1536,128]{1,0:T(8,128)(2,1)S(1)}, u32[]{:S(2)}, u32[]{:S(2)}) collective-permute-start(bf16[1536,128]{1,0:T(8,128)(2,1)S(1)} %shard_map.46.late), channel_id=1, source_target_pairs={{0,3},{4,7},{8,11},{12,15},{16,19},{20,23},{24,27},{28,31},{32,35}... | collective-permute-start | bytes 1179656 | tf_op jit(solution)/shard_map/ppermute | solution.py:30
  94.4 4.9 %collective-permute-start.27 = (bf16[1024,128]{1,0:T(8,128)(2,1)S(1)}, bf16[1024,128]{1,0:T(8,128)(2,1)S(1)}, u32[]{:S(2)}, u32[]{:S(2)}) collective-permute-start(bf16[1024,128]{1,0:T(8,128)(2,1)S(1)} %get-tuple-element.76), channel_id=1, source_target_pairs={{0,16},{1,17},{2,18},{3,19},{4,20},{5,21},{6,22},{7,23},{8,24},{9,... | collective-permute-start | bytes 786440 | tf_op jit(solution)/shard_map/ppermute | solution.py:30
  101.0 6.1 %collective-permute-start.31 = (bf16[1792,128]{1,0:T(8,128)(2,1)S(1)}, bf16[1792,128]{1,0:T(8,128)(2,1)S(1)}, u32[]{:S(2)}, u32[]{:S(2)}) collective-permute-start(bf16[1792,128]{1,0:T(8,128)(2,1)S(1)} %get-tuple-element.80), channel_id=1, source_target_pairs={{0,16},{1,17},{2,18},{3,19},{4,20},{5,21},{6,22},{7,23},{8,24},{9,... | collective-permute-start | bytes 1376264 | tf_op jit(solution)/shard_map/ppermute | solution.py:30
  103.2 3.9 %collective-permute-start.29 = (bf16[1792,128]{1,0:T(8,128)(2,1)S(1)}, bf16[1792,128]{1,0:T(8,128)(2,1)S(1)}, u32[]{:S(2)}, u32[]{:S(2)}) collective-permute-start(bf16[1792,128]{1,0:T(8,128)(2,1)S(1)} %get-tuple-element.78), channel_id=1, source_target_pairs={{0,16},{1,17},{2,18},{3,19},{4,20},{5,21},{6,22},{7,23},{8,24},{9,... | collective-permute-start | bytes 1376264 | tf_op jit(solution)/shard_map/ppermute | solution.py:30
  103.4 3.7 %copy-start = (f32[4096,128]{1,0:T(8,128)S(1)}, f32[4096,128]{1,0:T(8,128)}, u32[]{:S(2)}) copy-start(f32[4096,128]{1,0:T(8,128)} %b_ref.5) | copy-start | bytes 6291460

commit v10 on v9

--- a/solution.py
+++ b/solution.py
@@ -325,15 +325,14 @@
     y0 = call(combine_kernel, ids, (yb0, *hops), [vspec] * 4, bf(NB))
     early = [send(y0, y_move(t)) for t in (1, 2, 3)]
     top, bottom = call(
-        hold_kernel, ids, (own_t, own_b, *early, window[5]), [whole((half, HB))] * 2 + [ANY] * 4, (bf(half, HB),) * 2
+        hold_kernel, ids, (own_t, own_b, *hops), [whole((half, HB))] * 2 + [ANY] * 3, (bf(half, HB),) * 2
     )
     before_t, after_b = send(top, x_plus), send(bottom, x_minus)
     far_t, far_b = send(before_t, x_plus), send(after_b, x_minus)
-    _, w0, y_own, yb1 = forward(0, in_hbm(rhs), first, y0, y_z0, ())
+    _, w0, y_own, yb1 = forward(0, in_hbm(rhs), first, y0, y_z0, (), early)
     hops = [send(yb1, z_move(1, 2))]
     _, _, y_own, y12 = forward(1, w0, vspec, yb1, y_own, hops)
     y12_in = send(y12, z_move(2, 3))
-    top, bottom = call(hold_kernel, ids, (own_t, own_b, y12_in), [whole((half, HB))] * 2 + [ANY], (bf(half, HB),) * 2)
     before_b, after_t = send(bottom, x_plus), send(top, x_minus)
     p23, p1 = call(relay_kernel, ids, (p23, p1, y12), [whole((NB, HB)), mspec, ANY], (bf(NB, HB), bf(NB, 2 * HB)))
     p23_other, p1_other = send(p23, other_core), send(p1, other_core)

time: 111 us -> 116 us (1.045)
  waiting for transfers between devices: 35.6 us -> 47.6 us
  starting transfers between devices: 45.7 us -> 40.2 us
    ppermute x32, waiting for transfers between devices: 35.6 us -> 47.6 us  [send(): return lax.ppermute(value, ('row', 'col'), pairs(move))]
    ppermute x32, starting transfers between devices: 45.7 us -> 40.2 us  [send(): return lax.ppermute(value, ('row', 'col'), pairs(move))]
    pallas_call x15 -> x14, Pallas kernels: 26.7 us -> 26 us  [call(): pl.pallas_call(kernel, grid_spec=pltpu.PrefetchScalarGridSpec(num_scalar_...]
  transfers between devices with their start and end apart: 32 -> 32, of which waited for: 10 -> 9; matrix products, arithmetic and copies ran while one was open for 0% -> 0% of each run, Pallas kernels for 22% -> 17%
where the time goes in v10:
time: 116 us; the launch traced here: 115 us
  waiting for transfers between devices  47.6 us (41%)
  starting transfers between devices  40.2 us (35%)
  Pallas kernels  26 us (22%)
    ppermute x32, waiting for transfers between devices, send(): return lax.ppermute(value, ('row', 'col'), pairs(move))  47.6 us
    ppermute x32, starting transfers between devices, send(): return lax.ppermute(value, ('row', 'col'), pairs(move))  40.2 us
    pallas_call x14, Pallas kernels, call(): pl.pallas_call(kernel, grid_spec=pltpu.PrefetchScalarGridSpec(num_scalar_...  26 us
  transfers between devices with their start and end apart: 32, of which 9 were waited for; matrix products, arithmetic and copies ran while one was open for 0% of the time, Pallas kernels for 17%

profile of v10, /device:TPU:1, one launch (start us, length us, event | category | flops | bytes accessed | tf_op | source)
XLA Modules:
  0.0 115.4 jit_solution(6461431807218762307)
XLA Ops:
  0.0 1.0 slice.9.after_ref.b0.rest_0_
  1.0 0.1 pad_add_fusion.ids
  1.1 3.7 %shard_map.37 = (f32[512,128]{1,0:T(8,128)S(1)}, bf16[512,128]{1,0:T(8,128)(2,1)S(1)}, bf16[512,512]{1,0:T(8,128)(2,1)S(1)}, bf16[512,512]{1,0:T(8,128)(2,1)S(1)...) custom-call(s32[4]{0:T(128)S(1)} %pad_add_fusion.ids, ...), custom_call_target="tpu_custom_call" | custom-call | flops 1 | bytes 1 | tf_op jit(solution)/shard_map/pallas_call | solution.py:276
  4.8 4.4 %collective-permute-start = (bf16[512,128]{1,0:T(8,128)(2,1)S(1)}, bf16[512,128]{1,0:T(8,128)(2,1)S(1)}, u32[]{:S(2)}, u32[]{:S(2)}) collective-permute-start(bf16[512,128]{1,0:T(8,128)(2,1)S(1)} %get-tuple-element.41.own_ref), channel_id=1, source_target_pairs={{0,4},{16,20},{32,36},{48,52},{64,68},{80,84},{96,100},{112,116}} | collective-permute-start | bytes 393224 | tf_op jit(solution)/shard_map/ppermute | solution.py:30
  9.1 2.5 %collective-permute-start.6 = (bf16[512,256]{1,0:T(8,128)(2,1)S(1)}, bf16[512,256]{1,0:T(8,128)(2,1)S(1)}, u32[]{:S(2)}, u32[]{:S(2)}) collective-permute-start(bf16[512,256]{1,0:T(8,128)(2,1)S(1)} %slice.9.after_ref.b0.rest_0_), channel_id=1, source_target_pairs={{0,96},{1,97},{2,98},{3,99},{4,100},{5,101},{6,102},{7,103},{8,104... | collective-permute-start | bytes 786440 | tf_op jit(solution)/shard_map/ppermute | solution.py:30
  11.7 0.5 collective-permute-start.7
  12.2 0.6 collective-permute-start.8
  12.8 2.6 %collective-permute-start.1 = (bf16[512,128]{1,0:T(8,128)(2,1)S(1)}, bf16[512,128]{1,0:T(8,128)(2,1)S(1)}, u32[]{:S(2)}, u32[]{:S(2)}) collective-permute-start(bf16[512,128]{1,0:T(8,128)(2,1)S(1)} %get-tuple-element.41.own_ref), channel_id=1, source_target_pairs={{0,8},{16,24},{32,40},{48,56},{64,72},{80,88},{96,104},{112,120}} | collective-permute-start | bytes 393224 | tf_op jit(solution)/shard_map/ppermute | solution.py:30
  15.4 0.0 collective-permute-done.r1.rest_0_
  15.5 1.3 %collective-permute-start.2 = (bf16[512,128]{1,0:T(8,128)(2,1)S(1)}, bf16[512,128]{1,0:T(8,128)(2,1)S(1)}, u32[]{:S(2)}, u32[]{:S(2)}) collective-permute-start(bf16[512,128]{1,0:T(8,128)(2,1)S(1)} %get-tuple-element.41.own_ref), channel_id=1, source_target_pairs={{0,12},{16,28},{32,44},{48,60},{64,76},{80,92},{96,108},{112,124}} | collective-permute-start | bytes 393224 | tf_op jit(solution)/shard_map/ppermute | solution.py:30
  16.8 0.6 collective-permute-done.1.r2.rest_1_
  17.4 2.4 %collective-permute-start.9 = (bf16[512,256]{1,0:T(8,128)(2,1)S(1)}, bf16[512,256]{1,0:T(8,128)(2,1)S(1)}, u32[]{:S(2)}, u32[]{:S(2)}) collective-permute-start(bf16[512,256]{1,0:T(8,128)(2,1)S(1)} %slice.9.after_ref.b0.rest_0_), channel_id=1, source_target_pairs={{0,16},{1,17},{2,18},{3,19},{4,20},{5,21},{6,22},{7,23},{8,24},{9,... | collective-permute-start | bytes 786440 | tf_op jit(solution)/shard_map/ppermute | solution.py:30
  19.7 0.0 collective-permute-done.2.r3.rest_2_
  19.7 0.6 shard_map.38.own_ref.v0
  20.4 1.3 %collective-permute-start.3 = (bf16[512,128]{1,0:T(8,128)(2,1)S(1)}, bf16[512,128]{1,0:T(8,128)(2,1)S(1)}, u32[]{:S(2)}, u32[]{:S(2)}) collective-permute-start(bf16[512,128]{1,0:T(8,128)(2,1)S(1)} %shard_map.38.own_ref.v0), channel_id=1, source_target_pairs={{0,1},{4,5},{8,9},{12,13},{16,17},{20,21},{24,25},{28,29},{32,33},... | collective-permute-start | bytes 393224 | tf_op jit(solution)/shard_map/ppermute | solution.py:30
  21.7 1.3 %collective-permute-start.4 = (bf16[512,128]{1,0:T(8,128)(2,1)S(1)}, bf16[512,128]{1,0:T(8,128)(2,1)S(1)}, u32[]{:S(2)}, u32[]{:S(2)}) collective-permute-start(bf16[512,128]{1,0:T(8,128)(2,1)S(1)} %shard_map.38.own_ref.v0), channel_id=1, source_target_pairs={{0,2},{4,6},{8,10},{12,14},{16,18},{20,22},{24,26},{28,30},{32,34}... | collective-permute-start | bytes 393224 | tf_op jit(solution)/shard_map/ppermute | solution.py:30
  23.0 0.0 collective-permute-done.7.b2.rest_2_
  23.0 4.1 %collective-permute-done.8.b3.rest_3_ = bf16[512,256]{1,0:T(8,128)(2,1)S(1)} collective-permute-done((bf16[512,256]{1,0:T(8,128)(2,1)S(1)}, bf16[512,256]{1,0:T(8,128)(2,1)S(1)}, u32[]{:S(2)}, u32[]{:S(2)}) %collective-permute-start.8) | collective-permute-done | bytes 262176 | tf_op jit(solution)/shard_map/ppermute | solution.py:30
  27.0 0.7 shard_map.39
  27.8 0.6 collective-permute-start.10
  28.3 0.1 fusion
  28.5 1.8 %collective-permute-start.5 = (bf16[512,128]{1,0:T(8,128)(2,1)S(1)}, bf16[512,128]{1,0:T(8,128)(2,1)S(1)}, u32[]{:S(2)}, u32[]{:S(2)}) collective-permute-start(bf16[512,128]{1,0:T(8,128)(2,1)S(1)} %shard_map.38.own_ref.v0), channel_id=1, source_target_pairs={{0,3},{4,7},{8,11},{12,15},{16,19},{20,23},{24,27},{28,31},{32,35}... | collective-permute-start | bytes 393224 | tf_op jit(solution)/shard_map/ppermute | solution.py:30
  30.2 0.7 shard_map.43
  30.9 0.1 collective-permute-start.17
  31.0 2.7 %collective-permute-start.18 = (bf16[1792,256]{1,0:T(8,128)(2,1)S(1)}, bf16[1792,256]{1,0:T(8,128)(2,1)S(1)}, u32[]{:S(2)}, u32[]{:S(2)}) collective-permute-start(bf16[1792,256]{1,0:T(8,128)(2,1)S(1)} %get-tuple-element.62), channel_id=1, source_target_pairs={{0,96},{1,97},{2,98},{3,99},{4,100},{5,101},{6,102},{7,103},{8,104... | collective-permute-start | bytes 2752520 | tf_op jit(solution)/shard_map/ppermute | solution.py:30
  33.7 0.0 collective-permute-done.5.rest_8_.e3
  33.7 0.7 collective-permute-start.14
  34.4 0.7 collective-permute-start.13
  35.1 0.0 collective-permute-done.10.rest_5_
  35.1 2.7 %shard_map.40 = (bf16[512,128]{1,0:T(8,128)(2,1)}, f32[512,128]{1,0:T(8,128)S(1)}, f32[512,128]{1,0:T(8,128)S(1)}, bf16[512,128]{1,0:T(8,128)(2,1)S(1)}) custom-call(s32[4]{0:T(128)S(1)} %pad_add_fusion.ids, f32[4096,128]{1,0:T(8,128)} %b_ref.5, bf16[512,128]{1,0:T(8,128)(2,1)S(1)} %shard_map.38.own_ref.v0, f32[512,128]{1,0:T(8,128)S(1)} %get-tuple-element.42.prior_ref, ...), custom_call_target="tpu_custom_call" | custom-call | flops 1 | bytes 1 | tf_op jit(solution)/shard_map/pallas_call | solution.py:276
  37.8 0.7 collective-permute-start.11
  38.5 0.1 collective-permute-start.22
  38.6 2.7 %collective-permute-start.23 = (bf16[1792,256]{1,0:T(8,128)(2,1)S(1)}, bf16[1792,256]{1,0:T(8,128)(2,1)S(1)}, u32[]{:S(2)}, u32[]{:S(2)}) collective-permute-start(bf16[1792,256]{1,0:T(8,128)(2,1)S(1)} %get-tuple-element.61), channel_id=1, source_target_pairs={{0,96},{1,97},{2,98},{3,99},{4,100},{5,101},{6,102},{7,103},{8,104... | collective-permute-start | bytes 2752520 | tf_op jit(solution)/shard_map/ppermute | solution.py:30
  41.2 1.9 %shard_map.41 = (bf16[512,128]{1,0:T(8,128)(2,1)}, f32[512,128]{1,0:T(8,128)}, f32[512,128]{1,0:T(8,128)S(1)}, bf16[1024,128]{1,0:T(8,128)(2,1)S(1)}) custom-call(s32[4]{0:T(128)S(1)} %pad_add_fusion.ids, f32[512,128]{1,0:T(8,128)S(1)} %get-tuple-element.46.w_ref, bf16[512,128]{1,0:T(8,128)(2,1)S(1)} %get-tuple-element.47.own_ref, ...), custom_call_target="tpu_custom_call" | custom-call | flops 1 | bytes 1 | tf_op jit(solution)/shard_map/pallas_call | solution.py:276
  43.1 0.0 collective-permute-done.14.p1_ref
  43.1 0.6 shard_map.42
  43.7 1.5 %collective-permute-start.16 = (bf16[512,512]{1,0:T(8,128)(2,1)S(1)}, bf16[512,512]{1,0:T(8,128)(2,1)S(1)}, u32[]{:S(2)}, u32[]{:S(2)}) collective-permute-start(bf16[512,512]{1,0:T(8,128)(2,1)S(1)} %get-tuple-element.60.p1), channel_id=1, source_target_pairs={{0,16},{1,17},{2,18},{3,19},{4,20},{5,21},{6,22},{7,23},{8,24},{9,... | collective-permute-start | bytes 1572872 | tf_op jit(solution)/shard_map/ppermute | solution.py:30
  45.2 8.6 %collective-permute-done.17.rest_6_.rest_3_ = bf16[1792,256]{1,0:T(8,128)(2,1)S(1)} collective-permute-done((bf16[1792,256]{1,0:T(8,128)(2,1)S(1)}, bf16[1792,256]{1,0:T(8,128)(2,1)S(1)}, u32[]{:S(2)}, u32[]{:S(2)}) %collective-permute-start.17) | collective-permute-done | bytes 917536 | tf_op jit(solution)/shard_map/ppermute | solution.py:30
  53.8 1.9 %collective-permute-start.15 = (bf16[512,256]{1,0:T(8,128)(2,1)S(1)}, bf16[512,256]{1,0:T(8,128)(2,1)S(1)}, u32[]{:S(2)}, u32[]{:S(2)}) collective-permute-start(bf16[512,256]{1,0:T(8,128)(2,1)S(1)} %get-tuple-element.59.p23), channel_id=1, source_target_pairs={{0,16},{1,17},{2,18},{3,19},{4,20},{5,21},{6,22},{7,23},{8,24},{9,... | collective-permute-start | bytes 786440 | tf_op jit(solution)/shard_map/ppermute | solution.py:30
  55.7 0.0 collective-permute-done.18.rest_7_.rest_1_
  55.7 0.7 collective-permute-start.12
  56.4 0.5 collective-permute-done.15.p23_other
  56.9 4.0 %shard_map.44 = (bf16[512,128]{1,0:T(8,128)(2,1)S(1)}, bf16[512,128]{1,0:T(8,128)(2,1)S(1)}, f32[512,128]{1,0:T(8,128)S(1)}, bf16[512,128]{1,0:T(8,128)(2,1)S(1)...) custom-call(s32[4]{0:T(128)S(1)} %pad_add_fusion.ids, ...), custom_call_target="tpu_custom_call" | custom-call | flops 1 | bytes 1 | tf_op jit(solution)/shard_map/pallas_call | solution.py:276
  60.8 1.3 %collective-permute-start.19 = (bf16[1536,128]{1,0:T(8,128)(2,1)S(1)}, bf16[1536,128]{1,0:T(8,128)(2,1)S(1)}, u32[]{:S(2)}, u32[]{:S(2)}) collective-permute-start(bf16[1536,128]{1,0:T(8,128)(2,1)S(1)} %get-tuple-element.63), channel_id=1, source_target_pairs={{12,0},{28,16},{44,32},{60,48},{76,64},{92,80},{108,96},{124,112}} | collective-permute-start | bytes 1179656 | tf_op jit(solution)/shard_map/ppermute | solution.py:30
  62.1 0.7 collective-permute-start.20
  62.8 0.1 collective-permute-start.30
  62.9 10.6 %collective-permute-done.22.rest_0_.rest_3_ = bf16[1792,256]{1,0:T(8,128)(2,1)S(1)} collective-permute-done((bf16[1792,256]{1,0:T(8,128)(2,1)S(1)}, bf16[1792,256]{1,0:T(8,128)(2,1)S(1)}, u32[]{:S(2)}, u32[]{:S(2)}) %collective-permute-start.22) | collective-permute-done | bytes 917536 | tf_op jit(solution)/shard_map/ppermute | solution.py:30
  73.5 0.7 collective-permute-start.21
  74.2 9.0 %collective-permute-done.19.to0 = bf16[1536,128]{1,0:T(8,128)(2,1)S(1)} collective-permute-done((bf16[1536,128]{1,0:T(8,128)(2,1)S(1)}, bf16[1536,128]{1,0:T(8,128)(2,1)S(1)}, u32[]{:S(2)}, u32[]{:S(2)}) %collective-permute-start.19) | collective-permute-done | bytes 393248 | tf_op jit(solution)/shard_map/ppermute | solution.py:30
  83.2 0.7 shard_map.45.late
  83.9 1.3 %collective-permute-start.24 = (bf16[1536,128]{1,0:T(8,128)(2,1)S(1)}, bf16[1536,128]{1,0:T(8,128)(2,1)S(1)}, u32[]{:S(2)}, u32[]{:S(2)}) collective-permute-start(bf16[1536,128]{1,0:T(8,128)(2,1)S(1)} %shard_map.45.late), channel_id=1, source_target_pairs={{0,1},{4,5},{8,9},{12,13},{16,17},{20,21},{24,25},{28,29},{32,33},... | collective-permute-start | bytes 1179656 | tf_op jit(solution)/shard_map/ppermute | solution.py:30
  85.2 1.3 %collective-permute-start.25 = (bf16[1536,128]{1,0:T(8,128)(2,1)S(1)}, bf16[1536,128]{1,0:T(8,128)(2,1)S(1)}, u32[]{:S(2)}, u32[]{:S(2)}) collective-permute-start(bf16[1536,128]{1,0:T(8,128)(2,1)S(1)} %shard_map.45.late), channel_id=1, source_target_pairs={{0,2},{4,6},{8,10},{12,14},{16,18},{20,22},{24,26},{28,30},{32,34}... | collective-permute-start | bytes 1179656 | tf_op jit(solution)/shard_map/ppermute | solution.py:30
  86.5 1.3 %collective-permute-start.26 = (bf16[1536,128]{1,0:T(8,128)(2,1)S(1)}, bf16[1536,128]{1,0:T(8,128)(2,1)S(1)}, u32[]{:S(2)}, u32[]{:S(2)}) collective-permute-start(bf16[1536,128]{1,0:T(8,128)(2,1)S(1)} %shard_map.45.late), channel_id=1, source_target_pairs={{0,3},{4,7},{8,11},{12,15},{16,19},{20,23},{24,27},{28,31},{32,35}... | collective-permute-start | bytes 1179656 | tf_op jit(solution)/shard_map/ppermute | solution.py:30
  87.9 4.6 %collective-permute-done.24.s1 = bf16[1536,128]{1,0:T(8,128)(2,1)S(1)} collective-permute-done((bf16[1536,128]{1,0:T(8,128)(2,1)S(1)}, bf16[1536,128]{1,0:T(8,128)(2,1)S(1)}, u32[]{:S(2)}, u32[]{:S(2)}) %collective-permute-start.24) | collective-permute-done | bytes 393248 | tf_op jit(solution)/shard_map/ppermute | solution.py:30
  92.5 8.4 %collective-permute-done.25.s2 = bf16[1536,128]{1,0:T(8,128)(2,1)S(1)} collective-permute-done((bf16[1536,128]{1,0:T(8,128)(2,1)S(1)}, bf16[1536,128]{1,0:T(8,128)(2,1)S(1)}, u32[]{:S(2)}, u32[]{:S(2)}) %collective-permute-start.25) | collective-permute-done | bytes 393248 | tf_op jit(solution)/shard_map/ppermute | solution.py:30
  100.9 1.0 shard_map.46
  102.0 2.1 %collective-permute-start.27 = (bf16[1024,128]{1,0:T(8,128)(2,1)S(1)}, bf16[1024,128]{1,0:T(8,128)(2,1)S(1)}, u32[]{:S(2)}, u32[]{:S(2)}) collective-permute-start(bf16[1024,128]{1,0:T(8,128)(2,1)S(1)} %get-tuple-element.72), channel_id=1, source_target_pairs={{0,16},{1,17},{2,18},{3,19},{4,20},{5,21},{6,22},{7,23},{8,24},{9,... | collective-permute-start | bytes 786440 | tf_op jit(solution)/shard_map/ppermute | solution.py:30
  104.0 1.2 %collective-permute-done.27.other_ref = bf16[1024,128]{1,0:T(8,128)(2,1)S(1)} collective-permute-done((bf16[1024,128]{1,0:T(8,128)(2,1)S(1)}, bf16[1024,128]{1,0:T(8,128)(2,1)S(1)}, u32[]{:S(2)}, u32[]{:S(2)}) %collective-permute-start.27) | collective-permute-done | bytes 262176 | tf_op jit(solution)/shard_map/ppermute | solution.py:30
  105.2 1.7 %shard_map.49 = (f32[1792,128]{1,0:T(8,128)S(1)}, bf16[1792,128]{1,0:T(8,128)(2,1)S(1)}) custom-call(s32[4]{0:T(128)S(1)} %pad_add_fusion.ids, bf16[1024,128]{1,0:T(8,128)(2,1)S(1)} %get-tuple-element.71.mine_ref, bf16[1024,128]{1,0:T(8,128)(2,1)S(1)} %collective-permute-done.27.other_ref, bf16[1792,256]{1,0:T(8,128)(2,1)S(1)} %get-tuple-element.77.bottom.rest_0_, ...), custom_call_target="tpu_custom_call" | custom-call | flops 1 | bytes 1 | tf_op jit(solution)/shard_map/pallas_call | solution.py:276
  107.0 0.5 collective-permute-start.31
  107.4 1.7 %shard_map.48 = (f32[1792,128]{1,0:T(8,128)S(1)}, bf16[1792,128]{1,0:T(8,128)(2,1)S(1)}) custom-call(s32[4]{0:T(128)S(1)} %pad_add_fusion.ids, bf16[1024,128]{1,0:T(8,128)(2,1)S(1)} %get-tuple-element.71.mine_ref, bf16[1024,128]{1,0:T(8,128)(2,1)S(1)} %collective-permute-done.27.other_ref, bf16[1792,256]{1,0:T(8,128)(2,1)S(1)} %get-tuple-element.78.top.rest_0_, ...), custom_call_target="tpu_custom_call" | custom-call | flops 1 | bytes 1 | tf_op jit(solution)/shard_map/pallas_call | solution.py:276
  109.2 0.2 collective-permute-start.29
  109.4 3.7 %shard_map.47.out_in = f32[4096,128]{1,0:T(8,128)} custom-call(s32[4]{0:T(128)S(1)} %pad_add_fusion.ids, f32[4096,128]{1,0:T(8,128)} %b_ref.5, bf16[2048,128]{1,0:T(8,128)(2,1)S(1)} %get-tuple-element.69.v_ref, f32[512,128]{1,0:T(8,128)S(1)} %get-tuple-element.70.own_ref, bf16[512,512]{1,0:T(8,128)(2,1)S(1)} %get-tuple-element.51.u3h.uh_ref, ...), custom_call_target="tpu_custom_call" | custom-call | flops 1 | bytes 1 | tf_op jit(solution)/shard_map/pallas_call | solution.py:276
  113.1 2.4 %shard_map.50 = f32[4096,128]{1,0:T(8,128)} custom-call(s32[4]{0:T(128)S(1)} %pad_add_fusion.ids, f32[4096,128]{1,0:T(8,128)} %shard_map.47.out_in, f32[4096,128]{1,0:T(8,128)S(1)} %copy-done, f32[1792,128]{1,0:T(8,128)S(1)} %get-tuple-element.73.own_t, bf16[1792,128]{1,0:T(8,128)(2,1)S(1)} %collective-permute-done.29.part_t, ...), custom_call_target="tpu_custom_call", output_to_operand_aliasing={{}: (1, {})} | custom-call | flops 1 | bytes 1 | tf_op jit(solution)/shard_map/pallas_call | solution.py:276
  (21 shorter events, 0.1 us)
Async XLA Ops:
  1.1 27.3 %copy-start.1 = (bf16[4096,256]{1,0:T(8,128)(2,1)S(1)}, bf16[4096,256]{1,0:T(8,128)(2,1)}, u32[]{:S(2)}) copy-start(bf16[4096,256]{1,0:T(8,128)(2,1)} %param.4) | copy-start | bytes 6291460
  4.8 10.7 %collective-permute-start = (bf16[512,128]{1,0:T(8,128)(2,1)S(1)}, bf16[512,128]{1,0:T(8,128)(2,1)S(1)}, u32[]{:S(2)}, u32[]{:S(2)}) collective-permute-start(bf16[512,128]{1,0:T(8,128)(2,1)S(1)} %get-tuple-element.41.own_ref), channel_id=1, source_target_pairs={{0,4},{16,20},{32,36},{48,52},{64,68},{80,84},{96,100},{112,116}} | collective-permute-start | bytes 393224 | tf_op jit(solution)/shard_map/ppermute | solution.py:30
  9.1 12.5 %collective-permute-start.6 = (bf16[512,256]{1,0:T(8,128)(2,1)S(1)}, bf16[512,256]{1,0:T(8,128)(2,1)S(1)}, u32[]{:S(2)}, u32[]{:S(2)}) collective-permute-start(bf16[512,256]{1,0:T(8,128)(2,1)S(1)} %slice.9.after_ref.b0.rest_0_), channel_id=1, source_target_pairs={{0,96},{1,97},{2,98},{3,99},{4,100},{5,101},{6,102},{7,103},{8,104... | collective-permute-start | bytes 786440 | tf_op jit(solution)/shard_map/ppermute | solution.py:30
  11.7 11.3 %collective-permute-start.7 = (bf16[512,256]{1,0:T(8,128)(2,1)S(1)}, bf16[512,256]{1,0:T(8,128)(2,1)S(1)}, u32[]{:S(2)}, u32[]{:S(2)}) collective-permute-start(bf16[512,256]{1,0:T(8,128)(2,1)S(1)} %slice.9.after_ref.b0.rest_0_), channel_id=1, source_target_pairs={{0,64},{1,65},{2,66},{3,67},{4,68},{5,69},{6,70},{7,71},{8,72},{9,... | collective-permute-start | bytes 786440 | tf_op jit(solution)/shard_map/ppermute | solution.py:30
  12.2 14.8 %collective-permute-start.8 = (bf16[512,256]{1,0:T(8,128)(2,1)S(1)}, bf16[512,256]{1,0:T(8,128)(2,1)S(1)}, u32[]{:S(2)}, u32[]{:S(2)}) collective-permute-start(bf16[512,256]{1,0:T(8,128)(2,1)S(1)} %slice.9.after_ref.b0.rest_0_), channel_id=1, source_target_pairs={{0,32},{1,33},{2,34},{3,35},{4,36},{5,37},{6,38},{7,39},{8,40},{9,... | collective-permute-start | bytes 786440 | tf_op jit(solution)/shard_map/ppermute | solution.py:30
  12.8 4.5 %collective-permute-start.1 = (bf16[512,128]{1,0:T(8,128)(2,1)S(1)}, bf16[512,128]{1,0:T(8,128)(2,1)S(1)}, u32[]{:S(2)}, u32[]{:S(2)}) collective-permute-start(bf16[512,128]{1,0:T(8,128)(2,1)S(1)} %get-tuple-element.41.own_ref), channel_id=1, source_target_pairs={{0,8},{16,24},{32,40},{48,56},{64,72},{80,88},{96,104},{112,120}} | collective-permute-start | bytes 393224 | tf_op jit(solution)/shard_map/ppermute | solution.py:30
  15.5 4.3 %collective-permute-start.2 = (bf16[512,128]{1,0:T(8,128)(2,1)S(1)}, bf16[512,128]{1,0:T(8,128)(2,1)S(1)}, u32[]{:S(2)}, u32[]{:S(2)}) collective-permute-start(bf16[512,128]{1,0:T(8,128)(2,1)S(1)} %get-tuple-element.41.own_ref), channel_id=1, source_target_pairs={{0,12},{16,28},{32,44},{48,60},{64,76},{80,92},{96,108},{112,124}} | collective-permute-start | bytes 393224 | tf_op jit(solution)/shard_map/ppermute | solution.py:30
  17.4 17.0 %collective-permute-start.9 = (bf16[512,256]{1,0:T(8,128)(2,1)S(1)}, bf16[512,256]{1,0:T(8,128)(2,1)S(1)}, u32[]{:S(2)}, u32[]{:S(2)}) collective-permute-start(bf16[512,256]{1,0:T(8,128)(2,1)S(1)} %slice.9.after_ref.b0.rest_0_), channel_id=1, source_target_pairs={{0,16},{1,17},{2,18},{3,19},{4,20},{5,21},{6,22},{7,23},{8,24},{9,... | collective-permute-start | bytes 786440 | tf_op jit(solution)/shard_map/ppermute | solution.py:30
  20.4 10.6 %collective-permute-start.3 = (bf16[512,128]{1,0:T(8,128)(2,1)S(1)}, bf16[512,128]{1,0:T(8,128)(2,1)S(1)}, u32[]{:S(2)}, u32[]{:S(2)}) collective-permute-start(bf16[512,128]{1,0:T(8,128)(2,1)S(1)} %shard_map.38.own_ref.v0), channel_id=1, source_target_pairs={{0,1},{4,5},{8,9},{12,13},{16,17},{20,21},{24,25},{28,29},{32,33},... | collective-permute-start | bytes 393224 | tf_op jit(solution)/shard_map/ppermute | solution.py:30
  21.7 9.3 %collective-permute-start.4 = (bf16[512,128]{1,0:T(8,128)(2,1)S(1)}, bf16[512,128]{1,0:T(8,128)(2,1)S(1)}, u32[]{:S(2)}, u32[]{:S(2)}) collective-permute-start(bf16[512,128]{1,0:T(8,128)(2,1)S(1)} %shard_map.38.own_ref.v0), channel_id=1, source_target_pairs={{0,2},{4,6},{8,10},{12,14},{16,18},{20,22},{24,26},{28,30},{32,34}... | collective-permute-start | bytes 393224 | tf_op jit(solution)/shard_map/ppermute | solution.py:30
  27.8 7.3 %collective-permute-start.10 = (bf16[1536,256]{1,0:T(8,128)(2,1)S(1)}, bf16[1536,256]{1,0:T(8,128)(2,1)S(1)}, u32[]{:S(2)}, u32[]{:S(2)}) collective-permute-start(bf16[1536,256]{1,0:T(8,128)(2,1)S(1)} %get-tuple-element.45), channel_id=1, source_target_pairs={{0,16},{1,17},{2,18},{3,19},{4,20},{5,21},{6,22},{7,23},{8,24},{9,... | collective-permute-start | bytes 2359304 | tf_op jit(solution)/shard_map/ppermute | solution.py:30
  28.5 5.2 %collective-permute-start.5 = (bf16[512,128]{1,0:T(8,128)(2,1)S(1)}, bf16[512,128]{1,0:T(8,128)(2,1)S(1)}, u32[]{:S(2)}, u32[]{:S(2)}) collective-permute-start(bf16[512,128]{1,0:T(8,128)(2,1)S(1)} %shard_map.38.own_ref.v0), channel_id=1, source_target_pairs={{0,3},{4,7},{8,11},{12,15},{16,19},{20,23},{24,27},{28,31},{32,35}... | collective-permute-start | bytes 393224 | tf_op jit(solution)/shard_map/ppermute | solution.py:30
  30.9 22.9 %collective-permute-start.17 = (bf16[1792,256]{1,0:T(8,128)(2,1)S(1)}, bf16[1792,256]{1,0:T(8,128)(2,1)S(1)}, u32[]{:S(2)}, u32[]{:S(2)}) collective-permute-start(bf16[1792,256]{1,0:T(8,128)(2,1)S(1)} %get-tuple-element.61), channel_id=1, source_target_pairs={{0,32},{1,33},{2,34},{3,35},{4,36},{5,37},{6,38},{7,39},{8,40},{9,... | collective-permute-start | bytes 2752520 | tf_op jit(solution)/shard_map/ppermute | solution.py:30
  31.0 24.7 %collective-permute-start.18 = (bf16[1792,256]{1,0:T(8,128)(2,1)S(1)}, bf16[1792,256]{1,0:T(8,128)(2,1)S(1)}, u32[]{:S(2)}, u32[]{:S(2)}) collective-permute-start(bf16[1792,256]{1,0:T(8,128)(2,1)S(1)} %get-tuple-element.62), channel_id=1, source_target_pairs={{0,96},{1,97},{2,98},{3,99},{4,100},{5,101},{6,102},{7,103},{8,104... | collective-permute-start | bytes 2752520 | tf_op jit(solution)/shard_map/ppermute | solution.py:30
  33.7 9.4 %collective-permute-start.14 = (bf16[512,512]{1,0:T(8,128)(2,1)S(1)}, bf16[512,512]{1,0:T(8,128)(2,1)S(1)}, u32[]{:S(2)}, u32[]{:S(2)}) collective-permute-start(bf16[512,512]{1,0:T(8,128)(2,1)S(1)} %get-tuple-element.58), channel_id=1, source_target_pairs={{4,12},{20,28},{36,44},{52,60},{68,76},{84,92},{100,108},{116,124}} | collective-permute-start | bytes 1572872 | tf_op jit(solution)/shard_map/ppermute | solution.py:30
  34.4 4.1 %collective-permute-start.13 = (bf16[512,256]{1,0:T(8,128)(2,1)S(1)}, bf16[512,256]{1,0:T(8,128)(2,1)S(1)}, u32[]{:S(2)}, u32[]{:S(2)}) collective-permute-start(bf16[512,256]{1,0:T(8,128)(2,1)S(1)} %get-tuple-element.57), channel_id=1, source_target_pairs={{8,12},{24,28},{40,44},{56,60},{72,76},{88,92},{104,108},{120,124}} | collective-permute-start | bytes 786440 | tf_op jit(solution)/shard_map/ppermute | solution.py:30
  37.8 0.8 collective-permute-start.11
  38.5 35.0 %collective-permute-start.22 = (bf16[1792,256]{1,0:T(8,128)(2,1)S(1)}, bf16[1792,256]{1,0:T(8,128)(2,1)S(1)}, u32[]{:S(2)}, u32[]{:S(2)}) collective-permute-start(bf16[1792,256]{1,0:T(8,128)(2,1)S(1)} %get-tuple-element.62), channel_id=1, source_target_pairs={{0,32},{1,33},{2,34},{3,35},{4,36},{5,37},{6,38},{7,39},{8,40},{9,... | collective-permute-start | bytes 2752520 | tf_op jit(solution)/shard_map/ppermute | solution.py:30
  38.6 34.9 %collective-permute-start.23 = (bf16[1792,256]{1,0:T(8,128)(2,1)S(1)}, bf16[1792,256]{1,0:T(8,128)(2,1)S(1)}, u32[]{:S(2)}, u32[]{:S(2)}) collective-permute-start(bf16[1792,256]{1,0:T(8,128)(2,1)S(1)} %get-tuple-element.61), channel_id=1, source_target_pairs={{0,96},{1,97},{2,98},{3,99},{4,100},{5,101},{6,102},{7,103},{8,104... | collective-permute-start | bytes 2752520 | tf_op jit(solution)/shard_map/ppermute | solution.py:30
  43.7 13.2 %collective-permute-start.16 = (bf16[512,512]{1,0:T(8,128)(2,1)S(1)}, bf16[512,512]{1,0:T(8,128)(2,1)S(1)}, u32[]{:S(2)}, u32[]{:S(2)}) collective-permute-start(bf16[512,512]{1,0:T(8,128)(2,1)S(1)} %get-tuple-element.60.p1), channel_id=1, source_target_pairs={{0,16},{1,17},{2,18},{3,19},{4,20},{5,21},{6,22},{7,23},{8,24},{9,... | collective-permute-start | bytes 1572872 | tf_op jit(solution)/shard_map/ppermute | solution.py:30
  53.8 3.0 %collective-permute-start.15 = (bf16[512,256]{1,0:T(8,128)(2,1)S(1)}, bf16[512,256]{1,0:T(8,128)(2,1)S(1)}, u32[]{:S(2)}, u32[]{:S(2)}) collective-permute-start(bf16[512,256]{1,0:T(8,128)(2,1)S(1)} %get-tuple-element.59.p23), channel_id=1, source_target_pairs={{0,16},{1,17},{2,18},{3,19},{4,20},{5,21},{6,22},{7,23},{8,24},{9,... | collective-permute-start | bytes 786440 | tf_op jit(solution)/shard_map/ppermute | solution.py:30
  55.7 1.2 %collective-permute-start.12 = (bf16[1024,128]{1,0:T(8,128)(2,1)S(1)}, bf16[1024,128]{1,0:T(8,128)(2,1)S(1)}, u32[]{:S(2)}, u32[]{:S(2)}) collective-permute-start(bf16[1024,128]{1,0:T(8,128)(2,1)S(1)} %get-tuple-element.49.after_ref.y12_ref), channel_id=1, source_target_pairs={{8,12},{24,28},{40,44},{56,60},{72,76},{88,92},{104,108},{120,124}} | collective-permute-start | bytes 786440 | tf_op jit(solution)/shard_map/ppermute | solution.py:30
  60.8 22.4 %collective-permute-start.19 = (bf16[1536,128]{1,0:T(8,128)(2,1)S(1)}, bf16[1536,128]{1,0:T(8,128)(2,1)S(1)}, u32[]{:S(2)}, u32[]{:S(2)}) collective-permute-start(bf16[1536,128]{1,0:T(8,128)(2,1)S(1)} %get-tuple-element.63), channel_id=1, source_target_pairs={{12,0},{28,16},{44,32},{60,48},{76,64},{92,80},{108,96},{124,112}} | collective-permute-start | bytes 1179656 | tf_op jit(solution)/shard_map/ppermute | solution.py:30
  62.1 12.1 %collective-permute-start.20 = (bf16[1024,128]{1,0:T(8,128)(2,1)S(1)}, bf16[1024,128]{1,0:T(8,128)(2,1)S(1)}, u32[]{:S(2)}, u32[]{:S(2)}) collective-permute-start(bf16[1024,128]{1,0:T(8,128)(2,1)S(1)} %get-tuple-element.64), channel_id=1, source_target_pairs={{12,4},{28,20},{44,36},{60,52},{76,68},{92,84},{108,100},{124,116}} | collective-permute-start | bytes 786440 | tf_op jit(solution)/shard_map/ppermute | solution.py:30
  62.8 41.2 %collective-permute-start.30 = (bf16[1792,256]{1,0:T(8,128)(2,1)S(1)}, bf16[1792,256]{1,0:T(8,128)(2,1)S(1)}, u32[]{:S(2)}, u32[]{:S(2)}) collective-permute-start(bf16[1792,256]{1,0:T(8,128)(2,1)S(1)} %collective-permute-done.18.rest_7_.rest_1_), channel_id=1, source_target_pairs={{0,96},{1,97},{2,98},{3,99},{4,100},{5,101},{6,102},{7,103},{8,104... | collective-permute-start | bytes 2752520 | tf_op jit(solution)/shard_map/ppermute | solution.py:30
  73.5 33.9 %collective-permute-start.28 = (bf16[1792,256]{1,0:T(8,128)(2,1)S(1)}, bf16[1792,256]{1,0:T(8,128)(2,1)S(1)}, u32[]{:S(2)}, u32[]{:S(2)}) collective-permute-start(bf16[1792,256]{1,0:T(8,128)(2,1)S(1)} %collective-permute-done.17.rest_6_.rest_3_), channel_id=1, source_target_pairs={{0,32},{1,33},{2,34},{3,35},{4,36},{5,37},{6,38},{7,39},{8,40},{9,... | collective-permute-start | bytes 2752520 | tf_op jit(solution)/shard_map/ppermute | solution.py:30
  73.5 0.7 collective-permute-start.21
  83.9 8.6 %collective-permute-start.24 = (bf16[1536,128]{1,0:T(8,128)(2,1)S(1)}, bf16[1536,128]{1,0:T(8,128)(2,1)S(1)}, u32[]{:S(2)}, u32[]{:S(2)}) collective-permute-start(bf16[1536,128]{1,0:T(8,128)(2,1)S(1)} %shard_map.45.late), channel_id=1, source_target_pairs={{0,1},{4,5},{8,9},{12,13},{16,17},{20,21},{24,25},{28,29},{32,33},... | collective-permute-start | bytes 1179656 | tf_op jit(solution)/shard_map/ppermute | solution.py:30
  85.2 15.7 %collective-permute-start.25 = (bf16[1536,128]{1,0:T(8,128)(2,1)S(1)}, bf16[1536,128]{1,0:T(8,128)(2,1)S(1)}, u32[]{:S(2)}, u32[]{:S(2)}) collective-permute-start(bf16[1536,128]{1,0:T(8,128)(2,1)S(1)} %shard_map.45.late), channel_id=1, source_target_pairs={{0,2},{4,6},{8,10},{12,14},{16,18},{20,22},{24,26},{28,30},{32,34}... | collective-permute-start | bytes 1179656 | tf_op jit(solution)/shard_map/ppermute | solution.py:30
  86.5 14.4 %collective-permute-start.26 = (bf16[1536,128]{1,0:T(8,128)(2,1)S(1)}, bf16[1536,128]{1,0:T(8,128)(2,1)S(1)}, u32[]{:S(2)}, u32[]{:S(2)}) collective-permute-start(bf16[1536,128]{1,0:T(8,128)(2,1)S(1)} %shard_map.45.late), channel_id=1, source_target_pairs={{0,3},{4,7},{8,11},{12,15},{16,19},{20,23},{24,27},{28,31},{32,35}... | collective-permute-start | bytes 1179656 | tf_op jit(solution)/shard_map/ppermute | solution.py:30
  102.0 3.2 %collective-permute-start.27 = (bf16[1024,128]{1,0:T(8,128)(2,1)S(1)}, bf16[1024,128]{1,0:T(8,128)(2,1)S(1)}, u32[]{:S(2)}, u32[]{:S(2)}) collective-permute-start(bf16[1024,128]{1,0:T(8,128)(2,1)S(1)} %get-tuple-element.72), channel_id=1, source_target_pairs={{0,16},{1,17},{2,18},{3,19},{4,20},{5,21},{6,22},{7,23},{8,24},{9,... | collective-permute-start | bytes 786440 | tf_op jit(solution)/shard_map/ppermute | solution.py:30
  107.0 6.1 %collective-permute-start.31 = (bf16[1792,128]{1,0:T(8,128)(2,1)S(1)}, bf16[1792,128]{1,0:T(8,128)(2,1)S(1)}, u32[]{:S(2)}, u32[]{:S(2)}) collective-permute-start(bf16[1792,128]{1,0:T(8,128)(2,1)S(1)} %get-tuple-element.76), channel_id=1, source_target_pairs={{0,16},{1,17},{2,18},{3,19},{4,20},{5,21},{6,22},{7,23},{8,24},{9,... | collective-permute-start | bytes 1376264 | tf_op jit(solution)/shard_map/ppermute | solution.py:30
  109.2 3.9 %collective-permute-start.29 = (bf16[1792,128]{1,0:T(8,128)(2,1)S(1)}, bf16[1792,128]{1,0:T(8,128)(2,1)S(1)}, u32[]{:S(2)}, u32[]{:S(2)}) collective-permute-start(bf16[1792,128]{1,0:T(8,128)(2,1)S(1)} %get-tuple-element.74), channel_id=1, source_target_pairs={{0,16},{1,17},{2,18},{3,19},{4,20},{5,21},{6,22},{7,23},{8,24},{9,... | collective-permute-start | bytes 1376264 | tf_op jit(solution)/shard_map/ppermute | solution.py:30
  109.4 3.7 %copy-start = (f32[4096,128]{1,0:T(8,128)S(1)}, f32[4096,128]{1,0:T(8,128)}, u32[]{:S(2)}) copy-start(f32[4096,128]{1,0:T(8,128)} %b_ref.5) | copy-start | bytes 6291460

commit v11 on v9

--- a/solution.py
+++ b/solution.py
@@ -333,10 +333,10 @@
     hops = [send(yb1, z_move(1, 2))]
     _, _, y_own, y12 = forward(1, w0, vspec, yb1, y_own, hops)
     y12_in = send(y12, z_move(2, 3))
-    top, bottom = call(hold_kernel, ids, (own_t, own_b, y12_in), [whole((half, HB))] * 2 + [ANY], (bf(half, HB),) * 2)
-    before_b, after_t = send(bottom, x_plus), send(top, x_minus)
     p23, p1 = call(relay_kernel, ids, (p23, p1, y12), [whole((NB, HB)), mspec, ANY], (bf(NB, HB), bf(NB, 2 * HB)))
     p23_other, p1_other = send(p23, other_core), send(p1, other_core)
+    top, bottom = call(hold_kernel, ids, (own_t, own_b, p23_other), [whole((half, HB))] * 2 + [ANY], (bf(half, HB),) * 2)
+    before_b, after_t = send(bottom, x_plus), send(top, x_minus)
     y1, y2, y_own, yb3, xs, x23s, x3s = call(
         turn_kernel, ids,
         (w0, y12, y12_in, y_own, lh, ll, *uppers, p23, p23_other, p1, p1_other, *window, before_t, after_b),

time: 111 us -> 114 us (1.027)
  waiting for transfers between devices: 35.6 us -> 40.5 us
  starting transfers between devices: 45.7 us -> 42.8 us
    ppermute x32, waiting for transfers between devices: 35.6 us -> 40.5 us  [send(): return lax.ppermute(value, ('row', 'col'), pairs(move))]
    ppermute x32, starting transfers between devices: 45.7 us -> 42.8 us  [send(): return lax.ppermute(value, ('row', 'col'), pairs(move))]
where the time goes in v11:
time: 114 us; the launch traced here: 112 us
  starting transfers between devices  42.8 us (38%)
  waiting for transfers between devices  40.5 us (36%)
  Pallas kernels  26.7 us (23%)
    ppermute x32, starting transfers between devices, send(): return lax.ppermute(value, ('row', 'col'), pairs(move))  42.8 us
    ppermute x32, waiting for transfers between devices, send(): return lax.ppermute(value, ('row', 'col'), pairs(move))  40.5 us
    pallas_call x15, Pallas kernels, call(): pl.pallas_call(kernel, grid_spec=pltpu.PrefetchScalarGridSpec(num_scalar_...  26.7 us
  transfers between devices with their start and end apart: 32, of which 10 were waited for; matrix products, arithmetic and copies ran while one was open for 0% of the time, Pallas kernels for 22%

profile of v11, /device:TPU:1, one launch (start us, length us, event | category | flops | bytes accessed | tf_op | source)
XLA Modules:
  0.0 111.6 jit_solution(3472663384307115307)
XLA Ops:
  0.0 1.0 slice.9.after_ref.b0.rest_0_
  1.0 3.4 %collective-permute-start.6 = (bf16[512,256]{1,0:T(8,128)(2,1)S(1)}, bf16[512,256]{1,0:T(8,128)(2,1)S(1)}, u32[]{:S(2)}, u32[]{:S(2)}) collective-permute-start(bf16[512,256]{1,0:T(8,128)(2,1)S(1)} %slice.9.after_ref.b0.rest_0_), channel_id=1, source_target_pairs={{0,96},{1,97},{2,98},{3,99},{4,100},{5,101},{6,102},{7,103},{8,104... | collective-permute-start | bytes 786440 | tf_op jit(solution)/shard_map/ppermute | solution.py:30
  4.3 0.5 collective-permute-start.7
  4.9 0.6 collective-permute-start.8
  5.5 0.1 pad_add_fusion.ids
  5.6 3.7 %shard_map.37 = (f32[512,128]{1,0:T(8,128)S(1)}, bf16[512,128]{1,0:T(8,128)(2,1)S(1)}, bf16[512,512]{1,0:T(8,128)(2,1)S(1)}, bf16[512,512]{1,0:T(8,128)(2,1)S(1)...) custom-call(s32[4]{0:T(128)S(1)} %pad_add_fusion.ids, ...), custom_call_target="tpu_custom_call" | custom-call | flops 1 | bytes 1 | tf_op jit(solution)/shard_map/pallas_call | solution.py:276
  9.2 3.5 %collective-permute-start = (bf16[512,128]{1,0:T(8,128)(2,1)S(1)}, bf16[512,128]{1,0:T(8,128)(2,1)S(1)}, u32[]{:S(2)}, u32[]{:S(2)}) collective-permute-start(bf16[512,128]{1,0:T(8,128)(2,1)S(1)} %get-tuple-element.43.own_ref), channel_id=1, source_target_pairs={{0,4},{16,20},{32,36},{48,52},{64,68},{80,84},{96,100},{112,116}} | collective-permute-start | bytes 393224 | tf_op jit(solution)/shard_map/ppermute | solution.py:30
  12.8 2.6 %collective-permute-start.1 = (bf16[512,128]{1,0:T(8,128)(2,1)S(1)}, bf16[512,128]{1,0:T(8,128)(2,1)S(1)}, u32[]{:S(2)}, u32[]{:S(2)}) collective-permute-start(bf16[512,128]{1,0:T(8,128)(2,1)S(1)} %get-tuple-element.43.own_ref), channel_id=1, source_target_pairs={{0,8},{16,24},{32,40},{48,56},{64,72},{80,88},{96,104},{112,120}} | collective-permute-start | bytes 393224 | tf_op jit(solution)/shard_map/ppermute | solution.py:30
  15.4 1.3 %collective-permute-start.2 = (bf16[512,128]{1,0:T(8,128)(2,1)S(1)}, bf16[512,128]{1,0:T(8,128)(2,1)S(1)}, u32[]{:S(2)}, u32[]{:S(2)}) collective-permute-start(bf16[512,128]{1,0:T(8,128)(2,1)S(1)} %get-tuple-element.43.own_ref), channel_id=1, source_target_pairs={{0,12},{16,28},{32,44},{48,60},{64,76},{80,92},{96,108},{112,124}} | collective-permute-start | bytes 393224 | tf_op jit(solution)/shard_map/ppermute | solution.py:30
  16.8 0.0 collective-permute-done.7.b2.rest_2_
  16.8 2.9 %collective-permute-done.8.b3.rest_3_ = bf16[512,256]{1,0:T(8,128)(2,1)S(1)} collective-permute-done((bf16[512,256]{1,0:T(8,128)(2,1)S(1)}, bf16[512,256]{1,0:T(8,128)(2,1)S(1)}, u32[]{:S(2)}, u32[]{:S(2)}) %collective-permute-start.8) | collective-permute-done | bytes 262176 | tf_op jit(solution)/shard_map/ppermute | solution.py:30
  19.7 0.7 shard_map.39
  20.4 2.9 %collective-permute-start.10 = (bf16[1536,256]{1,0:T(8,128)(2,1)S(1)}, bf16[1536,256]{1,0:T(8,128)(2,1)S(1)}, u32[]{:S(2)}, u32[]{:S(2)}) collective-permute-start(bf16[1536,256]{1,0:T(8,128)(2,1)S(1)} %get-tuple-element.47), channel_id=1, source_target_pairs={{0,16},{1,17},{2,18},{3,19},{4,20},{5,21},{6,22},{7,23},{8,24},{9,... | collective-permute-start | bytes 2359304 | tf_op jit(solution)/shard_map/ppermute | solution.py:30
  23.3 0.0 collective-permute-done.1.r2
  23.3 0.0 collective-permute-done.2.r3
  23.3 0.6 shard_map.38.own_ref.v0
  23.9 1.3 %collective-permute-start.3 = (bf16[512,128]{1,0:T(8,128)(2,1)S(1)}, bf16[512,128]{1,0:T(8,128)(2,1)S(1)}, u32[]{:S(2)}, u32[]{:S(2)}) collective-permute-start(bf16[512,128]{1,0:T(8,128)(2,1)S(1)} %shard_map.38.own_ref.v0), channel_id=1, source_target_pairs={{0,1},{4,5},{8,9},{12,13},{16,17},{20,21},{24,25},{28,29},{32,33},... | collective-permute-start | bytes 393224 | tf_op jit(solution)/shard_map/ppermute | solution.py:30
  25.2 1.9 %collective-permute-start.4 = (bf16[512,128]{1,0:T(8,128)(2,1)S(1)}, bf16[512,128]{1,0:T(8,128)(2,1)S(1)}, u32[]{:S(2)}, u32[]{:S(2)}) collective-permute-start(bf16[512,128]{1,0:T(8,128)(2,1)S(1)} %shard_map.38.own_ref.v0), channel_id=1, source_target_pairs={{0,2},{4,6},{8,10},{12,14},{16,18},{20,22},{24,26},{28,30},{32,34}... | collective-permute-start | bytes 393224 | tf_op jit(solution)/shard_map/ppermute | solution.py:30
  27.1 1.1 %collective-permute-start.9 = (bf16[512,256]{1,0:T(8,128)(2,1)S(1)}, bf16[512,256]{1,0:T(8,128)(2,1)S(1)}, u32[]{:S(2)}, u32[]{:S(2)}) collective-permute-start(bf16[512,256]{1,0:T(8,128)(2,1)S(1)} %slice.9.after_ref.b0.rest_0_), channel_id=1, source_target_pairs={{0,16},{1,17},{2,18},{3,19},{4,20},{5,21},{6,22},{7,23},{8,24},{9,... | collective-permute-start | bytes 786440 | tf_op jit(solution)/shard_map/ppermute | solution.py:30
  28.3 1.3 %collective-permute-start.5 = (bf16[512,128]{1,0:T(8,128)(2,1)S(1)}, bf16[512,128]{1,0:T(8,128)(2,1)S(1)}, u32[]{:S(2)}, u32[]{:S(2)}) collective-permute-start(bf16[512,128]{1,0:T(8,128)(2,1)S(1)} %shard_map.38.own_ref.v0), channel_id=1, source_target_pairs={{0,3},{4,7},{8,11},{12,15},{16,19},{20,23},{24,27},{28,31},{32,35}... | collective-permute-start | bytes 393224 | tf_op jit(solution)/shard_map/ppermute | solution.py:30
  29.5 0.0 collective-permute-done.3.rest_0_.e1
  29.6 0.7 collective-permute-start.14
  30.3 0.1 collective-permute-done.4.rest_1_.e2
  30.4 0.7 collective-permute-start.13
  31.1 0.1 fusion
  31.2 1.4 %collective-permute-done.5.rest_2_.e3 = bf16[512,128]{1,0:T(8,128)(2,1)S(1)} collective-permute-done((bf16[512,128]{1,0:T(8,128)(2,1)S(1)}, bf16[512,128]{1,0:T(8,128)(2,1)S(1)}, u32[]{:S(2)}, u32[]{:S(2)}) %collective-permute-start.5) | collective-permute-done | bytes 131104 | tf_op jit(solution)/shard_map/ppermute | solution.py:30
  32.6 0.7 shard_map.43
  33.3 0.1 collective-permute-start.17
  33.4 3.4 %collective-permute-start.18 = (bf16[1792,256]{1,0:T(8,128)(2,1)S(1)}, bf16[1792,256]{1,0:T(8,128)(2,1)S(1)}, u32[]{:S(2)}, u32[]{:S(2)}) collective-permute-start(bf16[1792,256]{1,0:T(8,128)(2,1)S(1)} %get-tuple-element.64), channel_id=1, source_target_pairs={{0,96},{1,97},{2,98},{3,99},{4,100},{5,101},{6,102},{7,103},{8,104... | collective-permute-start | bytes 2752520 | tf_op jit(solution)/shard_map/ppermute | solution.py:30
  36.8 0.0 collective-permute-done.9.rest_4_
  36.8 2.7 %shard_map.40 = (bf16[512,128]{1,0:T(8,128)(2,1)}, f32[512,128]{1,0:T(8,128)S(1)}, f32[512,128]{1,0:T(8,128)S(1)}, bf16[512,128]{1,0:T(8,128)(2,1)S(1)}) custom-call(s32[4]{0:T(128)S(1)} %pad_add_fusion.ids, f32[4096,128]{1,0:T(8,128)} %b_ref.5, bf16[512,128]{1,0:T(8,128)(2,1)S(1)} %shard_map.38.own_ref.v0, f32[512,128]{1,0:T(8,128)S(1)} %get-tuple-element.44.prior_ref, ...), custom_call_target="tpu_custom_call" | custom-call | flops 1 | bytes 1 | tf_op jit(solution)/shard_map/pallas_call | solution.py:276
  39.6 0.7 collective-permute-start.11
  40.3 1.9 %shard_map.41 = (bf16[512,128]{1,0:T(8,128)(2,1)}, f32[512,128]{1,0:T(8,128)}, f32[512,128]{1,0:T(8,128)S(1)}, bf16[1024,128]{1,0:T(8,128)(2,1)S(1)}) custom-call(s32[4]{0:T(128)S(1)} %pad_add_fusion.ids, f32[512,128]{1,0:T(8,128)S(1)} %get-tuple-element.48.w_ref, bf16[512,128]{1,0:T(8,128)(2,1)S(1)} %get-tuple-element.49.own_ref, ...), custom_call_target="tpu_custom_call" | custom-call | flops 1 | bytes 1 | tf_op jit(solution)/shard_map/pallas_call | solution.py:276
  42.1 0.6 shard_map.42
  42.7 1.0 collective-permute-start.15
  43.7 0.7 collective-permute-start.12
  44.4 0.1 collective-permute-start.16
  44.5 0.4 collective-permute-done.15.p23_other.rest_0_
  44.9 0.7 shard_map.45
  45.5 0.1 collective-permute-start.22
  45.6 2.7 %collective-permute-start.23 = (bf16[1792,256]{1,0:T(8,128)(2,1)S(1)}, bf16[1792,256]{1,0:T(8,128)(2,1)S(1)}, u32[]{:S(2)}, u32[]{:S(2)}) collective-permute-start(bf16[1792,256]{1,0:T(8,128)(2,1)S(1)} %get-tuple-element.72), channel_id=1, source_target_pairs={{0,96},{1,97},{2,98},{3,99},{4,100},{5,101},{6,102},{7,103},{8,104... | collective-permute-start | bytes 2752520 | tf_op jit(solution)/shard_map/ppermute | solution.py:30
  48.3 8.6 %collective-permute-done.17.rest_6_.rest_3_ = bf16[1792,256]{1,0:T(8,128)(2,1)S(1)} collective-permute-done((bf16[1792,256]{1,0:T(8,128)(2,1)S(1)}, bf16[1792,256]{1,0:T(8,128)(2,1)S(1)}, u32[]{:S(2)}, u32[]{:S(2)}) %collective-permute-start.17) | collective-permute-done | bytes 917536 | tf_op jit(solution)/shard_map/ppermute | solution.py:30
  56.9 4.0 %shard_map.44 = (bf16[512,128]{1,0:T(8,128)(2,1)S(1)}, bf16[512,128]{1,0:T(8,128)(2,1)S(1)}, f32[512,128]{1,0:T(8,128)S(1)}, bf16[512,128]{1,0:T(8,128)(2,1)S(1)...) custom-call(s32[4]{0:T(128)S(1)} %pad_add_fusion.ids, ...), custom_call_target="tpu_custom_call" | custom-call | flops 1 | bytes 1 | tf_op jit(solution)/shard_map/pallas_call | solution.py:276
  60.9 0.7 collective-permute-start.20
  61.6 1.3 %collective-permute-start.19 = (bf16[1536,128]{1,0:T(8,128)(2,1)S(1)}, bf16[1536,128]{1,0:T(8,128)(2,1)S(1)}, u32[]{:S(2)}, u32[]{:S(2)}) collective-permute-start(bf16[1536,128]{1,0:T(8,128)(2,1)S(1)} %get-tuple-element.65), channel_id=1, source_target_pairs={{12,0},{28,16},{44,32},{60,48},{76,64},{92,80},{108,96},{124,112}} | collective-permute-start | bytes 1179656 | tf_op jit(solution)/shard_map/ppermute | solution.py:30
  62.9 0.7 collective-permute-start.21
  63.5 2.5 %collective-permute-start.30 = (bf16[1792,256]{1,0:T(8,128)(2,1)S(1)}, bf16[1792,256]{1,0:T(8,128)(2,1)S(1)}, u32[]{:S(2)}, u32[]{:S(2)}) collective-permute-start(bf16[1792,256]{1,0:T(8,128)(2,1)S(1)} %collective-permute-done.18.rest_7_.rest_1_), channel_id=1, source_target_pairs={{0,96},{1,97},{2,98},{3,99},{4,100},{5,101},{6,102},{7,103},{8,104... | collective-permute-start | bytes 2752520 | tf_op jit(solution)/shard_map/ppermute | solution.py:30
  66.0 10.5 %collective-permute-done.22.rest_0_.rest_3_ = bf16[1792,256]{1,0:T(8,128)(2,1)S(1)} collective-permute-done((bf16[1792,256]{1,0:T(8,128)(2,1)S(1)}, bf16[1792,256]{1,0:T(8,128)(2,1)S(1)}, u32[]{:S(2)}, u32[]{:S(2)}) %collective-permute-start.22) | collective-permute-done | bytes 917536 | tf_op jit(solution)/shard_map/ppermute | solution.py:30
  76.6 2.7 %collective-permute-done.19.to0 = bf16[1536,128]{1,0:T(8,128)(2,1)S(1)} collective-permute-done((bf16[1536,128]{1,0:T(8,128)(2,1)S(1)}, bf16[1536,128]{1,0:T(8,128)(2,1)S(1)}, u32[]{:S(2)}, u32[]{:S(2)}) %collective-permute-start.19) | collective-permute-done | bytes 393248 | tf_op jit(solution)/shard_map/ppermute | solution.py:30
  79.3 0.7 shard_map.46.late
  80.0 1.3 %collective-permute-start.24 = (bf16[1536,128]{1,0:T(8,128)(2,1)S(1)}, bf16[1536,128]{1,0:T(8,128)(2,1)S(1)}, u32[]{:S(2)}, u32[]{:S(2)}) collective-permute-start(bf16[1536,128]{1,0:T(8,128)(2,1)S(1)} %shard_map.46.late), channel_id=1, source_target_pairs={{0,1},{4,5},{8,9},{12,13},{16,17},{20,21},{24,25},{28,29},{32,33},... | collective-permute-start | bytes 1179656 | tf_op jit(solution)/shard_map/ppermute | solution.py:30
  81.3 1.3 %collective-permute-start.25 = (bf16[1536,128]{1,0:T(8,128)(2,1)S(1)}, bf16[1536,128]{1,0:T(8,128)(2,1)S(1)}, u32[]{:S(2)}, u32[]{:S(2)}) collective-permute-start(bf16[1536,128]{1,0:T(8,128)(2,1)S(1)} %shard_map.46.late), channel_id=1, source_target_pairs={{0,2},{4,6},{8,10},{12,14},{16,18},{20,22},{24,26},{28,30},{32,34}... | collective-permute-start | bytes 1179656 | tf_op jit(solution)/shard_map/ppermute | solution.py:30
  82.7 1.3 %collective-permute-start.26 = (bf16[1536,128]{1,0:T(8,128)(2,1)S(1)}, bf16[1536,128]{1,0:T(8,128)(2,1)S(1)}, u32[]{:S(2)}, u32[]{:S(2)}) collective-permute-start(bf16[1536,128]{1,0:T(8,128)(2,1)S(1)} %shard_map.46.late), channel_id=1, source_target_pairs={{0,3},{4,7},{8,11},{12,15},{16,19},{20,23},{24,27},{28,31},{32,35}... | collective-permute-start | bytes 1179656 | tf_op jit(solution)/shard_map/ppermute | solution.py:30
  84.0 4.1 %collective-permute-done.24.s1 = bf16[1536,128]{1,0:T(8,128)(2,1)S(1)} collective-permute-done((bf16[1536,128]{1,0:T(8,128)(2,1)S(1)}, bf16[1536,128]{1,0:T(8,128)(2,1)S(1)}, u32[]{:S(2)}, u32[]{:S(2)}) %collective-permute-start.24) | collective-permute-done | bytes 393248 | tf_op jit(solution)/shard_map/ppermute | solution.py:30
  88.1 8.4 %collective-permute-done.25.s2 = bf16[1536,128]{1,0:T(8,128)(2,1)S(1)} collective-permute-done((bf16[1536,128]{1,0:T(8,128)(2,1)S(1)}, bf16[1536,128]{1,0:T(8,128)(2,1)S(1)}, u32[]{:S(2)}, u32[]{:S(2)}) %collective-permute-start.25) | collective-permute-done | bytes 393248 | tf_op jit(solution)/shard_map/ppermute | solution.py:30
  96.5 1.0 shard_map.47
  97.6 2.6 %collective-permute-start.27 = (bf16[1024,128]{1,0:T(8,128)(2,1)S(1)}, bf16[1024,128]{1,0:T(8,128)(2,1)S(1)}, u32[]{:S(2)}, u32[]{:S(2)}) collective-permute-start(bf16[1024,128]{1,0:T(8,128)(2,1)S(1)} %get-tuple-element.76), channel_id=1, source_target_pairs={{0,16},{1,17},{2,18},{3,19},{4,20},{5,21},{6,22},{7,23},{8,24},{9,... | collective-permute-start | bytes 786440 | tf_op jit(solution)/shard_map/ppermute | solution.py:30
  100.2 1.2 %collective-permute-done.27.other_ref = bf16[1024,128]{1,0:T(8,128)(2,1)S(1)} collective-permute-done((bf16[1024,128]{1,0:T(8,128)(2,1)S(1)}, bf16[1024,128]{1,0:T(8,128)(2,1)S(1)}, u32[]{:S(2)}, u32[]{:S(2)}) %collective-permute-start.27) | collective-permute-done | bytes 262176 | tf_op jit(solution)/shard_map/ppermute | solution.py:30
  101.3 1.7 %shard_map.50 = (f32[1792,128]{1,0:T(8,128)S(1)}, bf16[1792,128]{1,0:T(8,128)(2,1)S(1)}) custom-call(s32[4]{0:T(128)S(1)} %pad_add_fusion.ids, bf16[1024,128]{1,0:T(8,128)(2,1)S(1)} %get-tuple-element.75.mine_ref, bf16[1024,128]{1,0:T(8,128)(2,1)S(1)} %collective-permute-done.27.other_ref, bf16[1792,256]{1,0:T(8,128)(2,1)S(1)} %get-tuple-element.81.bottom.rest_0_, ...), custom_call_target="tpu_custom_call" | custom-call | flops 1 | bytes 1 | tf_op jit(solution)/shard_map/pallas_call | solution.py:276
  103.1 0.5 collective-permute-start.31
  103.5 1.7 %shard_map.49 = (f32[1792,128]{1,0:T(8,128)S(1)}, bf16[1792,128]{1,0:T(8,128)(2,1)S(1)}) custom-call(s32[4]{0:T(128)S(1)} %pad_add_fusion.ids, bf16[1024,128]{1,0:T(8,128)(2,1)S(1)} %get-tuple-element.75.mine_ref, bf16[1024,128]{1,0:T(8,128)(2,1)S(1)} %collective-permute-done.27.other_ref, bf16[1792,256]{1,0:T(8,128)(2,1)S(1)} %get-tuple-element.82.top.rest_0_, ...), custom_call_target="tpu_custom_call" | custom-call | flops 1 | bytes 1 | tf_op jit(solution)/shard_map/pallas_call | solution.py:276
  105.3 0.2 collective-permute-start.29
  105.5 3.7 %shard_map.48.out_in = f32[4096,128]{1,0:T(8,128)} custom-call(s32[4]{0:T(128)S(1)} %pad_add_fusion.ids, f32[4096,128]{1,0:T(8,128)} %b_ref.5, bf16[2048,128]{1,0:T(8,128)(2,1)S(1)} %get-tuple-element.73.v_ref, f32[512,128]{1,0:T(8,128)S(1)} %get-tuple-element.74.own_ref, bf16[512,512]{1,0:T(8,128)(2,1)S(1)} %get-tuple-element.53.u3h.uh_ref, ...), custom_call_target="tpu_custom_call" | custom-call | flops 1 | bytes 1 | tf_op jit(solution)/shard_map/pallas_call | solution.py:276
  109.2 2.4 %shard_map.51 = f32[4096,128]{1,0:T(8,128)} custom-call(s32[4]{0:T(128)S(1)} %pad_add_fusion.ids, f32[4096,128]{1,0:T(8,128)} %shard_map.48.out_in, f32[4096,128]{1,0:T(8,128)S(1)} %copy-done, f32[1792,128]{1,0:T(8,128)S(1)} %get-tuple-element.77.own_t, bf16[1792,128]{1,0:T(8,128)(2,1)S(1)} %collective-permute-done.29.part_t, ...), custom_call_target="tpu_custom_call", output_to_operand_aliasing={{}: (1, {})} | custom-call | flops 1 | bytes 1 | tf_op jit(solution)/shard_map/pallas_call | solution.py:276
  (22 shorter events, 0.1 us)
Async XLA Ops:
  1.0 14.5 %collective-permute-start.6 = (bf16[512,256]{1,0:T(8,128)(2,1)S(1)}, bf16[512,256]{1,0:T(8,128)(2,1)S(1)}, u32[]{:S(2)}, u32[]{:S(2)}) collective-permute-start(bf16[512,256]{1,0:T(8,128)(2,1)S(1)} %slice.9.after_ref.b0.rest_0_), channel_id=1, source_target_pairs={{0,96},{1,97},{2,98},{3,99},{4,100},{5,101},{6,102},{7,103},{8,104... | collective-permute-start | bytes 786440 | tf_op jit(solution)/shard_map/ppermute | solution.py:30
  4.3 12.4 %collective-permute-start.7 = (bf16[512,256]{1,0:T(8,128)(2,1)S(1)}, bf16[512,256]{1,0:T(8,128)(2,1)S(1)}, u32[]{:S(2)}, u32[]{:S(2)}) collective-permute-start(bf16[512,256]{1,0:T(8,128)(2,1)S(1)} %slice.9.after_ref.b0.rest_0_), channel_id=1, source_target_pairs={{0,64},{1,65},{2,66},{3,67},{4,68},{5,69},{6,70},{7,71},{8,72},{9,... | collective-permute-start | bytes 786440 | tf_op jit(solution)/shard_map/ppermute | solution.py:30
  4.9 14.8 %collective-permute-start.8 = (bf16[512,256]{1,0:T(8,128)(2,1)S(1)}, bf16[512,256]{1,0:T(8,128)(2,1)S(1)}, u32[]{:S(2)}, u32[]{:S(2)}) collective-permute-start(bf16[512,256]{1,0:T(8,128)(2,1)S(1)} %slice.9.after_ref.b0.rest_0_), channel_id=1, source_target_pairs={{0,32},{1,33},{2,34},{3,35},{4,36},{5,37},{6,38},{7,39},{8,40},{9,... | collective-permute-start | bytes 786440 | tf_op jit(solution)/shard_map/ppermute | solution.py:30
  5.6 25.5 %copy-start.1 = (bf16[4096,256]{1,0:T(8,128)(2,1)S(1)}, bf16[4096,256]{1,0:T(8,128)(2,1)}, u32[]{:S(2)}) copy-start(bf16[4096,256]{1,0:T(8,128)(2,1)} %param.4) | copy-start | bytes 6291460
  9.2 14.0 %collective-permute-start = (bf16[512,128]{1,0:T(8,128)(2,1)S(1)}, bf16[512,128]{1,0:T(8,128)(2,1)S(1)}, u32[]{:S(2)}, u32[]{:S(2)}) collective-permute-start(bf16[512,128]{1,0:T(8,128)(2,1)S(1)} %get-tuple-element.43.own_ref), channel_id=1, source_target_pairs={{0,4},{16,20},{32,36},{48,52},{64,68},{80,84},{96,100},{112,116}} | collective-permute-start | bytes 393224 | tf_op jit(solution)/shard_map/ppermute | solution.py:30
  12.8 10.5 %collective-permute-start.1 = (bf16[512,128]{1,0:T(8,128)(2,1)S(1)}, bf16[512,128]{1,0:T(8,128)(2,1)S(1)}, u32[]{:S(2)}, u32[]{:S(2)}) collective-permute-start(bf16[512,128]{1,0:T(8,128)(2,1)S(1)} %get-tuple-element.43.own_ref), channel_id=1, source_target_pairs={{0,8},{16,24},{32,40},{48,56},{64,72},{80,88},{96,104},{112,120}} | collective-permute-start | bytes 393224 | tf_op jit(solution)/shard_map/ppermute | solution.py:30
  15.4 7.8 %collective-permute-start.2 = (bf16[512,128]{1,0:T(8,128)(2,1)S(1)}, bf16[512,128]{1,0:T(8,128)(2,1)S(1)}, u32[]{:S(2)}, u32[]{:S(2)}) collective-permute-start(bf16[512,128]{1,0:T(8,128)(2,1)S(1)} %get-tuple-element.43.own_ref), channel_id=1, source_target_pairs={{0,12},{16,28},{32,44},{48,60},{64,76},{80,92},{96,108},{112,124}} | collective-permute-start | bytes 393224 | tf_op jit(solution)/shard_map/ppermute | solution.py:30
  20.4 12.2 %collective-permute-start.10 = (bf16[1536,256]{1,0:T(8,128)(2,1)S(1)}, bf16[1536,256]{1,0:T(8,128)(2,1)S(1)}, u32[]{:S(2)}, u32[]{:S(2)}) collective-permute-start(bf16[1536,256]{1,0:T(8,128)(2,1)S(1)} %get-tuple-element.47), channel_id=1, source_target_pairs={{0,16},{1,17},{2,18},{3,19},{4,20},{5,21},{6,22},{7,23},{8,24},{9,... | collective-permute-start | bytes 2359304 | tf_op jit(solution)/shard_map/ppermute | solution.py:30
  23.9 5.6 %collective-permute-start.3 = (bf16[512,128]{1,0:T(8,128)(2,1)S(1)}, bf16[512,128]{1,0:T(8,128)(2,1)S(1)}, u32[]{:S(2)}, u32[]{:S(2)}) collective-permute-start(bf16[512,128]{1,0:T(8,128)(2,1)S(1)} %shard_map.38.own_ref.v0), channel_id=1, source_target_pairs={{0,1},{4,5},{8,9},{12,13},{16,17},{20,21},{24,25},{28,29},{32,33},... | collective-permute-start | bytes 393224 | tf_op jit(solution)/shard_map/ppermute | solution.py:30
  25.2 5.2 %collective-permute-start.4 = (bf16[512,128]{1,0:T(8,128)(2,1)S(1)}, bf16[512,128]{1,0:T(8,128)(2,1)S(1)}, u32[]{:S(2)}, u32[]{:S(2)}) collective-permute-start(bf16[512,128]{1,0:T(8,128)(2,1)S(1)} %shard_map.38.own_ref.v0), channel_id=1, source_target_pairs={{0,2},{4,6},{8,10},{12,14},{16,18},{20,22},{24,26},{28,30},{32,34}... | collective-permute-start | bytes 393224 | tf_op jit(solution)/shard_map/ppermute | solution.py:30
  27.1 9.7 %collective-permute-start.9 = (bf16[512,256]{1,0:T(8,128)(2,1)S(1)}, bf16[512,256]{1,0:T(8,128)(2,1)S(1)}, u32[]{:S(2)}, u32[]{:S(2)}) collective-permute-start(bf16[512,256]{1,0:T(8,128)(2,1)S(1)} %slice.9.after_ref.b0.rest_0_), channel_id=1, source_target_pairs={{0,16},{1,17},{2,18},{3,19},{4,20},{5,21},{6,22},{7,23},{8,24},{9,... | collective-permute-start | bytes 786440 | tf_op jit(solution)/shard_map/ppermute | solution.py:30
  28.3 4.4 %collective-permute-start.5 = (bf16[512,128]{1,0:T(8,128)(2,1)S(1)}, bf16[512,128]{1,0:T(8,128)(2,1)S(1)}, u32[]{:S(2)}, u32[]{:S(2)}) collective-permute-start(bf16[512,128]{1,0:T(8,128)(2,1)S(1)} %shard_map.38.own_ref.v0), channel_id=1, source_target_pairs={{0,3},{4,7},{8,11},{12,15},{16,19},{20,23},{24,27},{28,31},{32,35}... | collective-permute-start | bytes 393224 | tf_op jit(solution)/shard_map/ppermute | solution.py:30
  29.6 12.6 %collective-permute-start.14 = (bf16[512,512]{1,0:T(8,128)(2,1)S(1)}, bf16[512,512]{1,0:T(8,128)(2,1)S(1)}, u32[]{:S(2)}, u32[]{:S(2)}) collective-permute-start(bf16[512,512]{1,0:T(8,128)(2,1)S(1)} %get-tuple-element.60), channel_id=1, source_target_pairs={{4,12},{20,28},{36,44},{52,60},{68,76},{84,92},{100,108},{116,124}} | collective-permute-start | bytes 1572872 | tf_op jit(solution)/shard_map/ppermute | solution.py:30
  30.4 11.7 %collective-permute-start.13 = (bf16[512,256]{1,0:T(8,128)(2,1)S(1)}, bf16[512,256]{1,0:T(8,128)(2,1)S(1)}, u32[]{:S(2)}, u32[]{:S(2)}) collective-permute-start(bf16[512,256]{1,0:T(8,128)(2,1)S(1)} %get-tuple-element.59), channel_id=1, source_target_pairs={{8,12},{24,28},{40,44},{56,60},{72,76},{88,92},{104,108},{120,124}} | collective-permute-start | bytes 786440 | tf_op jit(solution)/shard_map/ppermute | solution.py:30
  33.3 23.6 %collective-permute-start.17 = (bf16[1792,256]{1,0:T(8,128)(2,1)S(1)}, bf16[1792,256]{1,0:T(8,128)(2,1)S(1)}, u32[]{:S(2)}, u32[]{:S(2)}) collective-permute-start(bf16[1792,256]{1,0:T(8,128)(2,1)S(1)} %get-tuple-element.63), channel_id=1, source_target_pairs={{0,32},{1,33},{2,34},{3,35},{4,36},{5,37},{6,38},{7,39},{8,40},{9,... | collective-permute-start | bytes 2752520 | tf_op jit(solution)/shard_map/ppermute | solution.py:30
  33.4 23.5 %collective-permute-start.18 = (bf16[1792,256]{1,0:T(8,128)(2,1)S(1)}, bf16[1792,256]{1,0:T(8,128)(2,1)S(1)}, u32[]{:S(2)}, u32[]{:S(2)}) collective-permute-start(bf16[1792,256]{1,0:T(8,128)(2,1)S(1)} %get-tuple-element.64), channel_id=1, source_target_pairs={{0,96},{1,97},{2,98},{3,99},{4,100},{5,101},{6,102},{7,103},{8,104... | collective-permute-start | bytes 2752520 | tf_op jit(solution)/shard_map/ppermute | solution.py:30
  39.6 0.7 collective-permute-start.11
  42.7 2.1 %collective-permute-start.15 = (bf16[512,256]{1,0:T(8,128)(2,1)S(1)}, bf16[512,256]{1,0:T(8,128)(2,1)S(1)}, u32[]{:S(2)}, u32[]{:S(2)}) collective-permute-start(bf16[512,256]{1,0:T(8,128)(2,1)S(1)} %get-tuple-element.61.p23), channel_id=1, source_target_pairs={{0,16},{1,17},{2,18},{3,19},{4,20},{5,21},{6,22},{7,23},{8,24},{9,... | collective-permute-start | bytes 786440 | tf_op jit(solution)/shard_map/ppermute | solution.py:30
  43.7 1.9 %collective-permute-start.12 = (bf16[1024,128]{1,0:T(8,128)(2,1)S(1)}, bf16[1024,128]{1,0:T(8,128)(2,1)S(1)}, u32[]{:S(2)}, u32[]{:S(2)}) collective-permute-start(bf16[1024,128]{1,0:T(8,128)(2,1)S(1)} %get-tuple-element.51.after_ref.y12_ref), channel_id=1, source_target_pairs={{8,12},{24,28},{40,44},{56,60},{72,76},{88,92},{104,108},{120,124}} | collective-permute-start | bytes 786440 | tf_op jit(solution)/shard_map/ppermute | solution.py:30
  44.4 3.9 %collective-permute-start.16 = (bf16[512,512]{1,0:T(8,128)(2,1)S(1)}, bf16[512,512]{1,0:T(8,128)(2,1)S(1)}, u32[]{:S(2)}, u32[]{:S(2)}) collective-permute-start(bf16[512,512]{1,0:T(8,128)(2,1)S(1)} %get-tuple-element.62.p1), channel_id=1, source_target_pairs={{0,16},{1,17},{2,18},{3,19},{4,20},{5,21},{6,22},{7,23},{8,24},{9,... | collective-permute-start | bytes 1572872 | tf_op jit(solution)/shard_map/ppermute | solution.py:30
  45.5 31.0 %collective-permute-start.22 = (bf16[1792,256]{1,0:T(8,128)(2,1)S(1)}, bf16[1792,256]{1,0:T(8,128)(2,1)S(1)}, u32[]{:S(2)}, u32[]{:S(2)}) collective-permute-start(bf16[1792,256]{1,0:T(8,128)(2,1)S(1)} %get-tuple-element.71), channel_id=1, source_target_pairs={{0,32},{1,33},{2,34},{3,35},{4,36},{5,37},{6,38},{7,39},{8,40},{9,... | collective-permute-start | bytes 2752520 | tf_op jit(solution)/shard_map/ppermute | solution.py:30
  45.6 31.0 %collective-permute-start.23 = (bf16[1792,256]{1,0:T(8,128)(2,1)S(1)}, bf16[1792,256]{1,0:T(8,128)(2,1)S(1)}, u32[]{:S(2)}, u32[]{:S(2)}) collective-permute-start(bf16[1792,256]{1,0:T(8,128)(2,1)S(1)} %get-tuple-element.72), channel_id=1, source_target_pairs={{0,96},{1,97},{2,98},{3,99},{4,100},{5,101},{6,102},{7,103},{8,104... | collective-permute-start | bytes 2752520 | tf_op jit(solution)/shard_map/ppermute | solution.py:30
  60.9 5.2 %collective-permute-start.20 = (bf16[1024,128]{1,0:T(8,128)(2,1)S(1)}, bf16[1024,128]{1,0:T(8,128)(2,1)S(1)}, u32[]{:S(2)}, u32[]{:S(2)}) collective-permute-start(bf16[1024,128]{1,0:T(8,128)(2,1)S(1)} %get-tuple-element.66), channel_id=1, source_target_pairs={{12,4},{28,20},{44,36},{60,52},{76,68},{92,84},{108,100},{124,116}} | collective-permute-start | bytes 786440 | tf_op jit(solution)/shard_map/ppermute | solution.py:30
  61.6 17.8 %collective-permute-start.19 = (bf16[1536,128]{1,0:T(8,128)(2,1)S(1)}, bf16[1536,128]{1,0:T(8,128)(2,1)S(1)}, u32[]{:S(2)}, u32[]{:S(2)}) collective-permute-start(bf16[1536,128]{1,0:T(8,128)(2,1)S(1)} %get-tuple-element.65), channel_id=1, source_target_pairs={{12,0},{28,16},{44,32},{60,48},{76,64},{92,80},{108,96},{124,112}} | collective-permute-start | bytes 1179656 | tf_op jit(solution)/shard_map/ppermute | solution.py:30
  62.9 0.7 collective-permute-start.21
  63.5 36.6 %collective-permute-start.30 = (bf16[1792,256]{1,0:T(8,128)(2,1)S(1)}, bf16[1792,256]{1,0:T(8,128)(2,1)S(1)}, u32[]{:S(2)}, u32[]{:S(2)}) collective-permute-start(bf16[1792,256]{1,0:T(8,128)(2,1)S(1)} %collective-permute-done.18.rest_7_.rest_1_), channel_id=1, source_target_pairs={{0,96},{1,97},{2,98},{3,99},{4,100},{5,101},{6,102},{7,103},{8,104... | collective-permute-start | bytes 2752520 | tf_op jit(solution)/shard_map/ppermute | solution.py:30
  66.0 37.5 %collective-permute-start.28 = (bf16[1792,256]{1,0:T(8,128)(2,1)S(1)}, bf16[1792,256]{1,0:T(8,128)(2,1)S(1)}, u32[]{:S(2)}, u32[]{:S(2)}) collective-permute-start(bf16[1792,256]{1,0:T(8,128)(2,1)S(1)} %collective-permute-done.17.rest_6_.rest_3_), channel_id=1, source_target_pairs={{0,32},{1,33},{2,34},{3,35},{4,36},{5,37},{6,38},{7,39},{8,40},{9,... | collective-permute-start | bytes 2752520 | tf_op jit(solution)/shard_map/ppermute | solution.py:30
  80.0 8.1 %collective-permute-start.24 = (bf16[1536,128]{1,0:T(8,128)(2,1)S(1)}, bf16[1536,128]{1,0:T(8,128)(2,1)S(1)}, u32[]{:S(2)}, u32[]{:S(2)}) collective-permute-start(bf16[1536,128]{1,0:T(8,128)(2,1)S(1)} %shard_map.46.late), channel_id=1, source_target_pairs={{0,1},{4,5},{8,9},{12,13},{16,17},{20,21},{24,25},{28,29},{32,33},... | collective-permute-start | bytes 1179656 | tf_op jit(solution)/shard_map/ppermute | solution.py:30
  81.3 15.2 %collective-permute-start.25 = (bf16[1536,128]{1,0:T(8,128)(2,1)S(1)}, bf16[1536,128]{1,0:T(8,128)(2,1)S(1)}, u32[]{:S(2)}, u32[]{:S(2)}) collective-permute-start(bf16[1536,128]{1,0:T(8,128)(2,1)S(1)} %shard_map.46.late), channel_id=1, source_target_pairs={{0,2},{4,6},{8,10},{12,14},{16,18},{20,22},{24,26},{28,30},{32,34}... | collective-permute-start | bytes 1179656 | tf_op jit(solution)/shard_map/ppermute | solution.py:30
  82.7 13.9 %collective-permute-start.26 = (bf16[1536,128]{1,0:T(8,128)(2,1)S(1)}, bf16[1536,128]{1,0:T(8,128)(2,1)S(1)}, u32[]{:S(2)}, u32[]{:S(2)}) collective-permute-start(bf16[1536,128]{1,0:T(8,128)(2,1)S(1)} %shard_map.46.late), channel_id=1, source_target_pairs={{0,3},{4,7},{8,11},{12,15},{16,19},{20,23},{24,27},{28,31},{32,35}... | collective-permute-start | bytes 1179656 | tf_op jit(solution)/shard_map/ppermute | solution.py:30
  97.6 3.7 %collective-permute-start.27 = (bf16[1024,128]{1,0:T(8,128)(2,1)S(1)}, bf16[1024,128]{1,0:T(8,128)(2,1)S(1)}, u32[]{:S(2)}, u32[]{:S(2)}) collective-permute-start(bf16[1024,128]{1,0:T(8,128)(2,1)S(1)} %get-tuple-element.76), channel_id=1, source_target_pairs={{0,16},{1,17},{2,18},{3,19},{4,20},{5,21},{6,22},{7,23},{8,24},{9,... | collective-permute-start | bytes 786440 | tf_op jit(solution)/shard_map/ppermute | solution.py:30
  103.1 6.1 %collective-permute-start.31 = (bf16[1792,128]{1,0:T(8,128)(2,1)S(1)}, bf16[1792,128]{1,0:T(8,128)(2,1)S(1)}, u32[]{:S(2)}, u32[]{:S(2)}) collective-permute-start(bf16[1792,128]{1,0:T(8,128)(2,1)S(1)} %get-tuple-element.80), channel_id=1, source_target_pairs={{0,16},{1,17},{2,18},{3,19},{4,20},{5,21},{6,22},{7,23},{8,24},{9,... | collective-permute-start | bytes 1376264 | tf_op jit(solution)/shard_map/ppermute | solution.py:30
  105.3 3.9 %collective-permute-start.29 = (bf16[1792,128]{1,0:T(8,128)(2,1)S(1)}, bf16[1792,128]{1,0:T(8,128)(2,1)S(1)}, u32[]{:S(2)}, u32[]{:S(2)}) collective-permute-start(bf16[1792,128]{1,0:T(8,128)(2,1)S(1)} %get-tuple-element.78), channel_id=1, source_target_pairs={{0,16},{1,17},{2,18},{3,19},{4,20},{5,21},{6,22},{7,23},{8,24},{9,... | collective-permute-start | bytes 1376264 | tf_op jit(solution)/shard_map/ppermute | solution.py:30
  105.5 3.7 %copy-start = (f32[4096,128]{1,0:T(8,128)S(1)}, f32[4096,128]{1,0:T(8,128)}, u32[]{:S(2)}) copy-start(f32[4096,128]{1,0:T(8,128)} %b_ref.5) | copy-start | bytes 6291460

commit v12 on v9

--- a/solution.py
+++ b/solution.py
@@ -69,6 +69,12 @@
     return wide[:, 0:128] + (wide[:, 128:] + dot(lo_ref[...], vh))
 
 
+def apply_high(hi_ref, v):
+    vh, vl = split(v)
+    wide = dot(hi_ref[...], jnp.concatenate([vh, vl], axis=1))
+    return wide[:, 0:128] + wide[:, 128:]
+
+
 def lower_mask(d):
     i = lax.broadcasted_iota(jnp.int32, d.shape, 0)
     j = lax.broadcasted_iota(jnp.int32, d.shape, 1)
@@ -125,7 +131,7 @@
     w_out[...] = w_ref[...]
     block_product(ids, blocks, j, v_ref, w_out)
     w = w_out[...]
-    y = w + apply(lh_ref, ll_ref, w)
+    y = w + apply_high(lh_ref, w)
     y_ref[...] = jnp.where(ids[2] == j + 1, y, prior_ref[...])
     if j == 0:
         yb_ref[...] = y.astype(BF16)
@@ -166,7 +172,7 @@
     block_product(ids, blocks, 1, y1_ref, acc)
     block_product(ids, blocks, 2, y2_ref, acc)
     w = acc[...]
-    y3 = w + apply(lh, ll, w)
+    y3 = w + apply_high(lh, w)
     y_ref[...] = jnp.where(ids[2] == 3, y3, prior_ref[...])
     yb_ref[...] = y3.astype(BF16)
 
@@ -175,16 +181,16 @@
             other, x_ref[pl.ds(pl.multiple_of(row + (1 - h) * HB, HB), HB), :]
         )
 
-    x3 = apply(u3h, u3l, y3).astype(BF16)
+    x3 = apply_high(u3h, y3).astype(BF16)
     x_ref[2 * NB :, :] = x3
     x23_ref[NB:, :] = x3
     x3_ref[...] = x3
     t = y2.astype(F32) - product(p23[...], p23_other[...], 2 * NB)
-    x2 = apply(u2h, u2l, t).astype(BF16)
+    x2 = apply_high(u2h, t).astype(BF16)
     x_ref[NB : 2 * NB, :] = x2
     x23_ref[0:NB, :] = x2
     t = y1_ref[...].astype(F32) - product(p1[:, 0:HB], p1_other[:, 0:HB], NB) - product(p1[:, HB:], p1_other[:, HB:], 2 * NB)
-    x_ref[0:NB, :] = apply(u1h, u1l, t).astype(BF16)
+    x_ref[0:NB, :] = apply_high(u1h, t).astype(BF16)
 
 
 def hold_kernel(ids, top, bottom, *rest):

time: 111 us -> 111 us (level)
  the two profiles are of different devices: /device:TPU:1 before, /device:TPU:55 now
where the time goes in v12:
time: 111 us
  waiting for transfers between devices  53.1 us (48%)
  starting transfers between devices  30.4 us (27%)
  Pallas kernels  25.9 us (23%)
    ppermute x32, waiting for transfers between devices, send(): return lax.ppermute(value, ('row', 'col'), pairs(move))  53.1 us
    ppermute x32, starting transfers between devices, send(): return lax.ppermute(value, ('row', 'col'), pairs(move))  30.4 us
    pallas_call x15, Pallas kernels, call(): pl.pallas_call(kernel, grid_spec=pltpu.PrefetchScalarGridSpec(num_scalar_...  25.9 us
  transfers between devices with their start and end apart: 32, of which 8 were waited for; matrix products, arithmetic and copies ran while one was open for 0% of the time, Pallas kernels for 21%

profile of v12, /device:TPU:55, one launch (start us, length us, event | category | flops | bytes accessed | tf_op | source)
XLA Modules:
  0.0 110.9 jit_solution(6965262038709273316)
XLA Ops:
  0.0 1.0 slice.9.after_ref.b0.rest_0_
  1.0 0.6 collective-permute-start.6
  1.6 0.8 collective-permute-start.7
  2.4 1.8 %collective-permute-start.8 = (bf16[512,256]{1,0:T(8,128)(2,1)S(1)}, bf16[512,256]{1,0:T(8,128)(2,1)S(1)}, u32[]{:S(2)}, u32[]{:S(2)}) collective-permute-start(bf16[512,256]{1,0:T(8,128)(2,1)S(1)} %slice.9.after_ref.b0.rest_0_), channel_id=1, source_target_pairs={{0,32},{1,33},{2,34},{3,35},{4,36},{5,37},{6,38},{7,39},{8,40},{9,... | collective-permute-start | bytes 786440 | tf_op jit(solution)/shard_map/ppermute | solution.py:30
  4.2 0.1 pad_add_fusion.ids
  4.3 3.7 %shard_map.37 = (f32[512,128]{1,0:T(8,128)S(1)}, bf16[512,128]{1,0:T(8,128)(2,1)S(1)}, bf16[512,512]{1,0:T(8,128)(2,1)S(1)}, bf16[512,512]{1,0:T(8,128)(2,1)S(1)...) custom-call(s32[4]{0:T(128)S(1)} %pad_add_fusion.ids, ...), custom_call_target="tpu_custom_call" | custom-call | flops 1 | bytes 1 | tf_op jit(solution)/shard_map/pallas_call | solution.py:282
  8.0 0.7 collective-permute-start
  8.7 0.7 collective-permute-start.1
  9.4 5.7 %collective-permute-done.6.b1.rest_1_ = bf16[512,256]{1,0:T(8,128)(2,1)S(1)} collective-permute-done((bf16[512,256]{1,0:T(8,128)(2,1)S(1)}, bf16[512,256]{1,0:T(8,128)(2,1)S(1)}, u32[]{:S(2)}, u32[]{:S(2)}) %collective-permute-start.6) | collective-permute-done | bytes 262176 | tf_op jit(solution)/shard_map/ppermute | solution.py:30
  15.0 0.7 collective-permute-start.2
  15.7 0.0 collective-permute-done.8.b3.rest_3_
  15.7 0.7 shard_map.39
  16.4 1.6 %collective-permute-start.10 = (bf16[1536,256]{1,0:T(8,128)(2,1)S(1)}, bf16[1536,256]{1,0:T(8,128)(2,1)S(1)}, u32[]{:S(2)}, u32[]{:S(2)}) collective-permute-start(bf16[1536,256]{1,0:T(8,128)(2,1)S(1)} %get-tuple-element.47), channel_id=1, source_target_pairs={{0,16},{1,17},{2,18},{3,19},{4,20},{5,21},{6,22},{7,23},{8,24},{9,... | collective-permute-start | bytes 2359304 | tf_op jit(solution)/shard_map/ppermute | solution.py:30
  18.1 0.0 collective-permute-done.r1
  18.1 0.0 collective-permute-done.1.r2
  18.1 0.0 collective-permute-done.2.r3
  18.1 0.6 shard_map.38.own_ref.v0
  18.7 0.7 collective-permute-start.3
  19.4 1.3 %collective-permute-start.4 = (bf16[512,128]{1,0:T(8,128)(2,1)S(1)}, bf16[512,128]{1,0:T(8,128)(2,1)S(1)}, u32[]{:S(2)}, u32[]{:S(2)}) collective-permute-start(bf16[512,128]{1,0:T(8,128)(2,1)S(1)} %shard_map.38.own_ref.v0), channel_id=1, source_target_pairs={{0,2},{4,6},{8,10},{12,14},{16,18},{20,22},{24,26},{28,30},{32,34}... | collective-permute-start | bytes 393224 | tf_op jit(solution)/shard_map/ppermute | solution.py:30
  20.7 0.1 collective-permute-start.9
  20.8 0.7 collective-permute-start.5
  21.5 0.0 collective-permute-done.3.rest_0_.e1
  21.5 0.7 collective-permute-start.14
  22.2 6.2 %collective-permute-done.4.rest_1_.e2 = bf16[512,128]{1,0:T(8,128)(2,1)S(1)} collective-permute-done((bf16[512,128]{1,0:T(8,128)(2,1)S(1)}, bf16[512,128]{1,0:T(8,128)(2,1)S(1)}, u32[]{:S(2)}, u32[]{:S(2)}) %collective-permute-start.4) | collective-permute-done | bytes 131104 | tf_op jit(solution)/shard_map/ppermute | solution.py:30
  28.4 0.7 collective-permute-start.13
  29.1 0.1 fusion
  29.2 0.0 collective-permute-done.5.rest_2_.e3
  29.2 0.0 collective-permute-done.10.rest_5_.rest_3_
  29.2 0.7 shard_map.43
  29.9 2.3 %collective-permute-start.17 = (bf16[1792,256]{1,0:T(8,128)(2,1)S(1)}, bf16[1792,256]{1,0:T(8,128)(2,1)S(1)}, u32[]{:S(2)}, u32[]{:S(2)}) collective-permute-start(bf16[1792,256]{1,0:T(8,128)(2,1)S(1)} %get-tuple-element.63), channel_id=1, source_target_pairs={{0,32},{1,33},{2,34},{3,35},{4,36},{5,37},{6,38},{7,39},{8,40},{9,... | collective-permute-start | bytes 2752520 | tf_op jit(solution)/shard_map/ppermute | solution.py:30
  32.2 0.0 collective-permute-start.18
  32.2 2.6 %shard_map.40 = (bf16[512,128]{1,0:T(8,128)(2,1)}, f32[512,128]{1,0:T(8,128)S(1)}, f32[512,128]{1,0:T(8,128)S(1)}, bf16[512,128]{1,0:T(8,128)(2,1)S(1)}) custom-call(s32[4]{0:T(128)S(1)} %pad_add_fusion.ids, f32[4096,128]{1,0:T(8,128)} %b_ref.5, bf16[512,128]{1,0:T(8,128)(2,1)S(1)} %shard_map.38.own_ref.v0, f32[512,128]{1,0:T(8,128)S(1)} %get-tuple-element.44.prior_ref, ...), custom_call_target="tpu_custom_call" | custom-call | flops 1 | bytes 1 | tf_op jit(solution)/shard_map/pallas_call | solution.py:282
  34.8 0.7 collective-permute-start.11
  35.5 1.7 %shard_map.41 = (bf16[512,128]{1,0:T(8,128)(2,1)}, f32[512,128]{1,0:T(8,128)}, f32[512,128]{1,0:T(8,128)S(1)}, bf16[1024,128]{1,0:T(8,128)(2,1)S(1)}) custom-call(s32[4]{0:T(128)S(1)} %pad_add_fusion.ids, f32[512,128]{1,0:T(8,128)S(1)} %get-tuple-element.48.w_ref, bf16[512,128]{1,0:T(8,128)(2,1)S(1)} %get-tuple-element.49.own_ref, ...), custom_call_target="tpu_custom_call" | custom-call | flops 1 | bytes 1 | tf_op jit(solution)/shard_map/pallas_call | solution.py:282
  37.2 0.7 collective-permute-start.12
  37.9 0.6 shard_map.42
  38.5 1.2 %collective-permute-start.15 = (bf16[512,256]{1,0:T(8,128)(2,1)S(1)}, bf16[512,256]{1,0:T(8,128)(2,1)S(1)}, u32[]{:S(2)}, u32[]{:S(2)}) collective-permute-start(bf16[512,256]{1,0:T(8,128)(2,1)S(1)} %get-tuple-element.61.p23), channel_id=1, source_target_pairs={{0,16},{1,17},{2,18},{3,19},{4,20},{5,21},{6,22},{7,23},{8,24},{9,... | collective-permute-start | bytes 786440 | tf_op jit(solution)/shard_map/ppermute | solution.py:30
  39.6 0.1 collective-permute-start.16
  39.7 0.7 shard_map.45
  40.4 3.0 %collective-permute-start.22 = (bf16[1792,256]{1,0:T(8,128)(2,1)S(1)}, bf16[1792,256]{1,0:T(8,128)(2,1)S(1)}, u32[]{:S(2)}, u32[]{:S(2)}) collective-permute-start(bf16[1792,256]{1,0:T(8,128)(2,1)S(1)} %get-tuple-element.71), channel_id=1, source_target_pairs={{0,32},{1,33},{2,34},{3,35},{4,36},{5,37},{6,38},{7,39},{8,40},{9,... | collective-permute-start | bytes 2752520 | tf_op jit(solution)/shard_map/ppermute | solution.py:30
  43.4 7.6 %collective-permute-done.17.rest_6_.rest_3_ = bf16[1792,256]{1,0:T(8,128)(2,1)S(1)} collective-permute-done((bf16[1792,256]{1,0:T(8,128)(2,1)S(1)}, bf16[1792,256]{1,0:T(8,128)(2,1)S(1)}, u32[]{:S(2)}, u32[]{:S(2)}) %collective-permute-start.17) | collective-permute-done | bytes 917536 | tf_op jit(solution)/shard_map/ppermute | solution.py:30
  51.1 3.1 %collective-permute-done.18.rest_7_.rest_1_ = bf16[1792,256]{1,0:T(8,128)(2,1)S(1)} collective-permute-done((bf16[1792,256]{1,0:T(8,128)(2,1)S(1)}, bf16[1792,256]{1,0:T(8,128)(2,1)S(1)}, u32[]{:S(2)}, u32[]{:S(2)}) %collective-permute-start.18) | collective-permute-done | bytes 917536 | tf_op jit(solution)/shard_map/ppermute | solution.py:30
  54.2 3.4 %shard_map.44 = (bf16[512,128]{1,0:T(8,128)(2,1)S(1)}, bf16[512,128]{1,0:T(8,128)(2,1)S(1)}, f32[512,128]{1,0:T(8,128)S(1)}, bf16[512,128]{1,0:T(8,128)(2,1)S(1)...) custom-call(s32[4]{0:T(128)S(1)} %pad_add_fusion.ids, ...), custom_call_target="tpu_custom_call" | custom-call | flops 1 | bytes 1 | tf_op jit(solution)/shard_map/pallas_call | solution.py:282
  57.6 0.7 collective-permute-start.20
  58.3 0.9 collective-permute-start.19
  59.2 0.7 collective-permute-start.21
  59.9 0.1 collective-permute-start.30
  60.0 2.7 %collective-permute-start.28 = (bf16[1792,256]{1,0:T(8,128)(2,1)S(1)}, bf16[1792,256]{1,0:T(8,128)(2,1)S(1)}, u32[]{:S(2)}, u32[]{:S(2)}) collective-permute-start(bf16[1792,256]{1,0:T(8,128)(2,1)S(1)} %collective-permute-done.17.rest_6_.rest_3_), channel_id=1, source_target_pairs={{0,32},{1,33},{2,34},{3,35},{4,36},{5,37},{6,38},{7,39},{8,40},{9,... | collective-permute-start | bytes 2752520 | tf_op jit(solution)/shard_map/ppermute | solution.py:30
  62.6 8.1 %collective-permute-done.22.rest_0_.rest_3_ = bf16[1792,256]{1,0:T(8,128)(2,1)S(1)} collective-permute-done((bf16[1792,256]{1,0:T(8,128)(2,1)S(1)}, bf16[1792,256]{1,0:T(8,128)(2,1)S(1)}, u32[]{:S(2)}, u32[]{:S(2)}) %collective-permute-start.22) | collective-permute-done | bytes 917536 | tf_op jit(solution)/shard_map/ppermute | solution.py:30
  70.8 3.1 %collective-permute-done.23.rest_1_ = bf16[1792,256]{1,0:T(8,128)(2,1)S(1)} collective-permute-done((bf16[1792,256]{1,0:T(8,128)(2,1)S(1)}, bf16[1792,256]{1,0:T(8,128)(2,1)S(1)}, u32[]{:S(2)}, u32[]{:S(2)}) %collective-permute-start.23) | collective-permute-done | bytes 917536 | tf_op jit(solution)/shard_map/ppermute | solution.py:30
  73.9 0.7 shard_map.46.late
  74.5 0.7 collective-permute-start.24
  75.2 1.3 %collective-permute-start.25 = (bf16[1536,128]{1,0:T(8,128)(2,1)S(1)}, bf16[1536,128]{1,0:T(8,128)(2,1)S(1)}, u32[]{:S(2)}, u32[]{:S(2)}) collective-permute-start(bf16[1536,128]{1,0:T(8,128)(2,1)S(1)} %shard_map.46.late), channel_id=1, source_target_pairs={{0,2},{4,6},{8,10},{12,14},{16,18},{20,22},{24,26},{28,30},{32,34}... | collective-permute-start | bytes 1179656 | tf_op jit(solution)/shard_map/ppermute | solution.py:30
  76.5 0.7 collective-permute-start.26
  77.2 18.0 %collective-permute-done.25.s2 = bf16[1536,128]{1,0:T(8,128)(2,1)S(1)} collective-permute-done((bf16[1536,128]{1,0:T(8,128)(2,1)S(1)}, bf16[1536,128]{1,0:T(8,128)(2,1)S(1)}, u32[]{:S(2)}, u32[]{:S(2)}) %collective-permute-start.25) | collective-permute-done | bytes 393248 | tf_op jit(solution)/shard_map/ppermute | solution.py:30
  95.2 1.0 shard_map.47
  96.2 3.2 %collective-permute-start.27 = (bf16[1024,128]{1,0:T(8,128)(2,1)S(1)}, bf16[1024,128]{1,0:T(8,128)(2,1)S(1)}, u32[]{:S(2)}, u32[]{:S(2)}) collective-permute-start(bf16[1024,128]{1,0:T(8,128)(2,1)S(1)} %get-tuple-element.76), channel_id=1, source_target_pairs={{0,16},{1,17},{2,18},{3,19},{4,20},{5,21},{6,22},{7,23},{8,24},{9,... | collective-permute-start | bytes 786440 | tf_op jit(solution)/shard_map/ppermute | solution.py:30
  99.4 1.2 %collective-permute-done.27.other_ref = bf16[1024,128]{1,0:T(8,128)(2,1)S(1)} collective-permute-done((bf16[1024,128]{1,0:T(8,128)(2,1)S(1)}, bf16[1024,128]{1,0:T(8,128)(2,1)S(1)}, u32[]{:S(2)}, u32[]{:S(2)}) %collective-permute-start.27) | collective-permute-done | bytes 262176 | tf_op jit(solution)/shard_map/ppermute | solution.py:30
  100.6 1.7 %shard_map.50 = (f32[1792,128]{1,0:T(8,128)S(1)}, bf16[1792,128]{1,0:T(8,128)(2,1)S(1)}) custom-call(s32[4]{0:T(128)S(1)} %pad_add_fusion.ids, bf16[1024,128]{1,0:T(8,128)(2,1)S(1)} %get-tuple-element.75.mine_ref, bf16[1024,128]{1,0:T(8,128)(2,1)S(1)} %collective-permute-done.27.other_ref, bf16[1792,256]{1,0:T(8,128)(2,1)S(1)} %get-tuple-element.81.bottom.rest_0_, ...), custom_call_target="tpu_custom_call" | custom-call | flops 1 | bytes 1 | tf_op jit(solution)/shard_map/pallas_call | solution.py:282
  102.3 0.5 collective-permute-start.31
  102.8 1.7 %shard_map.49 = (f32[1792,128]{1,0:T(8,128)S(1)}, bf16[1792,128]{1,0:T(8,128)(2,1)S(1)}) custom-call(s32[4]{0:T(128)S(1)} %pad_add_fusion.ids, bf16[1024,128]{1,0:T(8,128)(2,1)S(1)} %get-tuple-element.75.mine_ref, bf16[1024,128]{1,0:T(8,128)(2,1)S(1)} %collective-permute-done.27.other_ref, bf16[1792,256]{1,0:T(8,128)(2,1)S(1)} %get-tuple-element.82.top.rest_0_, ...), custom_call_target="tpu_custom_call" | custom-call | flops 1 | bytes 1 | tf_op jit(solution)/shard_map/pallas_call | solution.py:282
  104.5 0.2 collective-permute-start.29
  104.7 3.7 %shard_map.48.out_in = f32[4096,128]{1,0:T(8,128)} custom-call(s32[4]{0:T(128)S(1)} %pad_add_fusion.ids, f32[4096,128]{1,0:T(8,128)} %b_ref.5, bf16[2048,128]{1,0:T(8,128)(2,1)S(1)} %get-tuple-element.73.v_ref, f32[512,128]{1,0:T(8,128)S(1)} %get-tuple-element.74.own_ref, bf16[512,512]{1,0:T(8,128)(2,1)S(1)} %get-tuple-element.53.u3h.uh_ref, ...), custom_call_target="tpu_custom_call" | custom-call | flops 1 | bytes 1 | tf_op jit(solution)/shard_map/pallas_call | solution.py:282
  108.5 2.4 %shard_map.51 = f32[4096,128]{1,0:T(8,128)} custom-call(s32[4]{0:T(128)S(1)} %pad_add_fusion.ids, f32[4096,128]{1,0:T(8,128)} %shard_map.48.out_in, f32[4096,128]{1,0:T(8,128)S(1)} %copy-done, f32[1792,128]{1,0:T(8,128)S(1)} %get-tuple-element.77.own_t, bf16[1792,128]{1,0:T(8,128)(2,1)S(1)} %collective-permute-done.29.part_t, ...), custom_call_target="tpu_custom_call", output_to_operand_aliasing={{}: (1, {})} | custom-call | flops 1 | bytes 1 | tf_op jit(solution)/shard_map/pallas_call | solution.py:282
  (22 shorter events, 0.1 us)
Async XLA Ops:
  1.0 14.1 %collective-permute-start.6 = (bf16[512,256]{1,0:T(8,128)(2,1)S(1)}, bf16[512,256]{1,0:T(8,128)(2,1)S(1)}, u32[]{:S(2)}, u32[]{:S(2)}) collective-permute-start(bf16[512,256]{1,0:T(8,128)(2,1)S(1)} %slice.9.after_ref.b0.rest_0_), channel_id=1, source_target_pairs={{0,96},{1,97},{2,98},{3,99},{4,100},{5,101},{6,102},{7,103},{8,104... | collective-permute-start | bytes 786440 | tf_op jit(solution)/shard_map/ppermute | solution.py:30
  1.6 14.1 %collective-permute-start.7 = (bf16[512,256]{1,0:T(8,128)(2,1)S(1)}, bf16[512,256]{1,0:T(8,128)(2,1)S(1)}, u32[]{:S(2)}, u32[]{:S(2)}) collective-permute-start(bf16[512,256]{1,0:T(8,128)(2,1)S(1)} %slice.9.after_ref.b0.rest_0_), channel_id=1, source_target_pairs={{0,64},{1,65},{2,66},{3,67},{4,68},{5,69},{6,70},{7,71},{8,72},{9,... | collective-permute-start | bytes 786440 | tf_op jit(solution)/shard_map/ppermute | solution.py:30
  2.4 13.3 %collective-permute-start.8 = (bf16[512,256]{1,0:T(8,128)(2,1)S(1)}, bf16[512,256]{1,0:T(8,128)(2,1)S(1)}, u32[]{:S(2)}, u32[]{:S(2)}) collective-permute-start(bf16[512,256]{1,0:T(8,128)(2,1)S(1)} %slice.9.after_ref.b0.rest_0_), channel_id=1, source_target_pairs={{0,32},{1,33},{2,34},{3,35},{4,36},{5,37},{6,38},{7,39},{8,40},{9,... | collective-permute-start | bytes 786440 | tf_op jit(solution)/shard_map/ppermute | solution.py:30
  4.3 24.7 %copy-start.1 = (bf16[4096,256]{1,0:T(8,128)(2,1)S(1)}, bf16[4096,256]{1,0:T(8,128)(2,1)}, u32[]{:S(2)}) copy-start(bf16[4096,256]{1,0:T(8,128)(2,1)} %param.4) | copy-start | bytes 6291460
  8.0 10.1 %collective-permute-start = (bf16[512,128]{1,0:T(8,128)(2,1)S(1)}, bf16[512,128]{1,0:T(8,128)(2,1)S(1)}, u32[]{:S(2)}, u32[]{:S(2)}) collective-permute-start(bf16[512,128]{1,0:T(8,128)(2,1)S(1)} %get-tuple-element.43.own_ref), channel_id=1, source_target_pairs={{0,4},{16,20},{32,36},{48,52},{64,68},{80,84},{96,100},{112,116}} | collective-permute-start | bytes 393224 | tf_op jit(solution)/shard_map/ppermute | solution.py:30
  8.7 9.4 %collective-permute-start.1 = (bf16[512,128]{1,0:T(8,128)(2,1)S(1)}, bf16[512,128]{1,0:T(8,128)(2,1)S(1)}, u32[]{:S(2)}, u32[]{:S(2)}) collective-permute-start(bf16[512,128]{1,0:T(8,128)(2,1)S(1)} %get-tuple-element.43.own_ref), channel_id=1, source_target_pairs={{0,8},{16,24},{32,40},{48,56},{64,72},{80,88},{96,104},{112,120}} | collective-permute-start | bytes 393224 | tf_op jit(solution)/shard_map/ppermute | solution.py:30
  15.0 3.0 %collective-permute-start.2 = (bf16[512,128]{1,0:T(8,128)(2,1)S(1)}, bf16[512,128]{1,0:T(8,128)(2,1)S(1)}, u32[]{:S(2)}, u32[]{:S(2)}) collective-permute-start(bf16[512,128]{1,0:T(8,128)(2,1)S(1)} %get-tuple-element.43.own_ref), channel_id=1, source_target_pairs={{0,12},{16,28},{32,44},{48,60},{64,76},{80,92},{96,108},{112,124}} | collective-permute-start | bytes 393224 | tf_op jit(solution)/shard_map/ppermute | solution.py:30
  16.4 12.8 %collective-permute-start.10 = (bf16[1536,256]{1,0:T(8,128)(2,1)S(1)}, bf16[1536,256]{1,0:T(8,128)(2,1)S(1)}, u32[]{:S(2)}, u32[]{:S(2)}) collective-permute-start(bf16[1536,256]{1,0:T(8,128)(2,1)S(1)} %get-tuple-element.47), channel_id=1, source_target_pairs={{0,16},{1,17},{2,18},{3,19},{4,20},{5,21},{6,22},{7,23},{8,24},{9,... | collective-permute-start | bytes 2359304 | tf_op jit(solution)/shard_map/ppermute | solution.py:30
  18.7 2.8 %collective-permute-start.3 = (bf16[512,128]{1,0:T(8,128)(2,1)S(1)}, bf16[512,128]{1,0:T(8,128)(2,1)S(1)}, u32[]{:S(2)}, u32[]{:S(2)}) collective-permute-start(bf16[512,128]{1,0:T(8,128)(2,1)S(1)} %shard_map.38.own_ref.v0), channel_id=1, source_target_pairs={{0,1},{4,5},{8,9},{12,13},{16,17},{20,21},{24,25},{28,29},{32,33},... | collective-permute-start | bytes 393224 | tf_op jit(solution)/shard_map/ppermute | solution.py:30
  19.4 9.0 %collective-permute-start.4 = (bf16[512,128]{1,0:T(8,128)(2,1)S(1)}, bf16[512,128]{1,0:T(8,128)(2,1)S(1)}, u32[]{:S(2)}, u32[]{:S(2)}) collective-permute-start(bf16[512,128]{1,0:T(8,128)(2,1)S(1)} %shard_map.38.own_ref.v0), channel_id=1, source_target_pairs={{0,2},{4,6},{8,10},{12,14},{16,18},{20,22},{24,26},{28,30},{32,34}... | collective-permute-start | bytes 393224 | tf_op jit(solution)/shard_map/ppermute | solution.py:30
  20.7 11.6 %collective-permute-start.9 = (bf16[512,256]{1,0:T(8,128)(2,1)S(1)}, bf16[512,256]{1,0:T(8,128)(2,1)S(1)}, u32[]{:S(2)}, u32[]{:S(2)}) collective-permute-start(bf16[512,256]{1,0:T(8,128)(2,1)S(1)} %slice.9.after_ref.b0.rest_0_), channel_id=1, source_target_pairs={{0,16},{1,17},{2,18},{3,19},{4,20},{5,21},{6,22},{7,23},{8,24},{9,... | collective-permute-start | bytes 786440 | tf_op jit(solution)/shard_map/ppermute | solution.py:30
  20.8 8.4 %collective-permute-start.5 = (bf16[512,128]{1,0:T(8,128)(2,1)S(1)}, bf16[512,128]{1,0:T(8,128)(2,1)S(1)}, u32[]{:S(2)}, u32[]{:S(2)}) collective-permute-start(bf16[512,128]{1,0:T(8,128)(2,1)S(1)} %shard_map.38.own_ref.v0), channel_id=1, source_target_pairs={{0,3},{4,7},{8,11},{12,15},{16,19},{20,23},{24,27},{28,31},{32,35}... | collective-permute-start | bytes 393224 | tf_op jit(solution)/shard_map/ppermute | solution.py:30
  21.5 16.4 %collective-permute-start.14 = (bf16[512,512]{1,0:T(8,128)(2,1)S(1)}, bf16[512,512]{1,0:T(8,128)(2,1)S(1)}, u32[]{:S(2)}, u32[]{:S(2)}) collective-permute-start(bf16[512,512]{1,0:T(8,128)(2,1)S(1)} %get-tuple-element.60), channel_id=1, source_target_pairs={{4,12},{20,28},{36,44},{52,60},{68,76},{84,92},{100,108},{116,124}} | collective-permute-start | bytes 1572872 | tf_op jit(solution)/shard_map/ppermute | solution.py:30
  28.4 9.5 %collective-permute-start.13 = (bf16[512,256]{1,0:T(8,128)(2,1)S(1)}, bf16[512,256]{1,0:T(8,128)(2,1)S(1)}, u32[]{:S(2)}, u32[]{:S(2)}) collective-permute-start(bf16[512,256]{1,0:T(8,128)(2,1)S(1)} %get-tuple-element.59), channel_id=1, source_target_pairs={{8,12},{24,28},{40,44},{56,60},{72,76},{88,92},{104,108},{120,124}} | collective-permute-start | bytes 786440 | tf_op jit(solution)/shard_map/ppermute | solution.py:30
  29.9 21.2 %collective-permute-start.17 = (bf16[1792,256]{1,0:T(8,128)(2,1)S(1)}, bf16[1792,256]{1,0:T(8,128)(2,1)S(1)}, u32[]{:S(2)}, u32[]{:S(2)}) collective-permute-start(bf16[1792,256]{1,0:T(8,128)(2,1)S(1)} %get-tuple-element.63), channel_id=1, source_target_pairs={{0,32},{1,33},{2,34},{3,35},{4,36},{5,37},{6,38},{7,39},{8,40},{9,... | collective-permute-start | bytes 2752520 | tf_op jit(solution)/shard_map/ppermute | solution.py:30
  32.2 22.0 %collective-permute-start.18 = (bf16[1792,256]{1,0:T(8,128)(2,1)S(1)}, bf16[1792,256]{1,0:T(8,128)(2,1)S(1)}, u32[]{:S(2)}, u32[]{:S(2)}) collective-permute-start(bf16[1792,256]{1,0:T(8,128)(2,1)S(1)} %get-tuple-element.64), channel_id=1, source_target_pairs={{0,96},{1,97},{2,98},{3,99},{4,100},{5,101},{6,102},{7,103},{8,104... | collective-permute-start | bytes 2752520 | tf_op jit(solution)/shard_map/ppermute | solution.py:30
  34.8 0.7 collective-permute-start.11
  37.2 2.6 %collective-permute-start.12 = (bf16[1024,128]{1,0:T(8,128)(2,1)S(1)}, bf16[1024,128]{1,0:T(8,128)(2,1)S(1)}, u32[]{:S(2)}, u32[]{:S(2)}) collective-permute-start(bf16[1024,128]{1,0:T(8,128)(2,1)S(1)} %get-tuple-element.51.after_ref.y12_ref), channel_id=1, source_target_pairs={{8,12},{24,28},{40,44},{56,60},{72,76},{88,92},{104,108},{120,124}} | collective-permute-start | bytes 786440 | tf_op jit(solution)/shard_map/ppermute | solution.py:30
  38.5 5.0 %collective-permute-start.15 = (bf16[512,256]{1,0:T(8,128)(2,1)S(1)}, bf16[512,256]{1,0:T(8,128)(2,1)S(1)}, u32[]{:S(2)}, u32[]{:S(2)}) collective-permute-start(bf16[512,256]{1,0:T(8,128)(2,1)S(1)} %get-tuple-element.61.p23), channel_id=1, source_target_pairs={{0,16},{1,17},{2,18},{3,19},{4,20},{5,21},{6,22},{7,23},{8,24},{9,... | collective-permute-start | bytes 786440 | tf_op jit(solution)/shard_map/ppermute | solution.py:30
  39.6 3.8 %collective-permute-start.16 = (bf16[512,512]{1,0:T(8,128)(2,1)S(1)}, bf16[512,512]{1,0:T(8,128)(2,1)S(1)}, u32[]{:S(2)}, u32[]{:S(2)}) collective-permute-start(bf16[512,512]{1,0:T(8,128)(2,1)S(1)} %get-tuple-element.62.p1), channel_id=1, source_target_pairs={{0,16},{1,17},{2,18},{3,19},{4,20},{5,21},{6,22},{7,23},{8,24},{9,... | collective-permute-start | bytes 1572872 | tf_op jit(solution)/shard_map/ppermute | solution.py:30
  40.4 30.4 %collective-permute-start.22 = (bf16[1792,256]{1,0:T(8,128)(2,1)S(1)}, bf16[1792,256]{1,0:T(8,128)(2,1)S(1)}, u32[]{:S(2)}, u32[]{:S(2)}) collective-permute-start(bf16[1792,256]{1,0:T(8,128)(2,1)S(1)} %get-tuple-element.71), channel_id=1, source_target_pairs={{0,32},{1,33},{2,34},{3,35},{4,36},{5,37},{6,38},{7,39},{8,40},{9,... | collective-permute-start | bytes 2752520 | tf_op jit(solution)/shard_map/ppermute | solution.py:30
  43.4 30.4 %collective-permute-start.23 = (bf16[1792,256]{1,0:T(8,128)(2,1)S(1)}, bf16[1792,256]{1,0:T(8,128)(2,1)S(1)}, u32[]{:S(2)}, u32[]{:S(2)}) collective-permute-start(bf16[1792,256]{1,0:T(8,128)(2,1)S(1)} %get-tuple-element.72), channel_id=1, source_target_pairs={{0,96},{1,97},{2,98},{3,99},{4,100},{5,101},{6,102},{7,103},{8,104... | collective-permute-start | bytes 2752520 | tf_op jit(solution)/shard_map/ppermute | solution.py:30
  57.6 2.3 %collective-permute-start.20 = (bf16[1024,128]{1,0:T(8,128)(2,1)S(1)}, bf16[1024,128]{1,0:T(8,128)(2,1)S(1)}, u32[]{:S(2)}, u32[]{:S(2)}) collective-permute-start(bf16[1024,128]{1,0:T(8,128)(2,1)S(1)} %get-tuple-element.66), channel_id=1, source_target_pairs={{12,4},{28,20},{44,36},{60,52},{76,68},{92,84},{108,100},{124,116}} | collective-permute-start | bytes 786440 | tf_op jit(solution)/shard_map/ppermute | solution.py:30
  58.3 15.6 %collective-permute-start.19 = (bf16[1536,128]{1,0:T(8,128)(2,1)S(1)}, bf16[1536,128]{1,0:T(8,128)(2,1)S(1)}, u32[]{:S(2)}, u32[]{:S(2)}) collective-permute-start(bf16[1536,128]{1,0:T(8,128)(2,1)S(1)} %get-tuple-element.65), channel_id=1, source_target_pairs={{12,0},{28,16},{44,32},{60,48},{76,64},{92,80},{108,96},{124,112}} | collective-permute-start | bytes 1179656 | tf_op jit(solution)/shard_map/ppermute | solution.py:30
  59.2 0.7 collective-permute-start.21
  59.9 39.5 %collective-permute-start.30 = (bf16[1792,256]{1,0:T(8,128)(2,1)S(1)}, bf16[1792,256]{1,0:T(8,128)(2,1)S(1)}, u32[]{:S(2)}, u32[]{:S(2)}) collective-permute-start(bf16[1792,256]{1,0:T(8,128)(2,1)S(1)} %collective-permute-done.18.rest_7_.rest_1_), channel_id=1, source_target_pairs={{0,96},{1,97},{2,98},{3,99},{4,100},{5,101},{6,102},{7,103},{8,104... | collective-permute-start | bytes 2752520 | tf_op jit(solution)/shard_map/ppermute | solution.py:30
  60.0 42.8 %collective-permute-start.28 = (bf16[1792,256]{1,0:T(8,128)(2,1)S(1)}, bf16[1792,256]{1,0:T(8,128)(2,1)S(1)}, u32[]{:S(2)}, u32[]{:S(2)}) collective-permute-start(bf16[1792,256]{1,0:T(8,128)(2,1)S(1)} %collective-permute-done.17.rest_6_.rest_3_), channel_id=1, source_target_pairs={{0,32},{1,33},{2,34},{3,35},{4,36},{5,37},{6,38},{7,39},{8,40},{9,... | collective-permute-start | bytes 2752520 | tf_op jit(solution)/shard_map/ppermute | solution.py:30
  74.5 2.7 %collective-permute-start.24 = (bf16[1536,128]{1,0:T(8,128)(2,1)S(1)}, bf16[1536,128]{1,0:T(8,128)(2,1)S(1)}, u32[]{:S(2)}, u32[]{:S(2)}) collective-permute-start(bf16[1536,128]{1,0:T(8,128)(2,1)S(1)} %shard_map.46.late), channel_id=1, source_target_pairs={{0,1},{4,5},{8,9},{12,13},{16,17},{20,21},{24,25},{28,29},{32,33},... | collective-permute-start | bytes 1179656 | tf_op jit(solution)/shard_map/ppermute | solution.py:30
  75.2 20.0 %collective-permute-start.25 = (bf16[1536,128]{1,0:T(8,128)(2,1)S(1)}, bf16[1536,128]{1,0:T(8,128)(2,1)S(1)}, u32[]{:S(2)}, u32[]{:S(2)}) collective-permute-start(bf16[1536,128]{1,0:T(8,128)(2,1)S(1)} %shard_map.46.late), channel_id=1, source_target_pairs={{0,2},{4,6},{8,10},{12,14},{16,18},{20,22},{24,26},{28,30},{32,34}... | collective-permute-start | bytes 1179656 | tf_op jit(solution)/shard_map/ppermute | solution.py:30
  76.5 18.7 %collective-permute-start.26 = (bf16[1536,128]{1,0:T(8,128)(2,1)S(1)}, bf16[1536,128]{1,0:T(8,128)(2,1)S(1)}, u32[]{:S(2)}, u32[]{:S(2)}) collective-permute-start(bf16[1536,128]{1,0:T(8,128)(2,1)S(1)} %shard_map.46.late), channel_id=1, source_target_pairs={{0,3},{4,7},{8,11},{12,15},{16,19},{20,23},{24,27},{28,31},{32,35}... | collective-permute-start | bytes 1179656 | tf_op jit(solution)/shard_map/ppermute | solution.py:30
  96.2 4.3 %collective-permute-start.27 = (bf16[1024,128]{1,0:T(8,128)(2,1)S(1)}, bf16[1024,128]{1,0:T(8,128)(2,1)S(1)}, u32[]{:S(2)}, u32[]{:S(2)}) collective-permute-start(bf16[1024,128]{1,0:T(8,128)(2,1)S(1)} %get-tuple-element.76), channel_id=1, source_target_pairs={{0,16},{1,17},{2,18},{3,19},{4,20},{5,21},{6,22},{7,23},{8,24},{9,... | collective-permute-start | bytes 786440 | tf_op jit(solution)/shard_map/ppermute | solution.py:30
  102.3 6.1 %collective-permute-start.31 = (bf16[1792,128]{1,0:T(8,128)(2,1)S(1)}, bf16[1792,128]{1,0:T(8,128)(2,1)S(1)}, u32[]{:S(2)}, u32[]{:S(2)}) collective-permute-start(bf16[1792,128]{1,0:T(8,128)(2,1)S(1)} %get-tuple-element.80), channel_id=1, source_target_pairs={{0,16},{1,17},{2,18},{3,19},{4,20},{5,21},{6,22},{7,23},{8,24},{9,... | collective-permute-start | bytes 1376264 | tf_op jit(solution)/shard_map/ppermute | solution.py:30
  104.5 3.9 %collective-permute-start.29 = (bf16[1792,128]{1,0:T(8,128)(2,1)S(1)}, bf16[1792,128]{1,0:T(8,128)(2,1)S(1)}, u32[]{:S(2)}, u32[]{:S(2)}) collective-permute-start(bf16[1792,128]{1,0:T(8,128)(2,1)S(1)} %get-tuple-element.78), channel_id=1, source_target_pairs={{0,16},{1,17},{2,18},{3,19},{4,20},{5,21},{6,22},{7,23},{8,24},{9,... | collective-permute-start | bytes 1376264 | tf_op jit(solution)/shard_map/ppermute | solution.py:30
  104.7 3.7 %copy-start = (f32[4096,128]{1,0:T(8,128)S(1)}, f32[4096,128]{1,0:T(8,128)}, u32[]{:S(2)}) copy-start(f32[4096,128]{1,0:T(8,128)} %b_ref.5) | copy-start | bytes 6291460
